TPU v7x, 32 devices: a whole 2x2x4 slice. The times are simulated.
32 devices in a mesh: seq: 8 (over z, x), head: 4 (over y, core).
Axes of the slice: x: 2, y: 2, z: 4, core: 2. Of those that a mesh axis runs over, the one named last changes fastest.
Arguments:
- text_in: float32 [8192, 512], P(('seq', 'head')), may hold values from -1.7 to 1.7
- mel_in: float32 [8192, 1024], P(('seq', 'head')), may hold values from -1.7 to 1.7
- time_embed: float32 [8, 1024], replicated, may hold values from -2 to 2
- lengths: int32 [8], replicated, may hold values from 1 to 2816, 8192 in all
- text_mask: int32 [8192], P(('seq', 'head')), may hold values 0 or 1
- conv_weight: float32 [7, 512], replicated, may hold values from -2 to 2
- norm_gain: float32 [512], replicated, may hold values from 0.5 to 1.5
- norm_bias: float32 [512], replicated, may hold values from -0.85 to 0.85
- expand_weight: bfloat16 [512, 1024], P(None, 'head'), may hold values from -0.25 to 0.25
- grn_gamma: float32 [1024], P('head'), may hold values from -0.85 to 0.85
- grn_beta: float32 [1024], P('head'), may hold values from -0.85 to 0.85
- shrink_weight: bfloat16 [1024, 512], P('head'), may hold values from -0.1875 to 0.1875
- join_weight: bfloat16 [512, 1024], replicated, may hold values from -0.25 to 0.25
- modulation: bfloat16 [1024, 6144], P(None, 'head'), may hold values from -0.1875 to 0.1875
- qkv_weight: bfloat16 [1024, 3, 1024], P(None, None, 'head'), may hold values from -0.1875 to 0.1875
- out_weight: bfloat16 [1024, 1024], P('head'), may hold values from -0.75 to 0.75
- up_weight: bfloat16 [1024, 2048], P(None, 'head'), may hold values from -0.1875 to 0.1875
- down_weight: bfloat16 [2048, 1024], P('head'), may hold values from -0.125 to 0.125
- cotangent: float32 [8192, 1024], P(('seq', 'head')), may hold values from -0.5 to 0.5
Outputs:
- transformer_layer_output: float32 [8192, 1024], P(('seq', 'head'))
- grad_text: float32 [8192, 512], P(('seq', 'head'))
- grad_mel: float32 [8192, 1024], P(('seq', 'head'))
- grad_conv: float32 [7, 512], P(None, ('seq', 'head'))
- grad_gain: float32 [512], P(('seq', 'head'))
- grad_bias: float32 [512], P(('seq', 'head'))
- grad_expand: float32 [512, 1024], P('seq', 'head')
- grad_gamma: float32 [1024], P('head')
- grad_beta: float32 [1024], P('head')
- grad_shrink: float32 [1024, 512], P('head', 'seq')
- grad_join: float32 [512, 1024], P(None, ('seq', 'head'))
- grad_modulation: float32 [1024, 6144], P(None, ('seq', 'head'))
- grad_qkv: float32 [1024, 3, 1024], P('seq', None, 'head')
- grad_out: float32 [1024, 1024], P('head', 'seq')
- grad_up: float32 [1024, 2048], P('seq', 'head')
- grad_down: float32 [2048, 1024], P('head', 'seq')
Inputs may be any that keep to these rules, and one draw needn't show every extreme that they name: The lengths sum to 8192 and the longest is exactly 2816.
All inputs are finite; a program needn't handle non-finite values. No bound on the sum of `text_mask` on one device may be relied on, other than what follows from the above.
Results may differ from a plain program's by a relative error of at most 0.022.
The roundings to bfloat16 on the way count: a program that leaves them out, or rounds other values in their place, can miss the bound.
Values may be sent and summed in bfloat16 or wider, within the bound.
A program may use at most 512 MiB of HBM per device.

v0:
```python
from functools import partial

import jax
import jax.numpy as jnp
from jax import lax
from jax.sharding import PartitionSpec as P

HEAD_DIM = 64
REACH = 3


def with_halo(block, sides, width):
    for axis, dim in sides:
        count = lax.axis_size(axis)
        forward = [(i, i + 1) for i in range(count - 1)]
        backward = [(target, source) for source, target in forward]
        low = lax.ppermute(
            lax.slice_in_dim(block, block.shape[dim] - width, None, axis=dim), axis, forward
        )
        high = lax.ppermute(lax.slice_in_dim(block, 0, width, axis=dim), axis, backward)
        block = jnp.concatenate([low, block, high], axis=dim)
    return block


def from_behind(value, axis, steps):
    count = lax.axis_size(axis)
    first, last = (max(0, -steps), min(count, count - steps))
    return lax.ppermute(value, axis, [(source, source + steps) for source in range(first, last)])


def exact_dot(left, right):
    return jnp.dot(left, right, precision=lax.Precision.HIGHEST, preferred_element_type=jnp.float32)


def exact_inner(left, right):
    return lax.dot_general(
        left,
        right,
        (((0,), (0,)), ((), ())),
        precision=lax.Precision.HIGHEST,
        preferred_element_type=jnp.float32,
    )


def narrow_dot(left, right):
    return jnp.dot(left, right, preferred_element_type=jnp.float32)


def inner_rows(left, right):
    return lax.dot_general(
        left, right, (((0,), (0,)), ((), ())), preferred_element_type=jnp.float32
    )


def against_rows(left, right):
    return lax.dot_general(
        left, right, (((1,), (1,)), ((), ())), preferred_element_type=jnp.float32
    )


def plain_norm(values):
    center = values - jnp.mean(values, axis=-1, keepdims=True)
    spread = jnp.mean(center * center, axis=-1, keepdims=True)
    return center * lax.rsqrt(spread + 1e-06)


def modulate(values, shift_part, scale_part):
    return plain_norm(values) * (1.0 + scale_part) + shift_part


def text_affine(values, gain_part, bias_part):
    return plain_norm(values) * gain_part + bias_part


def turn_table(head_width, places):
    half_width = head_width // 2
    inverse = 10000.0 ** (-jnp.arange(half_width, dtype=jnp.float32) * 2.0 / head_width)
    angles = places.astype(jnp.float32)[:, None] * inverse[None, :]
    angles = jnp.concatenate([angles, angles], axis=-1)[:, None, :]
    return (jnp.cos(angles), jnp.sin(angles))


def rotate(values, places):
    cosine, sine = turn_table(values.shape[-1], places)
    half_width = values.shape[-1] // 2
    turned = jnp.concatenate([-values[..., half_width:], values[..., :half_width]], axis=-1)
    return values * cosine + turned * sine


def unrotate(gradient_tree, places):
    cosine, sine = turn_table(gradient_tree.shape[-1], places)
    half_width = gradient_tree.shape[-1] // 2
    scaled = gradient_tree * sine
    turned = jnp.concatenate([scaled[..., half_width:], -scaled[..., :half_width]], axis=-1)
    return gradient_tree * cosine + turned


def segment_of(frame_ids, lengths):
    bounds = jnp.cumsum(lengths)
    counted = jnp.sum((frame_ids[:, None] >= bounds[None, :]).astype(jnp.int32), axis=1)
    return jnp.where(frame_ids < 0, -1, counted)


def position_of(frame_ids, lengths, segment):
    starts = jnp.cumsum(lengths) - lengths
    chosen = (segment[:, None] == jnp.arange(lengths.shape[0], dtype=jnp.int32)[None, :]).astype(
        jnp.int32
    )
    return frame_ids - jnp.sum(chosen * starts[None, :], axis=1)


def head_rows(values):
    return lax.all_gather(values, "head", axis=0, tiled=True)


def head_sums(action, count_rows):
    return lax.psum_scatter(
        action(jnp.int32(0), lax.axis_size("head") * count_rows),
        "head",
        scatter_dimension=0,
        tiled=True,
    )


def frame_rim(values, reach):
    return with_halo(values, ((("seq", "head"), 0),), reach)


def fetch_near(values, offset):
    return from_behind(values, "seq", offset)


def return_near(values, offset):
    return from_behind(values, "seq", -offset)


def utter_sum(values):
    return lax.psum(values, "seq")


def channel_sum(values):
    return lax.psum(values, "head")


def split_pairs(stacked, local_heads):
    half_cols = stacked.shape[1] // 2
    key_heads = stacked[:, :half_cols].reshape(stacked.shape[0], local_heads, HEAD_DIM)
    value_heads = stacked[:, half_cols:].reshape(stacked.shape[0], local_heads, HEAD_DIM)
    return (key_heads, value_heads)


def on_device(
    text_in,
    mel_in,
    time_embed,
    lengths,
    text_mask,
    conv_weight,
    norm_gain,
    norm_bias,
    expand_weight,
    grn_gamma,
    grn_beta,
    shrink_weight,
    join_weight,
    modulation,
    qkv_weight,
    out_weight,
    up_weight,
    down_weight,
    cotangent,
):
    rows_here = text_in.shape[0]
    groups = lax.axis_size("head")
    frames_here = rows_here * groups
    seq_index = lax.axis_index("seq")
    head_index = lax.axis_index("head")
    utterances = lengths.shape[0]
    row_first = (seq_index * groups + head_index) * rows_here
    frame_first = seq_index * frames_here
    row_ids = row_first + jnp.arange(rows_here, dtype=jnp.int32)
    frame_ids = frame_first + jnp.arange(frames_here, dtype=jnp.int32)
    row_segment = segment_of(row_ids, lengths)
    frame_segment = segment_of(frame_ids, lengths)
    frame_places = position_of(frame_ids, lengths, frame_segment)
    utter_ids = jnp.arange(utterances, dtype=jnp.int32)
    row_onehot = (row_segment[:, None] == utter_ids[None, :]).astype(jnp.float32)
    frame_onehot = (frame_segment[:, None] == utter_ids[None, :]).astype(jnp.float32)
    mask_rows = text_mask.astype(jnp.float32)[:, None]
    taps_count = conv_weight.shape[0]
    half_kernel = taps_count // 2
    extended = frame_rim(text_in, half_kernel)
    extended_ids = (
        row_first - half_kernel + jnp.arange(rows_here + 2 * half_kernel, dtype=jnp.int32)
    )
    extended_segment = segment_of(extended_ids, lengths)
    same_taps = jnp.stack(
        [
            (extended_segment[tap_index : tap_index + rows_here] == row_segment).astype(jnp.float32)
            for tap_index in range(taps_count)
        ]
    )
    conv_out = jnp.zeros_like(text_in)
    for tap_index in range(taps_count):
        conv_out = (
            conv_out
            + extended[tap_index : tap_index + rows_here]
            * conv_weight[tap_index]
            * same_taps[tap_index][:, None]
        )
    text_norm, affine_back = jax.vjp(text_affine, conv_out, norm_gain, norm_bias)
    text_low = text_norm.astype(jnp.bfloat16)
    text_all = head_rows(text_low)
    expanded = narrow_dot(text_all, expand_weight)
    activated, gelu_exact_back = jax.vjp(partial(jax.nn.gelu, approximate=False), expanded)
    text_channels = expand_weight.shape[1] * groups
    squares_all = utter_sum(exact_inner(frame_onehot, activated * activated))
    grn_norm = jnp.sqrt(squares_all + 1.0)
    channel_total = channel_sum(jnp.sum(grn_norm, axis=1))
    denominator = channel_total / text_channels + 1e-06
    grn_ratio = grn_norm / denominator[:, None]
    ratio_rows = exact_dot(frame_onehot, grn_ratio)
    grn_out = grn_gamma * activated * ratio_rows + grn_beta + activated
    grn_low = grn_out.astype(jnp.bfloat16)

    def shrink_piece(start, count):
        return narrow_dot(lax.dynamic_slice_in_dim(grn_low, start, count, 0), shrink_weight)

    branch = head_sums(shrink_piece, rows_here)
    text_out = text_in + mask_rows * branch
    join_low = text_out.astype(jnp.bfloat16)
    hidden = mel_in + narrow_dot(join_low, join_weight)
    cond_low = jax.nn.silu(time_embed).astype(jnp.bfloat16)
    mod_all = lax.all_gather(narrow_dot(cond_low, modulation), "head", axis=1, tiled=True)
    mod_rows = exact_dot(row_onehot, mod_all)
    shift_attn, scale_attn, gate_attn, shift_ffn, scale_ffn, feedforward_gate = jnp.split(
        mod_rows, 6, axis=1
    )
    attn_in, attn_mod_back = jax.vjp(modulate, hidden, shift_attn, scale_attn)
    attn_all = head_rows(attn_in.astype(jnp.bfloat16))
    projected = jnp.einsum("fd,dtc->ftc", attn_all, qkv_weight, preferred_element_type=jnp.float32)
    head_cols = projected.shape[2]
    local_heads = head_cols // HEAD_DIM
    query_low = rotate(
        projected[:, 0].reshape(frames_here, local_heads, HEAD_DIM), frame_places
    ).astype(jnp.bfloat16)
    key_rot = rotate(projected[:, 1].reshape(frames_here, local_heads, HEAD_DIM), frame_places)
    key_value = jnp.concatenate(
        [key_rot.reshape(frames_here, head_cols), projected[:, 2]], axis=1
    ).astype(jnp.bfloat16)
    offset_list = [offset for offset in range(-REACH, REACH + 1) if offset != 0]
    near_blocks = [fetch_near(key_value, offset) for offset in offset_list]
    key_heads, value_heads = split_pairs(
        jnp.concatenate([key_value] + near_blocks, axis=0), local_heads
    )
    key_segment = jnp.concatenate(
        [segment_of(frame_ids - offset * frames_here, lengths) for offset in [0] + offset_list]
    )
    block_rows = min(512, frames_here)
    score_scale = HEAD_DIM ** (-0.5)

    def masked_scores(query_block, key_part, block_start):
        raw = (
            jnp.einsum("qhd,khd->hqk", query_block, key_part, preferred_element_type=jnp.float32)
            * score_scale
        )
        allowed = (
            frame_segment[block_start : block_start + block_rows][:, None] == key_segment[None, :]
        )
        return jnp.where(allowed[None, :, :], raw, -1e30)

    context_parts = []
    logsum_parts = []
    for block_start in range(0, frames_here, block_rows):
        scores = masked_scores(
            query_low[block_start : block_start + block_rows], key_heads, block_start
        )
        row_top = jnp.max(scores, axis=-1, keepdims=True)
        exponent = jnp.exp(scores - row_top)
        row_total = jnp.sum(exponent, axis=-1, keepdims=True)
        probs_low = (exponent / row_total).astype(jnp.bfloat16)
        context_parts.append(
            jnp.einsum("hqk,khd->qhd", probs_low, value_heads, preferred_element_type=jnp.float32)
        )
        logsum_parts.append(row_top + jnp.log(row_total))
    context_low = (
        jnp.concatenate(context_parts, axis=0).reshape(frames_here, head_cols).astype(jnp.bfloat16)
    )

    def output_piece(start, count):
        return narrow_dot(context_low, out_weight)

    attn_rows = head_sums(output_piece, rows_here)
    middle_activation = hidden + gate_attn * attn_rows
    ffn_in, ffn_mod_back = jax.vjp(modulate, middle_activation, shift_ffn, scale_ffn)
    ffn_low = ffn_in.astype(jnp.bfloat16)
    d_ffn_low = (cotangent * feedforward_gate).astype(jnp.bfloat16)
    ffn_all = head_rows(ffn_low)
    upward = narrow_dot(ffn_all, up_weight)
    gelu_value, gelu_tanh_back = jax.vjp(partial(jax.nn.gelu, approximate=True), upward)
    gelu_low = gelu_value.astype(jnp.bfloat16)

    def down_piece(start, count):
        return narrow_dot(lax.dynamic_slice_in_dim(gelu_low, start, count, 0), down_weight)

    feedforward_token_rows = head_sums(down_piece, rows_here)
    d_ffn_all = head_rows(d_ffn_low)
    d_up_low = gelu_tanh_back(against_rows(d_ffn_all, down_weight))[0].astype(jnp.bfloat16)
    grad_down_part = inner_rows(gelu_low, d_ffn_all)
    grad_up_part = inner_rows(ffn_all, d_up_low)

    def up_back_piece(start, count):
        return against_rows(lax.dynamic_slice_in_dim(d_up_low, start, count, 0), up_weight)

    d_ffn_in = head_sums(up_back_piece, rows_here)
    transformer_layer_output = middle_activation + feedforward_gate * feedforward_token_rows
    d_mid_part, d_shift_ffn, d_scale_ffn = ffn_mod_back(d_ffn_in)
    d_middle = cotangent + d_mid_part
    d_gate_ffn = cotangent * feedforward_token_rows
    d_gate_attn = d_middle * attn_rows
    d_attn_all = head_rows((d_middle * gate_attn).astype(jnp.bfloat16))
    grad_out_part = inner_rows(context_low, d_attn_all)
    d_context_low = (
        against_rows(d_attn_all, out_weight)
        .astype(jnp.bfloat16)
        .reshape(frames_here, local_heads, HEAD_DIM)
    )
    d_query_parts = []
    d_key_heads = jnp.zeros(key_heads.shape, jnp.float32)
    d_value_heads = jnp.zeros(value_heads.shape, jnp.float32)
    for block_number, block_start in enumerate(range(0, frames_here, block_rows)):
        query_block = query_low[block_start : block_start + block_rows]
        scores = masked_scores(query_block, key_heads, block_start)
        probs = jnp.exp(scores - logsum_parts[block_number])
        grad_block = d_context_low[block_start : block_start + block_rows]
        d_probs = jnp.einsum(
            "qhd,khd->hqk", grad_block, value_heads, preferred_element_type=jnp.float32
        )
        row_inner = jnp.sum(probs * d_probs, axis=-1, keepdims=True)
        d_scores_low = (probs * (d_probs - row_inner)).astype(jnp.bfloat16)
        d_query_parts.append(
            jnp.einsum("hqk,khd->qhd", d_scores_low, key_heads, preferred_element_type=jnp.float32)
            * score_scale
        )
        d_key_heads = (
            d_key_heads
            + jnp.einsum(
                "hqk,qhd->khd", d_scores_low, query_block, preferred_element_type=jnp.float32
            )
            * score_scale
        )
        d_value_heads = d_value_heads + jnp.einsum(
            "hqk,qhd->khd",
            probs.astype(jnp.bfloat16),
            grad_block,
            preferred_element_type=jnp.float32,
        )
    d_pairs = jnp.concatenate(
        [d_key_heads.reshape(-1, head_cols), d_value_heads.reshape(-1, head_cols)], axis=1
    )
    own_pairs = d_pairs[:frames_here]
    for position, offset in enumerate(offset_list):
        own_pairs = own_pairs + return_near(
            d_pairs[(position + 1) * frames_here : (position + 2) * frames_here], offset
        )
    d_query = unrotate(jnp.concatenate(d_query_parts, axis=0), frame_places).reshape(
        frames_here, head_cols
    )
    d_key = unrotate(
        own_pairs[:, :head_cols].reshape(frames_here, local_heads, HEAD_DIM), frame_places
    ).reshape(frames_here, head_cols)
    d_projected_low = jnp.stack([d_query, d_key, own_pairs[:, head_cols:]], axis=1).astype(
        jnp.bfloat16
    )
    grad_qkv_part = jnp.einsum(
        "fd,ftc->dtc", attn_all, d_projected_low, preferred_element_type=jnp.float32
    )

    def attn_back_piece(start, count):
        return jnp.einsum(
            "ftc,dtc->fd", d_projected_low, qkv_weight, preferred_element_type=jnp.float32
        )

    d_attn_in = head_sums(attn_back_piece, rows_here)
    d_hidden_part, d_shift_attn, d_scale_attn = attn_mod_back(d_attn_in)
    grad_mel = d_middle + d_hidden_part
    d_mod_rows = jnp.concatenate(
        [d_shift_attn, d_scale_attn, d_gate_attn, d_shift_ffn, d_scale_ffn, d_gate_ffn], axis=1
    )
    d_mod_part = exact_inner(row_onehot, d_mod_rows)
    d_joined_low = grad_mel.astype(jnp.bfloat16)
    grad_join_part = inner_rows(join_low, d_joined_low)
    d_text_out = against_rows(d_joined_low, join_weight)
    d_branch_all = head_rows((mask_rows * d_text_out).astype(jnp.bfloat16))
    grad_shrink_part = inner_rows(grn_low, d_branch_all)
    d_grn = against_rows(d_branch_all, shrink_weight)
    d_ratio, grad_gamma, grad_beta = utter_sum(
        (
            exact_inner(frame_onehot, d_grn * grn_gamma * activated),
            jnp.sum(d_grn * activated * ratio_rows, axis=0),
            jnp.sum(d_grn, axis=0),
        )
    )
    d_mean = channel_sum(-jnp.sum(d_ratio * grn_norm, axis=1) / (denominator * denominator))
    d_norm = d_ratio / denominator[:, None] + (d_mean / text_channels)[:, None]
    d_activated = d_grn * (grn_gamma * ratio_rows + 1.0) + activated * exact_dot(
        frame_onehot, d_norm / grn_norm
    )
    d_expanded_low = gelu_exact_back(d_activated)[0].astype(jnp.bfloat16)
    grad_expand_part = inner_rows(text_all, d_expanded_low)

    def expand_back_piece(start, count):
        return against_rows(d_expanded_low, expand_weight)

    d_text_norm = head_sums(expand_back_piece, rows_here)
    d_conv_out, grad_gain_part, grad_bias_part = affine_back(d_text_norm)
    d_extended = frame_rim(d_conv_out, half_kernel)
    grad_text = d_text_out
    conv_grads = []
    for tap_index in range(taps_count):
        mirror = 2 * half_kernel - tap_index
        grad_text = (
            grad_text
            + d_extended[mirror : mirror + rows_here]
            * conv_weight[tap_index]
            * same_taps[mirror][:, None]
        )
        conv_grads.append(
            jnp.sum(
                d_conv_out
                * extended[tap_index : tap_index + rows_here]
                * same_taps[tap_index][:, None],
                axis=0,
            )
        )
    grad_conv_part = jnp.stack(conv_grads)
    grad_expand, grad_shrink, grad_qkv, grad_out, grad_up, grad_down = (
        lax.psum_scatter(grad_expand_part, "seq", scatter_dimension=0, tiled=True),
        lax.psum_scatter(grad_shrink_part, "seq", scatter_dimension=1, tiled=True),
        lax.psum_scatter(grad_qkv_part, "seq", scatter_dimension=0, tiled=True),
        lax.psum_scatter(grad_out_part, "seq", scatter_dimension=1, tiled=True),
        lax.psum_scatter(grad_up_part, "seq", scatter_dimension=0, tiled=True),
        lax.psum_scatter(grad_down_part, "seq", scatter_dimension=1, tiled=True),
    )
    grad_conv, grad_gain, grad_bias, grad_join, mod_columns = (
        lax.psum_scatter(grad_conv_part, ("seq", "head"), scatter_dimension=1, tiled=True),
        lax.psum_scatter(grad_gain_part, ("seq", "head"), scatter_dimension=0, tiled=True),
        lax.psum_scatter(grad_bias_part, ("seq", "head"), scatter_dimension=0, tiled=True),
        lax.psum_scatter(grad_join_part, ("seq", "head"), scatter_dimension=1, tiled=True),
        lax.psum_scatter(d_mod_part, ("seq", "head"), scatter_dimension=1, tiled=True),
    )
    grad_modulation = exact_inner(cond_low.astype(jnp.float32), mod_columns)
    return (
        transformer_layer_output,
        grad_text,
        grad_mel,
        grad_conv,
        grad_gain,
        grad_bias,
        grad_expand,
        grad_gamma,
        grad_beta,
        grad_shrink,
        grad_join,
        grad_modulation,
        grad_qkv,
        grad_out,
        grad_up,
        grad_down,
    )


def solution(mesh):
    return jax.shard_map(
        on_device,
        mesh=mesh,
        in_specs=(
            P(("seq", "head"), None),
            P(("seq", "head"), None),
            P(),
            P(),
            P(("seq", "head")),
            P(),
            P(),
            P(),
            P(None, "head"),
            P("head"),
            P("head"),
            P("head", None),
            P(),
            P(None, "head"),
            P(None, None, "head"),
            P("head", None),
            P(None, "head"),
            P("head", None),
            P(("seq", "head"), None),
        ),
        out_specs=(
            P(("seq", "head"), None),
            P(("seq", "head"), None),
            P(("seq", "head"), None),
            P(None, ("seq", "head")),
            P(("seq", "head")),
            P(("seq", "head")),
            P("seq", "head"),
            P("head"),
            P("head"),
            P("head", "seq"),
            P(None, ("seq", "head")),
            P(None, ("seq", "head")),
            P("seq", None, "head"),
            P("head", "seq"),
            P("seq", "head"),
            P("head", "seq"),
        ),
        check_vma=False,
    )
```

profile of v0, /device:TPU:0, one launch (start us, length us, event | category | flops | bytes accessed | tf_op | source)
XLA Modules:
  0.0 2079.6 jit_solution(8677763731977481332)
XLA Ops:
  21.8 20.7 all-gather.7.cloned.1.call-done
  48.0 21.6 %psum.42 = f32[8,256]{1,0:T(8,128)S(1)} all-reduce(f32[8,256]{1,0:T(8,128)S(1)} %fusion.58), channel_id=1, replica_groups=mesh['seq'=8,'head'=4] {'seq'}, use_global_device_ids=true, to_apply=%region_6.7 | all-reduce | flops 2048 | bytes 16384 | tf_op jit(solution)/shard_map/psum | solution.py:138
  69.7 5.9 psum.43
  82.7 5.7 all_gather.22
  88.4 4.6 fusion.106
  93.0 16.7 reduce-scatter.20.cloned.1.call-done
  117.4 21.2 %all-gather.9.cloned.1.call-done = bf16[1024,1024]{1,0:T(8,128)(2,1)} async-done(((bf16[256,1024]{1,0:T(8,128)(2,1)}), bf16[1024,1024]{1,0:T(8,128)(2,1)}) %all-gather.9.cloned.1.call-update) | async-done | bytes 2097168 | tf_op jit(solution)/shard_map/all_gather | solution.py:113
  138.6 3.9 fusion.37
  148.6 4.6 collective-permute-start.5
  155.8 16.8 collective-permute-done.2
  172.6 5.3 collective-permute-start.7
  177.9 5.6 broadcast_compare_fusion.1
  183.5 41.6 %collective-permute-done.3 = bf16[1024,512]{0,1:T(8,128)(2,1)S(1)} collective-permute-done((bf16[1024,512]{0,1:T(8,128)(2,1)S(1)}, bf16[1024,512]{0,1:T(8,128)(2,1)S(1)}, u32[]{:S(2)}, u32[]{:S(2)}) %collective-permute-start.3) | collective-permute-done | bytes 1048608 | tf_op jit(solution)/shard_map/ppermute | solution.py:28
  229.2 24.1 %fusion.161 = (f32[4,512]{1,0:T(4,128)S(1)}, f32[4,512,7168]{2,1,0:T(8,128)}) fusion(bf16[7168,4,64]{0,2,1:T(8,128)(2,1)} %bitcast.137, bf16[1024,4,64]{0,2,1:T(8,128)(2,1)S(1)} %get-tuple-element.97, pred[512,7168]{1,0:T(8,128)(4,1)} %get-tuple-element.102), kind=kOutput, calls=%fused_computation.337 | convolution fusion | flops 1923086336 | bytes 66330624 | tf_op jit(solution)/shard_map/qhd,khd->hqk/dot_general | solution.py:264
  253.3 24.1 %fusion.162 = (f32[4,512]{1,0:T(4,128)S(1)}, f32[4,512,7168]{2,1,0:T(8,128)}) fusion(bf16[7168,4,64]{0,2,1:T(8,128)(2,1)} %bitcast.138, bf16[1024,4,64]{0,2,1:T(8,128)(2,1)S(1)} %get-tuple-element.97, pred[512,7168]{1,0:T(8,128)(4,1)} %get-tuple-element.101), kind=kOutput, calls=%fused_computation.338 | convolution fusion | flops 1923086336 | bytes 66330624 | tf_op jit(solution)/shard_map/qhd,khd->hqk/dot_general | solution.py:264
  277.4 19.0 fusion.1
  296.4 21.8 %fusion.43 = bf16[512,4,64]{0,2,1:T(8,128)(2,1)S(1)} fusion(bf16[7168,4,64]{0,2,1:T(8,128)(2,1)} %bitcast.145, f32[4,512,7168]{2,1,0:T(8,128)} %get-tuple-element.125, f32[4,512]{1,0:T(4,128)S(1)} %fusion.1, f32[4,512]{1,0:T(4,128)S(1)} %get-tuple-element.124), kind=kOutput, calls=%fused_computation.83 | convolution fusion | flops 1923219456 | bytes 62668800 | tf_op jit(solution)/shard_map/hqk,khd->qhd/dot_general | solution.py:283
  318.2 27.8 %fusion = f32[4,512]{1,0:T(4,128)S(1)} fusion(f32[4,512,7168]{2,1,0:T(8,128)} %get-tuple-element.127, f32[4,512]{1,0:T(4,128)S(1)} %get-tuple-element.126), kind=kLoop, calls=%fused_computation.12 | loop fusion | flops 29358080 | bytes 58736640 | tf_op jit(solution)/shard_map/reduce_sum | solution.py:280
  346.0 21.8 %fusion.42 = bf16[512,4,64]{0,2,1:T(8,128)(2,1)S(1)} fusion(bf16[7168,4,64]{0,2,1:T(8,128)(2,1)} %bitcast.146, f32[4,512,7168]{2,1,0:T(8,128)} %get-tuple-element.127, f32[4,512]{1,0:T(4,128)S(1)} %fusion, f32[4,512]{1,0:T(4,128)S(1)} %get-tuple-element.126), kind=kOutput, calls=%fused_computation.82 | convolution fusion | flops 1923219456 | bytes 62668800 | tf_op jit(solution)/shard_map/hqk,khd->qhd/dot_general | solution.py:283
  371.5 61.8 %reduce-scatter.22.cloned.1.call-done = f32[256,1024]{1,0:T(8,128)} async-done(((f32[1024,1024]{1,0:T(8,128)}), f32[256,1024]{1,0:T(8,128)}) %reduce-scatter.22.cloned.1.call-update) | async-done | bytes 1048592 | tf_op jit(solution)/shard_map/reduce_scatter | solution.py:117
  439.2 22.1 %all-gather.13.cloned.1.call-done = bf16[1024,1024]{1,0:T(8,128)(2,1)} async-done(((bf16[256,1024]{1,0:T(8,128)(2,1)}), bf16[1024,1024]{1,0:T(8,128)(2,1)}) %all-gather.13.cloned.1.call-update) | async-done | bytes 2097168 | tf_op jit(solution)/shard_map/all_gather | solution.py:113
  461.3 4.5 fusion.165
  465.8 20.2 all-gather.11.cloned.1.call-done
  485.9 5.8 fusion.22
  497.2 5.1 fusion.143
  502.4 38.3 %reduce-scatter.26.cloned.1.call-done = f32[256,1024]{1,0:T(8,128)} async-done(((f32[1024,1024]{1,0:T(8,128)}), f32[256,1024]{1,0:T(8,128)}) %reduce-scatter.26.cloned.1.call-update) | async-done | bytes 1048592 | tf_op jit(solution)/shard_map/reduce_scatter | solution.py:117
  542.7 45.3 %reduce-scatter.24.cloned.1.call-done = f32[256,1024]{1,0:T(8,128)} async-done(((f32[1024,1024]{1,0:T(8,128)}), f32[256,1024]{1,0:T(8,128)}) %reduce-scatter.24.cloned.1.call-update) | async-done | bytes 1048592 | tf_op jit(solution)/shard_map/reduce_scatter | solution.py:117
  594.0 22.7 %all-gather.15.cloned.1.call-done = bf16[1024,1024]{1,0:T(8,128)(2,1)} async-done(((bf16[256,1024]{1,0:T(8,128)(2,1)}), bf16[1024,1024]{1,0:T(8,128)(2,1)}) %all-gather.15.cloned.1.call-update) | async-done | bytes 2097168 | tf_op jit(solution)/shard_map/all_gather | solution.py:113
  619.0 24.1 %fusion.4 = f32[4,64,7168]{2,1,0:T(8,128)} fusion(bf16[512,4,64]{0,2,1:T(8,128)(2,1)S(1)} %bitcast.163, f32[4,512,7168]{2,1,0:T(8,128)} %get-tuple-element.125, f32[4,512]{1,0:T(4,128)S(1)} %log_add_fusion), kind=kOutput, calls=%fused_computation.16 | convolution fusion | flops 1908408320 | bytes 66330624 | tf_op jit(solution)/shard_map/hqk,qhd->khd/dot_general | solution.py:352
  643.1 38.2 %multiply_reduce_fusion = (f32[4,512]{1,0:T(4,128)S(1)}, f32[4,512,7168]{2,1,0:T(8,128)}) fusion(f32[4,512,7168]{2,1,0:T(8,128)} %get-tuple-element.125, f32[4,512]{1,0:T(4,128)S(1)} %log_add_fusion, bf16[512,4,64]{0,2,1:T(8,128)(2,1)S(1)} %bitcast.164, bf16[7168,4,64]{0,2,1:T(8,128)(2,1)} %bitcast.147), kind=kOutput, calls=%fused_computation.1 | convolution fusion | flops 1923086336 | bytes 121389056 | tf_op jit(solution)/shard_map/qhd,khd->hqk/dot_general | solution.py:336
  681.2 38.2 %multiply_reduce_fusion.1 = (f32[4,512]{1,0:T(4,128)S(1)}, f32[4,512,7168]{2,1,0:T(8,128)}) fusion(f32[4,512,7168]{2,1,0:T(8,128)} %get-tuple-element.127, f32[4,512]{1,0:T(4,128)S(1)} %log_add_fusion.1, bf16[512,4,64]{0,2,1:T(8,128)(2,1)S(1)} %bitcast.161, bf16[7168,4,64]{0,2,1:T(8,128)(2,1)} %bitcast.148), kind=kOutput, calls=%fused_computation.4 | convolution fusion | flops 1923086336 | bytes 121389056 | tf_op jit(solution)/shard_map/qhd,khd->hqk/dot_general | solution.py:336
  719.5 26.8 %fusion.13 = f32[4,64,7168]{2,1,0:T(8,128)} fusion(f32[4,64,7168]{2,1,0:T(8,128)} %fusion.4, bf16[512,4,64]{0,2,1:T(8,128)(2,1)S(1)} %bitcast.162, f32[4,512,7168]{2,1,0:T(8,128)} %get-tuple-element.127, f32[4,512]{1,0:T(4,128)S(1)} %log_add_fusion.1), kind=kOutput, calls=%fused_computation.36 | convolution fusion | flops 1910243328 | bytes 73670656 | tf_op jit(solution)/shard_map/hqk,qhd->khd/dot_general | solution.py:352
  746.3 47.3 %multiply_convert_fusion.1 = bf16[4,512,7168]{2,1,0:T(8,128)(2,1)} fusion(f32[4,512,7168]{2,1,0:T(8,128)} %get-tuple-element.131, f32[4,512,7168]{2,1,0:T(8,128)} %get-tuple-element.127, f32[4,512]{1,0:T(4,128)S(1)} %get-tuple-element.130, f32[4,512]{1,0:T(4,128)S(1)} %log_add_fusion.1), kind=kLoop, calls=%fused_computation.3 | loop fusion | flops 58720256 | bytes 146817024 | tf_op jit(solution)/shard_map/convert_element_type | solution.py:340
  793.6 17.5 fusion.103
  811.0 46.9 %multiply_convert_fusion = bf16[4,512,7168]{2,1,0:T(8,128)(2,1)} fusion(f32[4,512,7168]{2,1,0:T(8,128)} %get-tuple-element.133, f32[4,512,7168]{2,1,0:T(8,128)} %get-tuple-element.125, f32[4,512]{1,0:T(4,128)S(1)} %get-tuple-element.132, f32[4,512]{1,0:T(4,128)S(1)} %log_add_fusion), kind=kLoop, calls=%fused_computation | loop fusion | flops 58720256 | bytes 146817024 | tf_op jit(solution)/shard_map/convert_element_type | solution.py:340
  857.9 19.6 fusion.12
  877.5 9.0 fusion.31
  886.5 4.4 collective-permute-start.8
  900.4 70.4 %collective-permute-done.8 = f32[1024,512]{0,1:T(8,128)S(1)} collective-permute-done((f32[1024,512]{0,1:T(8,128)S(1)}, f32[1024,512]{0,1:T(8,128)S(1)}, u32[]{:S(2)}, u32[]{:S(2)}) %collective-permute-start.8) | collective-permute-done | bytes 2097184 | tf_op jit(solution)/shard_map/ppermute | solution.py:28
  972.2 14.1 convolution_multiply_fusion.2
  986.2 13.8 convolution_multiply_fusion.1
  1000.1 15.1 collective-permute-done.9
  1016.6 6.3 collective-permute-done.12
  1022.9 6.0 fusion.30
  1036.2 136.0 %reduce-scatter.28.cloned.1.call-done = f32[256,1024]{1,0:T(8,128)} async-done(((f32[1024,1024]{1,0:T(8,128)}), f32[256,1024]{1,0:T(8,128)}) %reduce-scatter.28.cloned.1.call-update) | async-done | bytes 1048592 | tf_op jit(solution)/shard_map/reduce_scatter | solution.py:117
  1180.7 16.9 all-gather.17.cloned.1.call-done
  1201.3 37.2 %all-reduce.3 = (f32[8,256]{1,0:T(8,128)S(1)}, f32[256]{0:T(256)}, f32[256]{0:T(256)}) all-reduce(f32[8,256]{1,0:T(8,128)S(1)} %fusion.55, f32[256]{0:T(256)S(1)} %get-tuple-element.25, f32[256]{0:T(256)S(1)} %get-tuple-element.24), channel_id=1, replica_groups=mesh['seq'=8,'head'=4] {'seq'}, use_global_device_ids=true, to_apply=%region_35.36 | all-reduce | flops 2560 | bytes 20480 | tf_op jit(solution)/shard_map/psum | solution.py:138
  1238.6 6.2 psum.45
  1253.2 10.0 convolution_bitcast_fusion
  1263.3 13.7 reduce-scatter.30.cloned.1.call-done
  1282.2 4.9 fusion.142
  1287.2 4.6 fusion.171
  1294.0 5.5 fusion.35
  1310.8 73.2 %reduce-scatter.48.cloned.1.call-done = f32[192,8]{1,0:T(8,128)} async-done(((f32[6144,8]{1,0:T(8,128)}), f32[192,8]{1,0:T(8,128)}) %reduce-scatter.48.cloned.1.call-update) | async-done | bytes 6160
  1386.2 39.9 %all-reduce.2 = (f32[512]{0:T(512)S(1)}, f32[512]{0:T(512)S(1)}) all-reduce(f32[512]{0:T(512)S(1)} %get-tuple-element.22, f32[512]{0:T(512)S(1)} %get-tuple-element.27), channel_id=9, replica_groups=mesh['seq'=8,'head'=4] {'seq','head'}, use_global_device_ids=true, to_apply=%region_50.51.clone | all-reduce | flops 1024 | bytes 8192
  1427.4 4.0 fusion.71
  1431.3 87.3 %reduce-scatter.46.cloned.1.call-done = f32[16,7]{1,0:T(8,128)} async-done(((f32[512,7]{1,0:T(8,128)}), f32[16,7]{1,0:T(8,128)}) %reduce-scatter.46.cloned.1.call-update) | async-done | bytes 464
  1520.0 67.2 %reduce-scatter.44.cloned.1.call-done = f32[512,128]{1,0:T(8,128)} async-done(((f32[512,1024]{1,0:T(8,128)}), f32[512,128]{1,0:T(8,128)}) %reduce-scatter.44.cloned.1.call-update) | async-done | bytes 262160 | tf_op jit(solution)/shard_map/reduce_scatter | solution.py:443
  1587.1 71.1 %reduce-scatter.42.cloned.1.call-done = f32[128,512]{1,0:T(8,128)} async-done(((f32[1024,512]{1,0:T(8,128)}), f32[128,512]{1,0:T(8,128)}) %reduce-scatter.42.cloned.1.call-update) | async-done | bytes 262160 | tf_op jit(solution)/shard_map/reduce_scatter | solution.py:442
  1658.2 67.1 %reduce-scatter.40.cloned.1.call-done = f32[256,128]{1,0:T(8,128)} async-done(((f32[256,1024]{1,0:T(8,128)}), f32[256,128]{1,0:T(8,128)}) %reduce-scatter.40.cloned.1.call-update) | async-done | bytes 131088 | tf_op jit(solution)/shard_map/reduce_scatter | solution.py:441
  1725.3 77.9 %reduce-scatter.38.cloned.1.call-done = f32[128,3,256]{2,0,1:T(8,128)} async-done(((f32[1024,3,256]{2,0,1:T(8,128)}), f32[128,3,256]{2,0,1:T(8,128)}) %reduce-scatter.38.cloned.1.call-update) | async-done | bytes 393232 | tf_op jit(solution)/shard_map/reduce_scatter | solution.py:440
  1803.3 65.2 %reduce-scatter.34.cloned.1.call-done = f32[256,64]{0,1:T(8,128)} async-done(((f32[256,512]{0,1:T(8,128)}), f32[256,64]{0,1:T(8,128)}) %reduce-scatter.34.cloned.1.call-update) | async-done | bytes 65552 | tf_op jit(solution)/shard_map/reduce_scatter | solution.py:439
  1868.5 65.1 %reduce-scatter.32.cloned.1.call-done = f32[64,256]{1,0:T(8,128)} async-done(((f32[512,256]{1,0:T(8,128)}), f32[64,256]{1,0:T(8,128)}) %reduce-scatter.32.cloned.1.call-update) | async-done | bytes 65552 | tf_op jit(solution)/shard_map/reduce_scatter | solution.py:438
  1933.6 138.7 %reduce-scatter.36.cloned.1.call-done = f32[512,32]{0,1:T(8,128)} async-done(((f32[512,1024]{0,1:T(8,128)}), f32[512,32]{0,1:T(8,128)}) %reduce-scatter.36.cloned.1.call-update) | async-done | bytes 65552 | tf_op jit(solution)/shard_map/reduce_scatter | solution.py:449
  (450 shorter events, 134.9 us)
Async XLA Ops:
  7.2 75.0 %copy-start = (bf16[1024,1536]{1,0:T(8,128)(2,1)S(1)}, bf16[1024,1536]{1,0:T(8,128)(2,1)}, u32[]{:S(2)}) copy-start(bf16[1024,1536]{1,0:T(8,128)(2,1)} %param.32) | copy-start | bytes 9437188
  7.2 35.3 %all-gather.7.cloned.1.call-start = ((), (), s32[]{:S(2)}) async-start(), calls=%async_computation.15 | async-start | bytes 1310720 | tf_op jit(solution)/shard_map/all_gather | solution.py:113
  8.2 7.7 collective-permute-start
  10.7 5.2 collective-permute-start.1
  13.0 75.4 %copy-start.105 = (s32[256]{0:T(256)}, s32[256]{0:T(256)S(1)}, u32[]{:S(2)}) copy-start(s32[256]{0:T(256)S(1)} %get-tuple-element.60) | copy-start | bytes 3076
  21.5 88.2 %reduce-scatter.20.cloned.1.call-start = ((), (), s32[]{:S(2)}) async-start(), calls=%async_computation.16 | async-start | bytes 2621440 | tf_op jit(solution)/shard_map/reduce_scatter | solution.py:117
  21.8 95.5 %copy-start.57 = (s32[1024]{0:T(1024)}, s32[1024]{0:T(1024)S(1)}, u32[]{:S(2)}) copy-start(s32[1024]{0:T(1024)S(1)} %get-tuple-element.56) | copy-start | bytes 12292
  21.8 54.3 %copy-start.115 = (f32[256]{0:T(256)S(1)}, f32[256]{0:T(256)}, u32[]{:S(2)}) copy-start(f32[256]{0:T(256)} %param.28) | copy-start | bytes 3076
  21.8 54.3 %copy-start.119 = (f32[256]{0:T(256)S(1)}, f32[256]{0:T(256)}, u32[]{:S(2)}) copy-start(f32[256]{0:T(256)} %param.29) | copy-start | bytes 3076
  82.1 56.5 %all-gather.9.cloned.1.call-start = ((), (), s32[]{:S(2)}) async-start(), calls=%async_computation.17 | async-start | bytes 2621440 | tf_op jit(solution)/shard_map/all_gather | solution.py:113
  115.8 317.5 %reduce-scatter.22.cloned.1.call-start = ((), (), s32[]{:S(2)}) async-start(), calls=%async_computation.18 | async-start | bytes 5242880 | tf_op jit(solution)/shard_map/reduce_scatter | solution.py:117
  143.3 109.9 %copy-start.8 = (bf16[1024,4,64]{0,2,1:T(8,128)(2,1)}, bf16[1024,4,64]{0,2,1:T(8,128)(2,1)S(1)}, u32[]{:S(2)}) copy-start(bf16[1024,4,64]{0,2,1:T(8,128)(2,1)S(1)} %get-tuple-element.97) | copy-start | bytes 1572868
  143.7 28.8 %collective-permute-start.2 = (bf16[1024,512]{0,1:T(8,128)(2,1)S(1)}, bf16[1024,512]{0,1:T(8,128)(2,1)S(1)}, u32[]{:S(2)}, u32[]{:S(2)}) collective-permute-start(bf16[1024,512]{0,1:T(8,128)(2,1)S(1)} %get-tuple-element.85), channel_id=1, source_target_pairs={{12,0},{16,4},{20,8},{24,12},{28,16},{13,1},{17,5},{21,9},{25,13},... | collective-permute-start | bytes 3145736 | tf_op jit(solution)/shard_map/ppermute | solution.py:28
  145.1 80.3 %collective-permute-start.6 = (bf16[1024,512]{0,1:T(8,128)(2,1)S(1)}, bf16[1024,512]{0,1:T(8,128)(2,1)S(1)}, u32[]{:S(2)}, u32[]{:S(2)}) collective-permute-start(bf16[1024,512]{0,1:T(8,128)(2,1)S(1)} %get-tuple-element.85), channel_id=1, source_target_pairs={{0,8},{4,12},{8,16},{12,20},{16,24},{20,28},{1,9},{5,13},{9,17},{1... | collective-permute-start | bytes 3145736 | tf_op jit(solution)/shard_map/ppermute | solution.py:28
  148.6 76.7 %collective-permute-start.5 = (bf16[1024,512]{0,1:T(8,128)(2,1)S(1)}, bf16[1024,512]{0,1:T(8,128)(2,1)S(1)}, u32[]{:S(2)}, u32[]{:S(2)}) collective-permute-start(bf16[1024,512]{0,1:T(8,128)(2,1)S(1)} %get-tuple-element.85), channel_id=1, source_target_pairs={{0,4},{4,8},{8,12},{12,16},{16,20},{20,24},{24,28},{1,5},{5,9},{9,... | collective-permute-start | bytes 3145736 | tf_op jit(solution)/shard_map/ppermute | solution.py:28
  153.2 72.0 %collective-permute-start.4 = (bf16[1024,512]{0,1:T(8,128)(2,1)S(1)}, bf16[1024,512]{0,1:T(8,128)(2,1)S(1)}, u32[]{:S(2)}, u32[]{:S(2)}) collective-permute-start(bf16[1024,512]{0,1:T(8,128)(2,1)S(1)} %get-tuple-element.85), channel_id=1, source_target_pairs={{4,0},{8,4},{12,8},{16,12},{20,16},{24,20},{28,24},{5,1},{9,5},{13... | collective-permute-start | bytes 3145736 | tf_op jit(solution)/shard_map/ppermute | solution.py:28
  154.5 70.7 %collective-permute-start.3 = (bf16[1024,512]{0,1:T(8,128)(2,1)S(1)}, bf16[1024,512]{0,1:T(8,128)(2,1)S(1)}, u32[]{:S(2)}, u32[]{:S(2)}) collective-permute-start(bf16[1024,512]{0,1:T(8,128)(2,1)S(1)} %get-tuple-element.85), channel_id=1, source_target_pairs={{8,0},{12,4},{16,8},{20,12},{24,16},{28,20},{9,1},{13,5},{17,9},{2... | collective-permute-start | bytes 3145736 | tf_op jit(solution)/shard_map/ppermute | solution.py:28
  172.6 52.9 %collective-permute-start.7 = (bf16[1024,512]{0,1:T(8,128)(2,1)S(1)}, bf16[1024,512]{0,1:T(8,128)(2,1)S(1)}, u32[]{:S(2)}, u32[]{:S(2)}) collective-permute-start(bf16[1024,512]{0,1:T(8,128)(2,1)S(1)} %get-tuple-element.85), channel_id=1, source_target_pairs={{0,12},{4,16},{8,20},{12,24},{16,28},{1,13},{5,17},{9,21},{13,25},... | collective-permute-start | bytes 3145736 | tf_op jit(solution)/shard_map/ppermute | solution.py:28
  371.4 61.9 %copy-start.4 = (f32[256,1024]{1,0:T(8,128)S(1)}, f32[256,1024]{1,0:T(8,128)}, u32[]{:S(2)}) copy-start(f32[256,1024]{1,0:T(8,128)} %copy-done.3) | copy-start | bytes 3145732
  371.5 63.9 %copy-start.20 = (f32[256,1024]{1,0:T(8,128)S(1)}, f32[256,1024]{1,0:T(8,128)}, u32[]{:S(2)}) copy-start(f32[256,1024]{1,0:T(8,128)} %param.37) | copy-start | bytes 3145732
  371.5 89.8 %all-gather.13.cloned.1.call-start = ((), (), s32[]{:S(2)}) async-start(), calls=%async_computation.21 | async-start | bytes 2621440 | tf_op jit(solution)/shard_map/all_gather | solution.py:113
  435.1 152.9 %copy-start.6 = (f32[256,1024]{1,0:T(8,128)}, f32[256,1024]{1,0:T(8,128)S(1)}, u32[]{:S(2)}) copy-start(f32[256,1024]{1,0:T(8,128)S(1)} %get-tuple-element.54) | copy-start | bytes 3145732
  435.1 152.9 %copy-start.63 = (f32[256]{0:T(256)}, f32[256]{0:T(256)S(1)}, u32[]{:S(2)}) copy-start(f32[256]{0:T(256)S(1)} %broadcast_multiply_fusion.2) | copy-start | bytes 3076
  435.4 152.6 %copy-start.89 = (f32[256]{0:T(256)}, f32[256]{0:T(256)S(1)}, u32[]{:S(2)}) copy-start(f32[256]{0:T(256)S(1)} %fusion.136) | copy-start | bytes 3076
  438.6 47.4 %all-gather.11.cloned.1.call-start = ((), (), s32[]{:S(2)}) async-start(), calls=%async_computation.19 | async-start | bytes 2621440 | tf_op jit(solution)/shard_map/all_gather | solution.py:113
  439.1 101.6 %reduce-scatter.26.cloned.1.call-start = ((), (), s32[]{:S(2)}) async-start(), calls=%async_computation.22 | async-start | bytes 5242880 | tf_op jit(solution)/shard_map/reduce_scatter | solution.py:117
  496.0 91.9 %reduce-scatter.24.cloned.1.call-start = ((), (), s32[]{:S(2)}) async-start(), calls=%async_computation.20 | async-start | bytes 5242880 | tf_op jit(solution)/shard_map/reduce_scatter | solution.py:117
  502.4 114.3 %all-gather.15.cloned.1.call-start = ((), (), s32[]{:S(2)}) async-start(), calls=%async_computation.23 | async-start | bytes 2621440 | tf_op jit(solution)/shard_map/all_gather | solution.py:113
  540.7 47.2 %copy-start.16 = (f32[256,1024]{1,0:T(8,128)S(1)}, f32[256,1024]{1,0:T(8,128)}, u32[]{:S(2)}) copy-start(f32[256,1024]{1,0:T(8,128)} %reduce-scatter.26.cloned.1.call-done) | copy-start | bytes 3145732
  593.9 578.3 %reduce-scatter.28.cloned.1.call-start = ((), (), s32[]{:S(2)}) async-start(), calls=%async_computation.24 | async-start | bytes 5242880 | tf_op jit(solution)/shard_map/reduce_scatter | solution.py:117
  746.3 47.3 %copy-start.9 = (bf16[1024,4,64]{0,2,1:T(8,128)(2,1)S(1)}, bf16[1024,4,64]{0,2,1:T(8,128)(2,1)}, u32[]{:S(2)}) copy-start(bf16[1024,4,64]{0,2,1:T(8,128)(2,1)} %copy-done.8) | copy-start | bytes 1572868
  877.5 94.7 %copy-start.2 = (bf16[7168,256]{0,1:T(8,128)(2,1)S(1)}, bf16[7168,256]{0,1:T(8,128)(2,1)}, u32[]{:S(2)}) copy-start(bf16[7168,256]{0,1:T(8,128)(2,1)} %get-tuple-element.68) | copy-start | bytes 11010052
  886.5 84.4 %collective-permute-start.8 = (f32[1024,512]{0,1:T(8,128)S(1)}, f32[1024,512]{0,1:T(8,128)S(1)}, u32[]{:S(2)}, u32[]{:S(2)}) collective-permute-start(f32[1024,512]{0,1:T(8,128)S(1)} %get-tuple-element.61), channel_id=1, source_target_pairs={{0,12},{4,16},{8,20},{12,24},{16,28},{1,13},{5,17},{9,21},{13,25},... | collective-permute-start | bytes 6291464 | tf_op jit(solution)/shard_map/ppermute | solution.py:28
  890.9 124.3 %collective-permute-start.9 = (f32[1024,512]{0,1:T(8,128)}, f32[1024,512]{0,1:T(8,128)S(1)}, u32[]{:S(2)}, u32[]{:S(2)}) collective-permute-start(f32[1024,512]{0,1:T(8,128)} %get-tuple-element.62), channel_id=1, source_target_pairs={{0,8},{4,12},{8,16},{12,20},{16,24},{20,28},{1,9},{5,13},{9,17},{1... | collective-permute-start | bytes 6291464 | tf_op jit(solution)/shard_map/ppermute | solution.py:28
  894.5 120.8 %collective-permute-start.10 = (f32[1024,512]{0,1:T(8,128)}, f32[1024,512]{0,1:T(8,128)S(1)}, u32[]{:S(2)}, u32[]{:S(2)}) collective-permute-start(f32[1024,512]{0,1:T(8,128)} %get-tuple-element.63), channel_id=1, source_target_pairs={{0,4},{4,8},{8,12},{12,16},{16,20},{20,24},{24,28},{1,5},{5,9},{9,... | collective-permute-start | bytes 6291464 | tf_op jit(solution)/shard_map/ppermute | solution.py:28
  897.8 117.4 %collective-permute-start.11 = (f32[1024,512]{0,1:T(8,128)}, f32[1024,512]{0,1:T(8,128)}, u32[]{:S(2)}, u32[]{:S(2)}) collective-permute-start(f32[1024,512]{0,1:T(8,128)} %get-tuple-element.64), channel_id=1, source_target_pairs={{4,0},{8,4},{12,8},{16,12},{20,16},{24,20},{28,24},{5,1},{9,5},{13... | collective-permute-start | bytes 6291464 | tf_op jit(solution)/shard_map/ppermute | solution.py:28
  899.1 116.1 %collective-permute-start.13 = (f32[1024,512]{0,1:T(8,128)}, f32[1024,512]{0,1:T(8,128)}, u32[]{:S(2)}, u32[]{:S(2)}) collective-permute-start(f32[1024,512]{0,1:T(8,128)} %get-tuple-element.65), channel_id=1, source_target_pairs={{12,0},{16,4},{20,8},{24,12},{28,16},{13,1},{17,5},{21,9},{25,13},... | collective-permute-start | bytes 6291464 | tf_op jit(solution)/shard_map/ppermute | solution.py:28
  970.9 52.0 %collective-permute-start.12 = (f32[1024,512]{0,1:T(8,128)}, f32[1024,512]{0,1:T(8,128)}, u32[]{:S(2)}, u32[]{:S(2)}) collective-permute-start(f32[1024,512]{0,1:T(8,128)} %get-tuple-element.66), channel_id=1, source_target_pairs={{8,0},{12,4},{16,8},{20,12},{24,16},{28,20},{9,1},{13,5},{17,9},{2... | collective-permute-start | bytes 6291464 | tf_op jit(solution)/shard_map/ppermute | solution.py:28
  1036.1 136.1 %copy-start.5 = (f32[256,1024]{1,0:T(8,128)S(1)}, f32[256,1024]{1,0:T(8,128)}, u32[]{:S(2)}) copy-start(f32[256,1024]{1,0:T(8,128)} %copy-done.3) | copy-start | bytes 3145732
  1036.1 136.1 %copy-start.70 = (f32[256]{0:T(256)S(1)}, f32[256]{0:T(256)}, u32[]{:S(2)}) copy-start(f32[256]{0:T(256)} %copy-done.69) | copy-start | bytes 3076
  1036.1 139.0 %copy-start.114 = (f32[256]{0:T(256)S(1)}, f32[256]{0:T(256)}, u32[]{:S(2)}) copy-start(f32[256]{0:T(256)} %copy-done.113) | copy-start | bytes 3076
  1036.1 139.0 %copy-start.108 = (f32[256]{0:T(256)S(1)}, f32[256]{0:T(256)}, u32[]{:S(2)}) copy-start(f32[256]{0:T(256)} %copy-done.107) | copy-start | bytes 3076
  1036.1 161.5 %all-gather.17.cloned.1.call-start = ((), (), s32[]{:S(2)}) async-start(), calls=%async_computation.25 | async-start | bytes 1310720 | tf_op jit(solution)/shard_map/all_gather | solution.py:113
  1180.7 96.3 %reduce-scatter.30.cloned.1.call-start = ((), (), s32[]{:S(2)}) async-start(), calls=%async_computation.26 | async-start | bytes 2621440 | tf_op jit(solution)/shard_map/reduce_scatter | solution.py:117
  1249.4 134.6 %reduce-scatter.48.cloned.1.call-start = ((), (), s32[]{:S(2)}) async-start(), calls=%async_computation.35 | async-start | bytes 3244032
  1263.3 255.3 %reduce-scatter.46.cloned.1.call-start = ((), (), s32[]{:S(2)}) async-start(), calls=%async_computation.34 | async-start | bytes 270336
  1282.1 305.0 %reduce-scatter.44.cloned.1.call-start = ((), (), s32[]{:S(2)}) async-start(), calls=%async_computation.33 | async-start | bytes 2359296 | tf_op jit(solution)/shard_map/reduce_scatter | solution.py:443
  1287.2 371.1 %reduce-scatter.42.cloned.1.call-start = ((), (), s32[]{:S(2)}) async-start(), calls=%async_computation.32 | async-start | bytes 2359296 | tf_op jit(solution)/shard_map/reduce_scatter | solution.py:442
  1291.9 433.5 %reduce-scatter.40.cloned.1.call-start = ((), (), s32[]{:S(2)}) async-start(), calls=%async_computation.31 | async-start | bytes 1179648 | tf_op jit(solution)/shard_map/reduce_scatter | solution.py:441
  1293.7 509.6 %reduce-scatter.38.cloned.1.call-start = ((), (), s32[]{:S(2)}) async-start(), calls=%async_computation.30 | async-start | bytes 3538944 | tf_op jit(solution)/shard_map/reduce_scatter | solution.py:440
  1299.6 568.9 %reduce-scatter.34.cloned.1.call-start = ((), (), s32[]{:S(2)}) async-start(), calls=%async_computation.28 | async-start | bytes 589824 | tf_op jit(solution)/shard_map/reduce_scatter | solution.py:439
  1301.0 83.0 %copy-start.60 = (f32[8,1024]{1,0:T(8,128)S(1)}, f32[8,1024]{1,0:T(8,128)}, u32[]{:S(2)}) copy-start(f32[8,1024]{1,0:T(8,128)} %param.21) | copy-start | bytes 98308
  1301.0 632.6 %reduce-scatter.32.cloned.1.call-start = ((), (), s32[]{:S(2)}) async-start(), calls=%async_computation.27 | async-start | bytes 589824 | tf_op jit(solution)/shard_map/reduce_scatter | solution.py:438
  1302.4 124.9 %copy-start.74 = (f32[1,512]{1,0:T(1,128)S(1)}, f32[1,512]{1,0:T(1,128)}, u32[]{:S(2)}) copy-start(f32[1,512]{1,0:T(1,128)} %copy-done.73) | copy-start | bytes 6148
  1302.4 124.9 %copy-start.76 = (f32[1,512]{1,0:T(1,128)S(1)}, f32[1,512]{1,0:T(1,128)}, u32[]{:S(2)}) copy-start(f32[1,512]{1,0:T(1,128)} %copy-done.75) | copy-start | bytes 6148
  1302.4 125.0 %copy-start.78 = (f32[1,512]{1,0:T(1,128)S(1)}, f32[1,512]{1,0:T(1,128)}, u32[]{:S(2)}) copy-start(f32[1,512]{1,0:T(1,128)} %copy-done.77) | copy-start | bytes 6148
  1302.4 125.0 %copy-start.80 = (f32[1,512]{1,0:T(1,128)S(1)}, f32[1,512]{1,0:T(1,128)}, u32[]{:S(2)}) copy-start(f32[1,512]{1,0:T(1,128)} %copy-done.79) | copy-start | bytes 6148
  1302.4 125.0 %copy-start.82 = (f32[1,512]{1,0:T(1,128)S(1)}, f32[1,512]{1,0:T(1,128)}, u32[]{:S(2)}) copy-start(f32[1,512]{1,0:T(1,128)} %copy-done.81) | copy-start | bytes 6148
  1302.4 125.0 %copy-start.84 = (f32[1,512]{1,0:T(1,128)S(1)}, f32[1,512]{1,0:T(1,128)}, u32[]{:S(2)}) copy-start(f32[1,512]{1,0:T(1,128)} %copy-done.83) | copy-start | bytes 6148
  1302.4 125.0 %copy-start.86 = (f32[1,512]{1,0:T(1,128)S(1)}, f32[1,512]{1,0:T(1,128)}, u32[]{:S(2)}) copy-start(f32[1,512]{1,0:T(1,128)} %copy-done.85) | copy-start | bytes 6148
  1302.4 769.8 %copy-start.1 = (bf16[1024,1536]{1,0:T(8,128)(2,1)S(1)}, bf16[1024,1536]{1,0:T(8,128)(2,1)}, u32[]{:S(2)}) copy-start(bf16[1024,1536]{1,0:T(8,128)(2,1)} %param.32) | copy-start | bytes 9437188
  1302.4 769.8 %reduce-scatter.36.cloned.1.call-start = ((), (), s32[]{:S(2)}) async-start(), calls=%async_computation.29 | async-start | bytes 2162688 | tf_op jit(solution)/shard_map/reduce_scatter | solution.py:449
  1306.5 120.8 %collective-permute-start.14 = (f32[3,512]{1,0:T(4,128)S(1)}, f32[3,512]{1,0:T(4,128)S(1)}, u32[]{:S(2)}, u32[]{:S(2)}) collective-permute-start(f32[3,512]{1,0:T(4,128)S(1)} %get-tuple-element.89), channel_id=1, source_target_pairs={{1,0},{2,1},{3,2},{4,3},{5,4},{6,5},{7,6},{8,7},{9,8},{10,9},{11,1... | collective-permute-start | bytes 18440 | tf_op jit(solution)/shard_map/ppermute | solution.py:20
  1307.8 119.5 %collective-permute-start.15 = (f32[3,512]{1,0:T(4,128)S(1)}, f32[3,512]{1,0:T(4,128)S(1)}, u32[]{:S(2)}, u32[]{:S(2)}) collective-permute-start(f32[3,512]{1,0:T(4,128)S(1)} %get-tuple-element.90), channel_id=1, source_target_pairs={{0,1},{1,2},{2,3},{3,4},{4,5},{5,6},{6,7},{7,8},{8,9},{9,10},{10,1... | collective-permute-start | bytes 18440 | tf_op jit(solution)/shard_map/ppermute | solution.py:17
  (103 other events, 1193.8 us)
Sparse Core Ops, SparseCore 0:
  21.6 20.8 all-gather.6
  82.2 27.5 reduce-scatter.19
  115.9 22.5 all-gather.8
  371.6 61.6 reduce-scatter.21
  438.7 22.5 all-gather.12
  463.3 22.5 all-gather.10
  496.2 44.5 reduce-scatter.25
  543.4 44.5 reduce-scatter.23
  594.0 22.5 all-gather.14
  1036.3 135.8 reduce-scatter.27
  1180.8 16.7 all-gather.16
  1249.5 27.5 reduce-scatter.29
  1282.5 101.4 reduce-scatter.47
  1386.1 132.4 reduce-scatter.45
  1523.0 64.1 reduce-scatter.43
  1591.5 66.6 reduce-scatter.41
  1662.5 62.8 reduce-scatter.39
  1729.4 73.8 reduce-scatter.37
  1807.2 61.2 reduce-scatter.33
  1872.6 60.9 reduce-scatter.31
  1936.4 135.8 reduce-scatter.35
where the time goes:
time: 2090 us; the launch traced here: 2080 us
  waiting for transfers between devices  1300 us (62%)
  matrix products  375 us (18%)
  other arithmetic  205 us (10%)
  blocking collectives  117 us (6%)
  starting transfers between devices  41.9 us (2%)
  local copies, waits for them, and re-layouts  24.9 us (1%)
    reduce_scatter x6, waiting for transfers between devices, head_sums(): lax.psum_scatter(action(jnp.int32(0), lax.axis_size('head') * count_rows)...  312 us
    unnamed x23, waiting for transfers between devices  161 us
    ppermute x12, waiting for transfers between devices, from_behind(): lax.ppermute(value, axis, [(source, source + steps) for source in range(f...  150 us
    reduce_scatter x1, waiting for transfers between devices, on_device(): lax.psum_scatter(grad_join_part, ('seq', 'head'), scatter_dimension=1, ti...  139 us
    all_gather x6, waiting for transfers between devices, head_rows(): return lax.all_gather(values, 'head', axis=0, tiled=True)  124 us
    convert_element_type x2, other arithmetic, on_device(): d_scores_low = (probs * (d_probs - row_inner)).astype(jnp.bfloat16)  94.2 us
    reduce_scatter x1, waiting for transfers between devices, on_device(): lax.psum_scatter(grad_qkv_part, 'seq', scatter_dimension=0, tiled=True)  77.9 us
    dot_general x2, matrix products, on_device(): jnp.einsum('qhd,khd->hqk', grad_block, value_heads, preferred_element_typ...  76.4 us
  transfers between devices with their start and end apart: 37, of which 27 were waited for; matrix products, arithmetic and copies ran while one was open for 5% of the time, Pallas kernels for 0%

commit v1 on v0

--- a/solution.py
+++ b/solution.py
@@ -3,6 +3,8 @@
 import jax
 import jax.numpy as jnp
 from jax import lax
+from jax.experimental import pallas as pl
+from jax.experimental.pallas import tpu as pltpu
 from jax.sharding import PartitionSpec as P
 
 HEAD_DIM = 64
@@ -470,9 +472,1334 @@
     )
 
 
+MESH = pl.DeviceIdType.MESH
+HBM = pl.BlockSpec(memory_space=pl.ANY)
+VMEM = pl.BlockSpec(memory_space=pltpu.VMEM)
+DMA = pltpu.SemaphoreType.DMA
+
+
+def send(src, dst, send_sem, recv_sem, seq, head):
+    return pltpu.make_async_remote_copy(
+        src_ref=src,
+        dst_ref=dst,
+        send_sem=send_sem,
+        recv_sem=recv_sem,
+        device_id=(seq, head),
+        device_id_type=MESH,
+    )
+
+
+def greet(peers):
+    barrier = pltpu.get_barrier_semaphore()
+    for seq, head in peers:
+        pl.semaphore_signal(barrier, inc=1, device_id=(seq, head), device_id_type=MESH)
+    pl.semaphore_wait(barrier, len(peers))
+
+
+def head_places():
+    seq = lax.axis_index("seq")
+    head = lax.axis_index("head")
+    core = lax.rem(head, 2)
+    mate = head + 1 - 2 * core
+    across = lax.rem(head + 2, 4)
+    diagonal = lax.rem(mate + 2, 4)
+    return seq, head, mate, across, diagonal
+
+
+def params(number, vmem=None):
+    return pltpu.CompilerParams(
+        collective_id=number, has_side_effects=True, vmem_limit_bytes=vmem
+    )
+
+
+def cuts_of(rows, cuts):
+    return cuts if rows % (16 * cuts) == 0 else 1
+
+
+def gather_kernel(count, most, *refs):
+    ins, outs = refs[:count], refs[count : 2 * count]
+    local, y_send, y_recv, c_send, c_recv, f_send, f_recv = refs[2 * count :]
+    seq, head, mate, across, _ = head_places()
+    greet([(seq, mate), (seq, across)])
+    waits = []
+    hops = []
+    for i in range(count):
+        cuts = cuts_of(ins[i].shape[0], most)
+        rows = ins[i].shape[0] // cuts
+        for k in range(cuts):
+            part = pl.ds(k * rows, rows)
+            hop = send(
+                ins[i].at[part], outs[i].at[head, part], y_send.at[i, k], y_recv.at[i, k], seq, across
+            )
+            hop.start()
+            hops.append((i, k, part, hop))
+    for i in range(count):
+        beside = send(ins[i], outs[i].at[head], c_send.at[i], c_recv.at[i], seq, mate)
+        beside.start()
+        own = pltpu.make_async_copy(ins[i], outs[i].at[head], local.at[i])
+        own.start()
+        waits += [beside, own]
+    for i, k, part, hop in hops:
+        hop.wait_recv()
+        onward = send(
+            outs[i].at[across, part],
+            outs[i].at[across, part],
+            f_send.at[i, k],
+            f_recv.at[i, k],
+            seq,
+            mate,
+        )
+        onward.start()
+        waits.append(onward)
+    for one in waits:
+        one.wait()
+    for _, _, _, hop in hops:
+        hop.wait_send()
+
+
+def head_gather(arrays, number, cuts=2):
+    count = len(arrays)
+    outs = pl.pallas_call(
+        partial(gather_kernel, count, cuts),
+        out_shape=[jax.ShapeDtypeStruct((4,) + a.shape, a.dtype) for a in arrays],
+        in_specs=[HBM] * count,
+        out_specs=[HBM] * count,
+        scratch_shapes=[
+            DMA((count,)),
+            DMA((count, cuts)),
+            DMA((count, cuts)),
+            DMA((count,)),
+            DMA((count,)),
+            DMA((count, cuts)),
+            DMA((count, cuts)),
+        ],
+        compiler_params=params(number),
+        name=f"head_gather_{number}",
+    )(*arrays)
+    return outs
+
+
+def product_scatter_kernel(turned, cuts, wire, a_ref, w_ref, o_ref, *scratch):
+    away, keep, inbox, final, post, c_send, c_recv, y_send, y_recv = scratch
+    seq, head, mate, across, diagonal = head_places()
+    rows = o_ref.shape[0]
+    step = rows // cuts
+    contract = (((1,), (1 if turned else 0,)), ((), ()))
+
+    def product(block, k):
+        start = pl.multiple_of(block * rows + k * step, step)
+        return lax.dot_general(
+            a_ref[pl.ds(start, step), :], w_ref[...], contract, preferred_element_type=jnp.float32
+        )
+
+    greet([(seq, mate), (seq, across)])
+    first = []
+    for side, (theirs, ours) in enumerate(((diagonal, across), (mate, head))):
+        for k in range(cuts):
+            part = pl.ds(k * step, step)
+            away[side, part, :] = product(theirs, k)
+            hop = send(
+                away.at[side, part],
+                inbox.at[side, part],
+                c_send.at[side, k],
+                c_recv.at[side, k],
+                seq,
+                mate,
+            )
+            hop.start()
+            first.append(hop)
+            keep[side, part, :] = product(ours, k)
+        if side == 0:
+            second = []
+            for k in range(cuts):
+                part = pl.ds(k * step, step)
+                first[k].wait_recv()
+                post[part, :] = (keep[0, part, :] + inbox[0, part, :]).astype(wire)
+                hop = send(post.at[part], final.at[part], y_send.at[k], y_recv.at[k], seq, across)
+                hop.start()
+                second.append(hop)
+    for k in range(cuts):
+        part = pl.ds(k * step, step)
+        first[cuts + k].wait_recv()
+        second[k].wait_recv()
+        o_ref[part, :] = keep[1, part, :] + inbox[1, part, :] + final[part, :].astype(jnp.float32)
+    for hop in first + second:
+        hop.wait_send()
+
+
+def product_scatter(a, w, number, turned=False, cuts=2, wire=jnp.float32):
+    rows = a.shape[0] // 4
+    width = w.shape[0] if turned else w.shape[1]
+    return pl.pallas_call(
+        partial(product_scatter_kernel, turned, cuts, wire),
+        out_shape=jax.ShapeDtypeStruct((rows, width), jnp.float32),
+        in_specs=[VMEM, VMEM],
+        out_specs=VMEM,
+        scratch_shapes=[
+            pltpu.VMEM((2, rows, width), jnp.float32),
+            pltpu.VMEM((2, rows, width), jnp.float32),
+            pltpu.VMEM((2, rows, width), jnp.float32),
+            pltpu.VMEM((rows, width), wire),
+            pltpu.VMEM((rows, width), wire),
+            DMA((2, cuts)),
+            DMA((2, cuts)),
+            DMA((cuts,)),
+            DMA((cuts,)),
+        ],
+        compiler_params=params(number, 40 << 20),
+        name=f"product_scatter_{number}",
+    )(a, w)
+
+
+def spread_kernel(x_ref, o_ref, local, out_send, in_recv, f_send, f_recv):
+    seq, head, mate, _, _ = head_places()
+    core = lax.rem(head, 2)
+    landing = core == seq // 4
+    barrier = pltpu.get_barrier_semaphore()
+    for o in range(1, 8):
+        peer = lax.rem(seq + o, 8)
+        pl.semaphore_signal(barrier, inc=1, device_id=(peer, head), device_id_type=MESH)
+    pl.semaphore_signal(barrier, inc=1, device_id=(seq, mate), device_id_type=MESH)
+    pl.semaphore_wait(barrier, 8)
+    for i in range(4):
+        j = lax.rem(seq + i, 4)
+        target = 4 * core + j
+
+        @pl.when(target != seq)
+        def _():
+            send(
+                x_ref.at[j], o_ref.at[seq], out_send.at[j], in_recv.at[seq], target, head
+            ).start()
+
+        @pl.when(target == seq)
+        def _():
+            pltpu.make_async_copy(x_ref.at[j], o_ref.at[seq], local).start()
+
+    @pl.when(landing)
+    def _():
+        pltpu.make_async_copy(x_ref.at[0], o_ref.at[seq], local).wait()
+        send(o_ref.at[seq], o_ref.at[seq], f_send.at[seq], f_recv.at[seq], seq, mate).start()
+        for o in (1, 7, 2, 6, 3, 5, 4):
+            source = lax.rem(seq + o, 8)
+            send(
+                x_ref.at[0], o_ref.at[source], out_send.at[0], in_recv.at[source], source, head
+            ).wait_recv()
+            send(
+                o_ref.at[source], o_ref.at[source], f_send.at[source], f_recv.at[source], seq, mate
+            ).start()
+        for source in range(8):
+            send(
+                o_ref.at[source], o_ref.at[source], f_send.at[source], f_recv.at[source], seq, mate
+            ).wait_send()
+
+    @pl.when(jnp.logical_not(landing))
+    def _():
+        for source in range(8):
+            send(
+                o_ref.at[source], o_ref.at[source], f_send.at[source], f_recv.at[source], seq, mate
+            ).wait_recv()
+
+    for j in range(4):
+        @pl.when(4 * core + j != seq)
+        def _():
+            send(
+                x_ref.at[j], o_ref.at[seq], out_send.at[j], in_recv.at[seq], seq, mate
+            ).wait_send()
+
+
+def spread(x, number):
+    _, rows, cols = x.shape
+    return pl.pallas_call(
+        spread_kernel,
+        out_shape=jax.ShapeDtypeStruct((8, rows, cols), x.dtype),
+        in_specs=[HBM],
+        out_specs=HBM,
+        scratch_shapes=[DMA, DMA((4,)), DMA((8,)), DMA((8,)), DMA((8,))],
+        compiler_params=params(number),
+        name=f"spread_{number}",
+    )(x)
+
+
+def to_heads_kernel(x_ref, o_ref, local, out_send, in_recv):
+    seq, head, mate, _, _ = head_places()
+    core = lax.rem(head, 2)
+    plane = head - core
+    mine = seq // 4
+    barrier = pltpu.get_barrier_semaphore()
+    for source in range(8):
+        @pl.when(jnp.logical_or(source != seq, core != mine))
+        def _():
+            pl.semaphore_signal(
+                barrier, inc=1, device_id=(source, plane + mine), device_id_type=MESH
+            )
+
+    own = core == mine
+    pl.semaphore_wait(barrier, jnp.where(own, 7, 8))
+    for i in range(4):
+        j = lax.rem(seq + i, 4)
+        target = 4 * core + j
+        for c in range(2):
+            here = jnp.logical_and(target == seq, core == c)
+
+            @pl.when(jnp.logical_not(here))
+            def _():
+                send(
+                    x_ref.at[j, c], o_ref.at[seq], out_send.at[j, c], in_recv.at[seq], target, plane + c
+                ).start()
+
+            @pl.when(here)
+            def _():
+                pltpu.make_async_copy(x_ref.at[j, c], o_ref.at[seq], local).start()
+
+    for source in range(8):
+        away = jnp.logical_or(source != seq, core != mine)
+
+        @pl.when(away)
+        def _():
+            send(
+                x_ref.at[0, 0], o_ref.at[source], out_send.at[0, 0], in_recv.at[source], seq, mate
+            ).wait_recv()
+
+        @pl.when(jnp.logical_not(away))
+        def _():
+            pltpu.make_async_copy(x_ref.at[0, 0], o_ref.at[source], local).wait()
+
+    for j in range(4):
+        for c in range(2):
+            @pl.when(jnp.logical_not(jnp.logical_and(4 * core + j == seq, core == c)))
+            def _():
+                send(
+                    x_ref.at[j, c], o_ref.at[seq], out_send.at[j, c], in_recv.at[seq], seq, mate
+                ).wait_send()
+
+
+def to_heads(x, number):
+    _, _, rows, cols = x.shape
+    return pl.pallas_call(
+        to_heads_kernel,
+        out_shape=jax.ShapeDtypeStruct((8, rows, cols), x.dtype),
+        in_specs=[HBM],
+        out_specs=HBM,
+        scratch_shapes=[DMA, DMA((4, 2)), DMA((8,))],
+        compiler_params=params(number),
+        name=f"to_heads_{number}",
+    )(x)
+
+
+def from_heads_kernel(x_ref, o_ref, local, out_send, in_recv):
+    seq, head, mate, _, _ = head_places()
+    core = lax.rem(head, 2)
+    plane = head - core
+    home = seq // 4
+    slot = lax.rem(seq, 4)
+    barrier = pltpu.get_barrier_semaphore()
+    for j in range(4):
+        for c in range(2):
+            @pl.when(jnp.logical_not(jnp.logical_and(4 * core + j == seq, core == c)))
+            def _():
+                pl.semaphore_signal(
+                    barrier, inc=1, device_id=(4 * core + j, plane + c), device_id_type=MESH
+                )
+
+    own = core == home
+    pl.semaphore_wait(barrier, jnp.where(own, 7, 8))
+    for i in range(8):
+        source = lax.rem(seq + 1 + i, 8)
+        away = jnp.logical_or(source != seq, core != home)
+
+        @pl.when(away)
+        def _():
+            send(
+                x_ref.at[source],
+                o_ref.at[slot, core],
+                out_send.at[source],
+                in_recv.at[slot, core],
+                source,
+                plane + home,
+            ).start()
+
+        @pl.when(jnp.logical_not(away))
+        def _():
+            pltpu.make_async_copy(x_ref.at[source], o_ref.at[slot, core], local).start()
+
+    for j in range(4):
+        for c in range(2):
+            here = jnp.logical_and(4 * core + j == seq, core == c)
+
+            @pl.when(jnp.logical_not(here))
+            def _():
+                send(
+                    x_ref.at[0], o_ref.at[j, c], out_send.at[0], in_recv.at[j, c], seq, mate
+                ).wait_recv()
+
+            @pl.when(here)
+            def _():
+                pltpu.make_async_copy(x_ref.at[0], o_ref.at[j, c], local).wait()
+
+    for source in range(8):
+        @pl.when(jnp.logical_or(source != seq, core != home))
+        def _():
+            send(
+                x_ref.at[source], o_ref.at[slot, core], out_send.at[source], in_recv.at[slot, core], seq, mate
+            ).wait_send()
+
+
+def from_heads(x, number):
+    _, rows, cols = x.shape
+    return pl.pallas_call(
+        from_heads_kernel,
+        out_shape=jax.ShapeDtypeStruct((4, 2, rows, cols), x.dtype),
+        in_specs=[HBM],
+        out_specs=HBM,
+        scratch_shapes=[DMA, DMA((8,)), DMA((4, 2))],
+        compiler_params=params(number),
+        name=f"from_heads_{number}",
+    )(x)
+
+
+def seq_scatter_kernel(count, *refs):
+    ins, outs = refs[:count], refs[count : 2 * count]
+    scratch = refs[2 * count :]
+    own, inbox, post, final = (scratch[k * count : (k + 1) * count] for k in range(4))
+    l_sem, x_send, x_recv, z_send, z_recv = scratch[4 * count :]
+    seq = lax.axis_index("seq")
+    head = lax.axis_index("head")
+    x = lax.rem(seq, 2)
+    z = seq // 2
+    beside = 2 * z + 1 - x
+    barrier = pltpu.get_barrier_semaphore()
+    peers = [beside] + [2 * lax.rem(z + o, 4) + x for o in (1, 2, 3)]
+    greet([(peer, head) for peer in peers])
+    hops = []
+    for i in range(count):
+        for o in (1, 2, 3, 0):
+            zt = lax.rem(z + o, 4)
+            hop = send(
+                ins[i].at[2 * zt + 1 - x],
+                inbox[i].at[o],
+                x_send.at[i, o],
+                x_recv.at[i, o],
+                beside,
+                head,
+            )
+            hop.start()
+            copy = pltpu.make_async_copy(ins[i].at[2 * zt + x], own[i].at[o], l_sem.at[i, o])
+            copy.start()
+            hops.append((i, o, hop, copy))
+    last = []
+    for i, o, hop, copy in hops:
+        copy.wait()
+        hop.wait_recv()
+        total = own[i][o].astype(jnp.float32) + inbox[i][o].astype(jnp.float32)
+        if o == 0:
+            outs[i][...] = total
+        else:
+            post[i][o - 1] = total.astype(post[i].dtype)
+            far = send(
+                post[i].at[o - 1],
+                final[i].at[o - 1],
+                z_send.at[i, o - 1],
+                z_recv.at[i, o - 1],
+                2 * lax.rem(z + o, 4) + x,
+                head,
+            )
+            far.start()
+            last.append((i, o, far))
+    for i, o, far in last:
+        far.wait_recv()
+        outs[i][...] += final[i][o - 1].astype(jnp.float32)
+    for _, _, hop, _ in hops:
+        hop.wait_send()
+    for _, _, far in last:
+        far.wait_send()
+
+
+def seq_scatter(arrays, number):
+    count = len(arrays)
+    shapes = [a.shape[1:] for a in arrays]
+    return pl.pallas_call(
+        partial(seq_scatter_kernel, count),
+        out_shape=[jax.ShapeDtypeStruct(s, jnp.float32) for s in shapes],
+        in_specs=[HBM] * count,
+        out_specs=[VMEM] * count,
+        scratch_shapes=(
+            [pltpu.VMEM((4,) + s, a.dtype) for s, a in zip(shapes, arrays)]
+            + [pltpu.VMEM((4,) + s, a.dtype) for s, a in zip(shapes, arrays)]
+            + [pltpu.VMEM((3,) + s, a.dtype) for s, a in zip(shapes, arrays)]
+            + [pltpu.VMEM((3,) + s, a.dtype) for s, a in zip(shapes, arrays)]
+            + [DMA((count, 4)), DMA((count, 4)), DMA((count, 4)), DMA((count, 3)), DMA((count, 3))]
+        ),
+        compiler_params=params(number, 48 << 20),
+        name=f"seq_scatter_{number}",
+    )(*arrays)
+
+
+def seq_sum_kernel(rule, x_ref, *refs):
+    if rule is None:
+        o_ref, inbox, s_send, s_recv = refs
+    else:
+        e_ref, o_ref, t_ref, inbox, s_send, s_recv, row, rows, h_send, h_recv = refs
+    seq = lax.axis_index("seq")
+    head = lax.axis_index("head")
+    peers = [(lax.rem(seq + o, 8), head) for o in range(1, 8)]
+    others = [(seq, lax.rem(head + o, 4)) for o in range(1, 4)]
+    greet(peers + (others if rule is not None else []))
+    hops = []
+    for o in range(1, 8):
+        hop = send(
+            x_ref, inbox.at[seq], s_send.at[o - 1], s_recv.at[seq], lax.rem(seq + o, 8), head
+        )
+        hop.start()
+        hops.append(hop)
+    inbox[seq] = x_ref[...]
+    for o in range(1, 8):
+        source = lax.rem(seq + o, 8)
+        send(
+            x_ref, inbox.at[source], s_send.at[o - 1], s_recv.at[source], source, head
+        ).wait_recv()
+    total = inbox[0]
+    for s in range(1, 8):
+        total = total + inbox[s]
+    o_ref[...] = total
+    if rule is not None:
+        summed = jnp.sum(rule(total, e_ref[...]), axis=1, keepdims=True)
+        row[...] = jnp.broadcast_to(summed, row.shape)
+        more = []
+        for o in range(1, 4):
+            hop = send(
+                row, rows.at[head], h_send.at[o - 1], h_recv.at[head], seq, lax.rem(head + o, 4)
+            )
+            hop.start()
+            more.append(hop)
+        rows[head] = row[...]
+        for o in range(1, 4):
+            source = lax.rem(head + o, 4)
+            send(row, rows.at[source], h_send.at[o - 1], h_recv.at[source], seq, source).wait_recv()
+        t_ref[...] = rows[0] + rows[1] + rows[2] + rows[3]
+        hops += more
+    for hop in hops:
+        hop.wait_send()
+
+
+def seq_sum(x, number, rule=None, extra=None):
+    height, width = x.shape
+    shape = jax.ShapeDtypeStruct(x.shape, jnp.float32)
+    scratch = [pltpu.VMEM((8, height, width), jnp.float32), DMA((7,)), DMA((8,))]
+    name = f"seq_sum_{number}"
+    if rule is None:
+        return pl.pallas_call(
+            partial(seq_sum_kernel, None),
+            out_shape=shape,
+            in_specs=[VMEM],
+            out_specs=VMEM,
+            scratch_shapes=scratch,
+            compiler_params=params(number),
+            name=name,
+        )(x)
+    tall = extra.shape[0]
+    return pl.pallas_call(
+        partial(seq_sum_kernel, rule),
+        out_shape=[shape, jax.ShapeDtypeStruct((tall, 128), jnp.float32)],
+        in_specs=[VMEM, VMEM],
+        out_specs=[VMEM, VMEM],
+        scratch_shapes=scratch
+        + [
+            pltpu.VMEM((tall, 128), jnp.float32),
+            pltpu.VMEM((4, tall, 128), jnp.float32),
+            DMA((3,)),
+            DMA((4,)),
+        ],
+        compiler_params=params(number),
+        name=name,
+    )(x, extra)
+
+
+def head_blocks_kernel(count, *refs):
+    ins, outs, inbox = refs[:count], refs[count : 2 * count], refs[2 * count : 3 * count]
+    h_send, h_recv = refs[3 * count :]
+    seq = lax.axis_index("seq")
+    head = lax.axis_index("head")
+    others = [lax.rem(head + o, 4) for o in range(1, 4)]
+    greet([(seq, other) for other in others])
+    hops = []
+    for i in range(count):
+        for o, other in enumerate(others):
+            hop = send(
+                ins[i].at[other], inbox[i].at[head], h_send.at[i, o], h_recv.at[i, head], seq, other
+            )
+            hop.start()
+            hops.append(hop)
+        inbox[i][head] = ins[i][head]
+    for i in range(count):
+        for o, other in enumerate(others):
+            send(
+                ins[i].at[other], inbox[i].at[other], h_send.at[i, o], h_recv.at[i, other], seq, other
+            ).wait_recv()
+        outs[i][...] = inbox[i][0] + inbox[i][1] + inbox[i][2] + inbox[i][3]
+    for hop in hops:
+        hop.wait_send()
+
+
+def head_blocks(arrays, number):
+    count = len(arrays)
+    return pl.pallas_call(
+        partial(head_blocks_kernel, count),
+        out_shape=[jax.ShapeDtypeStruct(a.shape[1:], a.dtype) for a in arrays],
+        in_specs=[VMEM] * count,
+        out_specs=[VMEM] * count,
+        scratch_shapes=[pltpu.VMEM(a.shape, a.dtype) for a in arrays]
+        + [DMA((count, 3)), DMA((count, 4))],
+        compiler_params=params(number),
+        name=f"head_blocks_{number}",
+    )(*arrays)
+
+
+QUARTER = 256
+SPAN = 256
+LOCAL = pltpu.CompilerParams(vmem_limit_bytes=56 << 20)
+SMEM = pl.BlockSpec(memory_space=pltpu.SMEM)
+
+
+def lane_of(shape):
+    return lax.broadcasted_iota(jnp.int32, shape, len(shape) - 1)
+
+
+def swap_halves(x):
+    return pltpu.roll(x, 64, x.ndim - 1)
+
+
+def turn(x, sign):
+    upper = pltpu.roll(x, x.shape[-1] - 32, x.ndim - 1)
+    lower = pltpu.roll(x, 32, x.ndim - 1)
+    first = lax.rem(lane_of(x.shape), 64) < 32
+    if sign > 0:
+        return jnp.where(first, -upper, lower)
+    return jnp.where(first, upper, -lower)
+
+
+def segments(places, table, count):
+    total = jnp.zeros(places.shape, jnp.int32)
+    for u in range(count):
+        total = total + (places >= table[u]).astype(jnp.int32)
+    return total
+
+
+def key_block(ref, j):
+    per = 1024 // SPAN
+    return ref[j // per, pl.ds(512 + pl.multiple_of(lax.rem(j, per) * SPAN, SPAN), SPAN), :]
+
+
+def attend_kernel(utterances, table, x_ref, o_ref, l_ref, held):
+    core = table[utterances]
+
+    def of_source(source, carry):
+        packed = x_ref[source, pl.ds(pl.multiple_of(core * QUARTER, QUARTER), QUARTER), :]
+        packed = packed.astype(jnp.float32)
+        left = lane_of(packed.shape) < 64
+        halves = []
+        for sub in range(2):
+            query = jnp.where(left, swap_halves(packed) if sub else packed, 0.0).astype(jnp.bfloat16)
+            quarter = source * 4 + core + 2 * sub
+            low, high = table[utterances + 1 + quarter], table[utterances + 33 + quarter]
+            rows = quarter * QUARTER + lax.broadcasted_iota(jnp.int32, (QUARTER, 1), 0)
+            mine = segments(rows, table, utterances)
+
+            def scores(j, top):
+                raw = lax.dot_general(
+                    query, key_block(x_ref, j), (((1,), (1,)), ((), ())),
+                    preferred_element_type=jnp.float32,
+                )
+                keys = j * SPAN + lax.broadcasted_iota(jnp.int32, (1, SPAN), 1)
+                raw = jnp.where(mine == segments(keys, table, utterances), raw, -1e30)
+                held[j] = raw
+                for k in range(SPAN // 128):
+                    top = jnp.maximum(top, raw[:, 128 * k : 128 * (k + 1)])
+                return top
+
+            top = lax.fori_loop(low, high, scores, jnp.full((QUARTER, 128), -1e30, jnp.float32))
+            top = jnp.max(top, axis=1, keepdims=True)
+
+            def weights(j, total):
+                raised = jnp.exp(held[j] - top)
+                held[j] = raised
+                for k in range(SPAN // 128):
+                    total = total + raised[:, 128 * k : 128 * (k + 1)]
+                return total
+
+            total = lax.fori_loop(low, high, weights, jnp.zeros((QUARTER, 128), jnp.float32))
+            total = jnp.sum(total, axis=1, keepdims=True)
+            share = 1.0 / total
+
+            def mix(j, acc):
+                probs = (held[j] * share).astype(jnp.bfloat16)
+                return acc + jnp.dot(probs, key_block(x_ref, j), preferred_element_type=jnp.float32)
+
+            acc = lax.fori_loop(low, high, mix, jnp.zeros((QUARTER, 128), jnp.float32))
+            halves.append(acc)
+            spread_sum = jnp.broadcast_to(top + jnp.log(total), (QUARTER, 128))
+            l_ref[source, sub] = spread_sum.T[:8, :]
+        o_ref[source] = jnp.where(left, swap_halves(halves[0]), halves[1]).astype(jnp.bfloat16)
+        return carry
+
+    lax.fori_loop(0, 8, of_source, 0)
+
+
+def attend(table, x, utterances):
+    return pl.pallas_call(
+        partial(attend_kernel, utterances),
+        out_shape=[
+            jax.ShapeDtypeStruct((8, QUARTER, 128), jnp.bfloat16),
+            jax.ShapeDtypeStruct((8, 2, 8, QUARTER), jnp.float32),
+        ],
+        in_specs=[SMEM, VMEM],
+        out_specs=[VMEM, VMEM],
+        scratch_shapes=[pltpu.VMEM((8192 // SPAN, QUARTER, SPAN), jnp.float32)],
+        compiler_params=LOCAL,
+        name="attend",
+    )(table, x)
+
+
+def attend_back_kernel(utterances, table, x_ref, g_ref, l_ref, c_ref, s_ref, dq_ref, dkv_ref, held_p, held_d):
+    core = table[utterances]
+    dkv_ref[...] = jnp.zeros_like(dkv_ref)
+    per = 1024 // SPAN
+
+    def of_source(source, carry):
+        packed = x_ref[source, pl.ds(pl.multiple_of(core * QUARTER, QUARTER), QUARTER), :]
+        packed = packed.astype(jnp.float32)
+        grads = g_ref[source].astype(jnp.float32)
+        left = lane_of(packed.shape) < 64
+        halves = []
+        for sub in range(2):
+            query = jnp.where(left, swap_halves(packed) if sub else packed, 0.0).astype(jnp.bfloat16)
+            grad = jnp.where(left, 0.0, grads if sub else swap_halves(grads)).astype(jnp.bfloat16)
+            quarter = source * 4 + core + 2 * sub
+            low, high = table[utterances + 1 + quarter], table[utterances + 33 + quarter]
+            rows = quarter * QUARTER + lax.broadcasted_iota(jnp.int32, (1, QUARTER), 1)
+            mine = segments(rows, table, utterances)
+            logsum = l_ref[source, sub][:1, :]
+
+            def first(j, inner):
+                block = key_block(x_ref, j)
+                raw = lax.dot_general(
+                    block, query, (((1,), (1,)), ((), ())), preferred_element_type=jnp.float32
+                )
+                keys = j * SPAN + lax.broadcasted_iota(jnp.int32, (SPAN, 1), 0)
+                raw = jnp.where(mine == segments(keys, table, utterances), raw, -1e30)
+                probs = jnp.exp(raw - logsum)
+                slopes = lax.dot_general(
+                    block, grad, (((1,), (1,)), ((), ())), preferred_element_type=jnp.float32
+                )
+                held_p[j] = probs
+                held_d[j] = slopes
+                both = probs * slopes
+                for k in range(SPAN // 8):
+                    inner = inner + both[8 * k : 8 * (k + 1), :]
+                return inner
+
+            inner = lax.fori_loop(low, high, first, jnp.zeros((8, QUARTER), jnp.float32))
+            inner = jnp.sum(inner, axis=0, keepdims=True)
+
+            def second(j, acc):
+                probs = held_p[j]
+                d_scores = (probs * (held_d[j] - inner)).astype(jnp.bfloat16)
+                rows_at = pl.ds(pl.multiple_of(lax.rem(j, per) * SPAN, SPAN), SPAN)
+                dkv_ref[j // per, rows_at, :] += jnp.dot(
+                    d_scores, query, preferred_element_type=jnp.float32
+                ) + jnp.dot(probs.astype(jnp.bfloat16), grad, preferred_element_type=jnp.float32)
+                return acc + lax.dot_general(
+                    d_scores, key_block(x_ref, j), (((0,), (0,)), ((), ())),
+                    preferred_element_type=jnp.float32,
+                )
+
+            acc = lax.fori_loop(low, high, second, jnp.zeros((QUARTER, 128), jnp.float32))
+            halves.append(acc)
+        d_query = jnp.where(left, halves[0], swap_halves(halves[1])) * 0.125
+        d_query = d_query * c_ref[source] + turn(d_query * s_ref[source], -1)
+        dq_ref[source] = d_query.astype(jnp.bfloat16)
+        return carry
+
+    lax.fori_loop(0, 8, of_source, 0)
+
+
+def attend_back(table, x, grads, logsum, cosine, sine, utterances):
+    spans = 8192 // SPAN
+    return pl.pallas_call(
+        partial(attend_back_kernel, utterances),
+        out_shape=[
+            jax.ShapeDtypeStruct((8, QUARTER, 128), jnp.bfloat16),
+            jax.ShapeDtypeStruct((8, 1024, 128), jnp.float32),
+        ],
+        in_specs=[SMEM] + [VMEM] * 5,
+        out_specs=[VMEM, VMEM],
+        scratch_shapes=[
+            pltpu.VMEM((spans, SPAN, QUARTER), jnp.float32),
+            pltpu.VMEM((spans, SPAN, QUARTER), jnp.float32),
+        ],
+        compiler_params=LOCAL,
+        name="attend_back",
+    )(table, x, grads, logsum, cosine, sine)
+
+
+def home_kernel(dq_ref, dkv_ref, c_ref, s_ref, o_ref, inbox, post, local, p_send, p_recv, k_send, q_send, k_recv, q_recv):
+    seq, head, mate, _, _ = head_places()
+    core = lax.rem(head, 2)
+    plane = head - core
+    home = seq // 4
+    slot = lax.rem(seq, 4)
+    barrier = pltpu.get_barrier_semaphore()
+    for j in range(4):
+        for c in range(2):
+            @pl.when(jnp.logical_not(jnp.logical_and(4 * core + j == seq, core == c)))
+            def _():
+                pl.semaphore_signal(
+                    barrier, inc=1, device_id=(4 * core + j, plane + c), device_id_type=MESH
+                )
+
+    pl.semaphore_signal(barrier, inc=1, device_id=(seq, mate), device_id_type=MESH)
+    own = core == home
+    pl.semaphore_wait(barrier, jnp.where(own, 8, 9))
+    halves = []
+    for i in range(8):
+        source = lax.rem(seq + 1 + i, 8)
+        away = pl.ds(pl.multiple_of((1 - core) * 512, 512), 512)
+        hop = send(
+            dkv_ref.at[source, away], inbox.at[source], p_send.at[source], p_recv.at[source], seq, mate
+        )
+        hop.start()
+        halves.append((source, hop))
+    for source, _ in halves:
+        here = jnp.logical_and(source == seq, core == home)
+        q_part, k_part = pl.ds(0, 256), pl.ds(256, 512)
+
+        @pl.when(jnp.logical_not(here))
+        def _():
+            send(
+                dq_ref.at[source],
+                o_ref.at[slot, core, q_part],
+                q_send.at[source],
+                q_recv.at[slot, core],
+                source,
+                plane + home,
+            ).start()
+
+        @pl.when(here)
+        def _():
+            pltpu.make_async_copy(dq_ref.at[source], o_ref.at[slot, core, q_part], local.at[0]).start()
+
+    for source, hop in halves:
+        here = jnp.logical_and(source == seq, core == home)
+        q_part, k_part = pl.ds(0, 256), pl.ds(256, 512)
+        hop.wait_recv()
+        kept = pl.ds(pl.multiple_of(core * 512, 512), 512)
+        total = dkv_ref[source, kept, :] + inbox[source]
+        total = total * c_ref[source] + turn(total * s_ref[source], -1)
+        post[source] = total.astype(jnp.bfloat16)
+
+        @pl.when(jnp.logical_not(here))
+        def _():
+            send(
+                post.at[source],
+                o_ref.at[slot, core, k_part],
+                k_send.at[source],
+                k_recv.at[slot, core],
+                source,
+                plane + home,
+            ).start()
+
+        @pl.when(here)
+        def _():
+            pltpu.make_async_copy(post.at[source], o_ref.at[slot, core, k_part], local.at[1]).start()
+
+    q_part, k_part = pl.ds(0, 256), pl.ds(256, 512)
+    for j in range(4):
+        for c in range(2):
+            here = jnp.logical_and(4 * core + j == seq, core == c)
+
+            @pl.when(jnp.logical_not(here))
+            def _():
+                send(
+                    dq_ref.at[0], o_ref.at[j, c, q_part], q_send.at[0], q_recv.at[j, c], seq, mate
+                ).wait_recv()
+                send(
+                    post.at[0], o_ref.at[j, c, k_part], k_send.at[0], k_recv.at[j, c], seq, mate
+                ).wait_recv()
+
+            @pl.when(here)
+            def _():
+                pltpu.make_async_copy(dq_ref.at[0], o_ref.at[j, c, q_part], local.at[0]).wait()
+                pltpu.make_async_copy(post.at[0], o_ref.at[j, c, k_part], local.at[1]).wait()
+
+    for source in range(8):
+        @pl.when(jnp.logical_or(source != seq, core != home))
+        def _():
+            send(
+                dq_ref.at[source], o_ref.at[slot, core, q_part], q_send.at[source], q_recv.at[slot, core], seq, mate
+            ).wait_send()
+            send(
+                post.at[source], o_ref.at[slot, core, k_part], k_send.at[source], k_recv.at[slot, core], seq, mate
+            ).wait_send()
+    for _, hop in halves:
+        hop.wait_send()
+
+
+def gradients_home(dq, dkv, cosine, sine, number):
+    return pl.pallas_call(
+        home_kernel,
+        out_shape=jax.ShapeDtypeStruct((4, 2, 768, 128), jnp.bfloat16),
+        in_specs=[VMEM] * 4,
+        out_specs=HBM,
+        scratch_shapes=[
+            pltpu.VMEM((8, 512, 128), jnp.float32),
+            pltpu.VMEM((8, 512, 128), jnp.bfloat16),
+            DMA((2,)),
+            DMA((8,)),
+            DMA((8,)),
+            DMA((8,)),
+            DMA((8,)),
+            DMA((4, 2)),
+            DMA((4, 2)),
+        ],
+        compiler_params=params(number, 48 << 20),
+        name=f"gradients_home_{number}",
+    )(dq, dkv, cosine, sine)
+
+
+def pair_up(even, odd):
+    left = lane_of(even.shape) < 64
+    return jnp.where(left, even, swap_halves(odd)), jnp.where(left, swap_halves(even), odd)
+
+
+def project_kernel(x_ref, w_ref, c_ref, s_ref, o_ref):
+    def rotated(part, width, which, cos, sin):
+        raw = jnp.dot(
+            part, w_ref[:, which * 256 : which * 256 + width], preferred_element_type=jnp.float32
+        )
+        if cos is None:
+            return raw
+        return raw * cos + turn(raw, 1) * sin
+
+    for core in range(2):
+        queries = []
+        for sub in range(2):
+            quarter = core + 2 * sub
+            rows = pl.ds(quarter * QUARTER, QUARTER)
+            part = x_ref[rows, :]
+            cos, sin = c_ref[rows, :], s_ref[rows, :]
+            queries.append(rotated(part, 256, 0, cos, sin) * 0.125)
+            keys = rotated(part, 256, 1, cos, sin)
+            values = rotated(part, 256, 2, None, None)
+            for pair in range(2):
+                lanes = slice(128 * pair, 128 * (pair + 1))
+                k, v = keys[:, lanes], values[:, lanes]
+                left = lane_of(k.shape) < 64
+                at = pl.ds(512 + quarter * QUARTER, QUARTER)
+                o_ref[2 * pair, at, :] = jnp.where(left, k, swap_halves(v)).astype(jnp.bfloat16)
+                o_ref[2 * pair + 1, at, :] = jnp.where(left, swap_halves(k), v).astype(jnp.bfloat16)
+        for pair in range(2):
+            lanes = slice(128 * pair, 128 * (pair + 1))
+            even, odd = pair_up(queries[0][:, lanes], queries[1][:, lanes])
+            at = pl.ds(core * QUARTER, QUARTER)
+            o_ref[2 * pair, at, :] = even.astype(jnp.bfloat16)
+            o_ref[2 * pair + 1, at, :] = odd.astype(jnp.bfloat16)
+
+
+def project(x, w, cosine, sine):
+    return pl.pallas_call(
+        project_kernel,
+        out_shape=jax.ShapeDtypeStruct((4, 1536, 128), jnp.bfloat16),
+        in_specs=[VMEM] * 4,
+        out_specs=VMEM,
+        compiler_params=LOCAL,
+        name="project",
+    )(x, w, cosine, sine)
+
+
+def join_heads_kernel(x_ref, o_ref):
+    for core in range(2):
+        for pair in range(2):
+            even = x_ref[2 * pair, core].astype(jnp.float32)
+            odd = x_ref[2 * pair + 1, core].astype(jnp.float32)
+            first, second = pair_up(even, odd)
+            lanes = slice(128 * pair, 128 * (pair + 1))
+            o_ref[pl.ds(core * QUARTER, QUARTER), lanes] = first.astype(jnp.bfloat16)
+            o_ref[pl.ds((core + 2) * QUARTER, QUARTER), lanes] = second.astype(jnp.bfloat16)
+
+
+def join_heads(x):
+    return pl.pallas_call(
+        join_heads_kernel,
+        out_shape=jax.ShapeDtypeStruct((1024, 256), jnp.bfloat16),
+        in_specs=[VMEM],
+        out_specs=VMEM,
+        compiler_params=LOCAL,
+        name="join_heads",
+    )(x)
+
+
+def split_heads_kernel(x_ref, w_ref, o_ref):
+    for core in range(2):
+        pieces = [
+            lax.dot_general(
+                x_ref[pl.ds((core + 2 * sub) * QUARTER, QUARTER), :],
+                w_ref[...],
+                (((1,), (1,)), ((), ())),
+                preferred_element_type=jnp.float32,
+            )
+            for sub in range(2)
+        ]
+        for pair in range(2):
+            lanes = slice(128 * pair, 128 * (pair + 1))
+            even, odd = pair_up(pieces[0][:, lanes], pieces[1][:, lanes])
+            o_ref[2 * pair, core] = even.astype(jnp.bfloat16)
+            o_ref[2 * pair + 1, core] = odd.astype(jnp.bfloat16)
+
+
+def split_heads(x, w):
+    return pl.pallas_call(
+        split_heads_kernel,
+        out_shape=jax.ShapeDtypeStruct((4, 2, QUARTER, 128), jnp.bfloat16),
+        in_specs=[VMEM] * 2,
+        out_specs=VMEM,
+        compiler_params=LOCAL,
+        name="split_heads",
+    )(x, w)
+
+
+def unpack_kernel(x_ref, o_ref):
+    for core in range(2):
+        for pair in range(2):
+            lanes = slice(128 * pair, 128 * (pair + 1))
+            even = x_ref[2 * pair, core, pl.ds(0, 256), :].astype(jnp.float32)
+            odd = x_ref[2 * pair + 1, core, pl.ds(0, 256), :].astype(jnp.float32)
+            first, second = pair_up(even, odd)
+            o_ref[pl.ds(core * QUARTER, QUARTER), lanes] = first.astype(jnp.bfloat16)
+            o_ref[pl.ds((core + 2) * QUARTER, QUARTER), lanes] = second.astype(jnp.bfloat16)
+            even = x_ref[2 * pair, core, pl.ds(256, 512), :].astype(jnp.float32)
+            odd = x_ref[2 * pair + 1, core, pl.ds(256, 512), :].astype(jnp.float32)
+            keys, values = pair_up(even, odd)
+            at = pl.ds(core * 512, 512)
+            o_ref[at, slice(256 + 128 * pair, 384 + 128 * pair)] = keys.astype(jnp.bfloat16)
+            o_ref[at, slice(512 + 128 * pair, 640 + 128 * pair)] = values.astype(jnp.bfloat16)
+
+
+def unpack(x):
+    return pl.pallas_call(
+        unpack_kernel,
+        out_shape=jax.ShapeDtypeStruct((1024, 768), jnp.bfloat16),
+        in_specs=[VMEM],
+        out_specs=VMEM,
+        compiler_params=LOCAL,
+        name="unpack",
+    )(x)
+
+
+def blocks_of(array):
+    return array.reshape((8, array.shape[0] // 8) + array.shape[1:])
+
+
+def rows_of(gathered):
+    return gathered.reshape((gathered.shape[0] * gathered.shape[1],) + gathered.shape[2:])
+
+
+def normed(values):
+    center = values - jnp.mean(values, axis=-1, keepdims=True)
+    spread_of = jnp.mean(center * center, axis=-1, keepdims=True)
+    inverse = lax.rsqrt(spread_of + 1e-06)
+    return center * inverse, inverse
+
+
+def normed_back(grad, unit, inverse):
+    return (
+        grad
+        - jnp.mean(grad, axis=-1, keepdims=True)
+        - unit * jnp.mean(grad * unit, axis=-1, keepdims=True)
+    ) * inverse
+
+
+def root_rule(total, extra):
+    return jnp.sqrt(total + 1.0)
+
+
+def product_rule(total, extra):
+    return total[: extra.shape[0]] * extra
+
+
+def angles_of(places, lanes):
+    half_width = HEAD_DIM // 2
+    inverse = 10000.0 ** (-jnp.arange(half_width, dtype=jnp.float32) * 2.0 / HEAD_DIM)
+    inverse = jnp.concatenate([inverse] * (lanes // half_width) + [jnp.zeros((128 - lanes,))])
+    return places.astype(jnp.float32) * inverse
+
+
+def on_eight_by_four(
+    text_in,
+    mel_in,
+    time_embed,
+    lengths,
+    text_mask,
+    conv_weight,
+    norm_gain,
+    norm_bias,
+    expand_weight,
+    grn_gamma,
+    grn_beta,
+    shrink_weight,
+    join_weight,
+    modulation,
+    qkv_weight,
+    out_weight,
+    up_weight,
+    down_weight,
+    cotangent,
+):
+    rows_here = text_in.shape[0]
+    frames_here = rows_here * 4
+    seq_index = lax.axis_index("seq")
+    head_index = lax.axis_index("head")
+    core = lax.rem(head_index, 2)
+    utterances = lengths.shape[0]
+    row_first = (seq_index * 4 + head_index) * rows_here
+    frame_first = seq_index * frames_here
+    row_ids = row_first + jnp.arange(rows_here, dtype=jnp.int32)
+    frame_ids = frame_first + jnp.arange(frames_here, dtype=jnp.int32)
+    row_segment = segment_of(row_ids, lengths)
+    frame_segment = segment_of(frame_ids, lengths)
+    utter_ids = jnp.arange(utterances, dtype=jnp.int32)
+    row_onehot = (row_segment[:, None] == utter_ids[None, :]).astype(jnp.float32)
+    frame_onehot = (frame_segment[:, None] == utter_ids[None, :]).astype(jnp.float32)
+    mask_rows = text_mask.astype(jnp.float32)[:, None]
+    taps_count = conv_weight.shape[0]
+    half_kernel = taps_count // 2
+
+    bounds = jnp.cumsum(lengths)
+    starts = bounds - lengths
+    all_ids = jnp.arange(8 * frames_here, dtype=jnp.int32)
+    places = position_of(all_ids, lengths, segment_of(all_ids, lengths))
+    quarter_first = jnp.arange(32, dtype=jnp.int32) * QUARTER
+    first_segment = segment_of(quarter_first, lengths)
+    last_segment = segment_of(quarter_first + QUARTER - 1, lengths)
+    low = jnp.sum(jnp.where(first_segment[:, None] == utter_ids[None, :], starts[None, :], 0), axis=1)
+    high = jnp.sum(jnp.where(last_segment[:, None] == utter_ids[None, :], bounds[None, :], 0), axis=1)
+    table = jnp.concatenate(
+        [bounds, core[None], low // SPAN, (high + SPAN - 1) // SPAN]
+    ).astype(jnp.int32)
+    own_angles = angles_of(
+        lax.dynamic_slice_in_dim(places, frame_first, frames_here)[:, None], 128
+    )
+    own_cos, own_sin = jnp.cos(own_angles), jnp.sin(own_angles)
+    quarters = places.reshape(8, 2, 2, QUARTER)
+    query_places = lax.dynamic_index_in_dim(quarters, core, 2, keepdims=False)
+    query_angles = angles_of(
+        jnp.where(
+            jnp.arange(128) < 64, query_places[:, 0, :, None], query_places[:, 1, :, None]
+        ),
+        128,
+    )
+    query_cos, query_sin = jnp.cos(query_angles), jnp.sin(query_angles)
+    key_places = lax.dynamic_index_in_dim(places.reshape(8, 2, 512), core, 1, keepdims=False)
+    key_angles = angles_of(key_places[:, :, None], 64)
+    key_cos, key_sin = jnp.cos(key_angles), jnp.sin(key_angles)
+
+    extended = frame_rim(text_in, half_kernel)
+    extended_ids = (
+        row_first - half_kernel + jnp.arange(rows_here + 2 * half_kernel, dtype=jnp.int32)
+    )
+    extended_segment = segment_of(extended_ids, lengths)
+    same_taps = jnp.stack(
+        [
+            (extended_segment[tap : tap + rows_here] == row_segment).astype(jnp.float32)
+            for tap in range(taps_count)
+        ]
+    )
+    conv_out = jnp.zeros_like(text_in)
+    for tap in range(taps_count):
+        conv_out = (
+            conv_out
+            + extended[tap : tap + rows_here] * conv_weight[tap] * same_taps[tap][:, None]
+        )
+    text_unit, text_inverse = normed(conv_out)
+    text_low = (text_unit * norm_gain + norm_bias).astype(jnp.bfloat16)
+    cond_low = jax.nn.silu(time_embed).astype(jnp.bfloat16)
+    text_all, mod_parts = head_gather([text_low, narrow_dot(cond_low, modulation)], 0)
+    text_all = rows_of(text_all)
+    mod_all = mod_parts.transpose(1, 0, 2).reshape(utterances, -1)
+    expanded = narrow_dot(text_all, expand_weight)
+    activated, gelu_exact_back = jax.vjp(partial(jax.nn.gelu, approximate=False), expanded)
+    text_channels = expand_weight.shape[1] * 4
+    squares = exact_inner(frame_onehot, activated * activated)
+    squares_all, channel_total = seq_sum(squares, 1, root_rule, squares)
+    grn_norm = jnp.sqrt(squares_all + 1.0)
+    denominator = channel_total[:, 0] / text_channels + 1e-06
+    grn_ratio = grn_norm / denominator[:, None]
+    ratio_rows = exact_dot(frame_onehot, grn_ratio)
+    grn_low = (grn_gamma * activated * ratio_rows + grn_beta + activated).astype(jnp.bfloat16)
+    branch = product_scatter(grn_low, shrink_weight, 2)
+    join_low = (text_in + mask_rows * branch).astype(jnp.bfloat16)
+    hidden = mel_in + narrow_dot(join_low, join_weight)
+
+    mod_rows = exact_dot(row_onehot, mod_all)
+    shift_attn, scale_attn, gate_attn, shift_ffn, scale_ffn, gate_ffn = jnp.split(
+        mod_rows, 6, axis=1
+    )
+    hidden_unit, hidden_inverse = normed(hidden)
+    attn_low = (hidden_unit * (1.0 + scale_attn) + shift_attn).astype(jnp.bfloat16)
+    d_ffn_low = (cotangent * gate_ffn).astype(jnp.bfloat16)
+    attn_all = rows_of(head_gather([attn_low], 3)[0])
+    qkv_flat = qkv_weight.reshape(qkv_weight.shape[0], -1)
+    head_cols = qkv_weight.shape[2]
+    packed = spread(
+        project(
+            attn_all,
+            qkv_flat,
+            jnp.concatenate([own_cos, own_cos], axis=1),
+            jnp.concatenate([own_sin, own_sin], axis=1),
+        ),
+        4,
+    )
+    context_here, logsum = attend(table, packed, utterances)
+    context_low = join_heads(from_heads(context_here, 5))
+    attn_rows = product_scatter(context_low, out_weight, 6)
+    middle = hidden + gate_attn * attn_rows
+
+    middle_unit, middle_inverse = normed(middle)
+    ffn_low = (middle_unit * (1.0 + scale_ffn) + shift_ffn).astype(jnp.bfloat16)
+    ffn_all, d_ffn_all = (rows_of(g) for g in head_gather([ffn_low, d_ffn_low], 7))
+    upward = narrow_dot(ffn_all, up_weight)
+    gelu_value, gelu_tanh_back = jax.vjp(partial(jax.nn.gelu, approximate=True), upward)
+    gelu_low = gelu_value.astype(jnp.bfloat16)
+    d_up_low = gelu_tanh_back(against_rows(d_ffn_all, down_weight))[0].astype(jnp.bfloat16)
+    d_ffn_in = product_scatter(d_up_low, up_weight, 8, turned=True)
+    ffn_rows = product_scatter(gelu_low, down_weight, 9)
+    transformer_layer_output = middle + gate_ffn * ffn_rows
+    d_middle = cotangent + normed_back(
+        d_ffn_in * (1.0 + scale_ffn), middle_unit, middle_inverse
+    )
+    d_attn_low = (d_middle * gate_attn).astype(jnp.bfloat16)
+
+    d_attn_all = rows_of(head_gather([d_attn_low], 10)[0])
+    d_context = to_heads(split_heads(d_attn_all, out_weight), 11)
+    d_query, d_pair = attend_back(
+        table, packed, d_context, logsum, query_cos, query_sin, utterances
+    )
+    d_projected = unpack(gradients_home(d_query, d_pair, key_cos, key_sin, 12))
+    d_attn_in = product_scatter(d_projected, qkv_flat, 13, turned=True)
+    grad_mel = d_middle + normed_back(
+        d_attn_in * (1.0 + scale_attn), hidden_unit, hidden_inverse
+    )
+    d_mod_rows = jnp.concatenate(
+        [
+            d_attn_in,
+            d_attn_in * hidden_unit,
+            d_middle * attn_rows,
+            d_ffn_in,
+            d_ffn_in * middle_unit,
+            cotangent * ffn_rows,
+        ],
+        axis=1,
+    )
+    d_mod_part = exact_inner(row_onehot, d_mod_rows)
+
+    d_joined_low = grad_mel.astype(jnp.bfloat16)
+    d_text_out = against_rows(d_joined_low, join_weight)
+    d_branch_all = rows_of(head_gather([(mask_rows * d_text_out).astype(jnp.bfloat16)], 14)[0])
+    d_grn = against_rows(d_branch_all, shrink_weight)
+    sums_here = jnp.concatenate(
+        [
+            exact_inner(frame_onehot, d_grn * grn_gamma * activated),
+            jnp.sum(d_grn * activated * ratio_rows, axis=0)[None, :],
+            jnp.sum(d_grn, axis=0)[None, :],
+            jnp.zeros((6, d_grn.shape[1]), jnp.float32),
+        ]
+    )
+    sums_all, inner_total = seq_sum(sums_here, 15, product_rule, grn_norm)
+    d_ratio = sums_all[:utterances]
+    grad_gamma, grad_beta = sums_all[utterances], sums_all[utterances + 1]
+    d_mean = -inner_total[:, 0] / (denominator * denominator)
+    d_norm = d_ratio / denominator[:, None] + (d_mean / text_channels)[:, None]
+    d_activated = d_grn * (grn_gamma * ratio_rows + 1.0) + activated * exact_dot(
+        frame_onehot, d_norm / grn_norm
+    )
+    d_expanded_low = gelu_exact_back(d_activated)[0].astype(jnp.bfloat16)
+    d_text_norm = product_scatter(d_expanded_low, expand_weight, 16, turned=True)
+    d_conv_out = normed_back(d_text_norm * norm_gain, text_unit, text_inverse)
+    grad_gain_part = jnp.sum(d_text_norm * text_unit, axis=0)
+    grad_bias_part = jnp.sum(d_text_norm, axis=0)
+    d_extended = frame_rim(d_conv_out, half_kernel)
+    grad_text = d_text_out
+    conv_grads = []
+    for tap in range(taps_count):
+        mirror = 2 * half_kernel - tap
+        grad_text = (
+            grad_text
+            + d_extended[mirror : mirror + rows_here]
+            * conv_weight[tap]
+            * same_taps[mirror][:, None]
+        )
+        conv_grads.append(
+            jnp.sum(
+                d_conv_out * extended[tap : tap + rows_here] * same_taps[tap][:, None], axis=0
+            )
+        )
+
+    def part(left, right):
+        return blocks_of(inner_rows(left, right).astype(jnp.bfloat16))
+
+    small = jnp.concatenate(
+        [
+            jnp.stack(conv_grads + [grad_gain_part, grad_bias_part]),
+            jnp.zeros((16 - taps_count - 2, text_in.shape[1]), jnp.float32),
+        ]
+    )
+    small = jnp.pad(small.reshape(16, 8, 64).transpose(1, 0, 2), ((0, 0), (0, 0), (0, 64)))
+    mod_blocks = d_mod_part.reshape(utterances, 8, -1).transpose(1, 0, 2)
+    up, down, qkv, out, shrink, expand, join, small, mod = seq_scatter(
+        [
+            part(ffn_all, d_up_low),
+            part(d_ffn_all, gelu_low),
+            part(attn_all, d_projected),
+            part(d_attn_all, context_low),
+            part(d_branch_all, grn_low),
+            part(text_all, d_expanded_low),
+            part(d_joined_low, join_low),
+            small,
+            mod_blocks,
+        ],
+        17,
+    )
+    join, small, mod = head_blocks(
+        [
+            join.reshape(4, -1, join.shape[1]),
+            jnp.pad(small[:, :64].reshape(16, 4, 16).transpose(1, 0, 2), ((0, 0), (0, 0), (0, 112))),
+            mod.reshape(utterances, 4, -1).transpose(1, 0, 2),
+        ],
+        18,
+    )
+    grad_modulation = exact_inner(cond_low.astype(jnp.float32), mod)
+    return (
+        transformer_layer_output,
+        grad_text,
+        grad_mel,
+        small[:taps_count, :16],
+        small[taps_count, :16],
+        small[taps_count + 1, :16],
+        expand,
+        grad_gamma,
+        grad_beta,
+        shrink.T,
+        join.T,
+        grad_modulation,
+        qkv.reshape(qkv.shape[0], 3, head_cols),
+        out.T,
+        up,
+        down.T,
+    )
+
+
 def solution(mesh):
+    fits = mesh.shape["seq"] == 8 and mesh.shape["head"] == 4
     return jax.shard_map(
-        on_device,
+        on_eight_by_four if fits else on_device,
         mesh=mesh,
         in_specs=(
             P(("seq", "head"), None),

time: 2090 us -> 796 us (0.38)
  waiting for transfers between devices: 1300 us -> 0.01 us
  Pallas kernels: 0 us -> 632 us
  matrix products: 375 us -> 51.9 us
  other arithmetic: 205 us -> 53.5 us
  blocking collectives: 117 us -> 0 us
  starting transfers between devices: 41.9 us -> 8.68 us
    reduce_scatter x13 -> x0, waiting for transfers between devices: 864 us -> none  [the longest x6 312 us: head_sums(): lax.psum_scatter(action(jnp.int32(0), lax.axis_size('head') * count_rows)...]
    pallas_call x0 -> x25, Pallas kernels: none -> 632 us  [the longest x6 144 us: product_scatter(): pl.pallas_call(partial(product_scatter_kernel, turned, cuts, wire), out_s...]
    dot_general x15 -> x0, matrix products: 297 us -> none  [the longest x2 76.4 us: on_device(): jnp.einsum('qhd,khd->hqk', grad_block, value_heads, preferred_element_typ...]
    unnamed x23 -> x0, waiting for transfers between devices: 161 us -> none
    ppermute x12 -> x0, waiting for transfers between devices: 150 us -> none  [from_behind(): lax.ppermute(value, axis, [(source, source + steps) for source in range(f...]
    all_gather x6 -> x0, waiting for transfers between devices: 124 us -> none  [head_rows(): return lax.all_gather(values, 'head', axis=0, tiled=True)]
    convert_element_type x12 -> x10, other arithmetic: 105 us -> 11 us  [the longest x1 4.09 us: on_eight_by_four(): d_attn_low = (d_middle * gate_attn).astype(jnp.bfloat16)]
    psum x4 -> x0, blocking collectives: 70.9 us -> none  [the longest x2 58.8 us: utter_sum(): return lax.psum(values, 'seq')]
  transfers between devices with their start and end apart: 37 -> 4, of which waited for: 27 -> 0; matrix products, arithmetic and copies ran while one was open for 5% -> 5% of each run, Pallas kernels for 0% -> 11%
where the time goes in v1:
time: 796 us; the launch traced here: 791 us
  Pallas kernels  632 us (79%)
  other arithmetic  53.5 us (7%)
  matrix products  51.9 us (7%)
  local copies, waits for them, and re-layouts  42.2 us (5%)
  starting transfers between devices  8.68 us (1%)
    pallas_call x6, Pallas kernels, product_scatter(): pl.pallas_call(partial(product_scatter_kernel, turned, cuts, wire), out_s...  144 us
    pallas_call x5, Pallas kernels, head_gather(): pl.pallas_call(partial(gather_kernel, count, cuts), out_shape=[jax.ShapeD...  94.6 us
    pallas_call x1, Pallas kernels, attend_back(): pl.pallas_call(partial(attend_back_kernel, utterances), out_shape=[jax.Sh...  82.7 us
    pallas_call x1, Pallas kernels, seq_scatter(): pl.pallas_call(partial(seq_scatter_kernel, count), out_shape=[jax.ShapeDt...  77.8 us
    pallas_call x1, Pallas kernels, attend(): pl.pallas_call(partial(attend_kernel, utterances), out_shape=[jax.ShapeDt...  69.9 us
    pallas_call x1, Pallas kernels, spread(): pl.pallas_call(spread_kernel, out_shape=jax.ShapeDtypeStruct((8, rows, co...  42.7 us
    pallas_call x2, Pallas kernels, seq_sum(): pl.pallas_call(partial(seq_sum_kernel, rule), out_shape=[shape, jax.Shape...  33.4 us
    pallas_call x1, Pallas kernels, gradients_home(): pl.pallas_call(home_kernel, out_shape=jax.ShapeDtypeStruct((4, 2, 768, 12...  32.9 us
  transfers between devices with their start and end apart: 4, of which 0 were waited for; matrix products, arithmetic and copies ran while one was open for 5% of the time, Pallas kernels for 11%

profile of v1, /device:TPU:0, one launch (start us, length us, event | category | flops | bytes accessed | tf_op | source)
XLA Modules:
  0.0 790.8 jit_solution(10431840655879704771)
XLA Ops:
  1.6 2.5 collective-permute-start
  7.3 1.9 constant_dynamic-update-slice_fusion.1
  11.1 1.9 fusion.78.refs_1_
  13.0 1.9 multiply_sine_fusion.1
  14.9 1.5 pad_maximum_fusion
  16.4 9.0 %multiply_sine_fusion = (f32[8,512,128]{2,1,0:T(8,128)}, f32[8,512,128]{2,1,0:T(8,128)}) fusion(f32[128]{0:T(128)S(1)} %get-tuple-element.197, f32[8,512]{1,0:T(8,128)S(1)} %bitcast.116), kind=kLoop, calls=%fused_computation | loop fusion | flops 524288 | bytes 4211200 | tf_op jit(solution)/shard_map/sin | solution.py:1602
  25.3 5.6 fusion.14
  31.5 1.7 copy.58
  33.3 1.6 copy.59.w_ref
  36.9 15.6 %head_gather_0.1 = (bf16[4,256,512]{2,1,0:T(8,128)(2,1)}, f32[4,8,1536]{2,1,0:T(8,128)}) custom-call(bf16[256,512]{1,0:T(8,128)(2,1)} %add_convert_fusion.3.refs_0_, f32[8,1536]{1,0:T(8,128)} %fusion.78.refs_1_), custom_call_target="tpu_custom_call" | custom-call | tf_op jit(solution)/shard_map/head_gather_0/pallas_call | solution.py:562
  52.5 3.6 fusion.8
  57.6 12.6 %seq_sum_1.1 = (f32[8,256]{1,0:T(8,128)}, f32[8,128]{1,0:T(8,128)}) custom-call(f32[8,256]{1,0:T(8,128)} %fusion.16.x_ref.refs_0_, f32[8,256]{1,0:T(8,128)} %fusion.16.x_ref.refs_0_), custom_call_target="tpu_custom_call" | custom-call | tf_op jit(solution)/shard_map/seq_sum_1/pallas_call | solution.py:1000
  72.3 2.3 add_convert_fusion.1
  74.7 16.0 %product_scatter_2.1 = f32[256,512]{1,0:T(8,128)S(1)} custom-call(bf16[1024,256]{1,0:T(8,128)(2,1)S(1)} %get-tuple-element.201.a_ref, bf16[256,512]{1,0:T(8,128)(2,1)S(1)} %copy-done.13), custom_call_target="tpu_custom_call" | custom-call | tf_op jit(solution)/shard_map/product_scatter_2/pallas_call | solution.py:633
  91.9 4.9 fusion.60
  96.8 2.6 fusion.10.refs_0_
  99.4 17.3 %head_gather_3.1 = bf16[4,256,1024]{2,1,0:T(8,128)(2,1)} custom-call(bf16[256,1024]{1,0:T(8,128)(2,1)} %fusion.10.refs_0_), custom_call_target="tpu_custom_call" | custom-call | tf_op jit(solution)/shard_map/head_gather_3/pallas_call | solution.py:562
  116.8 6.0 project.1.x_ref
  122.8 42.7 %spread_4.1.x_ref = bf16[8,1536,128]{2,1,0:T(8,128)(2,1)} custom-call(bf16[4,1536,128]{2,1,0:T(8,128)(2,1)} %project.1.x_ref), custom_call_target="tpu_custom_call" | custom-call | tf_op jit(solution)/shard_map/spread_4/pallas_call | solution.py:712
  165.5 69.9 %attend.1 = (bf16[8,256,128]{2,1,0:T(8,128)(2,1)}, f32[8,2,8,256]{3,2,1,0:T(8,128)}) custom-call(s32[73]{0:T(128)} %pad_add_fusion.table, bf16[8,1536,128]{2,1,0:T(8,128)(2,1)} %spread_4.1.x_ref), custom_call_target="tpu_custom_call" | custom-call | tf_op jit(solution)/shard_map/attend/pallas_call | solution.py:1148
  235.4 13.5 %from_heads_5.1.x_ref = bf16[4,2,256,128]{3,2,1,0:T(8,128)(2,1)} custom-call(bf16[8,256,128]{2,1,0:T(8,128)(2,1)} %get-tuple-element.44.x_ref), custom_call_target="tpu_custom_call" | custom-call | tf_op jit(solution)/shard_map/from_heads_5/pallas_call | solution.py:849
  248.9 2.1 join_heads.1.a_ref
  252.0 27.7 %product_scatter_6.1 = f32[256,1024]{1,0:T(8,128)S(1)} custom-call(bf16[1024,256]{1,0:T(8,128)(2,1)S(1)} %copy-done.8, bf16[256,1024]{1,0:T(8,128)(2,1)S(1)} %copy-done.9), custom_call_target="tpu_custom_call" | custom-call | tf_op jit(solution)/shard_map/product_scatter_6/pallas_call | solution.py:633
  279.8 1.5 fusion.81
  281.6 3.2 multiply_convert_fusion.2
  284.8 33.6 %head_gather_7.1 = (bf16[4,256,1024]{2,1,0:T(8,128)(2,1)}, bf16[4,256,1024]{2,1,0:T(8,128)(2,1)}) custom-call(bf16[256,1024]{1,0:T(8,128)(2,1)} %get-tuple-element.162.refs_0_, bf16[256,1024]{1,0:T(8,128)(2,1)} %get-tuple-element.161.refs_1_), custom_call_target="tpu_custom_call" | custom-call | tf_op jit(solution)/shard_map/head_gather_7/pallas_call | solution.py:562
  318.5 3.0 fusion.88
  321.5 2.5 fusion.6
  324.1 2.3 convolution_convert_fusion.3
  326.3 28.0 %product_scatter_8.1 = f32[256,1024]{1,0:T(8,128)S(1)} custom-call(bf16[1024,512]{1,0:T(8,128)(2,1)S(1)} %get-tuple-element.165.a_ref, bf16[1024,512]{1,0:T(8,128)(2,1)S(1)} %copy-done.10), custom_call_target="tpu_custom_call" | custom-call | tf_op jit(solution)/shard_map/product_scatter_8/pallas_call | solution.py:633
  354.3 2.3 convolution_convert_fusion.2
  356.6 27.8 %product_scatter_9.1 = f32[256,1024]{1,0:T(8,128)S(1)} custom-call(bf16[1024,512]{1,0:T(8,128)(2,1)S(1)} %get-tuple-element.166.a_ref, bf16[512,1024]{1,0:T(8,128)(2,1)S(1)} %copy-done.12), custom_call_target="tpu_custom_call" | custom-call | tf_op jit(solution)/shard_map/product_scatter_9/pallas_call | solution.py:633
  384.4 1.7 fusion.79
  386.1 4.1 multiply_convert_fusion.1
  390.2 18.4 %head_gather_10.1 = bf16[4,256,1024]{2,1,0:T(8,128)(2,1)} custom-call(bf16[256,1024]{1,0:T(8,128)(2,1)} %get-tuple-element.152.refs_0_), custom_call_target="tpu_custom_call" | custom-call | tf_op jit(solution)/shard_map/head_gather_10/pallas_call | solution.py:562
  408.7 3.2 convolution_convert_fusion.4
  411.9 3.3 split_heads.1.x_ref
  415.2 18.3 %to_heads_11.1.g_ref = bf16[8,256,128]{2,1,0:T(8,128)(2,1)} custom-call(bf16[4,2,256,128]{3,2,1,0:T(8,128)(2,1)} %split_heads.1.x_ref), custom_call_target="tpu_custom_call" | custom-call | tf_op jit(solution)/shard_map/to_heads_11/pallas_call | solution.py:778
  433.5 82.7 %attend_back.1 = (bf16[8,256,128]{2,1,0:T(8,128)(2,1)}, f32[8,1024,128]{2,1,0:T(8,128)}) custom-call(s32[73]{0:T(128)} %pad_add_fusion.table, bf16[8,1536,128]{2,1,0:T(8,128)(2,1)} %spread_4.1.x_ref, bf16[8,256,128]{2,1,0:T(8,128)(2,1)} %to_heads_11.1.g_ref, f32[8,2,8,256]{3,2,1,0:T(8,128)} %get-tuple-element.47.l_ref, ...), custom_call_target="tpu_custom_call" | custom-call | tf_op jit(solution)/shard_map/attend_back/pallas_call | solution.py:1227
  517.2 32.9 %gradients_home_12.1.x_ref = bf16[4,2,768,128]{3,2,1,0:T(8,128)(2,1)S(1)} custom-call(bf16[8,256,128]{2,1,0:T(8,128)(2,1)S(1)} %copy-done.17, f32[8,1024,128]{2,1,0:T(8,128)} %get-tuple-element.49.dkv_ref, f32[8,512,128]{2,1,0:T(8,128)S(1)} %copy-done.3, f32[8,512,128]{2,1,0:T(8,128)} %get-tuple-element.174.s_ref), custom_call_target="tpu_custom_call" | custom-call | tf_op jit(solution)/shard_map/gradients_home_12/pallas_call | solution.py:1347
  551.4 3.3 unpack.1.a_ref
  556.1 28.1 %product_scatter_13.1 = f32[256,1024]{1,0:T(8,128)S(1)} custom-call(bf16[1024,768]{1,0:T(8,128)(2,1)S(1)} %copy-done.5, bf16[1024,768]{1,0:T(8,128)(2,1)S(1)} %copy-done.2), custom_call_target="tpu_custom_call" | custom-call | tf_op jit(solution)/shard_map/product_scatter_13/pallas_call | solution.py:633
  584.2 3.0 convolution_convert_fusion
  587.3 1.7 fusion.80
  589.0 1.7 multiply_dynamic-update-slice_fusion.3
  591.8 1.9 multiply_convert_fusion.3
  594.0 9.6 %head_gather_14.1 = bf16[4,256,512]{2,1,0:T(8,128)(2,1)} custom-call(bf16[256,512]{1,0:T(8,128)(2,1)} %get-tuple-element.205.refs_0_), custom_call_target="tpu_custom_call" | custom-call | tf_op jit(solution)/shard_map/head_gather_14/pallas_call | solution.py:562
  603.7 2.7 convolution_convert_fusion.6
  606.4 2.0 multiply_reduce_fusion
  610.1 20.8 %seq_sum_15.1 = (f32[16,256]{1,0:T(8,128)}, f32[8,128]{1,0:T(8,128)}) custom-call(f32[16,256]{1,0:T(8,128)} %maximum_maximum_fusion.x_ref, f32[8,256]{1,0:T(8,128)} %add_sqrt_fusion.refs_0_), custom_call_target="tpu_custom_call" | custom-call | tf_op jit(solution)/shard_map/seq_sum_15/pallas_call | solution.py:1000
  633.0 3.4 add_convert_fusion.a_ref
  637.6 16.0 %product_scatter_16.1 = f32[256,512]{1,0:T(8,128)S(1)} custom-call(bf16[1024,256]{1,0:T(8,128)(2,1)S(1)} %add_convert_fusion.a_ref, bf16[512,256]{1,0:T(8,128)(2,1)S(1)} %copy-done.21), custom_call_target="tpu_custom_call" | custom-call | tf_op jit(solution)/shard_map/product_scatter_16/pallas_call | solution.py:633
  653.7 1.5 convolution_convert_fusion.1
  660.1 5.2 fusion.59
  666.4 1.5 multiply_reduce_fusion.6
  671.4 3.6 collective-permute-start.3
  677.9 77.8 %seq_scatter_17.1 = (f32[128,512]{1,0:T(8,128)S(1)}, f32[128,512]{1,0:T(8,128)S(1)}, f32[128,768]{1,0:T(8,128)S(1)}, f32[128,256]{1,0:T(8,128)S(1)}, f32[64,256]...) custom-call(bf16[8,128,512]{2,1,0:T(8,128)(2,1)S(1)} %bitcast.92, ...), custom_call_target="tpu_custom_call" | custom-call | tf_op jit(solution)/shard_map/seq_scatter_17/pallas_call | solution.py:920
  763.2 8.2 %head_blocks_18.1 = (f32[32,512]{1,0:T(8,128)}, f32[16,128]{1,0:T(8,128)}, f32[8,192]{1,0:T(8,128)}) custom-call(f32[4,32,512]{2,1,0:T(8,128)} %bitcast.98, f32[4,16,128]{2,1,0:T(8,128)} %pad.9.refs_1_, f32[4,8,192]{2,1,0:T(8,128)} %bitcast.114), custom_call_target="tpu_custom_call" | custom-call | tf_op jit(solution)/shard_map/head_blocks_18/pallas_call | solution.py:1045
  771.5 2.2 fusion.77
  776.1 1.7 copy.66
  777.8 1.9 copy.67
  780.7 2.0 copy.65
  782.7 4.4 fusion.29
  788.3 1.5 copy.89
  (279 shorter events, 49.7 us)
Async XLA Ops:
  0.6 10.5 %copy-start = (bf16[1024,1536]{1,0:T(8,128)(2,1)S(1)}, bf16[1024,1536]{1,0:T(8,128)(2,1)}, u32[]{:S(2)}) copy-start(bf16[1024,1536]{1,0:T(8,128)(2,1)} %param.32) | copy-start | bytes 9437188
  1.6 33.4 %collective-permute-start = (f32[3,512]{1,0:T(4,128)S(1)}, f32[3,512]{1,0:T(4,128)S(1)}, u32[]{:S(2)}, u32[]{:S(2)}) collective-permute-start(f32[3,512]{1,0:T(4,128)S(1)} %get-tuple-element.170), channel_id=1, source_target_pairs={{0,1},{1,2},{2,3},{3,4},{4,5},{5,6},{6,7},{7,8},{8,9},{9,10},{10,1... | collective-permute-start | bytes 18440 | tf_op jit(solution)/shard_map/ppermute | solution.py:19
  4.0 30.9 %collective-permute-start.1 = (f32[3,512]{1,0:T(4,128)S(1)}, f32[3,512]{1,0:T(4,128)S(1)}, u32[]{:S(2)}, u32[]{:S(2)}) collective-permute-start(f32[3,512]{1,0:T(4,128)S(1)} %get-tuple-element.171), channel_id=1, source_target_pairs={{1,0},{2,1},{3,2},{4,3},{5,4},{6,5},{7,6},{8,7},{9,8},{10,9},{11,1... | collective-permute-start | bytes 18440 | tf_op jit(solution)/shard_map/ppermute | solution.py:22
  9.7 656.0 %copy-start.74 = (f32[256]{0:T(256)}, f32[256]{0:T(256)S(1)}, u32[]{:S(2)}) copy-start(f32[256]{0:T(256)S(1)} %get-tuple-element.158) | copy-start | bytes 3076
  9.8 655.9 %copy-start.75 = (f32[256]{0:T(256)}, f32[256]{0:T(256)S(1)}, u32[]{:S(2)}) copy-start(f32[256]{0:T(256)S(1)} %get-tuple-element.191) | copy-start | bytes 3076
  9.8 655.9 %copy-start.76 = (f32[256]{0:T(256)}, f32[256]{0:T(256)S(1)}, u32[]{:S(2)}) copy-start(f32[256]{0:T(256)S(1)} %get-tuple-element.192) | copy-start | bytes 3076
  9.8 655.9 %copy-start.77 = (f32[256]{0:T(256)}, f32[256]{0:T(256)S(1)}, u32[]{:S(2)}) copy-start(f32[256]{0:T(256)S(1)} %get-tuple-element.193) | copy-start | bytes 3076
  9.8 655.9 %copy-start.78 = (f32[256]{0:T(256)}, f32[256]{0:T(256)S(1)}, u32[]{:S(2)}) copy-start(f32[256]{0:T(256)S(1)} %get-tuple-element.194) | copy-start | bytes 3076
  9.8 655.9 %copy-start.79 = (f32[256]{0:T(256)}, f32[256]{0:T(256)S(1)}, u32[]{:S(2)}) copy-start(f32[256]{0:T(256)S(1)} %get-tuple-element.195) | copy-start | bytes 3076
  9.8 655.9 %copy-start.80 = (f32[256]{0:T(256)}, f32[256]{0:T(256)S(1)}, u32[]{:S(2)}) copy-start(f32[256]{0:T(256)S(1)} %get-tuple-element.196) | copy-start | bytes 3076
  10.8 24.1 %copy-start.68 = (f32[1,512]{1,0:T(1,128)}, f32[1,512]{1,0:T(1,128)S(1)}, u32[]{:S(2)}) copy-start(f32[1,512]{1,0:T(1,128)S(1)} %get-tuple-element.182) | copy-start | bytes 6148
  10.9 24.1 %copy-start.69 = (f32[1,512]{1,0:T(1,128)}, f32[1,512]{1,0:T(1,128)S(1)}, u32[]{:S(2)}) copy-start(f32[1,512]{1,0:T(1,128)S(1)} %get-tuple-element.183) | copy-start | bytes 6148
  10.9 24.1 %copy-start.70 = (f32[1,512]{1,0:T(1,128)}, f32[1,512]{1,0:T(1,128)S(1)}, u32[]{:S(2)}) copy-start(f32[1,512]{1,0:T(1,128)S(1)} %get-tuple-element.184) | copy-start | bytes 6148
  10.9 24.1 %copy-start.71 = (f32[1,512]{1,0:T(1,128)}, f32[1,512]{1,0:T(1,128)S(1)}, u32[]{:S(2)}) copy-start(f32[1,512]{1,0:T(1,128)S(1)} %get-tuple-element.185) | copy-start | bytes 6148
  10.9 24.1 %copy-start.72 = (f32[1,512]{1,0:T(1,128)}, f32[1,512]{1,0:T(1,128)S(1)}, u32[]{:S(2)}) copy-start(f32[1,512]{1,0:T(1,128)S(1)} %get-tuple-element.186) | copy-start | bytes 6148
  25.3 6.2 copy-start.83
  34.9 17.6 %copy-start.40 = (f32[259,512]{1,0:T(8,128)}, f32[259,512]{1,0:T(8,128)S(1)}, u32[]{:S(2)}) copy-start(f32[259,512]{1,0:T(8,128)S(1)} %constant_dynamic-update-slice_fusion) | copy-start | bytes 1591300
  35.0 17.5 %copy-start.20 = (bf16[512,256]{1,0:T(8,128)(2,1)S(1)}, bf16[512,256]{1,0:T(8,128)(2,1)}, u32[]{:S(2)}) copy-start(bf16[512,256]{1,0:T(8,128)(2,1)} %w_ref.11) | copy-start | bytes 786436
  35.8 16.8 %copy-start.46 = (f32[256,512]{1,0:T(8,128)}, f32[256,512]{1,0:T(8,128)S(1)}, u32[]{:S(2)}) copy-start(f32[256,512]{1,0:T(8,128)S(1)} %get-tuple-element.157) | copy-start | bytes 1572868
  56.1 18.5 %copy-start.42 = (f32[1024,256]{1,0:T(8,128)}, f32[1024,256]{1,0:T(8,128)S(1)}, u32[]{:S(2)}) copy-start(f32[1024,256]{1,0:T(8,128)S(1)} %get-tuple-element.199) | copy-start | bytes 3145732
  56.1 18.5 %copy-start.44 = (f32[1024,256]{1,0:T(8,128)}, f32[1024,256]{1,0:T(8,128)S(1)}, u32[]{:S(2)}) copy-start(f32[1024,256]{1,0:T(8,128)S(1)} %get-tuple-element.200) | copy-start | bytes 3145732
  56.1 16.2 %copy-start.81 = (f32[256]{0:T(256)S(1)}, f32[256]{0:T(256)}, u32[]{:S(2)}) copy-start(f32[256]{0:T(256)} %param.28) | copy-start | bytes 3076
  56.1 16.2 %copy-start.84 = (f32[256]{0:T(256)S(1)}, f32[256]{0:T(256)}, u32[]{:S(2)}) copy-start(f32[256]{0:T(256)} %param.29) | copy-start | bytes 3076
  57.6 17.1 %copy-start.13 = (bf16[256,512]{1,0:T(8,128)(2,1)S(1)}, bf16[256,512]{1,0:T(8,128)(2,1)}, u32[]{:S(2)}) copy-start(bf16[256,512]{1,0:T(8,128)(2,1)} %w_ref.6) | copy-start | bytes 786436
  74.6 16.8 %copy-start.7 = (bf16[1024,256]{1,0:T(8,128)(2,1)}, bf16[1024,256]{1,0:T(8,128)(2,1)S(1)}, u32[]{:S(2)}) copy-start(bf16[1024,256]{1,0:T(8,128)(2,1)S(1)} %get-tuple-element.201.a_ref) | copy-start | bytes 1572868
  74.6 16.2 %copy-start.60 = (bf16[512,1024]{1,0:T(8,128)(2,1)S(1)}, bf16[512,1024]{1,0:T(8,128)(2,1)}, u32[]{:S(2)}) copy-start(bf16[512,1024]{1,0:T(8,128)(2,1)} %param.31) | copy-start | bytes 3145732
  74.6 16.2 %copy-start.64 = (f32[256,1024]{1,0:T(8,128)S(1)}, f32[256,1024]{1,0:T(8,128)}, u32[]{:S(2)}) copy-start(f32[256,1024]{1,0:T(8,128)} %param.20) | copy-start | bytes 3145732
  91.4 188.3 %copy-start.34 = (f32[256,1024]{1,0:T(8,128)}, f32[256,1024]{1,0:T(8,128)S(1)}, u32[]{:S(2)}) copy-start(f32[256,1024]{1,0:T(8,128)S(1)} %get-tuple-element.204) | copy-start | bytes 3145732
  165.5 85.5 %copy-start.9 = (bf16[256,1024]{1,0:T(8,128)(2,1)S(1)}, bf16[256,1024]{1,0:T(8,128)(2,1)}, u32[]{:S(2)}) copy-start(bf16[256,1024]{1,0:T(8,128)(2,1)} %w_ref.10) | copy-start | bytes 1572868
  279.7 1.8 copy-start.48
  281.3 3.5 copy-start.36
  281.6 36.9 %copy-start.11 = (bf16[512,1024]{1,0:T(8,128)(2,1)S(1)}, bf16[512,1024]{1,0:T(8,128)(2,1)}, u32[]{:S(2)}) copy-start(bf16[512,1024]{1,0:T(8,128)(2,1)} %w_ref.8) | copy-start | bytes 3145732
  318.5 3.1 copy-start.10
  318.5 3.1 copy-start.86
  326.3 28.0 %copy-start.85 = (bf16[4,256,1024]{2,1,0:T(8,128)(2,1)S(1)}, bf16[4,256,1024]{2,1,0:T(8,128)(2,1)}, u32[]{:S(2)}) copy-start(bf16[4,256,1024]{2,1,0:T(8,128)(2,1)} %get-tuple-element.46) | copy-start | bytes 6291460
  354.3 2.3 copy-start.12
  356.6 27.8 %copy-start.37 = (f32[256,1024]{1,0:T(8,128)S(1)}, f32[256,1024]{1,0:T(8,128)}, u32[]{:S(2)}) copy-start(f32[256,1024]{1,0:T(8,128)} %copy-done.36) | copy-start | bytes 3145732
  433.5 82.7 %copy-start.3 = (f32[8,512,128]{2,1,0:T(8,128)S(1)}, f32[8,512,128]{2,1,0:T(8,128)}, u32[]{:S(2)}) copy-start(f32[8,512,128]{2,1,0:T(8,128)} %get-tuple-element.175.c_ref) | copy-start | bytes 6291460
  551.4 3.3 copy-start.2
  556.1 28.1 %copy-start.58 = (bf16[4,256,1024]{2,1,0:T(8,128)(2,1)S(1)}, bf16[4,256,1024]{2,1,0:T(8,128)(2,1)}, u32[]{:S(2)}) copy-start(bf16[4,256,1024]{2,1,0:T(8,128)(2,1)} %head_gather_3.1) | copy-start | bytes 6291460
  584.2 3.0 copy-start.35
  589.0 2.7 copy-start.61
  590.8 3.2 copy-start.55
  603.6 2.7 copy-start.43
  603.6 2.7 copy-start.45
  608.4 22.5 %copy-start.73 = (f32[8,128]{1,0:T(8,128)S(1)}, f32[8,128]{1,0:T(8,128)}, u32[]{:S(2)}) copy-start(f32[8,128]{1,0:T(8,128)} %get-tuple-element.42) | copy-start | bytes 12292
  608.4 24.6 %copy-start.66 = (f32[8,256]{1,0:T(8,128)S(1)}, f32[8,256]{1,0:T(8,128)}, u32[]{:S(2)}) copy-start(f32[8,256]{1,0:T(8,128)} %get-tuple-element.41) | copy-start | bytes 24580
  633.0 3.4 copy-start.87
  636.4 17.3 %copy-start.54 = (f32[256,1024]{1,0:T(8,128)S(1)}, f32[256,1024]{1,0:T(8,128)}, u32[]{:S(2)}) copy-start(f32[256,1024]{1,0:T(8,128)} %copy-done.53) | copy-start | bytes 3145732
  636.4 17.3 %copy-start.63 = (bf16[256,512]{1,0:T(8,128)(2,1)S(1)}, bf16[256,512]{1,0:T(8,128)(2,1)}, u32[]{:S(2)}) copy-start(bf16[256,512]{1,0:T(8,128)(2,1)} %copy-done.62) | copy-start | bytes 786436
  637.6 17.6 %copy-start.52 = (f32[256,1024]{1,0:T(8,128)S(1)}, f32[256,1024]{1,0:T(8,128)}, u32[]{:S(2)}) copy-start(f32[256,1024]{1,0:T(8,128)} %get-tuple-element.153) | copy-start | bytes 3145732
  655.2 2.3 copy-start.38
  660.1 5.2 copy-start.47
  660.1 5.6 copy-start.57
  665.6 9.4 %copy-start.6 = (bf16[1024,512]{1,0:T(8,128)(2,1)S(1)}, bf16[1024,512]{1,0:T(8,128)(2,1)}, u32[]{:S(2)}) copy-start(bf16[1024,512]{1,0:T(8,128)(2,1)} %convolution_convert_fusion.1) | copy-start | bytes 3145732
  665.6 9.4 %copy-start.14 = (bf16[1024,512]{1,0:T(8,128)(2,1)S(1)}, bf16[1024,512]{1,0:T(8,128)(2,1)}, u32[]{:S(2)}) copy-start(bf16[1024,512]{1,0:T(8,128)(2,1)} %convolution_convert_fusion.3) | copy-start | bytes 3145732
  665.6 9.4 %copy-start.15 = (bf16[1024,512]{1,0:T(8,128)(2,1)S(1)}, bf16[1024,512]{1,0:T(8,128)(2,1)}, u32[]{:S(2)}) copy-start(bf16[1024,512]{1,0:T(8,128)(2,1)} %convolution_convert_fusion.2) | copy-start | bytes 3145732
  670.1 112.6 %collective-permute-start.2 = (f32[3,512]{1,0:T(4,128)}, f32[3,512]{1,0:T(4,128)}, u32[]{:S(2)}, u32[]{:S(2)}) collective-permute-start(f32[3,512]{1,0:T(4,128)} %get-tuple-element.168), channel_id=1, source_target_pairs={{1,0},{2,1},{3,2},{4,3},{5,4},{6,5},{7,6},{8,7},{9,8},{10,9},{11,1... | collective-permute-start | bytes 18440 | tf_op jit(solution)/shard_map/ppermute | solution.py:22
  671.4 111.3 %collective-permute-start.3 = (f32[3,512]{1,0:T(4,128)}, f32[3,512]{1,0:T(4,128)}, u32[]{:S(2)}, u32[]{:S(2)}) collective-permute-start(f32[3,512]{1,0:T(4,128)} %get-tuple-element.169), channel_id=1, source_target_pairs={{0,1},{1,2},{2,3},{3,4},{4,5},{5,6},{6,7},{7,8},{8,9},{9,10},{10,1... | collective-permute-start | bytes 18440 | tf_op jit(solution)/shard_map/ppermute | solution.py:19
  761.1 18.7 %copy-start.19 = (f32[128,768]{1,0:T(8,128)S(1)}, f32[128,768]{1,0:T(8,128)}, u32[]{:S(2)}) copy-start(f32[128,768]{1,0:T(8,128)} %copy-done.18) | copy-start | bytes 1179652
  777.8 12.7 %copy-start.1 = (bf16[1024,1536]{1,0:T(8,128)(2,1)S(1)}, bf16[1024,1536]{1,0:T(8,128)(2,1)}, u32[]{:S(2)}) copy-start(bf16[1024,1536]{1,0:T(8,128)(2,1)} %param.32) | copy-start | bytes 9437188
  780.7 6.4 copy-start.32
  780.7 7.0 copy-start.30
  780.7 9.1 %copy-start.26 = (f32[128,512]{1,0:T(8,128)S(1)}, f32[128,512]{1,0:T(8,128)}, u32[]{:S(2)}) copy-start(f32[128,512]{1,0:T(8,128)} %copy-done.25) | copy-start | bytes 786436
  (28 other events, 29.8 us)

commit v2 on v0

--- a/solution.py
+++ b/solution.py
@@ -3,6 +3,8 @@
 import jax
 import jax.numpy as jnp
 from jax import lax
+from jax.experimental import pallas as pl
+from jax.experimental.pallas import tpu as pltpu
 from jax.sharding import PartitionSpec as P
 
 HEAD_DIM = 64
@@ -469,10 +471,1465 @@
         grad_down,
     )
 
+MESH = pl.DeviceIdType.MESH
+HBM = pl.BlockSpec(memory_space=pl.ANY)
+VMEM = pl.BlockSpec(memory_space=pltpu.VMEM)
+DMA = pltpu.SemaphoreType.DMA
+
+
+def send(src, dst, send_sem, recv_sem, seq, head):
+    return pltpu.make_async_remote_copy(
+        src_ref=src,
+        dst_ref=dst,
+        send_sem=send_sem,
+        recv_sem=recv_sem,
+        device_id=(seq, head),
+        device_id_type=MESH,
+    )
+
+
+def hail(seq, head):
+    pl.semaphore_signal(
+        pltpu.get_barrier_semaphore(), inc=1, device_id=(seq, head), device_id_type=MESH
+    )
+
+
+def greet(peers):
+    for seq, head in peers:
+        hail(seq, head)
+    return len(peers)
+
+
+def head_places():
+    seq = lax.axis_index("seq")
+    head = lax.axis_index("head")
+    core = lax.rem(head, 2)
+    mate = head + 1 - 2 * core
+    across = lax.rem(head + 2, 4)
+    diagonal = lax.rem(mate + 2, 4)
+    return seq, head, mate, across, diagonal
+
+
+class Task:
+    def __init__(self, body, ins, outs, scratch, in_spec=HBM, out_spec=HBM):
+        self.body, self.ins, self.outs, self.scratch = body, list(ins), list(outs), list(scratch)
+        self.in_specs = in_spec if isinstance(in_spec, list) else [in_spec] * len(self.ins)
+        self.out_specs = out_spec if isinstance(out_spec, list) else [out_spec] * len(self.outs)
+
+
+def communicate(tasks, number, vmem=None):
+    sizes = [(len(t.ins), len(t.outs), len(t.scratch)) for t in tasks]
+
+    def kernel(*refs):
+        parts = []
+        at = 0
+        for kind in range(3):
+            for index, size in enumerate(sizes):
+                parts.append(refs[at : at + size[kind]])
+                at += size[kind]
+        count = len(tasks)
+        running = [
+            t.body(parts[i], parts[count + i], parts[2 * count + i]) for i, t in enumerate(tasks)
+        ]
+        expected = 0
+        for one in running:
+            expected = expected + next(one)
+        pl.semaphore_wait(pltpu.get_barrier_semaphore(), expected)
+        while running:
+            for one in list(running):
+                if next(one, "end") == "end":
+                    running.remove(one)
+
+    results = pl.pallas_call(
+        kernel,
+        out_shape=[o for t in tasks for o in t.outs],
+        in_specs=[s for t in tasks for s in t.in_specs],
+        out_specs=[s for t in tasks for s in t.out_specs],
+        scratch_shapes=[s for t in tasks for s in t.scratch],
+        compiler_params=pltpu.CompilerParams(
+            collective_id=number, has_side_effects=True, vmem_limit_bytes=vmem
+        ),
+        name=f"communicate_{number}",
+    )(*[a for t in tasks for a in t.ins])
+    split = []
+    for _, size, _ in sizes:
+        split.append(results[:size])
+        results = results[size:]
+    return split
+
+
+def like(array, *shape):
+    return jax.ShapeDtypeStruct(shape or array.shape, array.dtype)
+
+
+def cuts_of(rows, cuts):
+    return cuts if rows % (16 * cuts) == 0 else 1
+
+
+def gather_body(most, ins, outs, scratch):
+    local, y_send, y_recv, c_send, c_recv, f_send, f_recv = scratch
+    seq, head, mate, across, _ = head_places()
+    yield greet([(seq, mate), (seq, across)])
+    waits = []
+    hops = []
+    for i in range(len(ins)):
+        cuts = cuts_of(ins[i].shape[0], most)
+        rows = ins[i].shape[0] // cuts
+        for k in range(cuts):
+            part = pl.ds(k * rows, rows)
+            hop = send(
+                ins[i].at[part], outs[i].at[head, part], y_send.at[i, k], y_recv.at[i, k], seq, across
+            )
+            hop.start()
+            hops.append((i, k, part, hop))
+    for i in range(len(ins)):
+        beside = send(ins[i], outs[i].at[head], c_send.at[i], c_recv.at[i], seq, mate)
+        beside.start()
+        own = pltpu.make_async_copy(ins[i], outs[i].at[head], local.at[i])
+        own.start()
+        waits += [beside, own]
+    yield
+    for i, k, part, hop in hops:
+        hop.wait_recv()
+        onward = send(
+            outs[i].at[across, part],
+            outs[i].at[across, part],
+            f_send.at[i, k],
+            f_recv.at[i, k],
+            seq,
+            mate,
+        )
+        onward.start()
+        waits.append(onward)
+        yield
+    for one in waits:
+        one.wait()
+    for _, _, _, hop in hops:
+        hop.wait_send()
+
+
+def gathered(arrays, cuts=2):
+    count = len(arrays)
+    return Task(
+        partial(gather_body, cuts),
+        arrays,
+        [like(a, 4, *a.shape) for a in arrays],
+        [
+            DMA((count,)),
+            DMA((count, cuts)),
+            DMA((count, cuts)),
+            DMA((count,)),
+            DMA((count,)),
+            DMA((count, cuts)),
+            DMA((count, cuts)),
+        ],
+    )
+
+
+def exchange_body(ins, outs, scratch):
+    local, h_send, h_recv = scratch
+    seq, head, mate, across, diagonal = head_places()
+    others = (across, diagonal, mate)
+    yield greet([(seq, other) for other in others])
+    hops = []
+    for o, other in enumerate(others):
+        for i in range(len(ins)):
+            hop = send(
+                ins[i].at[other], outs[i].at[head], h_send.at[i, o], h_recv.at[i, head], seq, other
+            )
+            hop.start()
+            hops.append(hop)
+    owns = [
+        pltpu.make_async_copy(ins[i].at[head], outs[i].at[head], local.at[i])
+        for i in range(len(ins))
+    ]
+    for own in owns:
+        own.start()
+    yield
+    yield
+    for o, other in enumerate(others):
+        for i in range(len(ins)):
+            send(
+                ins[i].at[other], outs[i].at[other], h_send.at[i, o], h_recv.at[i, other], seq, other
+            ).wait_recv()
+    for one in owns:
+        one.wait()
+    for hop in hops:
+        hop.wait_send()
+
+
+def exchanged(arrays):
+    count = len(arrays)
+    return Task(
+        exchange_body,
+        arrays,
+        [like(a) for a in arrays],
+        [DMA((count,)), DMA((count, 3)), DMA((count, 4))],
+    )
+
+
+def product_body(turned, cuts, wire, ins, outs, scratch):
+    (a_ref, w_ref), (o_ref,) = ins, outs
+    away, keep, inbox, final, post, c_send, c_recv, y_send, y_recv = scratch
+    seq, head, mate, across, diagonal = head_places()
+    rows = o_ref.shape[0]
+    step = rows // cuts
+    contract = (((1,), (1 if turned else 0,)), ((), ()))
+
+    def product(block, k):
+        start = pl.multiple_of(block * rows + k * step, step)
+        return lax.dot_general(
+            a_ref[pl.ds(start, step), :], w_ref[...], contract, preferred_element_type=jnp.float32
+        )
+
+    yield greet([(seq, mate), (seq, across)])
+    first = []
+    second = []
+    for side, (theirs, ours) in enumerate(((diagonal, across), (mate, head))):
+        for k in range(cuts):
+            part = pl.ds(k * step, step)
+            away[side, part, :] = product(theirs, k)
+            hop = send(
+                away.at[side, part],
+                inbox.at[side, part],
+                c_send.at[side, k],
+                c_recv.at[side, k],
+                seq,
+                mate,
+            )
+            hop.start()
+            first.append(hop)
+            keep[side, part, :] = product(ours, k)
+        if side == 0:
+            for k in range(cuts):
+                part = pl.ds(k * step, step)
+                first[k].wait_recv()
+                post[part, :] = (keep[0, part, :] + inbox[0, part, :]).astype(wire)
+                hop = send(post.at[part], final.at[part], y_send.at[k], y_recv.at[k], seq, across)
+                hop.start()
+                second.append(hop)
+        yield
+    for k in range(cuts):
+        part = pl.ds(k * step, step)
+        first[cuts + k].wait_recv()
+        second[k].wait_recv()
+        o_ref[part, :] = keep[1, part, :] + inbox[1, part, :] + final[part, :].astype(jnp.float32)
+        yield
+    for hop in first + second:
+        hop.wait_send()
+
+
+def product_scattered(a, w, turned=False, cuts=2, wire=jnp.float32):
+    rows = a.shape[0] // 4
+    width = w.shape[0] if turned else w.shape[1]
+    return Task(
+        partial(product_body, turned, cuts, wire),
+        [a, w],
+        [jax.ShapeDtypeStruct((rows, width), jnp.float32)],
+        [
+            pltpu.VMEM((2, rows, width), jnp.float32),
+            pltpu.VMEM((2, rows, width), jnp.float32),
+            pltpu.VMEM((2, rows, width), jnp.float32),
+            pltpu.VMEM((rows, width), wire),
+            pltpu.VMEM((rows, width), wire),
+            DMA((2, cuts)),
+            DMA((2, cuts)),
+            DMA((cuts,)),
+            DMA((cuts,)),
+        ],
+        VMEM,
+        VMEM,
+    )
+
+
+def spread_body(ins, outs, scratch):
+    (x_ref,), (o_ref,) = ins, outs
+    local, out_send, in_recv, f_send, f_recv = scratch
+    seq, head, mate, _, _ = head_places()
+    core = lax.rem(head, 2)
+    landing = core == seq // 4
+    yield greet([(lax.rem(seq + o, 8), head) for o in range(1, 8)] + [(seq, mate)])
+    for i in range(4):
+        j = lax.rem(seq + i, 4)
+        target = 4 * core + j
+
+        @pl.when(target != seq)
+        def _():
+            send(
+                x_ref.at[j], o_ref.at[seq], out_send.at[j], in_recv.at[seq], target, head
+            ).start()
+
+        @pl.when(target == seq)
+        def _():
+            pltpu.make_async_copy(x_ref.at[j], o_ref.at[seq], local).start()
+
+    yield
+
+    @pl.when(landing)
+    def _():
+        pltpu.make_async_copy(x_ref.at[0], o_ref.at[seq], local).wait()
+        send(o_ref.at[seq], o_ref.at[seq], f_send.at[seq], f_recv.at[seq], seq, mate).start()
+
+    for o in (1, 7, 2, 6, 3, 5, 4):
+        source = lax.rem(seq + o, 8)
+
+        @pl.when(landing)
+        def _():
+            send(
+                x_ref.at[0], o_ref.at[source], out_send.at[0], in_recv.at[source], source, head
+            ).wait_recv()
+            send(
+                o_ref.at[source], o_ref.at[source], f_send.at[source], f_recv.at[source], seq, mate
+            ).start()
+
+        yield
+
+    @pl.when(landing)
+    def _():
+        for source in range(8):
+            send(
+                o_ref.at[source], o_ref.at[source], f_send.at[source], f_recv.at[source], seq, mate
+            ).wait_send()
+
+    @pl.when(jnp.logical_not(landing))
+    def _():
+        for source in range(8):
+            send(
+                o_ref.at[source], o_ref.at[source], f_send.at[source], f_recv.at[source], seq, mate
+            ).wait_recv()
+
+    for j in range(4):
+        @pl.when(4 * core + j != seq)
+        def _():
+            send(
+                x_ref.at[j], o_ref.at[seq], out_send.at[j], in_recv.at[seq], seq, mate
+            ).wait_send()
+
+
+def spread_out(x):
+    _, rows, cols = x.shape
+    return Task(
+        spread_body,
+        [x],
+        [like(x, 8, rows, cols)],
+        [DMA, DMA((4,)), DMA((8,)), DMA((8,)), DMA((8,))],
+    )
+
+
+def rows_heads_body(forward, ins, outs, scratch):
+    (x_ref,), (o_ref,) = ins, outs
+    local, out_send, in_recv = scratch
+    seq, head, _, _, _ = head_places()
+    core = lax.rem(head, 2)
+    plane = head // 2
+    mine = 8 * plane + seq
+    here = pl.ds(pl.multiple_of(plane * HALF, HALF), HALF)
+    yield greet(
+        [
+            (lax.rem(seq + o, 8), core + 2 * p)
+            for o in range(1, 8)
+            for p in range(2)
+        ]
+        + [(seq, core + 2 * (1 - plane))]
+    )
+
+    def tile(g):
+        return (g % 8, pl.ds(g // 8 * HALF, HALF))
+
+    def hop(o, q):
+        s, p = lax.rem(seq + o, 8), lax.rem(plane + q, 2)
+        g = 8 * p + s
+        if forward:
+            source, target = x_ref.at[g], o_ref.at[seq, here]
+            landed = o_ref.at[s, pl.ds(pl.multiple_of(p * HALF, HALF), HALF)]
+        else:
+            source = x_ref.at[s, pl.ds(pl.multiple_of(p * HALF, HALF), HALF)]
+            target = o_ref.at[mine]
+            landed = o_ref.at[g]
+        out = send(source, target, out_send.at[g], in_recv.at[mine], s, core + 2 * p)
+        back = send(source, landed, out_send.at[g], in_recv.at[g], s, core + 2 * p)
+        return out, back
+
+    order = [(o, q) for o in (4, 3, 5, 2, 6, 1, 7, 0) for q in (1, 0) if (o, q) != (0, 0)]
+    hops = [hop(o, q) for o, q in order]
+    for out, _ in hops:
+        out.start()
+    if forward:
+        own = pltpu.make_async_copy(x_ref.at[mine], o_ref.at[seq, here], local)
+    else:
+        own = pltpu.make_async_copy(x_ref.at[seq, here], o_ref.at[mine], local)
+    own.start()
+    yield
+    yield
+    yield
+    own.wait()
+    for _, back in hops:
+        back.wait_recv()
+    for out, _ in hops:
+        out.wait_send()
+
+
+def to_heads(x):
+    return Task(
+        partial(rows_heads_body, True),
+        [x],
+        [like(x, 8, 2 * HALF, x.shape[2])],
+        [DMA, DMA((16,)), DMA((16,))],
+    )
+
+
+def to_rows(x):
+    return Task(
+        partial(rows_heads_body, False),
+        [x],
+        [like(x, 16, HALF, x.shape[2])],
+        [DMA, DMA((16,)), DMA((16,))],
+    )
+
+
+def home_body(ins, outs, scratch):
+    (dq_ref, dkv_ref, c_ref, s_ref), (o_ref,) = ins, outs
+    inbox, post, local, p_send, p_recv, k_send, q_send, k_recv, q_recv = scratch
+    seq, head, mate, _, _ = head_places()
+    core = lax.rem(head, 2)
+    plane = head - core
+    home = seq // 4
+    slot = lax.rem(seq, 4)
+    for j in range(4):
+        for c in range(2):
+            @pl.when(jnp.logical_not(jnp.logical_and(4 * core + j == seq, core == c)))
+            def _():
+                hail(4 * core + j, plane + c)
+
+    hail(seq, mate)
+    yield jnp.where(core == home, 8, 9)
+    q_part, k_part = pl.ds(0, 256), pl.ds(256, 512)
+    halves = []
+    for i in range(8):
+        source = lax.rem(seq + 1 + i, 8)
+        away = pl.ds(pl.multiple_of(source * 1024 + (1 - core) * 512, 512), 512)
+        hop = send(
+            dkv_ref.at[away], inbox.at[source], p_send.at[source], p_recv.at[source], seq, mate
+        )
+        hop.start()
+        halves.append((source, hop))
+    for source, _ in halves:
+        here = jnp.logical_and(source == seq, core == home)
+
+        @pl.when(jnp.logical_not(here))
+        def _():
+            send(
+                dq_ref.at[source],
+                o_ref.at[slot, core, q_part],
+                q_send.at[source],
+                q_recv.at[slot, core],
+                source,
+                plane + home,
+            ).start()
+
+        @pl.when(here)
+        def _():
+            pltpu.make_async_copy(dq_ref.at[source], o_ref.at[slot, core, q_part], local.at[0]).start()
+
+    yield
+    for source, hop in halves:
+        here = jnp.logical_and(source == seq, core == home)
+        hop.wait_recv()
+        kept = pl.ds(pl.multiple_of(source * 1024 + core * 512, 512), 512)
+        total = dkv_ref[kept, :] + inbox[source]
+        total = total * c_ref[source] + turn(total * s_ref[source], -1)
+        post[source] = total.astype(jnp.bfloat16)
+
+        @pl.when(jnp.logical_not(here))
+        def _():
+            send(
+                post.at[source],
+                o_ref.at[slot, core, k_part],
+                k_send.at[source],
+                k_recv.at[slot, core],
+                source,
+                plane + home,
+            ).start()
+
+        @pl.when(here)
+        def _():
+            pltpu.make_async_copy(post.at[source], o_ref.at[slot, core, k_part], local.at[1]).start()
+
+        yield
+
+    for j in range(4):
+        for c in range(2):
+            here = jnp.logical_and(4 * core + j == seq, core == c)
+
+            @pl.when(jnp.logical_not(here))
+            def _():
+                send(
+                    dq_ref.at[0], o_ref.at[j, c, q_part], q_send.at[0], q_recv.at[j, c], seq, mate
+                ).wait_recv()
+                send(
+                    post.at[0], o_ref.at[j, c, k_part], k_send.at[0], k_recv.at[j, c], seq, mate
+                ).wait_recv()
+
+            @pl.when(here)
+            def _():
+                pltpu.make_async_copy(dq_ref.at[0], o_ref.at[j, c, q_part], local.at[0]).wait()
+                pltpu.make_async_copy(post.at[0], o_ref.at[j, c, k_part], local.at[1]).wait()
+
+    for source in range(8):
+        @pl.when(jnp.logical_or(source != seq, core != home))
+        def _():
+            send(
+                dq_ref.at[source], o_ref.at[slot, core, q_part], q_send.at[source], q_recv.at[slot, core], seq, mate
+            ).wait_send()
+            send(
+                post.at[source], o_ref.at[slot, core, k_part], k_send.at[source], k_recv.at[slot, core], seq, mate
+            ).wait_send()
+    for _, hop in halves:
+        hop.wait_send()
+
+
+def sent_home(dq, dkv, cosine, sine):
+    return Task(
+        home_body,
+        [dq, dkv, cosine, sine],
+        [jax.ShapeDtypeStruct((4, 2, 768, 128), jnp.bfloat16)],
+        [
+            pltpu.VMEM((8, 512, 128), jnp.float32),
+            pltpu.VMEM((8, 512, 128), jnp.bfloat16),
+            DMA((2,)),
+            DMA((8,)),
+            DMA((8,)),
+            DMA((8,)),
+            DMA((8,)),
+            DMA((4, 2)),
+            DMA((4, 2)),
+        ],
+        VMEM,
+        HBM,
+    )
+
+
+def seq_scatter_body(ins, outs, scratch):
+    count = len(ins)
+    own, inbox, post, final = (scratch[k * count : (k + 1) * count] for k in range(4))
+    l_sem, x_send, x_recv, z_send, z_recv = scratch[4 * count :]
+    seq = lax.axis_index("seq")
+    head = lax.axis_index("head")
+    x = lax.rem(seq, 2)
+    z = seq // 2
+    beside = 2 * z + 1 - x
+    yield greet([(peer, head) for peer in [beside] + [2 * lax.rem(z + o, 4) + x for o in (1, 2, 3)]])
+    hops = []
+    for i in range(count):
+        for o in (1, 2, 3, 0):
+            zt = lax.rem(z + o, 4)
+            hop = send(
+                ins[i].at[2 * zt + 1 - x],
+                inbox[i].at[o],
+                x_send.at[i, o],
+                x_recv.at[i, o],
+                beside,
+                head,
+            )
+            hop.start()
+            copy = pltpu.make_async_copy(ins[i].at[2 * zt + x], own[i].at[o], l_sem.at[i, o])
+            copy.start()
+            hops.append((i, o, hop, copy))
+    yield
+    last = []
+    for i, o, hop, copy in hops:
+        copy.wait()
+        hop.wait_recv()
+        total = own[i][o].astype(jnp.float32) + inbox[i][o].astype(jnp.float32)
+        if o == 0:
+            outs[i][...] = total
+        else:
+            post[i][o - 1] = total.astype(post[i].dtype)
+            far = send(
+                post[i].at[o - 1],
+                final[i].at[o - 1],
+                z_send.at[i, o - 1],
+                z_recv.at[i, o - 1],
+                2 * lax.rem(z + o, 4) + x,
+                head,
+            )
+            far.start()
+            last.append((i, o, far))
+        yield
+    for i, o, far in last:
+        far.wait_recv()
+        outs[i][...] += final[i][o - 1].astype(jnp.float32)
+    for _, _, hop, _ in hops:
+        hop.wait_send()
+    for _, _, far in last:
+        far.wait_send()
+
+
+def seq_scattered(arrays):
+    count = len(arrays)
+    shapes = [a.shape[1:] for a in arrays]
+    return Task(
+        seq_scatter_body,
+        arrays,
+        [jax.ShapeDtypeStruct(s, jnp.float32) for s in shapes],
+        [pltpu.VMEM((k,) + s, a.dtype) for k in (4, 4, 3, 3) for s, a in zip(shapes, arrays)]
+        + [DMA((count, 4)), DMA((count, 4)), DMA((count, 4)), DMA((count, 3)), DMA((count, 3))],
+        HBM,
+        VMEM,
+    )
+
+
+def seq_sum_body(rule, ins, outs, scratch):
+    (x_ref, e_ref), (o_ref, t_ref) = ins, outs
+    inbox, s_send, s_recv, row, rows, h_send, h_recv = scratch
+    seq = lax.axis_index("seq")
+    head = lax.axis_index("head")
+    yield greet(
+        [(lax.rem(seq + o, 8), head) for o in range(1, 8)]
+        + [(seq, lax.rem(head + o, 4)) for o in range(1, 4)]
+    )
+    hops = []
+    for o in range(1, 8):
+        hop = send(
+            x_ref, inbox.at[seq], s_send.at[o - 1], s_recv.at[seq], lax.rem(seq + o, 8), head
+        )
+        hop.start()
+        hops.append(hop)
+    inbox[seq] = x_ref[...]
+    for o in range(1, 8):
+        source = lax.rem(seq + o, 8)
+        send(
+            x_ref, inbox.at[source], s_send.at[o - 1], s_recv.at[source], source, head
+        ).wait_recv()
+    total = inbox[0]
+    for s in range(1, 8):
+        total = total + inbox[s]
+    o_ref[...] = total
+    summed = jnp.sum(rule(total, e_ref[...]), axis=1, keepdims=True)
+    row[...] = jnp.broadcast_to(summed, row.shape)
+    for o in range(1, 4):
+        hop = send(
+            row, rows.at[head], h_send.at[o - 1], h_recv.at[head], seq, lax.rem(head + o, 4)
+        )
+        hop.start()
+        hops.append(hop)
+    rows[head] = row[...]
+    for o in range(1, 4):
+        source = lax.rem(head + o, 4)
+        send(row, rows.at[source], h_send.at[o - 1], h_recv.at[source], seq, source).wait_recv()
+    t_ref[...] = rows[0] + rows[1] + rows[2] + rows[3]
+    for hop in hops:
+        hop.wait_send()
+
+
+def seq_summed(x, rule, extra):
+    height, width = x.shape
+    tall = extra.shape[0]
+    return Task(
+        partial(seq_sum_body, rule),
+        [x, extra],
+        [
+            jax.ShapeDtypeStruct(x.shape, jnp.float32),
+            jax.ShapeDtypeStruct((tall, 128), jnp.float32),
+        ],
+        [
+            pltpu.VMEM((8, height, width), jnp.float32),
+            DMA((7,)),
+            DMA((8,)),
+            pltpu.VMEM((tall, 128), jnp.float32),
+            pltpu.VMEM((4, tall, 128), jnp.float32),
+            DMA((3,)),
+            DMA((4,)),
+        ],
+        VMEM,
+        VMEM,
+    )
+
+
+def head_blocks_body(ins, outs, scratch):
+    count = len(ins)
+    inbox = scratch[:count]
+    h_send, h_recv = scratch[count:]
+    seq = lax.axis_index("seq")
+    head = lax.axis_index("head")
+    others = [lax.rem(head + o, 4) for o in range(1, 4)]
+    yield greet([(seq, other) for other in others])
+    hops = []
+    for i in range(count):
+        for o, other in enumerate(others):
+            hop = send(
+                ins[i].at[other], inbox[i].at[head], h_send.at[i, o], h_recv.at[i, head], seq, other
+            )
+            hop.start()
+            hops.append(hop)
+        inbox[i][head] = ins[i][head]
+    for i in range(count):
+        for o, other in enumerate(others):
+            send(
+                ins[i].at[other], inbox[i].at[other], h_send.at[i, o], h_recv.at[i, other], seq, other
+            ).wait_recv()
+        outs[i][...] = inbox[i][0] + inbox[i][1] + inbox[i][2] + inbox[i][3]
+    for hop in hops:
+        hop.wait_send()
+
+
+def head_blocks(arrays):
+    count = len(arrays)
+    return Task(
+        head_blocks_body,
+        arrays,
+        [like(a, *a.shape[1:]) for a in arrays],
+        [pltpu.VMEM(a.shape, a.dtype) for a in arrays] + [DMA((count, 3)), DMA((count, 4))],
+        VMEM,
+        VMEM,
+    )
+
+
+def turns_body(ins, outs, scratch):
+    yield 0
+    yield
+    count = len(ins)
+    for i in range(count):
+        for s in range(8):
+            angles = ins[i][s]
+            outs[2 * i][s] = jnp.cos(angles)
+            outs[2 * i + 1][s] = jnp.sin(angles)
+        yield
+
+
+def turns(angles):
+    return Task(
+        turns_body,
+        angles,
+        [like(a) for a in angles for _ in range(2)],
+        [],
+        VMEM,
+        VMEM,
+    )
+
+
+QUARTER = 256
+HALF = 128
+SPAN = 1024
+LOCAL = pltpu.CompilerParams(vmem_limit_bytes=60 << 20)
+SMEM = pl.BlockSpec(memory_space=pltpu.SMEM)
+ROWS_TO_ROWS = (((1,), (1,)), ((), ()))
+
+
+def lane_of(shape):
+    return lax.broadcasted_iota(jnp.int32, shape, len(shape) - 1)
+
+
+def swap_halves(x):
+    return pltpu.roll(x, 64, x.ndim - 1)
+
+
+def turn(x, sign):
+    upper = pltpu.roll(x, x.shape[-1] - 32, x.ndim - 1)
+    lower = pltpu.roll(x, 32, x.ndim - 1)
+    first = lax.rem(lane_of(x.shape), 64) < 32
+    if sign > 0:
+        return jnp.where(first, -upper, lower)
+    return jnp.where(first, upper, -lower)
+
+
+def opened(tile):
+    left = lane_of(tile.shape) < 64
+    return jnp.concatenate(
+        [jnp.where(left, tile, 0.0), jnp.where(left, swap_halves(tile), 0.0)], axis=0
+    )
+
+
+def closed(rows):
+    left = lane_of((HALF, 128)) < 64
+    return jnp.where(left, rows[:HALF], swap_halves(rows[HALF:]))
+
+
+def limits(rows, table, count):
+    low = jnp.zeros(rows.shape, jnp.int32)
+    high = jnp.full(rows.shape, 1 << 24, jnp.int32)
+    for u in range(count):
+        past = rows >= table[u]
+        low = jnp.where(past, table[u], low)
+        high = jnp.where(past, high, jnp.minimum(high, table[u]))
+    return low, high
+
+
+def fetch(x_ref, core, queries, pairs, turned, sems):
+    frames = 8 * 1024
+    own = pl.ds(pl.multiple_of(core * QUARTER, QUARTER), QUARTER)
+    mine = [
+        pltpu.make_async_copy(x_ref.at[s, own], queries.at[s], sems.at[8 + s]) for s in range(8)
+    ]
+    copies = [
+        pltpu.make_async_copy(
+            x_ref.at[s, pl.ds(512, 1024)], pairs.at[pl.ds(s * 1024, 1024)], sems.at[s]
+        )
+        for s in range(8)
+    ]
+    for copy in copies + mine:
+        copy.start()
+    pairs[pl.ds(frames, SPAN), :] = jnp.zeros((SPAN, 128), pairs.dtype)
+    turned[:, pl.ds(frames, SPAN)] = jnp.zeros((128, SPAN), turned.dtype)
+    for s, copy in enumerate(copies):
+        copy.wait()
+        turned[:, pl.ds(s * 1024, 1024)] = pairs[pl.ds(s * 1024, 1024), :].T
+    for copy in mine:
+        copy.wait()
+
+
+def quarter_of(step, table, utterances):
+    source, sub = step // 2, lax.rem(step, 2)
+    quarter = source * 4 + table[utterances] + 2 * sub
+    base = utterances + 1
+    first = pl.multiple_of(table[base + quarter] * 128, 128)
+    ends = [table[base + 32 * k + quarter] for k in (1, 2, 3)]
+    rows = quarter * QUARTER + lax.broadcasted_iota(jnp.int32, (1, QUARTER), 1)
+    return source, sub, first, ends, limits(rows, table, utterances)
+
+
+def in_three(ends, body, carry):
+    count, in_low, in_high = ends
+    carry = lax.fori_loop(0, in_low, partial(body, True), carry)
+    carry = lax.fori_loop(in_low, in_high, partial(body, False), carry)
+    return lax.fori_loop(in_high, count, partial(body, True), carry)
+
+
+def masked(raw, place, limit):
+    keys = place + lax.broadcasted_iota(jnp.int32, (raw.shape[0], 1), 0)
+    return jnp.where((keys >= limit[0]) & (keys < limit[1]), raw, -1e30)
+
+
+def fold(op, carry, x):
+    for k in range(x.shape[0] // 8):
+        carry = op(carry, x[8 * k : 8 * (k + 1), :])
+    return carry
+
+
+def attend_kernel(utterances, table, x_ref, o_ref, l_ref, held, q_ref, pairs, turned, sems):
+    fetch(x_ref, table[utterances], q_ref, pairs, turned, sems)
+
+    def of_quarter(step, carry):
+        source, sub, first, ends, limit = quarter_of(step, table, utterances)
+        at = pl.ds(pl.multiple_of(sub * HALF, HALF), HALF)
+        query = opened(q_ref[source, at, :].astype(jnp.float32)).astype(jnp.bfloat16)
+
+        def scores(edge, i, top):
+            place = pl.multiple_of(first + i * SPAN, 128)
+            raw = lax.dot_general(
+                pairs[pl.ds(place, SPAN), :], query, ROWS_TO_ROWS, preferred_element_type=jnp.float32
+            )
+            if edge:
+                raw = masked(raw, place, limit)
+            held[i] = raw
+            return fold(jnp.maximum, top, raw)
+
+        top = in_three(ends, scores, jnp.full((8, QUARTER), -1e30, jnp.float32))
+        top = jnp.max(top, axis=0, keepdims=True)
+
+        def weights(i, total):
+            raised = jnp.exp(held[i] - top)
+            held[i] = raised
+            return fold(jnp.add, total, raised)
+
+        total = lax.fori_loop(0, ends[0], weights, jnp.zeros((8, QUARTER), jnp.float32))
+        total = jnp.sum(total, axis=0, keepdims=True)
+        share = 1.0 / total
+
+        def mix(i, acc):
+            probs = (held[i] * share).astype(jnp.bfloat16)
+            place = pl.multiple_of(first + i * SPAN, 128)
+            return acc + jnp.dot(
+                turned[:, pl.ds(place, SPAN)], probs, preferred_element_type=jnp.float32
+            )
+
+        acc = lax.fori_loop(0, ends[0], mix, jnp.zeros((128, QUARTER), jnp.float32))
+        o_ref[source, at, :] = closed(swap_halves(acc.T)).astype(jnp.bfloat16)
+        l_ref[source, sub] = jnp.broadcast_to(top + jnp.log(total), (8, QUARTER))
+        return carry
+
+    lax.fori_loop(0, 16, of_quarter, 0)
+
+
+def key_scratch():
+    long = 8 * 1024 + SPAN
+    return [
+        pltpu.VMEM((8, QUARTER, 128), jnp.bfloat16),
+        pltpu.VMEM((long, 128), jnp.bfloat16),
+        pltpu.VMEM((128, long), jnp.bfloat16),
+        DMA((16,)),
+    ]
+
+
+def attend(table, x, utterances):
+    return pl.pallas_call(
+        partial(attend_kernel, utterances),
+        out_shape=[
+            jax.ShapeDtypeStruct((8, QUARTER, 128), jnp.bfloat16),
+            jax.ShapeDtypeStruct((8, 2, 8, QUARTER), jnp.float32),
+        ],
+        in_specs=[SMEM, HBM],
+        out_specs=[VMEM, VMEM],
+        scratch_shapes=[pltpu.VMEM((8 * 1024 // SPAN + 1, SPAN, QUARTER), jnp.float32)]
+        + key_scratch(),
+        compiler_params=LOCAL,
+        name="attend",
+    )(table, x)
+
+
+def attend_back_kernel(
+    utterances, table, x_ref, g_ref, l_ref, c_ref, s_ref, dq_ref, dkv_ref, held_p, held_d, q_ref, pairs, turned, sems
+):
+    fetch(x_ref, table[utterances], q_ref, pairs, turned, sems)
+    dkv_ref[...] = jnp.zeros_like(dkv_ref)
+
+    def of_quarter(step, carry):
+        source, sub, first, ends, limit = quarter_of(step, table, utterances)
+        at = pl.ds(pl.multiple_of(sub * HALF, HALF), HALF)
+        query = opened(q_ref[source, at, :].astype(jnp.float32))
+        grad = swap_halves(opened(g_ref[source, at, :].astype(jnp.float32)))
+        both = jnp.concatenate([query, grad], axis=0).astype(jnp.bfloat16)
+        logsum = l_ref[source, sub][:1, :]
+
+        def slopes(edge, i, inner):
+            place = pl.multiple_of(first + i * SPAN, 128)
+            pair = lax.dot_general(
+                pairs[pl.ds(place, SPAN), :], both, ROWS_TO_ROWS, preferred_element_type=jnp.float32
+            )
+            raw, d_probs = pair[:, :QUARTER], pair[:, QUARTER:]
+            if edge:
+                raw = masked(raw, place, limit)
+            probs = jnp.exp(raw - logsum)
+            held_p[i] = probs
+            held_d[i] = d_probs
+            return fold(jnp.add, inner, probs * d_probs)
+
+        inner = in_three(ends, slopes, jnp.zeros((8, QUARTER), jnp.float32))
+        inner = jnp.sum(inner, axis=0, keepdims=True)
+
+        def mix(i, acc):
+            place = pl.multiple_of(first + i * SPAN, 128)
+            probs = held_p[i]
+            d_scores = (probs * (held_d[i] - inner)).astype(jnp.bfloat16)
+            dkv_ref[pl.ds(place, SPAN), :] += jnp.dot(
+                jnp.concatenate([d_scores, probs.astype(jnp.bfloat16)], axis=1),
+                both,
+                preferred_element_type=jnp.float32,
+            )
+            return acc + jnp.dot(
+                turned[:, pl.ds(place, SPAN)], d_scores, preferred_element_type=jnp.float32
+            )
+
+        acc = lax.fori_loop(0, ends[0], mix, jnp.zeros((128, QUARTER), jnp.float32))
+        d_query = closed(acc.T) * 0.125
+        d_query = d_query * c_ref[source, at, :] + turn(d_query * s_ref[source, at, :], -1)
+        dq_ref[source, at, :] = d_query.astype(jnp.bfloat16)
+        return carry
+
+    lax.fori_loop(0, 16, of_quarter, 0)
+
+
+def attend_back(table, x, grads, logsum, cosine, sine, utterances):
+    spans = 8 * 1024 // SPAN + 1
+    return pl.pallas_call(
+        partial(attend_back_kernel, utterances),
+        out_shape=[
+            jax.ShapeDtypeStruct((8, QUARTER, 128), jnp.bfloat16),
+            jax.ShapeDtypeStruct((8 * 1024 + SPAN, 128), jnp.float32),
+        ],
+        in_specs=[SMEM, HBM] + [VMEM] * 4,
+        out_specs=[VMEM, VMEM],
+        scratch_shapes=[
+            pltpu.VMEM((spans, SPAN, QUARTER), jnp.float32),
+            pltpu.VMEM((spans, SPAN, QUARTER), jnp.float32),
+        ]
+        + key_scratch(),
+        compiler_params=LOCAL,
+        name="attend_back",
+    )(table, x, grads, logsum, cosine, sine)
+
+
+def attention_table(lengths, core):
+    bounds = jnp.cumsum(lengths)
+    starts = bounds - lengths
+    ids = jnp.arange(lengths.shape[0], dtype=jnp.int32)
+    first = jnp.arange(32, dtype=jnp.int32) * QUARTER
+    head_segment = segment_of(first, lengths)
+    tail_segment = segment_of(first + QUARTER - 1, lengths)
+    low = jnp.sum(jnp.where(head_segment[:, None] == ids[None, :], starts[None, :], 0), axis=1)
+    high = jnp.sum(jnp.where(tail_segment[:, None] == ids[None, :], bounds[None, :], 0), axis=1)
+    base = low // 128 * 128
+    count = (high - base + SPAN - 1) // SPAN
+    in_low = (low - base + SPAN - 1) // SPAN
+    in_high = (high - base) // SPAN
+    plain = (head_segment == tail_segment) & (in_low < in_high)
+    in_low, in_high = jnp.where(plain, in_low, count), jnp.where(plain, in_high, count)
+    return jnp.concatenate([bounds, core[None], base // 128, count, in_low, in_high]).astype(jnp.int32)
+
+
+def pair_up(even, odd):
+    left = lane_of(even.shape) < 64
+    return jnp.where(left, even, swap_halves(odd)), jnp.where(left, swap_halves(even), odd)
+
+
+def project_kernel(x_ref, w_ref, c_ref, s_ref, o_ref):
+    for quarter in range(4):
+        rows = pl.ds(quarter * QUARTER, QUARTER)
+        part = x_ref[rows, :]
+        cos, sin = c_ref[rows, :], s_ref[rows, :]
+        cos, sin = jnp.concatenate([cos, cos], axis=1), jnp.concatenate([sin, sin], axis=1)
+        queries, keys, values = (
+            jnp.dot(part, w_ref[:, 256 * k : 256 * (k + 1)], preferred_element_type=jnp.float32)
+            for k in range(3)
+        )
+        queries = (queries * cos + turn(queries, 1) * sin) * 0.125
+        keys = keys * cos + turn(keys, 1) * sin
+        at_q = pl.ds((quarter % 2) * QUARTER + (quarter // 2) * HALF, HALF)
+        at_k = pl.ds(512 + quarter * QUARTER, QUARTER)
+        for pair in range(2):
+            lanes = slice(128 * pair, 128 * (pair + 1))
+            q_even, q_odd = pair_up(queries[:HALF, lanes], queries[HALF:, lanes])
+            k_even, k_odd = pair_up(keys[:, lanes], values[:, lanes])
+            o_ref[2 * pair, at_q, :] = q_even.astype(jnp.bfloat16)
+            o_ref[2 * pair + 1, at_q, :] = q_odd.astype(jnp.bfloat16)
+            o_ref[2 * pair, at_k, :] = k_even.astype(jnp.bfloat16)
+            o_ref[2 * pair + 1, at_k, :] = k_odd.astype(jnp.bfloat16)
+
+
+def project(x, w, cosine, sine):
+    return pl.pallas_call(
+        project_kernel,
+        out_shape=jax.ShapeDtypeStruct((4, 1536, 128), jnp.bfloat16),
+        in_specs=[VMEM] * 4,
+        out_specs=VMEM,
+        compiler_params=LOCAL,
+        name="project",
+    )(x, w, cosine, sine)
+
+
+def attn_out_kernel(x_ref, w_ref, c_ref, o_ref):
+    for pair in range(8):
+        first, second = pair_up(
+            x_ref[2 * pair].astype(jnp.float32), x_ref[2 * pair + 1].astype(jnp.float32)
+        )
+        lanes = slice(128 * (pair % 2), 128 * (pair % 2) + 128)
+        c_ref[pair // 2, pl.ds(0, HALF), lanes] = first.astype(jnp.bfloat16)
+        c_ref[pair // 2, pl.ds(HALF, HALF), lanes] = second.astype(jnp.bfloat16)
+    total = jnp.dot(c_ref[0], w_ref[0], preferred_element_type=jnp.float32)
+    for h in range(1, 4):
+        total += jnp.dot(c_ref[h], w_ref[h], preferred_element_type=jnp.float32)
+    o_ref[...] = total
+
+
+def attn_out(x, w):
+    return pl.pallas_call(
+        attn_out_kernel,
+        out_shape=[
+            jax.ShapeDtypeStruct((4, 256, 256), jnp.bfloat16),
+            jax.ShapeDtypeStruct((256, w.shape[2]), jnp.float32),
+        ],
+        in_specs=[VMEM] * 2,
+        out_specs=[VMEM] * 2,
+        compiler_params=LOCAL,
+        name="attn_out",
+    )(x, w)
+
+
+def attn_out_back_kernel(x_ref, w_ref, o_ref):
+    for h in range(4):
+        piece = lax.dot_general(
+            x_ref[...], w_ref[h], ROWS_TO_ROWS, preferred_element_type=jnp.float32
+        )
+        for k in range(2):
+            lanes = slice(128 * k, 128 * (k + 1))
+            even, odd = pair_up(piece[:HALF, lanes], piece[HALF:, lanes])
+            o_ref[4 * h + 2 * k] = even.astype(jnp.bfloat16)
+            o_ref[4 * h + 2 * k + 1] = odd.astype(jnp.bfloat16)
+
+
+def attn_out_back(x, w):
+    return pl.pallas_call(
+        attn_out_back_kernel,
+        out_shape=jax.ShapeDtypeStruct((16, HALF, 128), jnp.bfloat16),
+        in_specs=[VMEM] * 2,
+        out_specs=VMEM,
+        compiler_params=LOCAL,
+        name="attn_out_back",
+    )(x, w)
+
+
+def unpack_kernel(x_ref, o_ref):
+    for core in range(2):
+        for pair in range(2):
+            lanes = slice(128 * pair, 128 * (pair + 1))
+            for sub in range(2):
+                part = pl.ds(sub * HALF, HALF)
+                first, second = pair_up(
+                    x_ref[2 * pair, core, part, :].astype(jnp.float32),
+                    x_ref[2 * pair + 1, core, part, :].astype(jnp.float32),
+                )
+                at = (core + 2 * sub) * QUARTER
+                o_ref[pl.ds(at, HALF), lanes] = first.astype(jnp.bfloat16)
+                o_ref[pl.ds(at + HALF, HALF), lanes] = second.astype(jnp.bfloat16)
+            part = pl.ds(256, 512)
+            keys, values = pair_up(
+                x_ref[2 * pair, core, part, :].astype(jnp.float32),
+                x_ref[2 * pair + 1, core, part, :].astype(jnp.float32),
+            )
+            at = pl.ds(core * 512, 512)
+            o_ref[at, slice(256 + 128 * pair, 384 + 128 * pair)] = keys.astype(jnp.bfloat16)
+            o_ref[at, slice(512 + 128 * pair, 640 + 128 * pair)] = values.astype(jnp.bfloat16)
+
+
+def unpack(x):
+    return pl.pallas_call(
+        unpack_kernel,
+        out_shape=jax.ShapeDtypeStruct((1024, 768), jnp.bfloat16),
+        in_specs=[VMEM],
+        out_specs=VMEM,
+        compiler_params=LOCAL,
+        name="unpack",
+    )(x)
+
+
+WIDE = 48 << 20
+
+
+def blocks_of(array):
+    return array.reshape((8, array.shape[0] // 8) + array.shape[1:])
+
+
+def rows_of(gathered):
+    return gathered.reshape((gathered.shape[0] * gathered.shape[1],) + gathered.shape[2:])
+
+
+def normed(values):
+    center = values - jnp.mean(values, axis=-1, keepdims=True)
+    spread_of = jnp.mean(center * center, axis=-1, keepdims=True)
+    inverse = lax.rsqrt(spread_of + 1e-06)
+    return center * inverse, inverse
+
+
+def normed_back(grad, unit, inverse):
+    return (
+        grad
+        - jnp.mean(grad, axis=-1, keepdims=True)
+        - unit * jnp.mean(grad * unit, axis=-1, keepdims=True)
+    ) * inverse
+
+
+def root_rule(total, extra):
+    return jnp.sqrt(total + 1.0)
+
+
+def product_rule(total, extra):
+    return total[: extra.shape[0]] * extra
+
+
+def angles_of(places, lanes):
+    half_width = HEAD_DIM // 2
+    inverse = 10000.0 ** (-jnp.arange(half_width, dtype=jnp.float32) * 2.0 / HEAD_DIM)
+    inverse = jnp.concatenate([inverse] * (lanes // half_width) + [jnp.zeros((128 - lanes,))])
+    return places.astype(jnp.float32) * inverse
+
+
+def on_eight_by_four(
+    text_in,
+    mel_in,
+    time_embed,
+    lengths,
+    text_mask,
+    conv_weight,
+    norm_gain,
+    norm_bias,
+    expand_weight,
+    grn_gamma,
+    grn_beta,
+    shrink_weight,
+    join_weight,
+    modulation,
+    qkv_weight,
+    out_weight,
+    up_weight,
+    down_weight,
+    cotangent,
+):
+    rows_here = text_in.shape[0]
+    frames_here = rows_here * 4
+    seq_index = lax.axis_index("seq")
+    head_index = lax.axis_index("head")
+    core = lax.rem(head_index, 2)
+    utterances = lengths.shape[0]
+    row_first = (seq_index * 4 + head_index) * rows_here
+    frame_first = seq_index * frames_here
+    row_ids = row_first + jnp.arange(rows_here, dtype=jnp.int32)
+    frame_ids = frame_first + jnp.arange(frames_here, dtype=jnp.int32)
+    row_segment = segment_of(row_ids, lengths)
+    frame_segment = segment_of(frame_ids, lengths)
+    utter_ids = jnp.arange(utterances, dtype=jnp.int32)
+    row_onehot = (row_segment[:, None] == utter_ids[None, :]).astype(jnp.float32)
+    frame_onehot = (frame_segment[:, None] == utter_ids[None, :]).astype(jnp.float32)
+    mask_rows = text_mask.astype(jnp.float32)[:, None]
+    taps_count = conv_weight.shape[0]
+    half_kernel = taps_count // 2
+
+    all_ids = jnp.arange(8 * frames_here, dtype=jnp.int32)
+    places = position_of(all_ids, lengths, segment_of(all_ids, lengths))
+    table = attention_table(lengths, core)
+    own_angles = angles_of(
+        lax.dynamic_slice_in_dim(places, frame_first, frames_here)[:, None], 128
+    )
+    own_cos, own_sin = jnp.cos(own_angles), jnp.sin(own_angles)
+    tiles = lax.dynamic_index_in_dim(
+        places.reshape(8, 2, 2, 2, HALF), core, 2, keepdims=False
+    )
+    query_angles = angles_of(
+        jnp.where(jnp.arange(128) < 64, tiles[:, :, 0, :, None], tiles[:, :, 1, :, None]), 128
+    ).reshape(8, QUARTER, 128)
+    key_places = lax.dynamic_index_in_dim(places.reshape(8, 2, 512), core, 1, keepdims=False)
+    key_angles = angles_of(key_places[:, :, None], 64)
+
+    extended = frame_rim(text_in, half_kernel)
+    extended_ids = (
+        row_first - half_kernel + jnp.arange(rows_here + 2 * half_kernel, dtype=jnp.int32)
+    )
+    extended_segment = segment_of(extended_ids, lengths)
+    same_taps = jnp.stack(
+        [
+            (extended_segment[tap : tap + rows_here] == row_segment).astype(jnp.float32)
+            for tap in range(taps_count)
+        ]
+    )
+    conv_out = jnp.zeros_like(text_in)
+    for tap in range(taps_count):
+        conv_out = (
+            conv_out
+            + extended[tap : tap + rows_here] * conv_weight[tap] * same_taps[tap][:, None]
+        )
+    text_unit, text_inverse = normed(conv_out)
+    text_low = (text_unit * norm_gain + norm_bias).astype(jnp.bfloat16)
+    cond_low = jax.nn.silu(time_embed).astype(jnp.bfloat16)
+    ((text_all, mod_parts),) = communicate(
+        [gathered([text_low, narrow_dot(cond_low, modulation)])], 0
+    )
+    text_all = rows_of(text_all)
+    mod_all = mod_parts.transpose(1, 0, 2).reshape(utterances, -1)
+    expanded = narrow_dot(text_all, expand_weight)
+    activated, gelu_exact_back = jax.vjp(partial(jax.nn.gelu, approximate=False), expanded)
+    text_channels = expand_weight.shape[1] * 4
+    squares = exact_inner(frame_onehot, activated * activated)
+    ((squares_all, channel_total),) = communicate([seq_summed(squares, root_rule, squares)], 1)
+    grn_norm = jnp.sqrt(squares_all + 1.0)
+    denominator = channel_total[:, 0] / text_channels + 1e-06
+    grn_ratio = grn_norm / denominator[:, None]
+    ratio_rows = exact_dot(frame_onehot, grn_ratio)
+    grn_low = (grn_gamma * activated * ratio_rows + grn_beta + activated).astype(jnp.bfloat16)
+    ((branch,),) = communicate([product_scattered(grn_low, shrink_weight)], 2, WIDE)
+    join_low = (text_in + mask_rows * branch).astype(jnp.bfloat16)
+    hidden = mel_in + narrow_dot(join_low, join_weight)
+
+    mod_rows = exact_dot(row_onehot, mod_all)
+    shift_attn, scale_attn, gate_attn, shift_ffn, scale_ffn, gate_ffn = jnp.split(
+        mod_rows, 6, axis=1
+    )
+    hidden_unit, hidden_inverse = normed(hidden)
+    attn_low = (hidden_unit * (1.0 + scale_attn) + shift_attn).astype(jnp.bfloat16)
+    d_ffn_low = (cotangent * gate_ffn).astype(jnp.bfloat16)
+    ((attn_all,),) = communicate([gathered([attn_low])], 3)
+    attn_all, out_near, up_near, down_near = lax.optimization_barrier(
+        (attn_all, out_weight, up_weight, down_weight)
+    )
+    out_full, up_full, down_full = (
+        lax.all_gather(w, "head", axis=0) for w in (out_near, up_near, down_near)
+    )
+    attn_all = rows_of(attn_all)
+    qkv_flat = qkv_weight.reshape(qkv_weight.shape[0], -1)
+    head_cols = qkv_weight.shape[2]
+    (packed,), (query_cos, query_sin, key_cos, key_sin), (d_ffn_all,) = communicate(
+        [
+            spread_out(project(attn_all, qkv_flat, own_cos, own_sin)),
+            turns([query_angles, key_angles]),
+            gathered([d_ffn_low]),
+        ],
+        4,
+        WIDE,
+    )
+    context_here, logsum = attend(table, packed, utterances)
+    ((context_tiles,),) = communicate([to_rows(context_here)], 5)
+    context_blocks, attn_rows = attn_out(context_tiles, out_full)
+    middle = hidden + gate_attn * attn_rows
+
+    middle_unit, middle_inverse = normed(middle)
+    ffn_low = (middle_unit * (1.0 + scale_ffn) + shift_ffn).astype(jnp.bfloat16)
+    gelu_low, d_up_low = [], []
+    ffn_rows = d_ffn_in = 0.0
+    for h in range(4):
+        upward = narrow_dot(ffn_low, up_full[h])
+        value, back = jax.vjp(partial(jax.nn.gelu, approximate=True), upward)
+        gelu_low.append(value.astype(jnp.bfloat16))
+        d_up_low.append(back(against_rows(d_ffn_low, down_full[h]))[0].astype(jnp.bfloat16))
+        ffn_rows += narrow_dot(gelu_low[h], down_full[h])
+        d_ffn_in += against_rows(d_up_low[h], up_full[h])
+    gelu_low, d_up_low = jnp.stack(gelu_low), jnp.stack(d_up_low)
+    transformer_layer_output = middle + gate_ffn * ffn_rows
+    d_middle = cotangent + normed_back(
+        d_ffn_in * (1.0 + scale_ffn), middle_unit, middle_inverse
+    )
+    d_attn_low = (d_middle * gate_attn).astype(jnp.bfloat16)
+
+    (d_context,), (ffn_all,), (context_all,) = communicate(
+        [
+            to_heads(attn_out_back(d_attn_low, out_full)),
+            gathered([ffn_low]),
+            exchanged([context_blocks]),
+        ],
+        6,
+    )
+    d_query, d_pair = attend_back(
+        table, packed, d_context, logsum, query_cos, query_sin, utterances
+    )
+    (d_tiles,), (d_attn_all,), (gelu_all, d_up_all) = communicate(
+        [
+            sent_home(d_query, d_pair, key_cos, key_sin),
+            gathered([d_attn_low]),
+            exchanged([gelu_low, d_up_low]),
+        ],
+        7,
+        WIDE,
+    )
+    ffn_all, d_ffn_all, context_all, d_attn_all, gelu_all, d_up_all = (
+        rows_of(g) for g in (ffn_all, d_ffn_all, context_all, d_attn_all, gelu_all, d_up_all)
+    )
+    d_projected = unpack(d_tiles)
+    ((d_attn_in,),) = communicate([product_scattered(d_projected, qkv_flat, True)], 8, WIDE)
+    grad_mel = d_middle + normed_back(
+        d_attn_in * (1.0 + scale_attn), hidden_unit, hidden_inverse
+    )
+    d_mod_rows = jnp.concatenate(
+        [
+            d_attn_in,
+            d_attn_in * hidden_unit,
+            d_middle * attn_rows,
+            d_ffn_in,
+            d_ffn_in * middle_unit,
+            cotangent * ffn_rows,
+        ],
+        axis=1,
+    )
+    d_mod_part = exact_inner(row_onehot, d_mod_rows)
+
+    d_joined_low = grad_mel.astype(jnp.bfloat16)
+    d_text_out = against_rows(d_joined_low, join_weight)
+    ((d_branch_all,),) = communicate([gathered([(mask_rows * d_text_out).astype(jnp.bfloat16)])], 9)
+    d_branch_all = rows_of(d_branch_all)
+    d_grn = against_rows(d_branch_all, shrink_weight)
+    sums_here = jnp.concatenate(
+        [
+            exact_inner(frame_onehot, d_grn * grn_gamma * activated),
+            jnp.sum(d_grn * activated * ratio_rows, axis=0)[None, :],
+            jnp.sum(d_grn, axis=0)[None, :],
+            jnp.zeros((6, d_grn.shape[1]), jnp.float32),
+        ]
+    )
+    ((sums_all, inner_total),) = communicate([seq_summed(sums_here, product_rule, grn_norm)], 10)
+    d_ratio = sums_all[:utterances]
+    grad_gamma, grad_beta = sums_all[utterances], sums_all[utterances + 1]
+    d_mean = -inner_total[:, 0] / (denominator * denominator)
+    d_norm = d_ratio / denominator[:, None] + (d_mean / text_channels)[:, None]
+    d_activated = d_grn * (grn_gamma * ratio_rows + 1.0) + activated * exact_dot(
+        frame_onehot, d_norm / grn_norm
+    )
+    d_expanded_low = gelu_exact_back(d_activated)[0].astype(jnp.bfloat16)
+    ((d_text_norm,),) = communicate(
+        [product_scattered(d_expanded_low, expand_weight, True)], 11, WIDE
+    )
+    d_conv_out = normed_back(d_text_norm * norm_gain, text_unit, text_inverse)
+    grad_gain_part = jnp.sum(d_text_norm * text_unit, axis=0)
+    grad_bias_part = jnp.sum(d_text_norm, axis=0)
+    d_extended = frame_rim(d_conv_out, half_kernel)
+    grad_text = d_text_out
+    conv_grads = []
+    for tap in range(taps_count):
+        mirror = 2 * half_kernel - tap
+        grad_text = (
+            grad_text
+            + d_extended[mirror : mirror + rows_here]
+            * conv_weight[tap]
+            * same_taps[mirror][:, None]
+        )
+        conv_grads.append(
+            jnp.sum(
+                d_conv_out * extended[tap : tap + rows_here] * same_taps[tap][:, None], axis=0
+            )
+        )
+
+    def part(left, right):
+        return blocks_of(inner_rows(left, right).astype(jnp.bfloat16))
+
+    small = jnp.concatenate(
+        [
+            jnp.stack(conv_grads + [grad_gain_part, grad_bias_part]),
+            jnp.zeros((16 - taps_count - 2, text_in.shape[1]), jnp.float32),
+        ]
+    )
+    small = jnp.pad(small.reshape(16, 8, 64).transpose(1, 0, 2), ((0, 0), (0, 0), (0, 64)))
+    mod_blocks = d_mod_part.reshape(utterances, 8, -1).transpose(1, 0, 2)
+    ((up, down, qkv, out, shrink, expand, join, small, mod),) = communicate(
+        [
+            seq_scattered(
+                [
+            part(ffn_all, d_up_all),
+            part(d_ffn_all, gelu_all),
+            part(attn_all, d_projected),
+            part(d_attn_all, context_all),
+            part(d_branch_all, grn_low),
+            part(text_all, d_expanded_low),
+            part(d_joined_low, join_low),
+            small,
+            mod_blocks,
+                ]
+            )
+        ],
+        12,
+        WIDE,
+    )
+    ((join, small, mod),) = communicate(
+        [
+            head_blocks(
+                [
+            join.reshape(4, -1, join.shape[1]),
+            jnp.pad(small[:, :64].reshape(16, 4, 16).transpose(1, 0, 2), ((0, 0), (0, 0), (0, 112))),
+            mod.reshape(utterances, 4, -1).transpose(1, 0, 2),
+                ]
+            )
+        ],
+        13,
+    )
+    grad_modulation = exact_inner(cond_low.astype(jnp.float32), mod)
+    return (
+        transformer_layer_output,
+        grad_text,
+        grad_mel,
+        small[:taps_count, :16],
+        small[taps_count, :16],
+        small[taps_count + 1, :16],
+        expand,
+        grad_gamma,
+        grad_beta,
+        shrink.T,
+        join.T,
+        grad_modulation,
+        qkv.reshape(qkv.shape[0], 3, head_cols),
+        out.T,
+        up,
+        down.T,
+    )
+
 
 def solution(mesh):
+    fits = mesh.shape["seq"] == 8 and mesh.shape["head"] == 4
     return jax.shard_map(
-        on_device,
+        on_eight_by_four if fits else on_device,
         mesh=mesh,
         in_specs=(
             P(("seq", "head"), None),

time: 2090 us -> 672 us (0.32)
  waiting for transfers between devices: 1300 us -> 0.76 us
  Pallas kernels: 0 us -> 489 us
  matrix products: 375 us -> 63.3 us
  other arithmetic: 205 us -> 37.6 us
  blocking collectives: 117 us -> 0 us
  starting transfers between devices: 41.9 us -> 8.41 us
  local copies, waits for them, and re-layouts: 24.9 us -> 52 us
    reduce_scatter x13 -> x0, waiting for transfers between devices: 864 us -> none  [the longest x6 312 us: head_sums(): lax.psum_scatter(action(jnp.int32(0), lax.axis_size('head') * count_rows)...]
    pallas_call x0 -> x20, Pallas kernels: none -> 489 us  [the longest x14 376 us: communicate(): pl.pallas_call(kernel, out_shape=[o for t in tasks for o in t.outs], in_s...]
    dot_general x15 -> x0, matrix products: 297 us -> none  [the longest x2 76.4 us: on_device(): jnp.einsum('qhd,khd->hqk', grad_block, value_heads, preferred_element_typ...]
    unnamed x23 -> x3, waiting for transfers between devices: 161 us -> 0.73 us
    ppermute x12 -> x0, waiting for transfers between devices: 150 us -> none  [from_behind(): lax.ppermute(value, axis, [(source, source + steps) for source in range(f...]
    all_gather x6 -> x3, waiting for transfers between devices: 124 us -> 0.02 us  [on_eight_by_four(): lax.all_gather(w, 'head', axis=0)]
    convert_element_type x12 -> x9, other arithmetic: 105 us -> 4.08 us  [the longest x1 1.82 us: on_eight_by_four(): ffn_low = (middle_unit * (1.0 + scale_ffn) + shift_ffn).astype(jnp.bfloat16)]
    psum x4 -> x0, blocking collectives: 70.9 us -> none  [the longest x2 58.8 us: utter_sum(): return lax.psum(values, 'seq')]
  transfers between devices with their start and end apart: 37 -> 7, of which waited for: 27 -> 0; matrix products, arithmetic and copies ran while one was open for 5% -> 10% of each run, Pallas kernels for 0% -> 32%
where the time goes in v2:
time: 672 us; the launch traced here: 667 us
  Pallas kernels  489 us (73%)
  matrix products  63.3 us (9%)
  local copies, waits for them, and re-layouts  52 us (8%)
  other arithmetic  37.6 us (6%)
  between operations  15.6 us (2%)
  starting transfers between devices  8.41 us (1%)
    pallas_call x14, Pallas kernels, communicate(): pl.pallas_call(kernel, out_shape=[o for t in tasks for o in t.outs], in_s...  376 us
    pallas_call x1, Pallas kernels, attend_back(): pl.pallas_call(partial(attend_back_kernel, utterances), out_shape=[jax.Sh...  56.5 us
    pallas_call x1, Pallas kernels, attend(): pl.pallas_call(partial(attend_kernel, utterances), out_shape=[jax.ShapeDt...  41 us
    unnamed x211, local copies, waits for them, and re-layouts  35.7 us
    dot_general x11, matrix products, narrow_dot(): return jnp.dot(left, right, preferred_element_type=jnp.float32)  17 us
    dot_general x10, matrix products, against_rows(): lax.dot_general(left, right, (((1,), (1,)), ((), ())), preferred_element_...  13.6 us
  transfers between devices with their start and end apart: 7, of which 0 were waited for; matrix products, arithmetic and copies ran while one was open for 10% of the time, Pallas kernels for 32%

profile of v2, /device:TPU:0, one launch (start us, length us, event | category | flops | bytes accessed | tf_op | source)
XLA Modules:
  0.0 667.1 jit_solution(5583340463241979150)
XLA Ops:
  8.2 1.4 collective-permute-start.1
  9.6 3.0 collective-permute-start
  15.0 1.9 fusion.134.refs_1_
  21.3 14.2 %communicate_0.1 = (bf16[4,256,512]{2,1,0:T(8,128)(2,1)}, f32[4,8,1536]{2,1,0:T(8,128)}) custom-call(bf16[256,512]{1,0:T(8,128)(2,1)} %add_convert_fusion.3.refs_0_, f32[8,1536]{1,0:T(8,128)} %fusion.134.refs_1_), custom_call_target="tpu_custom_call" | custom-call | tf_op jit(solution)/shard_map/communicate_0/pallas_call | solution.py:543
  35.5 5.6 fusion.114
  41.1 2.5 fusion.2
  44.7 1.4 fusion.8.refs_0_.refs_1_
  46.1 12.3 %communicate_1.1 = (f32[8,256]{1,0:T(8,128)}, f32[8,128]{1,0:T(8,128)}) custom-call(f32[8,256]{1,0:T(8,128)} %fusion.8.refs_0_.refs_1_, f32[8,256]{1,0:T(8,128)} %fusion.8.refs_0_.refs_1_), custom_call_target="tpu_custom_call" | custom-call | tf_op jit(solution)/shard_map/communicate_1/pallas_call | solution.py:543
  59.3 3.0 add_convert_fusion.1
  62.2 16.0 %communicate_2.1 = f32[256,512]{1,0:T(8,128)S(1)} custom-call(bf16[1024,256]{1,0:T(8,128)(2,1)S(1)} %get-tuple-element.236.refs_0_, bf16[256,512]{1,0:T(8,128)(2,1)S(1)} %copy-done.9), custom_call_target="tpu_custom_call" | custom-call | tf_op jit(solution)/shard_map/communicate_2/pallas_call | solution.py:543
  78.4 2.1 fusion.149
  81.9 18.1 %communicate_3.1 = bf16[4,256,1024]{2,1,0:T(8,128)(2,1)} custom-call(bf16[256,1024]{1,0:T(8,128)(2,1)} %get-tuple-element.202.refs_0_), custom_call_target="tpu_custom_call" | custom-call | tf_op jit(solution)/shard_map/communicate_3/pallas_call | solution.py:543
  100.9 2.7 copy.67
  103.5 2.6 copy.68.w_ref.refs_1_
  107.8 3.5 multiply_sine_fusion
  111.9 2.0 broadcast_multiply_fusion.refs_2_
  113.9 5.7 project.1.refs_0_
  121.0 45.6 %communicate_4.1 = (bf16[8,1536,128]{2,1,0:T(8,128)(2,1)}, f32[8,256,128]{2,1,0:T(8,128)S(1)}, f32[8,256,128]{2,1,0:T(8,128)S(1)}, f32[8,512,128]{2,1,0:T(8,128)...) custom-call(bf16[4,1536,128]{2,1,0:T(8,128)(2,1)S(1)} %copy-done.4, ...), custom_call_target="tpu_custom_call" | custom-call | tf_op jit(solution)/shard_map/communicate_4/pallas_call | solution.py:543
  168.6 41.0 %attend.1 = (bf16[8,256,128]{2,1,0:T(8,128)(2,1)}, f32[8,2,8,256]{3,2,1,0:T(8,128)}) custom-call(s32[137]{0:T(256)} %concatenate.62.table, bf16[8,1536,128]{2,1,0:T(8,128)(2,1)} %get-tuple-element.62.x_ref), custom_call_target="tpu_custom_call" | custom-call | tf_op jit(solution)/shard_map/attend/pallas_call | solution.py:1365
  209.6 28.1 %communicate_5.1.x_ref = bf16[16,128,128]{2,1,0:T(8,128)(2,1)} custom-call(bf16[8,256,128]{2,1,0:T(8,128)(2,1)} %get-tuple-element.63.refs_0_), custom_call_target="tpu_custom_call" | custom-call | tf_op jit(solution)/shard_map/communicate_5/pallas_call | solution.py:543
  238.4 3.5 attn_out.1
  241.9 1.8 fusion.141
  244.7 1.8 fusion.3.refs_1_
  246.5 1.9 fusion.20
  248.6 1.7 fusion.26
  254.6 2.2 fusion.49
  257.3 1.8 fusion.56
  263.1 2.1 fusion.139
  266.9 4.6 multiply_convert_fusion
  271.5 3.4 attn_out_back.1.refs_0_
  274.9 27.0 %communicate_6.1 = (bf16[8,256,128]{2,1,0:T(8,128)(2,1)}, bf16[4,256,1024]{2,1,0:T(8,128)(2,1)}, bf16[4,256,256]{2,1,0:T(8,128)(2,1)}) custom-call(bf16[16,128,128]{2,1,0:T(8,128)(2,1)} %attn_out_back.1.refs_0_, bf16[256,1024]{1,0:T(8,128)(2,1)} %copy-done.57, bf16[4,256,256]{2,1,0:T(8,128)(2,1)} %get-tuple-element.68.refs_2_), custom_call_target="tpu_custom_call" | custom-call | tf_op jit(solution)/shard_map/communicate_6/pallas_call | solution.py:543
  301.9 56.5 %attend_back.1 = (bf16[8,256,128]{2,1,0:T(8,128)(2,1)}, f32[9216,128]{1,0:T(8,128)}) custom-call(s32[137]{0:T(256)} %concatenate.62.table, bf16[8,1536,128]{2,1,0:T(8,128)(2,1)} %get-tuple-element.62.x_ref, bf16[8,256,128]{2,1,0:T(8,128)(2,1)} %get-tuple-element.69.g_ref, f32[8,2,8,256]{3,2,1,0:T(8,128)} %get-tuple-element.70.l_ref, ...), custom_call_target="tpu_custom_call" | custom-call | tf_op jit(solution)/shard_map/attend_back/pallas_call | solution.py:1434
  359.8 56.7 %communicate_7.1 = (bf16[4,2,768,128]{3,2,1,0:T(8,128)(2,1)}, bf16[4,256,1024]{2,1,0:T(8,128)(2,1)}, bf16[4,256,512]{2,1,0:T(8,128)(2,1)S(1)}, bf16[4,256,512]{2,1,0:T(8,128)(2,1)S(1)}) custom-call(bf16[8,256,128]{2,1,0:T(8,128)(2,1)S(1)} %copy-done.10, f32[9216,128]{1,0:T(8,128)} %get-tuple-element.74.refs_1_, f32[8,512,128]{2,1,0:T(8,128)} %get-tuple-element.75.refs_2_, ...), custom_call_target="tpu_custom_call" | custom-call | tf_op jit(solution)/shard_map/communicate_7/pallas_call | solution.py:543
  417.4 3.3 unpack.1.refs_0_
  420.8 1.4 copy-done.3
  422.2 28.1 %communicate_8.1 = f32[256,1024]{1,0:T(8,128)S(1)} custom-call(bf16[1024,768]{1,0:T(8,128)(2,1)S(1)} %copy-done.3, bf16[1024,768]{1,0:T(8,128)(2,1)S(1)} %copy-done.2), custom_call_target="tpu_custom_call" | custom-call | tf_op jit(solution)/shard_map/communicate_8/pallas_call | solution.py:543
  450.3 3.0 convolution_convert_fusion
  453.3 1.7 fusion.140
  455.1 1.7 multiply_dynamic-update-slice_fusion.3
  457.8 1.9 multiply_convert_fusion.2
  460.1 10.4 %communicate_9.1 = bf16[4,256,512]{2,1,0:T(8,128)(2,1)} custom-call(bf16[256,512]{1,0:T(8,128)(2,1)} %get-tuple-element.242.refs_0_), custom_call_target="tpu_custom_call" | custom-call | tf_op jit(solution)/shard_map/communicate_9/pallas_call | solution.py:543
  470.4 2.6 convolution_convert_fusion.3
  473.0 2.7 multiply_reduce_fusion
  477.5 17.2 %communicate_10.1 = (f32[16,256]{1,0:T(8,128)}, f32[8,128]{1,0:T(8,128)}) custom-call(f32[16,256]{1,0:T(8,128)} %maximum_maximum_fusion.refs_0_, f32[8,256]{1,0:T(8,128)} %add_sqrt_fusion.refs_1_), custom_call_target="tpu_custom_call" | custom-call | tf_op jit(solution)/shard_map/communicate_10/pallas_call | solution.py:543
  495.6 3.0 add_convert_fusion.refs_0_
  498.6 16.1 %communicate_11.1 = f32[256,512]{1,0:T(8,128)S(1)} custom-call(bf16[1024,256]{1,0:T(8,128)(2,1)S(1)} %add_convert_fusion.refs_0_, bf16[512,256]{1,0:T(8,128)(2,1)S(1)} %copy-done.11), custom_call_target="tpu_custom_call" | custom-call | tf_op jit(solution)/shard_map/communicate_11/pallas_call | solution.py:543
  516.1 1.4 convolution_convert_fusion.1
  521.7 2.6 collective-permute-start.3
  526.4 2.8 multiply_dynamic-update-slice_fusion.2
  529.3 2.3 constant_dynamic-update-slice_fusion.2
  531.6 2.4 multiply_dynamic-update-slice_fusion.1
  535.2 5.0 fusion.113
  544.6 78.0 %communicate_12.1 = (f32[128,512]{1,0:T(8,128)S(1)}, f32[128,512]{1,0:T(8,128)S(1)}, f32[128,768]{1,0:T(8,128)S(1)}, f32[128,256]{1,0:T(8,128)S(1)}, f32[64,256]...) custom-call(bf16[8,128,512]{2,1,0:T(8,128)(2,1)S(1)} %bitcast.119, ...), custom_call_target="tpu_custom_call" | custom-call | tf_op jit(solution)/shard_map/communicate_12/pallas_call | solution.py:543
  628.0 1.4 reshape.293
  630.9 8.3 %communicate_13.1 = (f32[32,512]{1,0:T(8,128)}, f32[16,128]{1,0:T(8,128)}, f32[8,192]{1,0:T(8,128)}) custom-call(f32[4,32,512]{2,1,0:T(8,128)} %bitcast.125, f32[4,16,128]{2,1,0:T(8,128)} %pad.9.refs_1_, f32[4,8,192]{2,1,0:T(8,128)} %bitcast.146), custom_call_target="tpu_custom_call" | custom-call | tf_op jit(solution)/shard_map/communicate_13/pallas_call | solution.py:543
  639.1 2.2 fusion.133
  644.7 1.9 copy.77
  646.6 1.7 copy.78
  648.2 1.8 copy.79
  650.0 4.2 fusion.75
  654.3 1.5 copy.102
  655.7 1.5 copy.103
  657.2 1.5 copy.104
  658.7 1.7 copy.105
  (324 shorter events, 58.6 us)
Async XLA Ops:
  7.2 7.8 %copy-start = (bf16[1024,1536]{1,0:T(8,128)(2,1)S(1)}, bf16[1024,1536]{1,0:T(8,128)(2,1)}, u32[]{:S(2)}) copy-start(bf16[1024,1536]{1,0:T(8,128)(2,1)} %param.32) | copy-start | bytes 9437188
  7.2 10.8 %copy-start.91 = (s32[256]{0:T(256)S(1)}, s32[256]{0:T(256)}, u32[]{:S(2)}) copy-start(s32[256]{0:T(256)} %param.23) | copy-start | bytes 3076
  7.2 13.2 %copy-start.90 = (f32[512]{0:T(512)S(1)}, f32[512]{0:T(512)}, u32[]{:S(2)}) copy-start(f32[512]{0:T(512)} %param.26) | copy-start | bytes 6148
  7.2 13.2 %copy-start.75 = (f32[512]{0:T(512)S(1)}, f32[512]{0:T(512)}, u32[]{:S(2)}) copy-start(f32[512]{0:T(512)} %param.25) | copy-start | bytes 6148
  7.2 231.2 %all-gather.7.cloned.1.call-start = ((), (), s32[]{:S(2)}) async-start(), calls=%async_computation | async-start | bytes 2621440 | tf_op jit(solution)/shard_map/all_gather | solution.py:1743
  8.2 9.9 %collective-permute-start.1 = (f32[3,512]{1,0:T(4,128)S(1)}, f32[3,512]{1,0:T(4,128)S(1)}, u32[]{:S(2)}, u32[]{:S(2)}) collective-permute-start(f32[3,512]{1,0:T(4,128)S(1)} %get-tuple-element.209), channel_id=1, source_target_pairs={{1,0},{2,1},{3,2},{4,3},{5,4},{6,5},{7,6},{8,7},{9,8},{10,9},{11,1... | collective-permute-start | bytes 18440 | tf_op jit(solution)/shard_map/ppermute | solution.py:22
  9.6 8.5 %collective-permute-start = (f32[3,512]{1,0:T(4,128)S(1)}, f32[3,512]{1,0:T(4,128)S(1)}, u32[]{:S(2)}, u32[]{:S(2)}) collective-permute-start(f32[3,512]{1,0:T(4,128)S(1)} %get-tuple-element.208), channel_id=1, source_target_pairs={{0,1},{1,2},{2,3},{3,4},{4,5},{5,6},{6,7},{7,8},{8,9},{9,10},{10,1... | collective-permute-start | bytes 18440 | tf_op jit(solution)/shard_map/ppermute | solution.py:19
  13.7 505.5 %copy-start.82 = (f32[256]{0:T(256)}, f32[256]{0:T(256)S(1)}, u32[]{:S(2)}) copy-start(f32[256]{0:T(256)S(1)} %get-tuple-element.198) | copy-start | bytes 3076
  13.8 505.5 %copy-start.83 = (f32[256]{0:T(256)}, f32[256]{0:T(256)S(1)}, u32[]{:S(2)}) copy-start(f32[256]{0:T(256)S(1)} %get-tuple-element.225) | copy-start | bytes 3076
  13.8 505.5 %copy-start.84 = (f32[256]{0:T(256)}, f32[256]{0:T(256)S(1)}, u32[]{:S(2)}) copy-start(f32[256]{0:T(256)S(1)} %get-tuple-element.226) | copy-start | bytes 3076
  13.8 505.5 %copy-start.85 = (f32[256]{0:T(256)}, f32[256]{0:T(256)S(1)}, u32[]{:S(2)}) copy-start(f32[256]{0:T(256)S(1)} %get-tuple-element.227) | copy-start | bytes 3076
  13.8 505.5 %copy-start.86 = (f32[256]{0:T(256)}, f32[256]{0:T(256)S(1)}, u32[]{:S(2)}) copy-start(f32[256]{0:T(256)S(1)} %get-tuple-element.228) | copy-start | bytes 3076
  13.8 505.5 %copy-start.87 = (f32[256]{0:T(256)}, f32[256]{0:T(256)S(1)}, u32[]{:S(2)}) copy-start(f32[256]{0:T(256)S(1)} %get-tuple-element.229) | copy-start | bytes 3076
  13.8 505.5 %copy-start.88 = (f32[256]{0:T(256)}, f32[256]{0:T(256)S(1)}, u32[]{:S(2)}) copy-start(f32[256]{0:T(256)S(1)} %get-tuple-element.230) | copy-start | bytes 3076
  14.8 4.8 copy-start.76
  14.8 20.7 %copy-start.77 = (f32[1,512]{1,0:T(1,128)}, f32[1,512]{1,0:T(1,128)S(1)}, u32[]{:S(2)}) copy-start(f32[1,512]{1,0:T(1,128)S(1)} %get-tuple-element.217) | copy-start | bytes 6148
  14.8 20.7 %copy-start.78 = (f32[1,512]{1,0:T(1,128)}, f32[1,512]{1,0:T(1,128)S(1)}, u32[]{:S(2)}) copy-start(f32[1,512]{1,0:T(1,128)S(1)} %get-tuple-element.218) | copy-start | bytes 6148
  14.8 20.7 %copy-start.79 = (f32[1,512]{1,0:T(1,128)}, f32[1,512]{1,0:T(1,128)S(1)}, u32[]{:S(2)}) copy-start(f32[1,512]{1,0:T(1,128)S(1)} %get-tuple-element.219) | copy-start | bytes 6148
  14.8 20.7 %copy-start.80 = (f32[1,512]{1,0:T(1,128)}, f32[1,512]{1,0:T(1,128)S(1)}, u32[]{:S(2)}) copy-start(f32[1,512]{1,0:T(1,128)S(1)} %get-tuple-element.220) | copy-start | bytes 6148
  14.9 4.0 copy-start.46
  19.6 21.5 %copy-start.11 = (bf16[512,256]{1,0:T(8,128)(2,1)S(1)}, bf16[512,256]{1,0:T(8,128)(2,1)}, u32[]{:S(2)}) copy-start(bf16[512,256]{1,0:T(8,128)(2,1)} %refs_1_.3) | copy-start | bytes 786436
  35.5 5.6 copy-start.96
  41.1 18.1 %copy-start.89 = (f32[256]{0:T(256)S(1)}, f32[256]{0:T(256)}, u32[]{:S(2)}) copy-start(f32[256]{0:T(256)} %param.28) | copy-start | bytes 3076
  41.1 18.1 %copy-start.92 = (f32[256]{0:T(256)S(1)}, f32[256]{0:T(256)}, u32[]{:S(2)}) copy-start(f32[256]{0:T(256)} %param.29) | copy-start | bytes 3076
  43.7 34.6 %copy-start.31 = (f32[1024,256]{1,0:T(8,128)}, f32[1024,256]{1,0:T(8,128)S(1)}, u32[]{:S(2)}) copy-start(f32[1024,256]{1,0:T(8,128)S(1)} %get-tuple-element.234) | copy-start | bytes 3145732
  43.7 18.5 %copy-start.9 = (bf16[256,512]{1,0:T(8,128)(2,1)S(1)}, bf16[256,512]{1,0:T(8,128)(2,1)}, u32[]{:S(2)}) copy-start(bf16[256,512]{1,0:T(8,128)(2,1)} %refs_1_.2) | copy-start | bytes 786436
  43.7 34.6 %copy-start.47 = (f32[256,512]{1,0:T(8,128)S(1)}, f32[256,512]{1,0:T(8,128)}, u32[]{:S(2)}) copy-start(f32[256,512]{1,0:T(8,128)} %param.19) | copy-start | bytes 1572868
  59.3 21.5 %copy-start.39 = (f32[256,1024]{1,0:T(8,128)S(1)}, f32[256,1024]{1,0:T(8,128)}, u32[]{:S(2)}) copy-start(f32[256,1024]{1,0:T(8,128)} %param.37) | copy-start | bytes 3145732
  62.2 18.5 %copy-start.23 = (f32[256,6144]{1,0:T(8,128)S(1)}, f32[256,6144]{1,0:T(8,128)}, u32[]{:S(2)}) copy-start(f32[256,6144]{1,0:T(8,128)} %fusion.114) | copy-start | bytes 18874372
  80.4 161.4 %copy-start.24 = (f32[256,1024]{1,0:T(8,128)}, f32[256,1024]{1,0:T(8,128)S(1)}, u32[]{:S(2)}) copy-start(f32[256,1024]{1,0:T(8,128)S(1)} %get-tuple-element.239) | copy-start | bytes 3145732
  100.0 6.2 copy-start.99
  100.1 146.5 %all-gather.9.cloned.1.call-start = ((), (), s32[]{:S(2)}) async-start(), calls=%async_computation.1 | async-start | bytes 5242880 | tf_op jit(solution)/shard_map/all_gather | solution.py:1743
  100.8 153.8 %all-gather.11.cloned.1.call-start = ((), (), s32[]{:S(2)}) async-start(), calls=%async_computation.2 | async-start | bytes 5242880 | tf_op jit(solution)/shard_map/all_gather | solution.py:1743
  121.0 116.8 %copy-start.74 = (f32[8,256]{1,0:T(8,128)S(1)}, f32[8,256]{1,0:T(8,128)}, u32[]{:S(2)}) copy-start(f32[8,256]{1,0:T(8,128)} %get-tuple-element.58) | copy-start | bytes 24580
  246.5 6.0 copy-start.57
  246.5 4.6 copy-start.53
  254.6 4.6 copy-start.59
  257.3 3.3 copy-start.65
  274.9 83.5 %copy-start.62 = (bf16[1,256,512]{2,1,0:T(8,128)(2,1)S(1)}, bf16[1,256,512]{2,1,0:T(8,128)(2,1)}, u32[]{:S(2)}) copy-start(bf16[1,256,512]{2,1,0:T(8,128)(2,1)} %fusion.137) | copy-start | bytes 786436
  274.9 83.5 %copy-start.63 = (bf16[1,256,512]{2,1,0:T(8,128)(2,1)S(1)}, bf16[1,256,512]{2,1,0:T(8,128)(2,1)}, u32[]{:S(2)}) copy-start(bf16[1,256,512]{2,1,0:T(8,128)(2,1)} %fusion.136) | copy-start | bytes 786436
  274.9 83.6 %copy-start.64 = (bf16[1,256,512]{2,1,0:T(8,128)(2,1)S(1)}, bf16[1,256,512]{2,1,0:T(8,128)(2,1)}, u32[]{:S(2)}) copy-start(bf16[1,256,512]{2,1,0:T(8,128)(2,1)} %fusion.135) | copy-start | bytes 786436
  301.9 56.8 %copy-start.66 = (bf16[256,512]{1,0:T(8,128)(2,1)S(1)}, bf16[256,512]{1,0:T(8,128)(2,1)}, u32[]{:S(2)}) copy-start(bf16[256,512]{1,0:T(8,128)(2,1)} %copy-done.65) | copy-start | bytes 786436
  301.9 56.8 %copy-start.68 = (bf16[256,512]{1,0:T(8,128)(2,1)S(1)}, bf16[256,512]{1,0:T(8,128)(2,1)}, u32[]{:S(2)}) copy-start(bf16[256,512]{1,0:T(8,128)(2,1)} %copy-done.67) | copy-start | bytes 786436
  301.9 56.8 %copy-start.70 = (bf16[256,512]{1,0:T(8,128)(2,1)S(1)}, bf16[256,512]{1,0:T(8,128)(2,1)}, u32[]{:S(2)}) copy-start(bf16[256,512]{1,0:T(8,128)(2,1)} %copy-done.69) | copy-start | bytes 786436
  301.9 57.8 %copy-start.5 = (bf16[256,1024]{1,0:T(8,128)(2,1)S(1)}, bf16[256,1024]{1,0:T(8,128)(2,1)}, u32[]{:S(2)}) copy-start(bf16[256,1024]{1,0:T(8,128)(2,1)} %get-tuple-element.186.x_ref.refs_4_) | copy-start | bytes 1572868
  417.4 3.3 copy-start.2
  422.2 28.1 %copy-start.49 = (bf16[4,256,1024]{2,1,0:T(8,128)(2,1)S(1)}, bf16[4,256,1024]{2,1,0:T(8,128)(2,1)}, u32[]{:S(2)}) copy-start(bf16[4,256,1024]{2,1,0:T(8,128)(2,1)} %communicate_3.1) | copy-start | bytes 6291460
  470.4 5.3 copy-start.32
  470.4 5.3 copy-start.35
  473.0 21.6 %copy-start.81 = (f32[8,128]{1,0:T(8,128)S(1)}, f32[8,128]{1,0:T(8,128)}, u32[]{:S(2)}) copy-start(f32[8,128]{1,0:T(8,128)} %get-tuple-element.59) | copy-start | bytes 12292
  473.0 22.5 %copy-start.33 = (f32[1024,256]{1,0:T(8,128)S(1)}, f32[1024,256]{1,0:T(8,128)}, u32[]{:S(2)}) copy-start(f32[1024,256]{1,0:T(8,128)} %copy-done.31) | copy-start | bytes 3145732
  494.6 20.1 %copy-start.97 = (bf16[4,256,512]{2,1,0:T(8,128)(2,1)S(1)}, bf16[4,256,512]{2,1,0:T(8,128)(2,1)}, u32[]{:S(2)}) copy-start(bf16[4,256,512]{2,1,0:T(8,128)(2,1)} %get-tuple-element.57) | copy-start | bytes 3145732
  495.6 20.5 %copy-start.44 = (f32[256,1024]{1,0:T(8,128)S(1)}, f32[256,1024]{1,0:T(8,128)}, u32[]{:S(2)}) copy-start(f32[256,1024]{1,0:T(8,128)} %copy-done.43) | copy-start | bytes 3145732
  498.6 20.3 %copy-start.38 = (f32[256,512]{1,0:T(8,128)S(1)}, f32[256,512]{1,0:T(8,128)}, u32[]{:S(2)}) copy-start(f32[256,512]{1,0:T(8,128)} %copy-done.37) | copy-start | bytes 1572868
  498.6 20.7 %copy-start.30 = (f32[259,512]{1,0:T(8,128)S(1)}, f32[259,512]{1,0:T(8,128)}, u32[]{:S(2)}) copy-start(f32[259,512]{1,0:T(8,128)} %copy-done.29) | copy-start | bytes 1591300
  498.6 20.7 %copy-start.48 = (f32[256,512]{1,0:T(8,128)S(1)}, f32[256,512]{1,0:T(8,128)}, u32[]{:S(2)}) copy-start(f32[256,512]{1,0:T(8,128)} %param.19) | copy-start | bytes 1572868
  519.3 12.3 %copy-start.28 = (f32[256,1024]{1,0:T(8,128)S(1)}, f32[256,1024]{1,0:T(8,128)}, u32[]{:S(2)}) copy-start(f32[256,1024]{1,0:T(8,128)} %copy-done.26) | copy-start | bytes 3145732
  521.7 128.3 %collective-permute-start.3 = (f32[3,512]{1,0:T(4,128)}, f32[3,512]{1,0:T(4,128)}, u32[]{:S(2)}, u32[]{:S(2)}) collective-permute-start(f32[3,512]{1,0:T(4,128)} %get-tuple-element.207), channel_id=1, source_target_pairs={{0,1},{1,2},{2,3},{3,4},{4,5},{5,6},{6,7},{7,8},{8,9},{9,10},{10,1... | collective-permute-start | bytes 18440 | tf_op jit(solution)/shard_map/ppermute | solution.py:19
  524.3 125.8 %collective-permute-start.2 = (f32[3,512]{1,0:T(4,128)}, f32[3,512]{1,0:T(4,128)}, u32[]{:S(2)}, u32[]{:S(2)}) collective-permute-start(f32[3,512]{1,0:T(4,128)} %get-tuple-element.206), channel_id=1, source_target_pairs={{1,0},{2,1},{3,2},{4,3},{5,4},{6,5},{7,6},{8,7},{9,8},{10,9},{11,1... | collective-permute-start | bytes 18440 | tf_op jit(solution)/shard_map/ppermute | solution.py:22
  526.4 7.6 %copy-start.41 = (f32[256,1024]{1,0:T(8,128)S(1)}, f32[256,1024]{1,0:T(8,128)}, u32[]{:S(2)}) copy-start(f32[256,1024]{1,0:T(8,128)} %param.37) | copy-start | bytes 3145732
  526.4 7.6 %copy-start.50 = (f32[256,1024]{1,0:T(8,128)S(1)}, f32[256,1024]{1,0:T(8,128)}, u32[]{:S(2)}) copy-start(f32[256,1024]{1,0:T(8,128)} %get-tuple-element.241) | copy-start | bytes 3145732
  534.0 6.2 copy-start.22
  534.0 6.2 copy-start.94
  544.6 115.8 %copy-start.1 = (bf16[1024,1536]{1,0:T(8,128)(2,1)S(1)}, bf16[1024,1536]{1,0:T(8,128)(2,1)}, u32[]{:S(2)}) copy-start(bf16[1024,1536]{1,0:T(8,128)(2,1)} %param.32) | copy-start | bytes 9437188
  (43 other events, 64.5 us)
Sparse Core Ops, SparseCore 0:
  100.2 22.3 all-gather.6
  124.2 38.6 all-gather.8
  164.5 31.8 all-gather.10

commit v3 on v2

--- a/solution.py
+++ b/solution.py
@@ -668,80 +668,6 @@
     )
 
 
-def product_body(turned, cuts, wire, ins, outs, scratch):
-    (a_ref, w_ref), (o_ref,) = ins, outs
-    away, keep, inbox, final, post, c_send, c_recv, y_send, y_recv = scratch
-    seq, head, mate, across, diagonal = head_places()
-    rows = o_ref.shape[0]
-    step = rows // cuts
-    contract = (((1,), (1 if turned else 0,)), ((), ()))
-
-    def product(block, k):
-        start = pl.multiple_of(block * rows + k * step, step)
-        return lax.dot_general(
-            a_ref[pl.ds(start, step), :], w_ref[...], contract, preferred_element_type=jnp.float32
-        )
-
-    yield greet([(seq, mate), (seq, across)])
-    first = []
-    second = []
-    for side, (theirs, ours) in enumerate(((diagonal, across), (mate, head))):
-        for k in range(cuts):
-            part = pl.ds(k * step, step)
-            away[side, part, :] = product(theirs, k)
-            hop = send(
-                away.at[side, part],
-                inbox.at[side, part],
-                c_send.at[side, k],
-                c_recv.at[side, k],
-                seq,
-                mate,
-            )
-            hop.start()
-            first.append(hop)
-            keep[side, part, :] = product(ours, k)
-        if side == 0:
-            for k in range(cuts):
-                part = pl.ds(k * step, step)
-                first[k].wait_recv()
-                post[part, :] = (keep[0, part, :] + inbox[0, part, :]).astype(wire)
-                hop = send(post.at[part], final.at[part], y_send.at[k], y_recv.at[k], seq, across)
-                hop.start()
-                second.append(hop)
-        yield
-    for k in range(cuts):
-        part = pl.ds(k * step, step)
-        first[cuts + k].wait_recv()
-        second[k].wait_recv()
-        o_ref[part, :] = keep[1, part, :] + inbox[1, part, :] + final[part, :].astype(jnp.float32)
-        yield
-    for hop in first + second:
-        hop.wait_send()
-
-
-def product_scattered(a, w, turned=False, cuts=2, wire=jnp.float32):
-    rows = a.shape[0] // 4
-    width = w.shape[0] if turned else w.shape[1]
-    return Task(
-        partial(product_body, turned, cuts, wire),
-        [a, w],
-        [jax.ShapeDtypeStruct((rows, width), jnp.float32)],
-        [
-            pltpu.VMEM((2, rows, width), jnp.float32),
-            pltpu.VMEM((2, rows, width), jnp.float32),
-            pltpu.VMEM((2, rows, width), jnp.float32),
-            pltpu.VMEM((rows, width), wire),
-            pltpu.VMEM((rows, width), wire),
-            DMA((2, cuts)),
-            DMA((2, cuts)),
-            DMA((cuts,)),
-            DMA((cuts,)),
-        ],
-        VMEM,
-        VMEM,
-    )
-
-
 def spread_body(ins, outs, scratch):
     (x_ref,), (o_ref,) = ins, outs
     local, out_send, in_recv, f_send, f_recv = scratch
@@ -892,99 +818,73 @@
     inbox, post, local, p_send, p_recv, k_send, q_send, k_recv, q_recv = scratch
     seq, head, mate, _, _ = head_places()
     core = lax.rem(head, 2)
-    plane = head - core
-    home = seq // 4
-    slot = lax.rem(seq, 4)
-    for j in range(4):
-        for c in range(2):
-            @pl.when(jnp.logical_not(jnp.logical_and(4 * core + j == seq, core == c)))
-            def _():
-                hail(4 * core + j, plane + c)
-
-    hail(seq, mate)
-    yield jnp.where(core == home, 8, 9)
-    q_part, k_part = pl.ds(0, 256), pl.ds(256, 512)
+    plane = head // 2
+    mine = 8 * plane + seq
+    q_part, k_part = pl.ds(0, HALF), pl.ds(HALF, QUARTER)
+    yield greet(
+        [(lax.rem(seq + o, 8), core + 2 * p) for o in range(1, 8) for p in range(2)]
+        + [(seq, core + 2 * (1 - plane)), (seq, mate)]
+    )
+    order = [(o, q) for o in (4, 3, 5, 2, 6, 1, 7, 0) for q in (1, 0)]
+    places = [(lax.rem(seq + o, 8), lax.rem(plane + q, 2)) for o, q in order]
+
+    def rows(s, p, c):
+        return pl.ds(pl.multiple_of(s * 1024 + (c + 2 * p) * QUARTER, QUARTER), QUARTER)
+
     halves = []
-    for i in range(8):
-        source = lax.rem(seq + 1 + i, 8)
-        away = pl.ds(pl.multiple_of(source * 1024 + (1 - core) * 512, 512), 512)
+    for s, p in places:
         hop = send(
-            dkv_ref.at[away], inbox.at[source], p_send.at[source], p_recv.at[source], seq, mate
+            dkv_ref.at[rows(s, p, 1 - core)],
+            inbox.at[s, p],
+            p_send.at[s, p],
+            p_recv.at[s, p],
+            seq,
+            mate,
         )
         hop.start()
-        halves.append((source, hop))
-    for source, _ in halves:
-        here = jnp.logical_and(source == seq, core == home)
-
-        @pl.when(jnp.logical_not(here))
-        def _():
-            send(
-                dq_ref.at[source],
-                o_ref.at[slot, core, q_part],
-                q_send.at[source],
-                q_recv.at[slot, core],
-                source,
-                plane + home,
-            ).start()
-
-        @pl.when(here)
-        def _():
-            pltpu.make_async_copy(dq_ref.at[source], o_ref.at[slot, core, q_part], local.at[0]).start()
-
+        halves.append(hop)
+    finals = []
+    for s, p in places[:-1]:
+        g = 8 * p + s
+        tile = dq_ref.at[s, pl.ds(pl.multiple_of(p * HALF, HALF), HALF)]
+        out = send(tile, o_ref.at[mine, q_part], q_send.at[g], q_recv.at[mine], s, core + 2 * p)
+        out.start()
+        finals.append(
+            (out, send(tile, o_ref.at[g, q_part], q_send.at[g], q_recv.at[g], s, core + 2 * p))
+        )
+    own = pltpu.make_async_copy(
+        dq_ref.at[seq, pl.ds(pl.multiple_of(plane * HALF, HALF), HALF)],
+        o_ref.at[mine, q_part],
+        local.at[0],
+    )
+    own.start()
     yield
-    for source, hop in halves:
-        here = jnp.logical_and(source == seq, core == home)
-        hop.wait_recv()
-        kept = pl.ds(pl.multiple_of(source * 1024 + core * 512, 512), 512)
-        total = dkv_ref[kept, :] + inbox[source]
-        total = total * c_ref[source] + turn(total * s_ref[source], -1)
-        post[source] = total.astype(jnp.bfloat16)
-
-        @pl.when(jnp.logical_not(here))
-        def _():
-            send(
-                post.at[source],
-                o_ref.at[slot, core, k_part],
-                k_send.at[source],
-                k_recv.at[slot, core],
-                source,
-                plane + home,
-            ).start()
-
-        @pl.when(here)
-        def _():
-            pltpu.make_async_copy(post.at[source], o_ref.at[slot, core, k_part], local.at[1]).start()
-
-        yield
-
-    for j in range(4):
-        for c in range(2):
-            here = jnp.logical_and(4 * core + j == seq, core == c)
-
-            @pl.when(jnp.logical_not(here))
-            def _():
-                send(
-                    dq_ref.at[0], o_ref.at[j, c, q_part], q_send.at[0], q_recv.at[j, c], seq, mate
-                ).wait_recv()
-                send(
-                    post.at[0], o_ref.at[j, c, k_part], k_send.at[0], k_recv.at[j, c], seq, mate
-                ).wait_recv()
-
-            @pl.when(here)
-            def _():
-                pltpu.make_async_copy(dq_ref.at[0], o_ref.at[j, c, q_part], local.at[0]).wait()
-                pltpu.make_async_copy(post.at[0], o_ref.at[j, c, k_part], local.at[1]).wait()
-
-    for source in range(8):
-        @pl.when(jnp.logical_or(source != seq, core != home))
-        def _():
-            send(
-                dq_ref.at[source], o_ref.at[slot, core, q_part], q_send.at[source], q_recv.at[slot, core], seq, mate
-            ).wait_send()
-            send(
-                post.at[source], o_ref.at[slot, core, k_part], k_send.at[source], k_recv.at[slot, core], seq, mate
-            ).wait_send()
-    for _, hop in halves:
+    for k, (s, p) in enumerate(places):
+        g = 8 * p + s
+        halves[k].wait_recv()
+        total = dkv_ref[rows(s, p, core), :] + inbox[s, p]
+        total = total * c_ref[s, p] + turn(total * s_ref[s, p], -1)
+        post[s, p] = total.astype(jnp.bfloat16)
+        if k < 15:
+            out = send(
+                post.at[s, p], o_ref.at[mine, k_part], k_send.at[g], k_recv.at[mine], s, core + 2 * p
+            )
+            out.start()
+            finals.append(
+                (out, send(post.at[s, p], o_ref.at[g, k_part], k_send.at[g], k_recv.at[g], s, core + 2 * p))
+            )
+        else:
+            kept = pltpu.make_async_copy(post.at[s, p], o_ref.at[mine, k_part], local.at[1])
+            kept.start()
+        if k % 2:
+            yield
+    own.wait()
+    kept.wait()
+    for _, back in finals:
+        back.wait_recv()
+    for out, _ in finals:
+        out.wait_send()
+    for hop in halves:
         hop.wait_send()
 
 
@@ -992,21 +892,28 @@
     return Task(
         home_body,
         [dq, dkv, cosine, sine],
-        [jax.ShapeDtypeStruct((4, 2, 768, 128), jnp.bfloat16)],
+        [jax.ShapeDtypeStruct((16, HALF + QUARTER, 128), jnp.bfloat16)],
         [
-            pltpu.VMEM((8, 512, 128), jnp.float32),
-            pltpu.VMEM((8, 512, 128), jnp.bfloat16),
+            pltpu.VMEM((8, 2, QUARTER, 128), jnp.float32),
+            pltpu.VMEM((8, 2, QUARTER, 128), jnp.bfloat16),
             DMA((2,)),
-            DMA((8,)),
-            DMA((8,)),
-            DMA((8,)),
-            DMA((8,)),
-            DMA((4, 2)),
-            DMA((4, 2)),
+            DMA((8, 2)),
+            DMA((8, 2)),
+            DMA((16,)),
+            DMA((16,)),
+            DMA((16,)),
+            DMA((16,)),
         ],
         VMEM,
         HBM,
     )
+
+
+def owned(ref, owner):
+    if len(ref.shape) == 3:
+        return ref.at[owner]
+    width = ref.shape[1] // 8
+    return ref.at[:, pl.ds(pl.multiple_of(owner * width, width), width)]
 
 
 def seq_scatter_body(ins, outs, scratch):
@@ -1024,7 +931,7 @@
         for o in (1, 2, 3, 0):
             zt = lax.rem(z + o, 4)
             hop = send(
-                ins[i].at[2 * zt + 1 - x],
+                owned(ins[i], 2 * zt + 1 - x),
                 inbox[i].at[o],
                 x_send.at[i, o],
                 x_recv.at[i, o],
@@ -1032,7 +939,7 @@
                 head,
             )
             hop.start()
-            copy = pltpu.make_async_copy(ins[i].at[2 * zt + x], own[i].at[o], l_sem.at[i, o])
+            copy = pltpu.make_async_copy(owned(ins[i], 2 * zt + x), own[i].at[o], l_sem.at[i, o])
             copy.start()
             hops.append((i, o, hop, copy))
     yield
@@ -1067,7 +974,7 @@
 
 def seq_scattered(arrays):
     count = len(arrays)
-    shapes = [a.shape[1:] for a in arrays]
+    shapes = [a.shape[1:] if a.ndim == 3 else (a.shape[0], a.shape[1] // 8) for a in arrays]
     return Task(
         seq_scatter_body,
         arrays,
@@ -1079,71 +986,120 @@
     )
 
 
-def seq_sum_body(rule, ins, outs, scratch):
-    (x_ref, e_ref), (o_ref, t_ref) = ins, outs
-    inbox, s_send, s_recv, row, rows, h_send, h_recv = scratch
+def all_sum_body(ins, outs, scratch):
+    (x_ref,), (o_ref, q_ref) = ins, outs
+    parts, inbox, part, a_send, a_recv, s_send, s_recv, h_send, h_recv = scratch
     seq = lax.axis_index("seq")
     head = lax.axis_index("head")
-    yield greet(
-        [(lax.rem(seq + o, 8), head) for o in range(1, 8)]
-        + [(seq, lax.rem(head + o, 4)) for o in range(1, 4)]
-    )
+    others = [lax.rem(head + o, 4) for o in (2, 1, 3)]
+    sources = [lax.rem(seq + o, 8) for o in (4, 3, 5, 2, 6, 1, 7)]
+    yield greet([(s, head) for s in sources] + [(seq, other) for other in others])
     hops = []
-    for o in range(1, 8):
-        hop = send(
-            x_ref, inbox.at[seq], s_send.at[o - 1], s_recv.at[seq], lax.rem(seq + o, 8), head
-        )
+    for o, other in enumerate(others):
+        hop = send(x_ref.at[other], parts.at[head], a_send.at[o], a_recv.at[head], seq, other)
         hop.start()
         hops.append(hop)
-    inbox[seq] = x_ref[...]
-    for o in range(1, 8):
-        source = lax.rem(seq + o, 8)
-        send(
-            x_ref, inbox.at[source], s_send.at[o - 1], s_recv.at[source], source, head
-        ).wait_recv()
+    parts[head] = x_ref[head]
+    for o, other in enumerate(others):
+        send(x_ref.at[other], parts.at[other], a_send.at[o], a_recv.at[other], seq, other).wait_recv()
+    part[...] = parts[0] + parts[1] + parts[2] + parts[3]
+    for o, source in enumerate(sources):
+        hop = send(part, inbox.at[seq], s_send.at[o], s_recv.at[seq], source, head)
+        hop.start()
+        hops.append(hop)
+    inbox[seq] = part[...]
+    yield
+    for o, source in enumerate(sources):
+        send(part, inbox.at[source], s_send.at[o], s_recv.at[source], source, head).wait_recv()
     total = inbox[0]
     for s in range(1, 8):
         total = total + inbox[s]
-    o_ref[...] = total
-    summed = jnp.sum(rule(total, e_ref[...]), axis=1, keepdims=True)
-    row[...] = jnp.broadcast_to(summed, row.shape)
-    for o in range(1, 4):
-        hop = send(
-            row, rows.at[head], h_send.at[o - 1], h_recv.at[head], seq, lax.rem(head + o, 4)
-        )
+    q_ref[...] = total
+    for o, other in enumerate(others):
+        hop = send(q_ref, o_ref.at[head], h_send.at[o], h_recv.at[head], seq, other)
         hop.start()
         hops.append(hop)
-    rows[head] = row[...]
-    for o in range(1, 4):
-        source = lax.rem(head + o, 4)
-        send(row, rows.at[source], h_send.at[o - 1], h_recv.at[source], seq, source).wait_recv()
-    t_ref[...] = rows[0] + rows[1] + rows[2] + rows[3]
+    o_ref[head] = total
+    for o, other in enumerate(others):
+        send(q_ref, o_ref.at[other], h_send.at[o], h_recv.at[other], seq, other).wait_recv()
     for hop in hops:
         hop.wait_send()
 
 
-def seq_summed(x, rule, extra):
-    height, width = x.shape
-    tall = extra.shape[0]
-    return Task(
-        partial(seq_sum_body, rule),
-        [x, extra],
-        [
-            jax.ShapeDtypeStruct(x.shape, jnp.float32),
-            jax.ShapeDtypeStruct((tall, 128), jnp.float32),
-        ],
-        [
-            pltpu.VMEM((8, height, width), jnp.float32),
-            DMA((7,)),
-            DMA((8,)),
-            pltpu.VMEM((tall, 128), jnp.float32),
-            pltpu.VMEM((4, tall, 128), jnp.float32),
-            DMA((3,)),
-            DMA((4,)),
-        ],
-        VMEM,
-        VMEM,
-    )
+def all_sum_scratch(height, width):
+    return [
+        pltpu.VMEM((4, height, width), jnp.float32),
+        pltpu.VMEM((8, height, width), jnp.float32),
+        pltpu.VMEM((height, width), jnp.float32),
+        DMA((3,)),
+        DMA((4,)),
+        DMA((7,)),
+        DMA((8,)),
+        DMA((3,)),
+        DMA((4,)),
+    ]
+
+
+def rim_body(x_ref, o_ref, sems):
+    seq = lax.axis_index("seq")
+    head = lax.axis_index("head")
+    place = 4 * seq + head
+    rows = x_ref.shape[0]
+    up_send, up_recv, down_send, down_recv = (sems.at[k] for k in range(4))
+    before, after = place - 1, place + 1
+
+    @pl.when(place > 0)
+    def _():
+        hail(before // 4, lax.rem(before, 4))
+
+    @pl.when(place < 31)
+    def _():
+        hail(after // 4, lax.rem(after, 4))
+
+    yield jnp.where(place > 0, 1, 0) + jnp.where(place < 31, 1, 0)
+    below = send(
+        x_ref.at[pl.ds(rows - 8, 8)], o_ref.at[pl.ds(0, 8)], up_send, up_recv, after // 4, lax.rem(after, 4)
+    )
+    above = send(
+        x_ref.at[pl.ds(0, 8)], o_ref.at[pl.ds(rows + 8, 8)], down_send, down_recv, before // 4, lax.rem(before, 4)
+    )
+    mate = head + 1 - 2 * lax.rem(head, 2)
+    landed_low = send(
+        x_ref.at[pl.ds(rows - 8, 8)], o_ref.at[pl.ds(0, 8)], up_send, up_recv, seq, mate
+    )
+    landed_high = send(
+        x_ref.at[pl.ds(0, 8)], o_ref.at[pl.ds(rows + 8, 8)], down_send, down_recv, seq, mate
+    )
+
+    @pl.when(place < 31)
+    def _():
+        below.start()
+
+    @pl.when(place > 0)
+    def _():
+        above.start()
+
+    o_ref[pl.ds(8, rows), :] = x_ref[...]
+
+    @pl.when(place == 0)
+    def _():
+        o_ref[pl.ds(0, 8), :] = jnp.zeros((8, x_ref.shape[1]), x_ref.dtype)
+
+    @pl.when(place == 31)
+    def _():
+        o_ref[pl.ds(rows + 8, 8), :] = jnp.zeros((8, x_ref.shape[1]), x_ref.dtype)
+
+    yield
+
+    @pl.when(place > 0)
+    def _():
+        landed_low.wait_recv()
+        above.wait_send()
+
+    @pl.when(place < 31)
+    def _():
+        landed_high.wait_recv()
+        below.wait_send()
 
 
 def head_blocks_body(ins, outs, scratch):
@@ -1479,7 +1435,7 @@
         cos, sin = c_ref[rows, :], s_ref[rows, :]
         cos, sin = jnp.concatenate([cos, cos], axis=1), jnp.concatenate([sin, sin], axis=1)
         queries, keys, values = (
-            jnp.dot(part, w_ref[:, 256 * k : 256 * (k + 1)], preferred_element_type=jnp.float32)
+            jnp.dot(part, w_ref[k], preferred_element_type=jnp.float32)
             for k in range(3)
         )
         queries = (queries * cos + turn(queries, 1) * sin) * 0.125
@@ -1507,100 +1463,45 @@
     )(x, w, cosine, sine)
 
 
-def attn_out_kernel(x_ref, w_ref, c_ref, o_ref):
-    for pair in range(8):
-        first, second = pair_up(
-            x_ref[2 * pair].astype(jnp.float32), x_ref[2 * pair + 1].astype(jnp.float32)
-        )
-        lanes = slice(128 * (pair % 2), 128 * (pair % 2) + 128)
-        c_ref[pair // 2, pl.ds(0, HALF), lanes] = first.astype(jnp.bfloat16)
-        c_ref[pair // 2, pl.ds(HALF, HALF), lanes] = second.astype(jnp.bfloat16)
-    total = jnp.dot(c_ref[0], w_ref[0], preferred_element_type=jnp.float32)
-    for h in range(1, 4):
-        total += jnp.dot(c_ref[h], w_ref[h], preferred_element_type=jnp.float32)
-    o_ref[...] = total
-
-
-def attn_out(x, w):
-    return pl.pallas_call(
-        attn_out_kernel,
-        out_shape=[
-            jax.ShapeDtypeStruct((4, 256, 256), jnp.bfloat16),
-            jax.ShapeDtypeStruct((256, w.shape[2]), jnp.float32),
-        ],
-        in_specs=[VMEM] * 2,
-        out_specs=[VMEM] * 2,
-        compiler_params=LOCAL,
-        name="attn_out",
-    )(x, w)
-
-
-def attn_out_back_kernel(x_ref, w_ref, o_ref):
-    for h in range(4):
-        piece = lax.dot_general(
-            x_ref[...], w_ref[h], ROWS_TO_ROWS, preferred_element_type=jnp.float32
-        )
-        for k in range(2):
-            lanes = slice(128 * k, 128 * (k + 1))
-            even, odd = pair_up(piece[:HALF, lanes], piece[HALF:, lanes])
-            o_ref[4 * h + 2 * k] = even.astype(jnp.bfloat16)
-            o_ref[4 * h + 2 * k + 1] = odd.astype(jnp.bfloat16)
-
-
-def attn_out_back(x, w):
-    return pl.pallas_call(
-        attn_out_back_kernel,
-        out_shape=jax.ShapeDtypeStruct((16, HALF, 128), jnp.bfloat16),
-        in_specs=[VMEM] * 2,
-        out_specs=VMEM,
-        compiler_params=LOCAL,
-        name="attn_out_back",
-    )(x, w)
-
-
-def unpack_kernel(x_ref, o_ref):
-    for core in range(2):
-        for pair in range(2):
-            lanes = slice(128 * pair, 128 * (pair + 1))
-            for sub in range(2):
-                part = pl.ds(sub * HALF, HALF)
-                first, second = pair_up(
-                    x_ref[2 * pair, core, part, :].astype(jnp.float32),
-                    x_ref[2 * pair + 1, core, part, :].astype(jnp.float32),
-                )
-                at = (core + 2 * sub) * QUARTER
-                o_ref[pl.ds(at, HALF), lanes] = first.astype(jnp.bfloat16)
-                o_ref[pl.ds(at + HALF, HALF), lanes] = second.astype(jnp.bfloat16)
-            part = pl.ds(256, 512)
-            keys, values = pair_up(
-                x_ref[2 * pair, core, part, :].astype(jnp.float32),
-                x_ref[2 * pair + 1, core, part, :].astype(jnp.float32),
-            )
-            at = pl.ds(core * 512, 512)
-            o_ref[at, slice(256 + 128 * pair, 384 + 128 * pair)] = keys.astype(jnp.bfloat16)
-            o_ref[at, slice(512 + 128 * pair, 640 + 128 * pair)] = values.astype(jnp.bfloat16)
-
-
-def unpack(x):
-    return pl.pallas_call(
-        unpack_kernel,
-        out_shape=jax.ShapeDtypeStruct((1024, 768), jnp.bfloat16),
-        in_specs=[VMEM],
-        out_specs=VMEM,
-        compiler_params=LOCAL,
-        name="unpack",
-    )(x)
-
-
-WIDE = 48 << 20
-
-
-def blocks_of(array):
-    return array.reshape((8, array.shape[0] // 8) + array.shape[1:])
-
-
-def rows_of(gathered):
-    return gathered.reshape((gathered.shape[0] * gathered.shape[1],) + gathered.shape[2:])
+ROWS = 256
+ROOT_HALF = 0.7071067811865476
+
+
+def by_rows(size, body):
+    def one(i, carry):
+        body(pl.ds(pl.multiple_of(i * size, size), size), i * size)
+        return carry
+
+    lax.fori_loop(0, ROWS // size, one, 0)
+
+
+def three(x):
+    high = x.astype(jnp.bfloat16)
+    rest = x - high.astype(jnp.float32)
+    middle = rest.astype(jnp.bfloat16)
+    return high, middle, (rest - middle.astype(jnp.float32)).astype(jnp.bfloat16)
+
+
+def pick(onehot, rows):
+    high, middle, low = (jnp.dot(onehot, t, preferred_element_type=jnp.float32) for t in rows)
+    return high + (middle + low)
+
+
+def sum_by(onehot, x):
+    high, middle, low = (
+        lax.dot_general(onehot, t, (((0,), (0,)), ((), ())), preferred_element_type=jnp.float32)
+        for t in three(x)
+    )
+    return high + (middle + low)
+
+
+def onehot_of(first, count, table, utterances):
+    rows = first + lax.broadcasted_iota(jnp.int32, (count, 1), 0)
+    segment = jnp.zeros((count, 1), jnp.int32)
+    for u in range(utterances):
+        segment = segment + (rows >= table[u]).astype(jnp.int32)
+    spots = lax.broadcasted_iota(jnp.int32, (count, 16), 1)
+    return (segment == spots).astype(jnp.float32).astype(jnp.bfloat16)
 
 
 def normed(values):
@@ -1618,12 +1519,616 @@
     ) * inverse
 
 
-def root_rule(total, extra):
-    return jnp.sqrt(total + 1.0)
-
-
-def product_rule(total, extra):
-    return total[: extra.shape[0]] * extra
+def gelu_exact(x):
+    return x * (0.5 * (1.0 + lax.erf(x * ROOT_HALF)))
+
+
+def gelu_exact_slope(x):
+    return 0.5 * (1.0 + lax.erf(x * ROOT_HALF)) + x * (0.3989422804014327 * jnp.exp(-0.5 * x * x))
+
+
+def gelu_tanh(x):
+    t = jnp.tanh(0.7978845608028654 * (x + 0.044715 * x * x * x))
+    half = 0.5 * (1.0 + t)
+    slope = half + 0.5 * x * (1.0 - t * t) * (0.7978845608028654 * (1.0 + 0.134145 * x * x))
+    return x * half, slope
+
+
+def own_first():
+    return (4 * lax.axis_index("seq") + lax.axis_index("head")) * ROWS
+
+
+def tap_rows(window, first, start, end, tap):
+    there = first + tap - 3 + lax.broadcasted_iota(jnp.int32, (32, 1), 0)
+    return jnp.where((there >= start) & (there < end), window[5 + tap : 37 + tap], 0.0)
+
+
+def ratio_of(total):
+    norm = jnp.sqrt(total + 1.0)
+    mean = jnp.sum(jnp.sum(norm, axis=2, keepdims=True), axis=0, keepdims=True) / (4 * norm.shape[2])
+    return norm, mean + 1e-06
+
+
+def text_body(utterances, ins, outs, scratch):
+    (
+        table,
+        text_ref,
+        mel_ref,
+        cot_ref,
+        mask_ref,
+        taps_ref,
+        gain_ref,
+        bias_ref,
+        expand_ref,
+        shrink_ref,
+        join_ref,
+        share_ref,
+    ) = ins
+    (
+        ext_ref,
+        unit_ref,
+        inverse_ref,
+        text_low_ref,
+        expand_all,
+        shrink_all,
+        mods_ref,
+        scale_ref,
+        expanded_ref,
+        grn_ref,
+        total_ref,
+        join_low_ref,
+        hidden_ref,
+        attn_low_ref,
+        attn_all_ref,
+        d_ffn_ref,
+        text_all_ref,
+    ) = outs
+    own_ref, act_ref, sums_ref, share_all, branch_ref, rim_sems = scratch[:6]
+    rest = scratch[6:]
+    weights = gather_body(1, (expand_ref, shrink_ref), (expand_all, shrink_all), rest[:7])
+    shares = gather_body(1, (share_ref,), (share_all,), rest[7:14])
+    rows_out = gather_body(2, (attn_low_ref,), (attn_all_ref,), rest[14:21])
+    text_out = gather_body(1, (text_low_ref,), (text_all_ref,), rest[21:28])
+    rim = rim_body(text_ref, ext_ref, rim_sems)
+    sums = all_sum_body((sums_ref,), (total_ref, own_ref), rest[28:])
+    running = (weights, shares, rows_out, text_out, rim, sums)
+    yield sum(next(one) for one in running)
+    first = own_first()
+    next(rim)
+    next(weights)
+    next(shares)
+    next(rim, None)
+
+    def conv(at, i):
+        rows = first + i + lax.broadcasted_iota(jnp.int32, (32, 1), 0)
+        start, end = limits(rows, table, utterances)
+        window = ext_ref[pl.ds(pl.multiple_of(i, 32), 48), :]
+        total = jnp.zeros((32, window.shape[1]), jnp.float32)
+        for tap in range(7):
+            total = total + tap_rows(window, first + i, start, end, tap) * taps_ref[tap : tap + 1, :]
+        unit, inverse = normed(total)
+        unit_ref[at, :] = unit
+        inverse_ref[at, :] = jnp.broadcast_to(inverse, (32, 128))
+        text_low_ref[at, :] = (unit * gain_ref[...] + bias_ref[...]).astype(jnp.bfloat16)
+
+    by_rows(32, conv)
+    yield
+    for _ in weights:
+        pass
+    for _ in shares:
+        pass
+    onehot = onehot_of(first, ROWS, table, utterances)
+
+    def expand(h, carry):
+        expanded = jnp.dot(text_low_ref[...], expand_all[h], preferred_element_type=jnp.float32)
+        expanded_ref[h] = expanded
+        active = gelu_exact(expanded)
+        act_ref[h] = active
+        sums_ref[h] = sum_by(onehot, active * active)
+        return carry
+
+    lax.fori_loop(0, 4, expand, 0)
+    next(sums)
+    for h in range(4):
+        mods_ref[:, 1536 * h : 1536 * (h + 1)] = share_all[h, :16]
+        scale_ref[h] = share_all[h, 16:, :512]
+    mods = three(mods_ref[:, 5120:6144])
+
+    def d_ffn(at, i):
+        gate = pick(onehot_of(first + i, 64, table, utterances), mods)
+        d_ffn_ref[at, :] = (cot_ref[at, :] * gate).astype(jnp.bfloat16)
+
+    by_rows(64, d_ffn)
+    for _ in sums:
+        pass
+    next(text_out)
+    norm, mean = ratio_of(total_ref[...])
+    sums_ref[...] = norm / mean
+    branch_ref[...] = jnp.zeros_like(branch_ref)
+
+    def shrink(h, carry):
+        active = act_ref[h]
+        ratio = pick(onehot, three(sums_ref[h]))
+        gamma, beta = scale_ref[h, 0:1, :256], scale_ref[h, 0:1, 256:]
+        low = (gamma * active * ratio + beta + active).astype(jnp.bfloat16)
+        grn_ref[h] = low
+        branch_ref[...] += jnp.dot(low, shrink_all[h], preferred_element_type=jnp.float32)
+        return carry
+
+    lax.fori_loop(0, 4, shrink, 0)
+    join_low_ref[...] = (text_ref[...] + mask_ref[...] * branch_ref[...]).astype(jnp.bfloat16)
+
+    def join(n, carry):
+        lanes = pl.ds(pl.multiple_of(n * 256, 256), 256)
+        hidden_ref[:, lanes] = mel_ref[:, lanes] + jnp.dot(
+            join_low_ref[...], join_ref[:, lanes], preferred_element_type=jnp.float32
+        )
+        return carry
+
+    lax.fori_loop(0, 4, join, 0)
+    shift, scale = three(mods_ref[:, :1024]), three(mods_ref[:, 1024:2048])
+
+    def attn(at, i):
+        spots = onehot_of(first + i, 32, table, utterances)
+        unit, _ = normed(hidden_ref[at, :])
+        attn_low_ref[at, :] = (unit * (1.0 + pick(spots, scale)) + pick(spots, shift)).astype(
+            jnp.bfloat16
+        )
+
+    by_rows(32, attn)
+    for _ in rows_out:
+        pass
+    for _ in text_out:
+        pass
+
+
+def gather_scratch(count, cuts):
+    return [DMA((count,)), DMA((count, cuts)), DMA((count, cuts)), DMA((count,)), DMA((count,)), DMA((count, cuts)), DMA((count, cuts))]
+
+
+def text_forward(table, text, mel, cot, mask, taps, gain, bias, expand, shrink, join, share, utterances):
+    def f32(*shape):
+        return jax.ShapeDtypeStruct(shape, jnp.float32)
+
+    def low(*shape):
+        return jax.ShapeDtypeStruct(shape, jnp.bfloat16)
+
+    width, wide = text.shape[1], mel.shape[1]
+    outs = [
+        (f32(ROWS + 16, width), VMEM),
+        (f32(ROWS, width), VMEM),
+        (f32(ROWS, 128), VMEM),
+        (low(ROWS, width), VMEM),
+        (low(4, width, 256), VMEM),
+        (low(4, 256, width), VMEM),
+        (f32(16, 6 * wide), VMEM),
+        (f32(4, 8, 512), VMEM),
+        (f32(4, ROWS, 256), VMEM),
+        (low(4, ROWS, 256), VMEM),
+        (f32(4, 16, 256), VMEM),
+        (low(ROWS, width), VMEM),
+        (f32(ROWS, wide), VMEM),
+        (low(ROWS, wide), VMEM),
+        (low(4, ROWS, wide), HBM),
+        (low(ROWS, wide), VMEM),
+        (low(4, ROWS, width), HBM),
+    ]
+    return Task(
+        partial(text_body, utterances),
+        [table, text, mel, cot, mask, taps, gain, bias, expand, shrink, join, share],
+        [o for o, _ in outs],
+        [
+            pltpu.VMEM((16, 256), jnp.float32),
+            pltpu.VMEM((4, ROWS, 256), jnp.float32),
+            pltpu.VMEM((4, 16, 256), jnp.float32),
+            pltpu.VMEM((4,) + share.shape, jnp.float32),
+            pltpu.VMEM((ROWS, width), jnp.float32),
+            DMA((4,)),
+        ]
+        + gather_scratch(2, 1)
+        + gather_scratch(1, 1)
+        + gather_scratch(1, 2)
+        + gather_scratch(1, 1)
+        + all_sum_scratch(16, 256),
+        [SMEM] + [VMEM] * 11,
+        [s for _, s in outs],
+    )
+
+
+def middle_kernel(
+    utterances,
+    table,
+    tiles_ref,
+    out_ref,
+    up_hbm,
+    down_hbm,
+    hidden_ref,
+    mods_ref,
+    cot_ref,
+    d_ffn_ref,
+    context_ref,
+    layer_ref,
+    ffn_low_ref,
+    gelu_ref,
+    d_up_ref,
+    d_attn_ref,
+    d_middle_ref,
+    d_tiles_ref,
+    d_mods_ref,
+    up_ref,
+    down_ref,
+    attn_ref,
+    middle_ref,
+    rows_ref,
+    d_in_ref,
+    sems,
+):
+    copies = []
+    for h in range(4):
+        copies.append(
+            (
+                pltpu.make_async_copy(up_hbm.at[h], up_ref.at[h], sems.at[h]),
+                pltpu.make_async_copy(down_hbm.at[h], down_ref.at[h], sems.at[4 + h]),
+            )
+        )
+        for copy in copies[-1]:
+            copy.start()
+    first = own_first()
+    for pair in range(8):
+        upper, lower = pair_up(
+            tiles_ref[2 * pair].astype(jnp.float32), tiles_ref[2 * pair + 1].astype(jnp.float32)
+        )
+        lanes = slice(128 * (pair % 2), 128 * (pair % 2) + 128)
+        context_ref[pair // 2, pl.ds(0, HALF), lanes] = upper.astype(jnp.bfloat16)
+        context_ref[pair // 2, pl.ds(HALF, HALF), lanes] = lower.astype(jnp.bfloat16)
+    attn_ref[...] = jnp.zeros_like(attn_ref)
+
+    def project_out(h, carry):
+        attn_ref[...] += jnp.dot(context_ref[h], out_ref[h], preferred_element_type=jnp.float32)
+        return carry
+
+    lax.fori_loop(0, 4, project_out, 0)
+    mods = [three(mods_ref[:, 1024 * k : 1024 * (k + 1)]) for k in range(6)]
+
+    def enter(at, i):
+        spots = onehot_of(first + i, 32, table, utterances)
+        middle = hidden_ref[at, :] + pick(spots, mods[2]) * attn_ref[at, :]
+        middle_ref[at, :] = middle
+        unit, _ = normed(middle)
+        ffn_low_ref[at, :] = (unit * (1.0 + pick(spots, mods[4])) + pick(spots, mods[3])).astype(
+            jnp.bfloat16
+        )
+
+    by_rows(32, enter)
+    rows_ref[...] = jnp.zeros_like(rows_ref)
+    d_in_ref[...] = jnp.zeros_like(d_in_ref)
+    for h in range(4):
+        for copy in copies[h]:
+            copy.wait()
+
+    def feed(h, carry):
+        upward = jnp.dot(ffn_low_ref[...], up_ref[h], preferred_element_type=jnp.float32)
+        value, slope = gelu_tanh(upward)
+        gelu_ref[h] = value.astype(jnp.bfloat16)
+        grad = lax.dot_general(
+            d_ffn_ref[...], down_ref[h], ROWS_TO_ROWS, preferred_element_type=jnp.float32
+        )
+        d_up_ref[h] = (grad * slope).astype(jnp.bfloat16)
+        rows_ref[...] += jnp.dot(gelu_ref[h], down_ref[h], preferred_element_type=jnp.float32)
+        d_in_ref[...] += lax.dot_general(
+            d_up_ref[h], up_ref[h], ROWS_TO_ROWS, preferred_element_type=jnp.float32
+        )
+        return carry
+
+    lax.fori_loop(0, 4, feed, 0)
+    d_mods_ref[...] = jnp.zeros_like(d_mods_ref)
+
+    def leave(at, i):
+        spots = onehot_of(first + i, 32, table, utterances)
+        middle, cot, d_in, rows = middle_ref[at, :], cot_ref[at, :], d_in_ref[at, :], rows_ref[at, :]
+        layer_ref[at, :] = middle + pick(spots, mods[5]) * rows
+        unit, inverse = normed(middle)
+        d_middle = cot + normed_back(d_in * (1.0 + pick(spots, mods[4])), unit, inverse)
+        d_middle_ref[at, :] = d_middle
+        d_attn_ref[at, :] = (d_middle * pick(spots, mods[2])).astype(jnp.bfloat16)
+        for k, grad in enumerate((d_middle * attn_ref[at, :], d_in, d_in * unit, cot * rows)):
+            d_mods_ref[:, 1024 * k : 1024 * (k + 1)] += sum_by(spots, grad)
+
+    by_rows(32, leave)
+    for h in range(4):
+        piece = lax.dot_general(
+            d_attn_ref[...], out_ref[h], ROWS_TO_ROWS, preferred_element_type=jnp.float32
+        )
+        for k in range(2):
+            lanes = slice(128 * k, 128 * (k + 1))
+            even, odd = pair_up(piece[:HALF, lanes], piece[HALF:, lanes])
+            d_tiles_ref[4 * h + 2 * k] = even.astype(jnp.bfloat16)
+            d_tiles_ref[4 * h + 2 * k + 1] = odd.astype(jnp.bfloat16)
+
+
+def middle_part(table, tiles, out, up, down, hidden, mods, cot, d_ffn, utterances):
+    wide = hidden.shape[1]
+
+    def f32(*shape):
+        return jax.ShapeDtypeStruct(shape, jnp.float32)
+
+    def low(*shape):
+        return jax.ShapeDtypeStruct(shape, jnp.bfloat16)
+
+    return pl.pallas_call(
+        partial(middle_kernel, utterances),
+        out_shape=[
+            low(4, ROWS, 256),
+            f32(ROWS, wide),
+            low(ROWS, wide),
+            low(4, ROWS, up.shape[2]),
+            low(4, ROWS, up.shape[2]),
+            low(ROWS, wide),
+            f32(ROWS, wide),
+            low(16, HALF, 128),
+            f32(16, 4 * wide),
+        ],
+        in_specs=[SMEM, VMEM, VMEM, HBM, HBM] + [VMEM] * 4,
+        out_specs=[VMEM] * 9,
+        scratch_shapes=[
+            pltpu.VMEM(up.shape, jnp.bfloat16),
+            pltpu.VMEM(down.shape, jnp.bfloat16),
+            pltpu.VMEM((ROWS, wide), jnp.float32),
+            pltpu.VMEM((ROWS, wide), jnp.float32),
+            pltpu.VMEM((ROWS, wide), jnp.float32),
+            pltpu.VMEM((ROWS, wide), jnp.float32),
+            DMA((8,)),
+        ],
+        compiler_params=LOCAL,
+        name="middle_part",
+    )(table, tiles, out, up, down, hidden, mods, cot, d_ffn)
+
+
+def back_body(utterances, ins, outs, scratch):
+    (
+        table,
+        tiles_ref,
+        qkv_ref,
+        hidden_ref,
+        d_middle_ref,
+        mods_ref,
+        join_ref,
+        shrink_all,
+        expand_all,
+        expanded_ref,
+        squares_ref,
+        scale_ref,
+        mask_ref,
+        unit_ref,
+        inverse_ref,
+        gain_ref,
+        taps_ref,
+        ext_ref,
+    ) = ins
+    (
+        d_qkv_ref,
+        mel_ref,
+        d_joined_ref,
+        d_branch_ref,
+        d_expanded_ref,
+        text_ref,
+        d_mods_ref,
+        small_ref,
+        own_ref,
+        d_qkv_all,
+        d_branch_all,
+        d_expanded_all,
+    ) = outs
+    d_in_ref, d_text_ref, d_grn_ref, sums_ref, total_ref, d_norm_ref, ratio_ref, d_conv_ref, d_ext_ref = (
+        scratch[:9]
+    )
+    rim_sems, rest = scratch[9], scratch[10:]
+    swap = exchange_body((d_qkv_ref,), (d_qkv_all,), rest[:3])
+    branch_out = gather_body(1, (d_branch_ref,), (d_branch_all,), rest[3:10])
+    expanded_out = exchange_body((d_expanded_ref,), (d_expanded_all,), rest[10:13])
+    sums = all_sum_body((sums_ref,), (total_ref, own_ref), rest[13:22])
+    rim = rim_body(d_conv_ref, d_ext_ref, rim_sems)
+    running = (swap, branch_out, expanded_out, sums, rim)
+    yield sum(next(one) for one in running)
+    first = own_first()
+    for pair in range(8):
+        even, odd = tiles_ref.at[2 * pair], tiles_ref.at[2 * pair + 1]
+        lanes = slice(128 * (pair % 2), 128 * (pair % 2) + 128)
+        upper, lower = pair_up(
+            even[pl.ds(0, HALF), :].astype(jnp.float32), odd[pl.ds(0, HALF), :].astype(jnp.float32)
+        )
+        d_qkv_ref[pair // 2, pl.ds(0, HALF), lanes] = upper.astype(jnp.bfloat16)
+        d_qkv_ref[pair // 2, pl.ds(HALF, HALF), lanes] = lower.astype(jnp.bfloat16)
+        keys, values = pair_up(
+            even[pl.ds(HALF, QUARTER), :].astype(jnp.float32),
+            odd[pl.ds(HALF, QUARTER), :].astype(jnp.float32),
+        )
+        at = 128 * (pair % 2)
+        d_qkv_ref[pair // 2, :, 256 + at : 384 + at] = keys.astype(jnp.bfloat16)
+        d_qkv_ref[pair // 2, :, 512 + at : 640 + at] = values.astype(jnp.bfloat16)
+    next(swap)
+    d_in_ref[...] = jnp.zeros_like(d_in_ref)
+
+    def enter(h, carry):
+        for k in range(3):
+            d_in_ref[...] += lax.dot_general(
+                d_qkv_ref[h, :, 256 * k : 256 * (k + 1)], qkv_ref[h, k], ROWS_TO_ROWS, preferred_element_type=jnp.float32
+            )
+        return carry
+
+    lax.fori_loop(0, 4, enter, 0)
+    yield
+    scale = three(mods_ref[:, 1024:2048])
+    d_mods_ref[...] = jnp.zeros_like(d_mods_ref)
+
+    def hidden_back(at, i):
+        spots = onehot_of(first + i, 32, table, utterances)
+        unit, inverse = normed(hidden_ref[at, :])
+        d_in = d_in_ref[at, :]
+        mel = d_middle_ref[at, :] + normed_back(d_in * (1.0 + pick(spots, scale)), unit, inverse)
+        mel_ref[at, :] = mel
+        d_joined_ref[at, :] = mel.astype(jnp.bfloat16)
+        for k, grad in enumerate((d_in, d_in * unit)):
+            d_mods_ref[:, 1024 * k : 1024 * (k + 1)] += sum_by(spots, grad)
+
+    by_rows(32, hidden_back)
+    d_text = lax.dot_general(
+        d_joined_ref[...], join_ref[...], ROWS_TO_ROWS, preferred_element_type=jnp.float32
+    )
+    d_text_ref[...] = d_text
+    d_branch_ref[...] = (mask_ref[...] * d_text).astype(jnp.bfloat16)
+    next(branch_out)
+    onehot = onehot_of(first, ROWS, table, utterances)
+    norm, mean = ratio_of(squares_ref[...])
+    ratio_ref[...] = norm / mean
+
+    def grn_back(h, carry):
+        grad = lax.dot_general(
+            d_branch_ref[...], shrink_all[h], ROWS_TO_ROWS, preferred_element_type=jnp.float32
+        )
+        d_grn_ref[h] = grad
+        active = gelu_exact(expanded_ref[h])
+        gamma = scale_ref[h, 0:1, :256]
+        both = grad * active
+        sums_ref[h, pl.ds(0, 8), :] = sum_by(onehot, both * gamma)[:8]
+        sums_ref[h, pl.ds(8, 8), :] = jnp.concatenate(
+            [
+                jnp.sum(both * pick(onehot, three(ratio_ref[h])), axis=0, keepdims=True),
+                jnp.sum(grad, axis=0, keepdims=True),
+                jnp.zeros((6, 256), jnp.float32),
+            ],
+            axis=0,
+        )
+        return carry
+
+    lax.fori_loop(0, 4, grn_back, 0)
+    next(sums)
+    yield
+    for _ in sums:
+        pass
+    d_ratio = total_ref[...]
+    d_mean = -jnp.sum(jnp.sum(d_ratio * norm, axis=2, keepdims=True), axis=0, keepdims=True) / (
+        mean * mean
+    )
+    d_norm_ref[...] = (d_ratio / mean + d_mean / (4 * norm.shape[2])) / norm
+    d_text_ref_norm = d_conv_ref
+    d_text_ref_norm[...] = jnp.zeros_like(d_text_ref_norm)
+
+    def expand_back(h, carry):
+        expanded = expanded_ref[h]
+        active = gelu_exact(expanded)
+        gamma = scale_ref[h, 0:1, :256]
+        ratio = pick(onehot, three(ratio_ref[h]))
+        slope = pick(onehot, three(d_norm_ref[h]))
+        d_active = d_grn_ref[h] * (gamma * ratio + 1.0) + active * slope
+        low = (d_active * gelu_exact_slope(expanded)).astype(jnp.bfloat16)
+        d_expanded_ref[h] = low
+        d_text_ref_norm[...] += lax.dot_general(
+            low, expand_all[h], ROWS_TO_ROWS, preferred_element_type=jnp.float32
+        )
+        return carry
+
+    lax.fori_loop(0, 4, expand_back, 0)
+    next(expanded_out)
+    small_ref[...] = jnp.zeros_like(small_ref)
+
+    def norm_back(at, i):
+        grad, unit = d_text_ref_norm[at, :], unit_ref[at, :]
+        small_ref[7:8, :] += jnp.sum(grad * unit, axis=0, keepdims=True)
+        small_ref[8:9, :] += jnp.sum(grad, axis=0, keepdims=True)
+        d_conv_ref[at, :] = normed_back(grad * gain_ref[...], unit, inverse_ref[at, :1])
+
+    by_rows(32, norm_back)
+    next(rim)
+    yield
+
+    def taps_back(at, i):
+        rows = first + i + lax.broadcasted_iota(jnp.int32, (32, 1), 0)
+        start, end = limits(rows, table, utterances)
+        window = ext_ref[pl.ds(pl.multiple_of(i, 32), 48), :]
+        grad = d_conv_ref[at, :]
+        for tap in range(7):
+            small_ref[tap : tap + 1, :] += jnp.sum(
+                grad * tap_rows(window, first + i, start, end, tap), axis=0, keepdims=True
+            )
+
+    by_rows(32, taps_back)
+    next(rim, None)
+
+    def text_back(at, i):
+        rows = first + i + lax.broadcasted_iota(jnp.int32, (32, 1), 0)
+        start, end = limits(rows, table, utterances)
+        window = d_ext_ref[pl.ds(pl.multiple_of(i, 32), 48), :]
+        total = d_text_ref[at, :]
+        for tap in range(7):
+            total = (
+                total
+                + tap_rows(window, first + i, start, end, 6 - tap) * taps_ref[tap : tap + 1, :]
+            )
+        text_ref[at, :] = total
+
+    by_rows(32, text_back)
+    for one in (swap, branch_out, expanded_out):
+        for _ in one:
+            pass
+
+
+def text_backward(operands, utterances):
+    def f32(*shape):
+        return jax.ShapeDtypeStruct(shape, jnp.float32)
+
+    def low(*shape):
+        return jax.ShapeDtypeStruct(shape, jnp.bfloat16)
+
+    wide, width = 1024, 512
+    outs = [
+        (low(4, ROWS, 768), VMEM),
+        (f32(ROWS, wide), VMEM),
+        (low(ROWS, wide), VMEM),
+        (low(ROWS, width), VMEM),
+        (low(4, ROWS, 256), VMEM),
+        (f32(ROWS, width), VMEM),
+        (f32(16, 2 * wide), VMEM),
+        (f32(16, width), VMEM),
+        (f32(16, 256), VMEM),
+        (low(4, ROWS, 768), HBM),
+        (low(4, ROWS, width), HBM),
+        (low(4, ROWS, 256), HBM),
+    ]
+    return Task(
+        partial(back_body, utterances),
+        operands,
+        [o for o, _ in outs],
+        [
+            pltpu.VMEM((ROWS, wide), jnp.float32),
+            pltpu.VMEM((ROWS, width), jnp.float32),
+            pltpu.VMEM((4, ROWS, 256), jnp.float32),
+            pltpu.VMEM((4, 16, 256), jnp.float32),
+            pltpu.VMEM((4, 16, 256), jnp.float32),
+            pltpu.VMEM((4, 16, 256), jnp.float32),
+            pltpu.VMEM((4, 16, 256), jnp.float32),
+            pltpu.VMEM((ROWS, width), jnp.float32),
+            pltpu.VMEM((ROWS + 16, width), jnp.float32),
+            DMA((4,)),
+        ]
+        + [DMA((1,)), DMA((1, 3)), DMA((1, 4))]
+        + gather_scratch(1, 1)
+        + [DMA((1,)), DMA((1, 3)), DMA((1, 4))]
+        + all_sum_scratch(16, 256),
+        [SMEM] + [VMEM] * (len(operands) - 1),
+        [s for _, s in outs],
+    )
+
+
+WIDE = 48 << 20
+
+
+def blocks_of(array):
+    return array.reshape((8, array.shape[0] // 8) + array.shape[1:])
+
+
+def rows_of(gathered):
+    return gathered.reshape((gathered.shape[0] * gathered.shape[1],) + gathered.shape[2:])
 
 
 def angles_of(places, lanes):
@@ -1660,24 +2165,14 @@
     head_index = lax.axis_index("head")
     core = lax.rem(head_index, 2)
     utterances = lengths.shape[0]
-    row_first = (seq_index * 4 + head_index) * rows_here
-    frame_first = seq_index * frames_here
-    row_ids = row_first + jnp.arange(rows_here, dtype=jnp.int32)
-    frame_ids = frame_first + jnp.arange(frames_here, dtype=jnp.int32)
-    row_segment = segment_of(row_ids, lengths)
-    frame_segment = segment_of(frame_ids, lengths)
-    utter_ids = jnp.arange(utterances, dtype=jnp.int32)
-    row_onehot = (row_segment[:, None] == utter_ids[None, :]).astype(jnp.float32)
-    frame_onehot = (frame_segment[:, None] == utter_ids[None, :]).astype(jnp.float32)
-    mask_rows = text_mask.astype(jnp.float32)[:, None]
     taps_count = conv_weight.shape[0]
-    half_kernel = taps_count // 2
+    wide = mel_in.shape[1]
 
     all_ids = jnp.arange(8 * frames_here, dtype=jnp.int32)
     places = position_of(all_ids, lengths, segment_of(all_ids, lengths))
     table = attention_table(lengths, core)
     own_angles = angles_of(
-        lax.dynamic_slice_in_dim(places, frame_first, frames_here)[:, None], 128
+        lax.dynamic_slice_in_dim(places, seq_index * frames_here, frames_here)[:, None], 128
     )
     own_cos, own_sin = jnp.cos(own_angles), jnp.sin(own_angles)
     tiles = lax.dynamic_index_in_dim(
@@ -1686,226 +2181,207 @@
     query_angles = angles_of(
         jnp.where(jnp.arange(128) < 64, tiles[:, :, 0, :, None], tiles[:, :, 1, :, None]), 128
     ).reshape(8, QUARTER, 128)
-    key_places = lax.dynamic_index_in_dim(places.reshape(8, 2, 512), core, 1, keepdims=False)
-    key_angles = angles_of(key_places[:, :, None], 64)
-
-    extended = frame_rim(text_in, half_kernel)
-    extended_ids = (
-        row_first - half_kernel + jnp.arange(rows_here + 2 * half_kernel, dtype=jnp.int32)
-    )
-    extended_segment = segment_of(extended_ids, lengths)
-    same_taps = jnp.stack(
+    key_angles = angles_of(tiles.reshape(8, 2 * QUARTER)[:, :, None], 64)
+
+    cond_low = jax.nn.silu(time_embed).astype(jnp.bfloat16)
+    mod_part = narrow_dot(cond_low, modulation)
+    share = jnp.concatenate(
         [
-            (extended_segment[tap : tap + rows_here] == row_segment).astype(jnp.float32)
-            for tap in range(taps_count)
+            mod_part,
+            jnp.zeros((16 - utterances, mod_part.shape[1]), jnp.float32),
+            jnp.pad(
+                jnp.concatenate([grn_gamma, grn_beta])[None, :],
+                ((0, 7), (0, mod_part.shape[1] - 2 * grn_gamma.shape[0])),
+            ),
         ]
     )
-    conv_out = jnp.zeros_like(text_in)
-    for tap in range(taps_count):
-        conv_out = (
-            conv_out
-            + extended[tap : tap + rows_here] * conv_weight[tap] * same_taps[tap][:, None]
-        )
-    text_unit, text_inverse = normed(conv_out)
-    text_low = (text_unit * norm_gain + norm_bias).astype(jnp.bfloat16)
-    cond_low = jax.nn.silu(time_embed).astype(jnp.bfloat16)
-    ((text_all, mod_parts),) = communicate(
-        [gathered([text_low, narrow_dot(cond_low, modulation)])], 0
-    )
-    text_all = rows_of(text_all)
-    mod_all = mod_parts.transpose(1, 0, 2).reshape(utterances, -1)
-    expanded = narrow_dot(text_all, expand_weight)
-    activated, gelu_exact_back = jax.vjp(partial(jax.nn.gelu, approximate=False), expanded)
-    text_channels = expand_weight.shape[1] * 4
-    squares = exact_inner(frame_onehot, activated * activated)
-    ((squares_all, channel_total),) = communicate([seq_summed(squares, root_rule, squares)], 1)
-    grn_norm = jnp.sqrt(squares_all + 1.0)
-    denominator = channel_total[:, 0] / text_channels + 1e-06
-    grn_ratio = grn_norm / denominator[:, None]
-    ratio_rows = exact_dot(frame_onehot, grn_ratio)
-    grn_low = (grn_gamma * activated * ratio_rows + grn_beta + activated).astype(jnp.bfloat16)
-    ((branch,),) = communicate([product_scattered(grn_low, shrink_weight)], 2, WIDE)
-    join_low = (text_in + mask_rows * branch).astype(jnp.bfloat16)
-    hidden = mel_in + narrow_dot(join_low, join_weight)
-
-    mod_rows = exact_dot(row_onehot, mod_all)
-    shift_attn, scale_attn, gate_attn, shift_ffn, scale_ffn, gate_ffn = jnp.split(
-        mod_rows, 6, axis=1
-    )
-    hidden_unit, hidden_inverse = normed(hidden)
-    attn_low = (hidden_unit * (1.0 + scale_attn) + shift_attn).astype(jnp.bfloat16)
-    d_ffn_low = (cotangent * gate_ffn).astype(jnp.bfloat16)
-    ((attn_all,),) = communicate([gathered([attn_low])], 3)
-    attn_all, out_near, up_near, down_near = lax.optimization_barrier(
-        (attn_all, out_weight, up_weight, down_weight)
-    )
-    out_full, up_full, down_full = (
-        lax.all_gather(w, "head", axis=0) for w in (out_near, up_near, down_near)
+    mask_rows = text_mask.astype(jnp.float32)[:, None]
+    (
+        (
+            extended,
+            text_unit,
+            text_inverse,
+            _,
+            expand_all,
+            shrink_all,
+            mods,
+            scale,
+            expanded,
+            grn_low,
+            squares,
+            join_low,
+            hidden,
+            _,
+            attn_all,
+            d_ffn_low,
+            text_all,
+        ),
+    ) = communicate(
+        [
+            text_forward(
+                table,
+                text_in,
+                mel_in,
+                cotangent,
+                mask_rows,
+                conv_weight,
+                norm_gain[None, :],
+                norm_bias[None, :],
+                expand_weight,
+                shrink_weight,
+                join_weight,
+                share,
+                utterances,
+            )
+        ],
+        0,
+        WIDE,
+    )
+
+    qkv_near = qkv_weight.transpose(1, 0, 2)
+    attn_all, out_near, up_near, down_near, qkv_late = lax.optimization_barrier(
+        (attn_all, out_weight, up_weight, down_weight, qkv_near)
+    )
+    out_full, up_full, down_full, qkv_full = (
+        lax.all_gather(w, "head", axis=0) for w in (out_near, up_near, down_near, qkv_late)
     )
     attn_all = rows_of(attn_all)
-    qkv_flat = qkv_weight.reshape(qkv_weight.shape[0], -1)
-    head_cols = qkv_weight.shape[2]
     (packed,), (query_cos, query_sin, key_cos, key_sin), (d_ffn_all,) = communicate(
         [
-            spread_out(project(attn_all, qkv_flat, own_cos, own_sin)),
+            spread_out(project(attn_all, qkv_near, own_cos, own_sin)),
             turns([query_angles, key_angles]),
             gathered([d_ffn_low]),
         ],
-        4,
+        1,
         WIDE,
     )
     context_here, logsum = attend(table, packed, utterances)
-    ((context_tiles,),) = communicate([to_rows(context_here)], 5)
-    context_blocks, attn_rows = attn_out(context_tiles, out_full)
-    middle = hidden + gate_attn * attn_rows
-
-    middle_unit, middle_inverse = normed(middle)
-    ffn_low = (middle_unit * (1.0 + scale_ffn) + shift_ffn).astype(jnp.bfloat16)
-    gelu_low, d_up_low = [], []
-    ffn_rows = d_ffn_in = 0.0
-    for h in range(4):
-        upward = narrow_dot(ffn_low, up_full[h])
-        value, back = jax.vjp(partial(jax.nn.gelu, approximate=True), upward)
-        gelu_low.append(value.astype(jnp.bfloat16))
-        d_up_low.append(back(against_rows(d_ffn_low, down_full[h]))[0].astype(jnp.bfloat16))
-        ffn_rows += narrow_dot(gelu_low[h], down_full[h])
-        d_ffn_in += against_rows(d_up_low[h], up_full[h])
-    gelu_low, d_up_low = jnp.stack(gelu_low), jnp.stack(d_up_low)
-    transformer_layer_output = middle + gate_ffn * ffn_rows
-    d_middle = cotangent + normed_back(
-        d_ffn_in * (1.0 + scale_ffn), middle_unit, middle_inverse
-    )
-    d_attn_low = (d_middle * gate_attn).astype(jnp.bfloat16)
+    (context_tiles,), (grn_all,) = communicate([to_rows(context_here), exchanged([grn_low])], 2)
+
+    (
+        context_blocks,
+        transformer_layer_output,
+        ffn_low,
+        gelu_low,
+        d_up_low,
+        d_attn_low,
+        d_middle,
+        d_context_tiles,
+        d_mods_middle,
+    ) = middle_part(
+        table, context_tiles, out_full, up_full, down_full, hidden, mods, cotangent, d_ffn_low, utterances
+    )
 
     (d_context,), (ffn_all,), (context_all,) = communicate(
-        [
-            to_heads(attn_out_back(d_attn_low, out_full)),
-            gathered([ffn_low]),
-            exchanged([context_blocks]),
-        ],
-        6,
+        [to_heads(d_context_tiles), gathered([ffn_low]), exchanged([context_blocks])], 3
     )
     d_query, d_pair = attend_back(
         table, packed, d_context, logsum, query_cos, query_sin, utterances
     )
+    halves = (8, 2, QUARTER, 128)
     (d_tiles,), (d_attn_all,), (gelu_all, d_up_all) = communicate(
         [
-            sent_home(d_query, d_pair, key_cos, key_sin),
+            sent_home(d_query, d_pair, key_cos.reshape(halves), key_sin.reshape(halves)),
             gathered([d_attn_low]),
             exchanged([gelu_low, d_up_low]),
         ],
-        7,
+        4,
         WIDE,
     )
-    ffn_all, d_ffn_all, context_all, d_attn_all, gelu_all, d_up_all = (
-        rows_of(g) for g in (ffn_all, d_ffn_all, context_all, d_attn_all, gelu_all, d_up_all)
-    )
-    d_projected = unpack(d_tiles)
-    ((d_attn_in,),) = communicate([product_scattered(d_projected, qkv_flat, True)], 8, WIDE)
-    grad_mel = d_middle + normed_back(
-        d_attn_in * (1.0 + scale_attn), hidden_unit, hidden_inverse
-    )
-    d_mod_rows = jnp.concatenate(
+    ffn_all, d_ffn_all, context_all, d_attn_all, gelu_all, d_up_all, grn_all, text_all = (
+        rows_of(g)
+        for g in (ffn_all, d_ffn_all, context_all, d_attn_all, gelu_all, d_up_all, grn_all, text_all)
+    )
+
+    def part(left, right):
+        return inner_rows(left, right).astype(jnp.bfloat16)
+
+    (
+        (
+            _,
+            grad_mel,
+            d_joined_low,
+            _,
+            _,
+            grad_text,
+            d_mods_attn,
+            small,
+            own_sums,
+            d_qkv_all,
+            d_branch_all,
+            d_expanded_all,
+        ),
+        (up, down, out),
+    ) = communicate(
         [
-            d_attn_in,
-            d_attn_in * hidden_unit,
-            d_middle * attn_rows,
-            d_ffn_in,
-            d_ffn_in * middle_unit,
-            cotangent * ffn_rows,
+            text_backward(
+                [
+                    table,
+                    d_tiles,
+                    qkv_full,
+                    hidden,
+                    d_middle,
+                    mods,
+                    join_weight,
+                    shrink_all,
+                    expand_all,
+                    expanded,
+                    squares,
+                    scale,
+                    mask_rows,
+                    text_unit,
+                    text_inverse,
+                    norm_gain[None, :],
+                    conv_weight,
+                    extended,
+                ],
+                utterances,
+            ),
+            seq_scattered(
+                [
+                    blocks_of(part(ffn_all, d_up_all)),
+                    part(gelu_all, d_ffn_all),
+                    part(context_all, d_attn_all),
+                ]
+            ),
         ],
-        axis=1,
-    )
-    d_mod_part = exact_inner(row_onehot, d_mod_rows)
-
-    d_joined_low = grad_mel.astype(jnp.bfloat16)
-    d_text_out = against_rows(d_joined_low, join_weight)
-    ((d_branch_all,),) = communicate([gathered([(mask_rows * d_text_out).astype(jnp.bfloat16)])], 9)
-    d_branch_all = rows_of(d_branch_all)
-    d_grn = against_rows(d_branch_all, shrink_weight)
-    sums_here = jnp.concatenate(
-        [
-            exact_inner(frame_onehot, d_grn * grn_gamma * activated),
-            jnp.sum(d_grn * activated * ratio_rows, axis=0)[None, :],
-            jnp.sum(d_grn, axis=0)[None, :],
-            jnp.zeros((6, d_grn.shape[1]), jnp.float32),
-        ]
-    )
-    ((sums_all, inner_total),) = communicate([seq_summed(sums_here, product_rule, grn_norm)], 10)
-    d_ratio = sums_all[:utterances]
-    grad_gamma, grad_beta = sums_all[utterances], sums_all[utterances + 1]
-    d_mean = -inner_total[:, 0] / (denominator * denominator)
-    d_norm = d_ratio / denominator[:, None] + (d_mean / text_channels)[:, None]
-    d_activated = d_grn * (grn_gamma * ratio_rows + 1.0) + activated * exact_dot(
-        frame_onehot, d_norm / grn_norm
-    )
-    d_expanded_low = gelu_exact_back(d_activated)[0].astype(jnp.bfloat16)
-    ((d_text_norm,),) = communicate(
-        [product_scattered(d_expanded_low, expand_weight, True)], 11, WIDE
-    )
-    d_conv_out = normed_back(d_text_norm * norm_gain, text_unit, text_inverse)
-    grad_gain_part = jnp.sum(d_text_norm * text_unit, axis=0)
-    grad_bias_part = jnp.sum(d_text_norm, axis=0)
-    d_extended = frame_rim(d_conv_out, half_kernel)
-    grad_text = d_text_out
-    conv_grads = []
-    for tap in range(taps_count):
-        mirror = 2 * half_kernel - tap
-        grad_text = (
-            grad_text
-            + d_extended[mirror : mirror + rows_here]
-            * conv_weight[tap]
-            * same_taps[mirror][:, None]
-        )
-        conv_grads.append(
-            jnp.sum(
-                d_conv_out * extended[tap : tap + rows_here] * same_taps[tap][:, None], axis=0
-            )
-        )
-
-    def part(left, right):
-        return blocks_of(inner_rows(left, right).astype(jnp.bfloat16))
-
-    small = jnp.concatenate(
-        [
-            jnp.stack(conv_grads + [grad_gain_part, grad_bias_part]),
-            jnp.zeros((16 - taps_count - 2, text_in.shape[1]), jnp.float32),
-        ]
-    )
+        5,
+        56 << 20,
+    )
+
     small = jnp.pad(small.reshape(16, 8, 64).transpose(1, 0, 2), ((0, 0), (0, 0), (0, 64)))
-    mod_blocks = d_mod_part.reshape(utterances, 8, -1).transpose(1, 0, 2)
-    ((up, down, qkv, out, shrink, expand, join, small, mod),) = communicate(
+    d_mods = jnp.concatenate([d_mods_attn, d_mods_middle], axis=1)[:utterances]
+    ((qkv, shrink, expand, join, small, mod),) = communicate(
         [
             seq_scattered(
                 [
-            part(ffn_all, d_up_all),
-            part(d_ffn_all, gelu_all),
-            part(attn_all, d_projected),
-            part(d_attn_all, context_all),
-            part(d_branch_all, grn_low),
-            part(text_all, d_expanded_low),
-            part(d_joined_low, join_low),
-            small,
-            mod_blocks,
+                    blocks_of(part(attn_all, rows_of(d_qkv_all))),
+                    blocks_of(part(rows_of(d_branch_all), grn_all)),
+                    blocks_of(part(text_all, rows_of(d_expanded_all))),
+                    blocks_of(part(d_joined_low, join_low)),
+                    small,
+                    d_mods.reshape(utterances, 8, -1).transpose(1, 0, 2),
                 ]
             )
         ],
-        12,
+        6,
         WIDE,
     )
     ((join, small, mod),) = communicate(
         [
             head_blocks(
                 [
-            join.reshape(4, -1, join.shape[1]),
-            jnp.pad(small[:, :64].reshape(16, 4, 16).transpose(1, 0, 2), ((0, 0), (0, 0), (0, 112))),
-            mod.reshape(utterances, 4, -1).transpose(1, 0, 2),
+                    join.reshape(4, -1, join.shape[1]),
+                    jnp.pad(
+                        small[:, :64].reshape(16, 4, 16).transpose(1, 0, 2),
+                        ((0, 0), (0, 0), (0, 112)),
+                    ),
+                    mod.reshape(utterances, 4, -1).transpose(1, 0, 2),
                 ]
             )
         ],
-        13,
-    )
-    grad_modulation = exact_inner(cond_low.astype(jnp.float32), mod)
+        7,
+    )
     return (
         transformer_layer_output,
         grad_text,
@@ -1914,15 +2390,15 @@
         small[taps_count, :16],
         small[taps_count + 1, :16],
         expand,
-        grad_gamma,
-        grad_beta,
+        own_sums[8],
+        own_sums[9],
         shrink.T,
         join.T,
-        grad_modulation,
-        qkv.reshape(qkv.shape[0], 3, head_cols),
-        out.T,
+        exact_inner(mod, cond_low.astype(jnp.float32)).T,
+        qkv.reshape(qkv.shape[0], 3, -1),
+        out,
         up,
-        down.T,
+        down,
     )
 
 

time: 672 us -> 573 us (0.85)
  matrix products: 63.3 us -> 17 us
  other arithmetic: 37.6 us -> 13.6 us
  local copies, waits for them, and re-layouts: 52 us -> 30.2 us
  starting transfers between devices: 8.41 us -> 0.16 us
    dot_general x13 -> x0, matrix products: 25.2 us -> none  [the longest x10 13.6 us: against_rows(): lax.dot_general(left, right, (((1,), (1,)), ((), ())), preferred_element_...]
    dot_general x11 -> x1, matrix products: 17 us -> 1.26 us  [narrow_dot(): return jnp.dot(left, right, preferred_element_type=jnp.float32)]
    unnamed x211 -> x109, local copies, waits for them, and re-layouts: 35.7 us -> 23.1 us
    pallas_call x3 -> x1, Pallas kernels: 10.2 us -> 20.1 us  [middle_part(): pl.pallas_call(partial(middle_kernel, utterances), out_shape=[low(4, ROWS...]
    ppermute x4 -> x0, starting transfers between devices: 8.3 us -> none  [the longest x2 5.61 us: with_halo(): lax.ppermute(lax.slice_in_dim(block, block.shape[dim] - width, None, axis...]
    pallas_call x1, Pallas kernels: 56.5 us -> 48.6 us  [attend_back(): pl.pallas_call(partial(attend_back_kernel, utterances), out_shape=[jax.Sh...]
    dot_general x4 -> x1, matrix products: 9.48 us -> 2.09 us  [exact_inner(): lax.dot_general(left, right, (((0,), (0,)), ((), ())), precision=lax.Prec...]
    unnamed x3 -> x0, other arithmetic: 6.99 us -> none
  transfers between devices with their start and end apart: 7 -> 4, of which waited for: 0 -> 0; matrix products, arithmetic and copies ran while one was open for 10% -> 2% of each run, Pallas kernels for 32% -> 51%
where the time goes in v3:
time: 573 us; the launch traced here: 564 us
  Pallas kernels  487 us (85%)
  local copies, waits for them, and re-layouts  30.2 us (5%)
  matrix products  17 us (3%)
  between operations  14.6 us (3%)
  other arithmetic  13.6 us (2%)
    pallas_call x8, Pallas kernels, communicate(): pl.pallas_call(kernel, out_shape=[o for t in tasks for o in t.outs], in_s...  377 us
    pallas_call x1, Pallas kernels, attend_back(): pl.pallas_call(partial(attend_back_kernel, utterances), out_shape=[jax.Sh...  48.6 us
    pallas_call x1, Pallas kernels, attend(): pl.pallas_call(partial(attend_kernel, utterances), out_shape=[jax.ShapeDt...  35.1 us
    unnamed x109, local copies, waits for them, and re-layouts  23.1 us
    pallas_call x1, Pallas kernels, middle_part(): pl.pallas_call(partial(middle_kernel, utterances), out_shape=[low(4, ROWS...  20.1 us
    dot_general x7, matrix products, inner_rows(): lax.dot_general(left, right, (((0,), (0,)), ((), ())), preferred_element_...  13.6 us
  transfers between devices with their start and end apart: 4, of which 0 were waited for; matrix products, arithmetic and copies ran while one was open for 2% of the time, Pallas kernels for 51%

profile of v3, /device:TPU:0, one launch (start us, length us, event | category | flops | bytes accessed | tf_op | source)
XLA Modules:
  0.0 564.4 jit_solution(5310313799922085208)
XLA Ops:
  7.3 1.0 reduce-window.8
  8.3 1.2 bitcast_subtract_fusion
  10.0 0.6 select_reduce_fusion.1
  11.6 1.2 convert_element_type.65
  12.9 0.8 copy.70.refs_4_.refs_12_
  13.7 0.8 select_reduce_fusion.2
  14.6 0.7 and_select_fusion
  15.2 1.2 fusion.11
  16.4 1.3 fusion.9
  17.9 0.8 concatenate.19.refs_0_.table
  18.7 1.0 copy-done.15
  19.8 0.9 copy-done.17
  20.7 0.7 copy-done.24
  21.4 0.7 copy-done.25
  22.1 62.9 %communicate_0.1 = (f32[272,512]{1,0:T(8,128)S(1)}, f32[256,512]{1,0:T(8,128)S(1)}, f32[256,128]{1,0:T(8,128)S(1)}, bf16[256,512]{1,0:T(8,128)(2,1)}, bf16[4,512...) custom-call(s32[137]{0:T(256)S(1)} %concatenate.19.refs_0_.table, ...), custom_call_target="tpu_custom_call" | custom-call | tf_op jit(solution)/shard_map/communicate_0/pallas_call | solution.py:543
  85.0 0.7 copy-done.4
  85.7 0.8 copy-done.10
  86.5 0.8 copy-done.11
  87.3 0.8 copy-done.14
  88.1 0.6 copy-done.19
  88.8 0.6 copy-done.20
  89.4 0.6 copy-done.21
  90.1 0.7 all-gather.11.cloned.1.call-update
  90.9 0.7 all-gather.13.cloned.1.call-update
  91.6 0.5 all-gather.15.cloned.1.call-update
  92.6 3.2 multiply_sine_fusion
  95.8 6.1 %project.1.refs_0_ = bf16[4,1536,128]{2,1,0:T(8,128)(2,1)} custom-call(bf16[1024,1024]{1,0:T(8,128)(2,1)} %bitcast.102, bf16[3,1024,256]{2,1,0:T(8,128)(2,1)} %bitcast.98, f32[1024,128]{1,0:T(8,128)} %get-tuple-element.235.c_ref, f32[1024,128]{1,0:T(8,128)} %get-tuple-element.234.s_ref), custom_call_target="tpu_custom_call" | custom-call | tf_op jit(solution)/shard_map/project/pallas_call | solution.py:1456
  102.0 0.6 convert_multiply_fusion.refs_1_
  102.6 2.0 broadcast_multiply_fusion.refs_2_
  104.6 45.4 %communicate_1.1 = (bf16[8,1536,128]{2,1,0:T(8,128)(2,1)}, f32[8,256,128]{2,1,0:T(8,128)S(1)}, f32[8,256,128]{2,1,0:T(8,128)S(1)}, f32[8,512,128]{2,1,0:T(8,128)...) custom-call(bf16[4,1536,128]{2,1,0:T(8,128)(2,1)S(1)} %copy-done.2, ...), custom_call_target="tpu_custom_call" | custom-call | tf_op jit(solution)/shard_map/communicate_1/pallas_call | solution.py:543
  150.0 1.0 copy-done.6
  151.0 1.0 copy-done.7
  152.0 35.1 %attend.1 = (bf16[8,256,128]{2,1,0:T(8,128)(2,1)}, f32[8,2,8,256]{3,2,1,0:T(8,128)}) custom-call(s32[137]{0:T(256)} %copy-done.23, bf16[8,1536,128]{2,1,0:T(8,128)(2,1)} %get-tuple-element.88.x_ref), custom_call_target="tpu_custom_call" | custom-call | tf_op jit(solution)/shard_map/attend/pallas_call | solution.py:1321
  187.0 36.3 %communicate_2.1 = (bf16[16,128,128]{2,1,0:T(8,128)(2,1)}, bf16[4,256,256]{2,1,0:T(8,128)(2,1)}) custom-call(bf16[8,256,128]{2,1,0:T(8,128)(2,1)} %get-tuple-element.89.refs_0_, bf16[4,256,256]{2,1,0:T(8,128)(2,1)} %copy-done.14), custom_call_target="tpu_custom_call" | custom-call | tf_op jit(solution)/shard_map/communicate_2/pallas_call | solution.py:543
  223.4 20.1 %middle_part.1 = (bf16[4,256,256]{2,1,0:T(8,128)(2,1)}, f32[256,1024]{1,0:T(8,128)}, bf16[256,1024]{1,0:T(8,128)(2,1)}, bf16[4,256,512]{2,1,0:T(8,128)(2,1)}, bf...) custom-call(s32[137]{0:T(256)} %copy-done.23, ...), custom_call_target="tpu_custom_call" | custom-call | tf_op jit(solution)/shard_map/middle_part/pallas_call | solution.py:1858
  243.6 27.5 %communicate_3.1 = (bf16[8,256,128]{2,1,0:T(8,128)(2,1)}, bf16[4,256,1024]{2,1,0:T(8,128)(2,1)}, bf16[4,256,256]{2,1,0:T(8,128)(2,1)}) custom-call(bf16[16,128,128]{2,1,0:T(8,128)(2,1)} %get-tuple-element.98.refs_0_, bf16[256,1024]{1,0:T(8,128)(2,1)} %get-tuple-element.99.refs_1_, bf16[4,256,256]{2,1,0:T(8,128)(2,1)} %get-tuple-element.100.refs_2_), custom_call_target="tpu_custom_call" | custom-call | tf_op jit(solution)/shard_map/communicate_3/pallas_call | solution.py:543
  271.1 48.6 %attend_back.1 = (bf16[8,256,128]{2,1,0:T(8,128)(2,1)}, f32[9216,128]{1,0:T(8,128)}) custom-call(s32[137]{0:T(256)} %copy-done.23, bf16[8,1536,128]{2,1,0:T(8,128)(2,1)} %get-tuple-element.88.x_ref, bf16[8,256,128]{2,1,0:T(8,128)(2,1)} %get-tuple-element.101.g_ref, f32[8,2,8,256]{3,2,1,0:T(8,128)} %get-tuple-element.102.l_ref, f32[8,256,128]{2,1,0:T(8,128)} %copy-done.6, ...), custom_call_target="tpu_custom_call" | custom-call | tf_op jit(solution)/shard_map/attend_back/pallas_call | solution.py:1390
  319.7 1.0 copy-done.13
  320.8 67.0 %communicate_4.1 = (bf16[16,384,128]{2,1,0:T(8,128)(2,1)}, bf16[4,256,1024]{2,1,0:T(8,128)(2,1)}, bf16[4,256,512]{2,1,0:T(8,128)(2,1)S(1)}, bf16[4,256,512]{2,1,0:T(8,128)(2,1)S(1)}) custom-call(bf16[8,256,128]{2,1,0:T(8,128)(2,1)S(1)} %copy-done.13, f32[9216,128]{1,0:T(8,128)} %get-tuple-element.106.refs_1_, f32[8,2,256,128]{3,2,1,0:T(8,128)} %bitcast.104, ...), custom_call_target="tpu_custom_call" | custom-call | tf_op jit(solution)/shard_map/communicate_4/pallas_call | solution.py:543
  387.8 3.3 fusion.refs_20_
  391.0 2.3 bitcast_convert_fusion.1.refs_19_
  393.3 2.3 bitcast_convert_fusion.2
  395.6 81.4 %communicate_5.1 = (bf16[4,256,768]{2,1,0:T(8,128)(2,1)}, f32[256,1024]{1,0:T(8,128)}, bf16[256,1024]{1,0:T(8,128)(2,1)}, bf16[256,512]{1,0:T(8,128)(2,1)}, bf16...) custom-call(s32[137]{0:T(256)} %copy-done.23, ...), custom_call_target="tpu_custom_call" | custom-call | tf_op jit(solution)/shard_map/communicate_5/pallas_call | solution.py:543
  477.1 3.3 bitcast_convert_fusion
  481.1 0.6 copy-done.47
  481.7 1.5 fusion.2
  483.8 48.1 %communicate_6.1 = (f32[128,768]{1,0:T(8,128)S(1)}, f32[64,256]{1,0:T(8,128)S(1)}, f32[64,256]{1,0:T(8,128)S(1)}, f32[128,512]{1,0:T(8,128)S(1)}, f32[16,128]{1,0:T(8,128)S(1)}, /*index=5*/f32[8,768]{1,0:T(8,128)S(1)}) custom-call(bf16[8,128,768]{2,1,0:T(8,128)(2,1)S(1)} %bitcast.87, bf16[8,64,256]{2,1,0:T(8,128)(2,1)S(1)} %bitcast.91, ...), custom_call_target="tpu_custom_call" | custom-call | tf_op jit(solution)/shard_map/communicate_6/pallas_call | solution.py:543
  531.9 0.7 copy-done.18
  532.7 0.6 pad.14.refs_1_
  533.4 0.6 copy.95
  534.0 8.3 %communicate_7.1 = (f32[32,512]{1,0:T(8,128)}, f32[16,128]{1,0:T(8,128)}, f32[8,192]{1,0:T(8,128)}) custom-call(f32[4,32,512]{2,1,0:T(8,128)} %bitcast.89, f32[4,16,128]{2,1,0:T(8,128)} %pad.14.refs_1_, f32[4,8,192]{2,1,0:T(8,128)} %bitcast.109), custom_call_target="tpu_custom_call" | custom-call | tf_op jit(solution)/shard_map/communicate_7/pallas_call | solution.py:543
  542.4 1.3 slice.31
  543.6 1.2 slice_bitcast_fusion.2
  544.8 2.1 fusion.8
  547.1 0.9 copy.83
  548.0 1.3 fusion.13
  549.4 2.0 copy.106
  551.4 2.3 copy.107
  553.7 0.6 copy.108
  554.3 0.6 copy.109
  554.9 0.6 copy.110
  555.6 0.7 copy.111
  556.2 0.7 copy.112
  556.9 0.7 copy.113
  (123 shorter events, 4.1 us)
Async XLA Ops:
  7.2 9.3 %copy-start = (bf16[1024,1536]{1,0:T(8,128)(2,1)S(1)}, bf16[1024,1536]{1,0:T(8,128)(2,1)}, u32[]{:S(2)}) copy-start(bf16[1024,1536]{1,0:T(8,128)(2,1)} %param.32) | copy-start | bytes 9437188
  7.2 11.5 %copy-start.22 = (f32[7,512]{1,0:T(8,128)S(1)}, f32[7,512]{1,0:T(8,128)}, u32[]{:S(2)}) copy-start(f32[7,512]{1,0:T(8,128)} %refs_16_.1) | copy-start | bytes 43012
  7.2 11.5 %copy-start.16 = (bf16[512,256]{1,0:T(8,128)(2,1)S(1)}, bf16[512,256]{1,0:T(8,128)(2,1)}, u32[]{:S(2)}) copy-start(bf16[512,256]{1,0:T(8,128)(2,1)} %refs_8_.1) | copy-start | bytes 786436
  7.2 216.2 %all-gather.9.cloned.1.call-start = ((), (), s32[]{:S(2)}) async-start(), calls=%async_computation | async-start | bytes 2621440 | tf_op jit(solution)/shard_map/all_gather | solution.py:2246
  8.3 4.6 copy-start.38
  9.5 0.5 copy-start.45
  10.6 0.5 copy-start.41
  13.7 71.3 %copy-start.5 = (f32[256,1]{1,0:T(8,128)}, f32[256,1]{1,0:T(8,128)S(1)}, u32[]{:S(2)}) copy-start(f32[256,1]{1,0:T(8,128)S(1)} %copy.70.refs_4_.refs_12_) | copy-start | bytes 3076
  13.7 4.0 copy-start.42
  13.7 4.0 copy-start.43
  16.4 1.5 copy-start.40
  18.7 66.3 %copy-start.23 = (s32[137]{0:T(256)}, s32[137]{0:T(256)S(1)}, u32[]{:S(2)}) copy-start(s32[137]{0:T(256)S(1)} %concatenate.19.refs_0_.table) | copy-start | bytes 1648
  18.7 1.0 copy-start.15
  19.8 0.9 copy-start.17
  20.7 0.7 copy-start.24
  21.4 0.7 copy-start.25
  85.0 0.7 copy-start.4
  85.7 0.8 copy-start.10
  86.5 0.8 copy-start.11
  87.3 0.8 copy-start.14
  88.1 0.6 copy-start.19
  88.8 0.6 copy-start.20
  89.4 0.6 copy-start.21
  90.0 14.5 %copy-start.3 = (bf16[256,1024]{1,0:T(8,128)(2,1)}, bf16[256,1024]{1,0:T(8,128)(2,1)S(1)}, u32[]{:S(2)}) copy-start(bf16[256,1024]{1,0:T(8,128)(2,1)S(1)} %get-tuple-element.87.refs_3_.d_ffn_ref) | copy-start | bytes 1572868
  90.0 2.1 copy-start.39
  90.0 2.3 copy-start.44
  90.1 133.4 %all-gather.11.cloned.1.call-start = ((), (), s32[]{:S(2)}) async-start(), calls=%async_computation.1 | async-start | bytes 5242880 | tf_op jit(solution)/shard_map/all_gather | solution.py:2246
  90.8 132.6 %all-gather.13.cloned.1.call-start = ((), (), s32[]{:S(2)}) async-start(), calls=%async_computation.2 | async-start | bytes 5242880 | tf_op jit(solution)/shard_map/all_gather | solution.py:2246
  91.5 304.0 %all-gather.15.cloned.1.call-start = ((), (), s32[]{:S(2)}) async-start(), calls=%async_computation.3 | async-start | bytes 7864320 | tf_op jit(solution)/shard_map/all_gather | solution.py:2246
  102.0 2.6 copy-start.2
  150.0 1.0 copy-start.6
  151.0 1.0 copy-start.7
  271.1 48.7 %copy-start.8 = (bf16[4,256,512]{2,1,0:T(8,128)(2,1)S(1)}, bf16[4,256,512]{2,1,0:T(8,128)(2,1)}, u32[]{:S(2)}) copy-start(bf16[4,256,512]{2,1,0:T(8,128)(2,1)} %get-tuple-element.110.refs_5_) | copy-start | bytes 3145732
  271.1 48.7 %copy-start.9 = (bf16[4,256,512]{2,1,0:T(8,128)(2,1)S(1)}, bf16[4,256,512]{2,1,0:T(8,128)(2,1)}, u32[]{:S(2)}) copy-start(bf16[4,256,512]{2,1,0:T(8,128)(2,1)} %get-tuple-element.111.refs_6_) | copy-start | bytes 3145732
  271.1 48.7 %copy-start.12 = (bf16[256,1024]{1,0:T(8,128)(2,1)S(1)}, bf16[256,1024]{1,0:T(8,128)(2,1)}, u32[]{:S(2)}) copy-start(bf16[256,1024]{1,0:T(8,128)(2,1)} %get-tuple-element.109.refs_4_) | copy-start | bytes 1572868
  319.7 1.0 copy-start.13
  320.8 67.0 %copy-start.29 = (bf16[4,256,256]{2,1,0:T(8,128)(2,1)S(1)}, bf16[4,256,256]{2,1,0:T(8,128)(2,1)}, u32[]{:S(2)}) copy-start(bf16[4,256,256]{2,1,0:T(8,128)(2,1)} %get-tuple-element.127) | copy-start | bytes 1572868
  387.7 3.3 copy-start.27
  391.0 2.3 copy-start.46
  395.6 81.4 %copy-start.26 = (bf16[4,256,1024]{2,1,0:T(8,128)(2,1)S(1)}, bf16[4,256,1024]{2,1,0:T(8,128)(2,1)}, u32[]{:S(2)}) copy-start(bf16[4,256,1024]{2,1,0:T(8,128)(2,1)} %get-tuple-element.86) | copy-start | bytes 6291460
  477.0 3.4 copy-start.37
  477.0 3.5 copy-start.32
  477.0 3.5 copy-start.35
  477.1 3.5 copy-start.28
  480.5 1.2 copy-start.47
  480.6 2.7 copy-start.48
  480.6 2.7 copy-start.49
  483.8 61.1 %copy-start.33 = (f32[8,1024]{1,0:T(8,128)S(1)}, f32[8,1024]{1,0:T(8,128)}, u32[]{:S(2)}) copy-start(f32[8,1024]{1,0:T(8,128)} %param.21) | copy-start | bytes 98308
  531.9 0.7 copy-start.18
  547.1 7.9 %copy-start.36 = (f32[32,512]{1,0:T(8,128)S(1)}, f32[32,512]{1,0:T(8,128)}, u32[]{:S(2)}) copy-start(f32[32,512]{1,0:T(8,128)} %get-tuple-element.148) | copy-start | bytes 196612
  547.1 8.5 %copy-start.34 = (f32[256,128]{1,0:T(8,128)S(1)}, f32[256,128]{1,0:T(8,128)}, u32[]{:S(2)}) copy-start(f32[256,128]{1,0:T(8,128)} %get-tuple-element.270) | copy-start | bytes 393220
  548.0 8.2 %copy-start.31 = (f32[128,512]{1,0:T(8,128)S(1)}, f32[128,512]{1,0:T(8,128)}, u32[]{:S(2)}) copy-start(f32[128,512]{1,0:T(8,128)} %get-tuple-element.271) | copy-start | bytes 786436
  549.4 7.6 %copy-start.30 = (f32[512,128]{1,0:T(8,128)S(1)}, f32[512,128]{1,0:T(8,128)}, u32[]{:S(2)}) copy-start(f32[512,128]{1,0:T(8,128)} %get-tuple-element.272) | copy-start | bytes 786436
  549.4 8.3 %copy-start.1 = (bf16[1024,1536]{1,0:T(8,128)(2,1)S(1)}, bf16[1024,1536]{1,0:T(8,128)(2,1)}, u32[]{:S(2)}) copy-start(bf16[1024,1536]{1,0:T(8,128)(2,1)} %param.32) | copy-start | bytes 9437188
Sparse Core Ops, SparseCore 0:
  90.2 21.9 all-gather.8
  113.7 37.0 all-gather.10
  152.4 34.7 all-gather.12
  188.6 57.6 all-gather.14

commit v4 on v3

--- a/solution.py
+++ b/solution.py
@@ -472,7 +472,7 @@
     )
 
 MESH = pl.DeviceIdType.MESH
-HBM = pl.BlockSpec(memory_space=pl.ANY)
+HBM = pl.BlockSpec(memory_space=pltpu.HBM)
 VMEM = pl.BlockSpec(memory_space=pltpu.VMEM)
 DMA = pltpu.SemaphoreType.DMA
 
@@ -517,10 +517,21 @@
         self.out_specs = out_spec if isinstance(out_spec, list) else [out_spec] * len(self.outs)
 
 
-def communicate(tasks, number, vmem=None):
+def communicate(tasks, number):
     sizes = [(len(t.ins), len(t.outs), len(t.scratch)) for t in tasks]
+    specs = [s for t in tasks for s in t.in_specs]
+    arrays = [a for t in tasks for a in t.ins]
+    moved = [k for k, s in enumerate(specs) if s is VMEM]
 
     def kernel(*refs):
+        fetched, sems = refs[-1 - len(moved) : -1], refs[-1]
+        given = list(refs[: len(arrays)])
+        copies = []
+        for k, (place, room_for) in enumerate(zip(moved, fetched)):
+            copies.append(pltpu.make_async_copy(given[place], room_for, sems.at[k]))
+            copies[-1].start()
+            given[place] = room_for
+        refs = given + list(refs[len(arrays) :])
         parts = []
         at = 0
         for kind in range(3):
@@ -535,6 +546,8 @@
         for one in running:
             expected = expected + next(one)
         pl.semaphore_wait(pltpu.get_barrier_semaphore(), expected)
+        for copy in copies:
+            copy.wait()
         while running:
             for one in list(running):
                 if next(one, "end") == "end":
@@ -543,14 +556,16 @@
     results = pl.pallas_call(
         kernel,
         out_shape=[o for t in tasks for o in t.outs],
-        in_specs=[s for t in tasks for s in t.in_specs],
+        in_specs=[HBM if s is VMEM else s for s in specs],
         out_specs=[s for t in tasks for s in t.out_specs],
-        scratch_shapes=[s for t in tasks for s in t.scratch],
+        scratch_shapes=[s for t in tasks for s in t.scratch]
+        + [pltpu.VMEM(arrays[k].shape, arrays[k].dtype) for k in moved]
+        + [DMA((max(1, len(moved)),))],
         compiler_params=pltpu.CompilerParams(
-            collective_id=number, has_side_effects=True, vmem_limit_bytes=vmem
+            collective_id=number, has_side_effects=True, vmem_limit_bytes=60 << 20
         ),
         name=f"communicate_{number}",
-    )(*[a for t in tasks for a in t.ins])
+    )(*arrays)
     split = []
     for _, size, _ in sizes:
         split.append(results[:size])
@@ -669,27 +684,33 @@
 
 
 def spread_body(ins, outs, scratch):
-    (x_ref,), (o_ref,) = ins, outs
-    local, out_send, in_recv, f_send, f_recv = scratch
+    (rows_ref, w_ref, c_ref, s_ref), (o_ref,) = ins, outs
+    x_ref, local, out_send, in_recv, f_send, f_recv = scratch
     seq, head, mate, _, _ = head_places()
     core = lax.rem(head, 2)
     landing = core == seq // 4
     yield greet([(lax.rem(seq + o, 8), head) for o in range(1, 8)] + [(seq, mate)])
-    for i in range(4):
-        j = lax.rem(seq + i, 4)
-        target = 4 * core + j
-
-        @pl.when(target != seq)
-        def _():
-            send(
-                x_ref.at[j], o_ref.at[seq], out_send.at[j], in_recv.at[seq], target, head
-            ).start()
-
-        @pl.when(target == seq)
-        def _():
-            pltpu.make_async_copy(x_ref.at[j], o_ref.at[seq], local).start()
-
-    yield
+
+    def pieces(ref, quarter):
+        first = (quarter % 2) * QUARTER + (quarter // 2) * HALF
+        return ref.at[pl.ds(first, HALF)], ref.at[pl.ds(512 + quarter * QUARTER, QUARTER)]
+
+    for quarter in range(4):
+        project_quarter(quarter, rows_ref, w_ref, c_ref, s_ref, x_ref)
+        for i in range(4):
+            j = lax.rem(seq + i, 4)
+            target = 4 * core + j
+            for source, goal in zip(pieces(x_ref.at[j], quarter), pieces(o_ref.at[seq], quarter)):
+
+                @pl.when(target != seq)
+                def _():
+                    send(source, goal, out_send.at[j], in_recv.at[seq], target, head).start()
+
+                @pl.when(target == seq)
+                def _():
+                    pltpu.make_async_copy(source, goal, local).start()
+
+        yield
 
     @pl.when(landing)
     def _():
@@ -732,13 +753,15 @@
             ).wait_send()
 
 
-def spread_out(x):
-    _, rows, cols = x.shape
+def spread_out(rows, weights, cosine, sine):
+    shape = jax.ShapeDtypeStruct((8, 1536, 128), jnp.bfloat16)
     return Task(
         spread_body,
-        [x],
-        [like(x, 8, rows, cols)],
-        [DMA, DMA((4,)), DMA((8,)), DMA((8,)), DMA((8,))],
+        [rows, weights, cosine, sine],
+        [shape],
+        [pltpu.VMEM((4, 1536, 128), jnp.bfloat16), DMA, DMA((4,)), DMA((8,)), DMA((8,)), DMA((8,))],
+        VMEM,
+        HBM,
     )
 
 
@@ -962,7 +985,8 @@
             )
             far.start()
             last.append((i, o, far))
-        yield
+        if o == 0:
+            yield
     for i, o, far in last:
         far.wait_recv()
         outs[i][...] += final[i][o - 1].astype(jnp.float32)
@@ -1102,66 +1126,132 @@
         below.wait_send()
 
 
-def head_blocks_body(ins, outs, scratch):
+def all_scatter_body(tail, ins, outs, scratch):
     count = len(ins)
-    inbox = scratch[:count]
-    h_send, h_recv = scratch[count:]
+    split = count - tail
+    fixed = 4 * count + 5
+    sums = scratch[fixed : fixed + tail]
+    inbox = scratch[fixed + tail : fixed + 2 * tail]
+    h_send, h_recv = scratch[fixed + 2 * tail :]
     seq = lax.axis_index("seq")
     head = lax.axis_index("head")
-    others = [lax.rem(head + o, 4) for o in range(1, 4)]
-    yield greet([(seq, other) for other in others])
+    others = [lax.rem(head + o, 4) for o in (2, 1, 3)]
+    inner = seq_scatter_body(ins, list(outs[:split]) + list(sums), scratch[:fixed])
+    yield next(inner) + greet([(seq, other) for other in others])
+    for _ in inner:
+        yield
     hops = []
-    for i in range(count):
+
+    def rows(i, h):
+        count_of = sums[i].shape[0] // 4
+        return pl.ds(pl.multiple_of(h * count_of, 8), count_of)
+
+    for i in range(tail):
         for o, other in enumerate(others):
             hop = send(
-                ins[i].at[other], inbox[i].at[head], h_send.at[i, o], h_recv.at[i, head], seq, other
+                sums[i].at[rows(i, other)],
+                inbox[i].at[head],
+                h_send.at[i, o],
+                h_recv.at[i, head],
+                seq,
+                other,
             )
             hop.start()
             hops.append(hop)
-        inbox[i][head] = ins[i][head]
-    for i in range(count):
+        inbox[i][head] = sums[i][rows(i, head), :]
+    for i in range(tail):
         for o, other in enumerate(others):
             send(
-                ins[i].at[other], inbox[i].at[other], h_send.at[i, o], h_recv.at[i, other], seq, other
+                sums[i].at[rows(i, other)],
+                inbox[i].at[other],
+                h_send.at[i, o],
+                h_recv.at[i, other],
+                seq,
+                other,
             ).wait_recv()
-        outs[i][...] = inbox[i][0] + inbox[i][1] + inbox[i][2] + inbox[i][3]
+        outs[split + i][...] = inbox[i][0] + inbox[i][1] + inbox[i][2] + inbox[i][3]
     for hop in hops:
         hop.wait_send()
 
 
-def head_blocks(arrays):
-    count = len(arrays)
+def all_scattered(arrays, tail):
+    inner = seq_scattered(arrays)
+    last = inner.outs[len(arrays) - tail :]
+    short = [(o.shape[0] // 4,) + o.shape[1:] for o in last]
     return Task(
-        head_blocks_body,
+        partial(all_scatter_body, tail),
         arrays,
-        [like(a, *a.shape[1:]) for a in arrays],
-        [pltpu.VMEM(a.shape, a.dtype) for a in arrays] + [DMA((count, 3)), DMA((count, 4))],
+        inner.outs[: len(arrays) - tail] + [jax.ShapeDtypeStruct(s, jnp.float32) for s in short],
+        inner.scratch
+        + [pltpu.VMEM(o.shape, jnp.float32) for o in last]
+        + [pltpu.VMEM((4,) + s, jnp.float32) for s in short]
+        + [DMA((tail, 3)), DMA((tail, 4))],
+        HBM,
         VMEM,
-        VMEM,
-    )
-
-
-def turns_body(ins, outs, scratch):
+    )
+
+
+def places_of(rows, bounds):
+    start, _ = limits(rows, bounds)
+    return (rows - start).astype(jnp.float32)
+
+
+def column(first, count):
+    return first + lax.broadcasted_iota(jnp.int32, (count, 1), 0)
+
+
+def own_turns_body(ins, outs, scratch):
+    (lengths, rates_ref), (cos_ref, sin_ref) = ins, outs
     yield 0
     yield
-    count = len(ins)
-    for i in range(count):
-        for s in range(8):
-            angles = ins[i][s]
-            outs[2 * i][s] = jnp.cos(angles)
-            outs[2 * i + 1][s] = jnp.sin(angles)
+    bounds = bounds_of(lengths)
+    seq = lax.axis_index("seq")
+
+    def one(i, carry):
+        at = pl.ds(pl.multiple_of(i * QUARTER, QUARTER), QUARTER)
+        angles = places_of(column(seq * 1024 + i * QUARTER, QUARTER), bounds) * rates_ref[0:1, :]
+        cos_ref[at, :] = jnp.cos(angles)
+        sin_ref[at, :] = jnp.sin(angles)
+        return carry
+
+    lax.fori_loop(0, 4, one, 0)
+
+
+def own_turns(lengths, rates):
+    shape = jax.ShapeDtypeStruct((1024, 128), jnp.float32)
+    return Task(own_turns_body, [lengths, rates], [shape, shape], [], [SMEM, VMEM], VMEM)
+
+
+def turns_body(ins, outs, scratch):
+    (lengths, rates_ref), (q_cos, q_sin, k_cos, k_sin) = ins, outs
+    yield 0
+    yield
+    bounds = bounds_of(lengths)
+    core = lax.rem(lax.axis_index("head"), 2)
+
+    def one(step, carry):
+        source, sub = step // 2, lax.rem(step, 2)
+        first = source * 1024 + (core + 2 * sub) * QUARTER
+        upper = places_of(column(first, HALF), bounds)
+        lower = places_of(column(first + HALF, HALF), bounds)
+        angles = jnp.where(lane_of((HALF, 128)) < 64, upper, lower) * rates_ref[0:1, :]
+        at = pl.ds(pl.multiple_of(sub * HALF, HALF), HALF)
+        q_cos[source, at, :] = jnp.cos(angles)
+        q_sin[source, at, :] = jnp.sin(angles)
+        angles = places_of(column(first, QUARTER), bounds) * rates_ref[1:2, :]
+        k_cos[source, sub] = jnp.cos(angles)
+        k_sin[source, sub] = jnp.sin(angles)
+        return carry
+
+    for part in range(4):
+        lax.fori_loop(4 * part, 4 * part + 4, one, 0)
         yield
 
 
-def turns(angles):
-    return Task(
-        turns_body,
-        angles,
-        [like(a) for a in angles for _ in range(2)],
-        [],
-        VMEM,
-        VMEM,
-    )
+def turns(lengths, rates):
+    query = jax.ShapeDtypeStruct((8, QUARTER, 128), jnp.float32)
+    key = jax.ShapeDtypeStruct((8, 2, QUARTER, 128), jnp.float32)
+    return Task(turns_body, [lengths, rates], [query, query, key, key], [], [SMEM, VMEM], VMEM)
 
 
 QUARTER = 256
@@ -1201,13 +1291,22 @@
     return jnp.where(left, rows[:HALF], swap_halves(rows[HALF:]))
 
 
-def limits(rows, table, count):
+def bounds_of(lengths):
+    bounds = []
+    total = 0
+    for u in range(lengths.shape[0]):
+        total = total + lengths[u]
+        bounds.append(total)
+    return bounds
+
+
+def limits(rows, bounds):
     low = jnp.zeros(rows.shape, jnp.int32)
     high = jnp.full(rows.shape, 1 << 24, jnp.int32)
-    for u in range(count):
-        past = rows >= table[u]
-        low = jnp.where(past, table[u], low)
-        high = jnp.where(past, high, jnp.minimum(high, table[u]))
+    for bound in bounds:
+        past = rows >= bound
+        low = jnp.where(past, bound, low)
+        high = jnp.where(past, high, jnp.minimum(high, bound))
     return low, high
 
 
@@ -1234,14 +1333,23 @@
         copy.wait()
 
 
-def quarter_of(step, table, utterances):
+def quarter_of(step, bounds, core):
     source, sub = step // 2, lax.rem(step, 2)
-    quarter = source * 4 + table[utterances] + 2 * sub
-    base = utterances + 1
-    first = pl.multiple_of(table[base + quarter] * 128, 128)
-    ends = [table[base + 32 * k + quarter] for k in (1, 2, 3)]
-    rows = quarter * QUARTER + lax.broadcasted_iota(jnp.int32, (1, QUARTER), 1)
-    return source, sub, first, ends, limits(rows, table, utterances)
+    top = (source * 4 + core + 2 * sub) * QUARTER
+    low = base_end = high = jnp.int32(0)
+    for bound in reversed(bounds):
+        base_end = jnp.where(bound > top, bound, base_end)
+        high = jnp.where(bound > top + QUARTER - 1, bound, high)
+    for bound in bounds:
+        low = jnp.where(bound <= top, bound, low)
+    first = low // 128 * 128
+    count = (high - first + SPAN - 1) // SPAN
+    in_low = (low - first + SPAN - 1) // SPAN
+    in_high = (high - first) // SPAN
+    plain = jnp.logical_and(base_end == high, in_low < in_high)
+    ends = (count, jnp.where(plain, in_low, count), jnp.where(plain, in_high, count))
+    rows = top + lax.broadcasted_iota(jnp.int32, (1, QUARTER), 1)
+    return source, sub, pl.multiple_of(first, 128), ends, limits(rows, bounds)
 
 
 def in_three(ends, body, carry):
@@ -1262,11 +1370,12 @@
     return carry
 
 
-def attend_kernel(utterances, table, x_ref, o_ref, l_ref, held, q_ref, pairs, turned, sems):
-    fetch(x_ref, table[utterances], q_ref, pairs, turned, sems)
+def attend_kernel(lengths, x_ref, o_ref, l_ref, held, q_ref, pairs, turned, sems):
+    bounds, core = bounds_of(lengths), lax.rem(lax.axis_index("head"), 2)
+    fetch(x_ref, core, q_ref, pairs, turned, sems)
 
     def of_quarter(step, carry):
-        source, sub, first, ends, limit = quarter_of(step, table, utterances)
+        source, sub, first, ends, limit = quarter_of(step, bounds, core)
         at = pl.ds(pl.multiple_of(sub * HALF, HALF), HALF)
         query = opened(q_ref[source, at, :].astype(jnp.float32)).astype(jnp.bfloat16)
 
@@ -1317,9 +1426,9 @@
     ]
 
 
-def attend(table, x, utterances):
+def attend(lengths, x):
     return pl.pallas_call(
-        partial(attend_kernel, utterances),
+        attend_kernel,
         out_shape=[
             jax.ShapeDtypeStruct((8, QUARTER, 128), jnp.bfloat16),
             jax.ShapeDtypeStruct((8, 2, 8, QUARTER), jnp.float32),
@@ -1330,17 +1439,18 @@
         + key_scratch(),
         compiler_params=LOCAL,
         name="attend",
-    )(table, x)
+    )(lengths, x)
 
 
 def attend_back_kernel(
-    utterances, table, x_ref, g_ref, l_ref, c_ref, s_ref, dq_ref, dkv_ref, held_p, held_d, q_ref, pairs, turned, sems
+    lengths, x_ref, g_ref, l_ref, c_ref, s_ref, dq_ref, dkv_ref, held_p, held_d, q_ref, pairs, turned, sems
 ):
-    fetch(x_ref, table[utterances], q_ref, pairs, turned, sems)
+    bounds, core = bounds_of(lengths), lax.rem(lax.axis_index("head"), 2)
+    fetch(x_ref, core, q_ref, pairs, turned, sems)
     dkv_ref[...] = jnp.zeros_like(dkv_ref)
 
     def of_quarter(step, carry):
-        source, sub, first, ends, limit = quarter_of(step, table, utterances)
+        source, sub, first, ends, limit = quarter_of(step, bounds, core)
         at = pl.ds(pl.multiple_of(sub * HALF, HALF), HALF)
         query = opened(q_ref[source, at, :].astype(jnp.float32))
         grad = swap_halves(opened(g_ref[source, at, :].astype(jnp.float32)))
@@ -1385,10 +1495,10 @@
     lax.fori_loop(0, 16, of_quarter, 0)
 
 
-def attend_back(table, x, grads, logsum, cosine, sine, utterances):
+def attend_back(lengths, x, grads, logsum, cosine, sine):
     spans = 8 * 1024 // SPAN + 1
     return pl.pallas_call(
-        partial(attend_back_kernel, utterances),
+        attend_back_kernel,
         out_shape=[
             jax.ShapeDtypeStruct((8, QUARTER, 128), jnp.bfloat16),
             jax.ShapeDtypeStruct((8 * 1024 + SPAN, 128), jnp.float32),
@@ -1402,25 +1512,7 @@
         + key_scratch(),
         compiler_params=LOCAL,
         name="attend_back",
-    )(table, x, grads, logsum, cosine, sine)
-
-
-def attention_table(lengths, core):
-    bounds = jnp.cumsum(lengths)
-    starts = bounds - lengths
-    ids = jnp.arange(lengths.shape[0], dtype=jnp.int32)
-    first = jnp.arange(32, dtype=jnp.int32) * QUARTER
-    head_segment = segment_of(first, lengths)
-    tail_segment = segment_of(first + QUARTER - 1, lengths)
-    low = jnp.sum(jnp.where(head_segment[:, None] == ids[None, :], starts[None, :], 0), axis=1)
-    high = jnp.sum(jnp.where(tail_segment[:, None] == ids[None, :], bounds[None, :], 0), axis=1)
-    base = low // 128 * 128
-    count = (high - base + SPAN - 1) // SPAN
-    in_low = (low - base + SPAN - 1) // SPAN
-    in_high = (high - base) // SPAN
-    plain = (head_segment == tail_segment) & (in_low < in_high)
-    in_low, in_high = jnp.where(plain, in_low, count), jnp.where(plain, in_high, count)
-    return jnp.concatenate([bounds, core[None], base // 128, count, in_low, in_high]).astype(jnp.int32)
+    )(lengths, x, grads, logsum, cosine, sine)
 
 
 def pair_up(even, odd):
@@ -1428,39 +1520,26 @@
     return jnp.where(left, even, swap_halves(odd)), jnp.where(left, swap_halves(even), odd)
 
 
-def project_kernel(x_ref, w_ref, c_ref, s_ref, o_ref):
-    for quarter in range(4):
-        rows = pl.ds(quarter * QUARTER, QUARTER)
-        part = x_ref[rows, :]
-        cos, sin = c_ref[rows, :], s_ref[rows, :]
-        cos, sin = jnp.concatenate([cos, cos], axis=1), jnp.concatenate([sin, sin], axis=1)
-        queries, keys, values = (
-            jnp.dot(part, w_ref[k], preferred_element_type=jnp.float32)
-            for k in range(3)
-        )
-        queries = (queries * cos + turn(queries, 1) * sin) * 0.125
-        keys = keys * cos + turn(keys, 1) * sin
-        at_q = pl.ds((quarter % 2) * QUARTER + (quarter // 2) * HALF, HALF)
-        at_k = pl.ds(512 + quarter * QUARTER, QUARTER)
-        for pair in range(2):
-            lanes = slice(128 * pair, 128 * (pair + 1))
-            q_even, q_odd = pair_up(queries[:HALF, lanes], queries[HALF:, lanes])
-            k_even, k_odd = pair_up(keys[:, lanes], values[:, lanes])
-            o_ref[2 * pair, at_q, :] = q_even.astype(jnp.bfloat16)
-            o_ref[2 * pair + 1, at_q, :] = q_odd.astype(jnp.bfloat16)
-            o_ref[2 * pair, at_k, :] = k_even.astype(jnp.bfloat16)
-            o_ref[2 * pair + 1, at_k, :] = k_odd.astype(jnp.bfloat16)
-
-
-def project(x, w, cosine, sine):
-    return pl.pallas_call(
-        project_kernel,
-        out_shape=jax.ShapeDtypeStruct((4, 1536, 128), jnp.bfloat16),
-        in_specs=[VMEM] * 4,
-        out_specs=VMEM,
-        compiler_params=LOCAL,
-        name="project",
-    )(x, w, cosine, sine)
+def project_quarter(quarter, x_ref, w_ref, c_ref, s_ref, o_ref):
+    rows = pl.ds(quarter * QUARTER, QUARTER)
+    part = x_ref[rows, :]
+    cos, sin = c_ref[rows, :], s_ref[rows, :]
+    cos, sin = jnp.concatenate([cos, cos], axis=1), jnp.concatenate([sin, sin], axis=1)
+    queries, keys, values = (
+        jnp.dot(part, w_ref[k], preferred_element_type=jnp.float32) for k in range(3)
+    )
+    queries = (queries * cos + turn(queries, 1) * sin) * 0.125
+    keys = keys * cos + turn(keys, 1) * sin
+    at_q = pl.ds((quarter % 2) * QUARTER + (quarter // 2) * HALF, HALF)
+    at_k = pl.ds(512 + quarter * QUARTER, QUARTER)
+    for pair in range(2):
+        lanes = slice(128 * pair, 128 * (pair + 1))
+        q_even, q_odd = pair_up(queries[:HALF, lanes], queries[HALF:, lanes])
+        k_even, k_odd = pair_up(keys[:, lanes], values[:, lanes])
+        o_ref[2 * pair, at_q, :] = q_even.astype(jnp.bfloat16)
+        o_ref[2 * pair + 1, at_q, :] = q_odd.astype(jnp.bfloat16)
+        o_ref[2 * pair, at_k, :] = k_even.astype(jnp.bfloat16)
+        o_ref[2 * pair + 1, at_k, :] = k_odd.astype(jnp.bfloat16)
 
 
 ROWS = 256
@@ -1495,11 +1574,11 @@
     return high + (middle + low)
 
 
-def onehot_of(first, count, table, utterances):
+def onehot_of(first, count, bounds):
     rows = first + lax.broadcasted_iota(jnp.int32, (count, 1), 0)
     segment = jnp.zeros((count, 1), jnp.int32)
-    for u in range(utterances):
-        segment = segment + (rows >= table[u]).astype(jnp.int32)
+    for bound in bounds:
+        segment = segment + (rows >= bound).astype(jnp.int32)
     spots = lax.broadcasted_iota(jnp.int32, (count, 16), 1)
     return (segment == spots).astype(jnp.float32).astype(jnp.bfloat16)
 
@@ -1549,26 +1628,56 @@
     return norm, mean + 1e-06
 
 
-def text_body(utterances, ins, outs, scratch):
+class Staged:
+    def __init__(self, pairs, sems):
+        self.pairs, self.sems, self.open = pairs, sems, []
+
+    def ship(self, *names):
+        for name in names:
+            k = list(self.pairs).index(name)
+            copy = pltpu.make_async_copy(*self.pairs[name], self.sems.at[k])
+            copy.start()
+            self.open.append(copy)
+
+    def wait(self):
+        for copy in self.open:
+            copy.wait()
+
+
+TEXT_STAGED = (
+    "ext", "unit", "inverse", "expand", "shrink", "mods", "scale", "expanded", "grn", "total",
+    "join_low", "hidden", "d_ffn", "mask",
+)
+
+
+def text_body(ins, outs, scratch):
     (
-        table,
+        lengths,
         text_ref,
-        mel_ref,
-        cot_ref,
-        mask_ref,
+        mel_hbm,
+        cot_hbm,
+        mask_in,
         taps_ref,
         gain_ref,
         bias_ref,
         expand_ref,
         shrink_ref,
-        join_ref,
-        share_ref,
+        join_hbm,
+        embed_ref,
+        modulation_hbm,
+        gamma_ref,
+        beta_ref,
     ) = ins
+    staged_count = len(TEXT_STAGED)
+    staged = Staged(
+        dict(zip(TEXT_STAGED, zip(scratch[:staged_count], outs[:staged_count]))),
+        scratch[staged_count],
+    )
+    attn_all_ref, text_all_ref = outs[staged_count:]
     (
         ext_ref,
         unit_ref,
         inverse_ref,
-        text_low_ref,
         expand_all,
         shrink_all,
         mods_ref,
@@ -1578,30 +1687,70 @@
         total_ref,
         join_low_ref,
         hidden_ref,
+        d_ffn_ref,
+        mask_ref,
+    ) = scratch[:staged_count]
+    (
+        text_low_ref,
         attn_low_ref,
-        attn_all_ref,
-        d_ffn_ref,
-        text_all_ref,
-    ) = outs
-    own_ref, act_ref, sums_ref, share_all, branch_ref, rim_sems = scratch[:6]
-    rest = scratch[6:]
-    weights = gather_body(1, (expand_ref, shrink_ref), (expand_all, shrink_all), rest[:7])
-    shares = gather_body(1, (share_ref,), (share_all,), rest[7:14])
-    rows_out = gather_body(2, (attn_low_ref,), (attn_all_ref,), rest[14:21])
-    text_out = gather_body(1, (text_low_ref,), (text_all_ref,), rest[21:28])
+        own_ref,
+        act_ref,
+        sums_ref,
+        share_ref,
+        share_all,
+        branch_ref,
+        mel_ref,
+        cot_ref,
+        join_ref,
+        modulation_ref,
+        in_sems,
+        rim_sems,
+    ) = scratch[staged_count + 1 : staged_count + 15]
+    rest = scratch[staged_count + 15 :]
+    bounds = bounds_of(lengths)
+    arriving = [
+        pltpu.make_async_copy(source, target, in_sems.at[k])
+        for k, (source, target) in enumerate(
+            (
+                (modulation_hbm, modulation_ref),
+                (cot_hbm, cot_ref),
+                (join_hbm, join_ref),
+                (mel_hbm, mel_ref),
+            )
+        )
+    ]
+    for copy in arriving:
+        copy.start()
+    expands = gather_body(1, (expand_ref,), (expand_all,), rest[:7])
+    shrinks = gather_body(1, (shrink_ref,), (shrink_all,), rest[7:14])
+    shares = gather_body(1, (share_ref,), (share_all,), rest[14:21])
+    rows_out = gather_body(4, (attn_low_ref,), (attn_all_ref,), rest[21:28])
+    text_out = gather_body(1, (text_low_ref,), (text_all_ref,), rest[28:35])
     rim = rim_body(text_ref, ext_ref, rim_sems)
-    sums = all_sum_body((sums_ref,), (total_ref, own_ref), rest[28:])
-    running = (weights, shares, rows_out, text_out, rim, sums)
+    sums = all_sum_body((sums_ref,), (total_ref, own_ref), rest[35:])
+    running = (expands, shrinks, shares, rows_out, text_out, rim, sums)
     yield sum(next(one) for one in running)
     first = own_first()
     next(rim)
-    next(weights)
+    next(expands)
+    next(shrinks)
+    mask_ref[...] = jnp.broadcast_to(mask_in[...].astype(jnp.float32), (128, ROWS)).T
+    embed = embed_ref[...]
+    cond_low = (embed * (1.0 / (1.0 + jnp.exp(-embed)))).astype(jnp.bfloat16)
+    share_ref[...] = jnp.zeros_like(share_ref)
+    share_ref[16:17, :256] = gamma_ref[...]
+    share_ref[16:17, 256:512] = beta_ref[...]
+    arriving[0].wait()
+    count = cond_low.shape[0]
+    share_ref[:count, :] = jnp.dot(
+        cond_low, modulation_ref[...], preferred_element_type=jnp.float32
+    )
     next(shares)
     next(rim, None)
 
     def conv(at, i):
         rows = first + i + lax.broadcasted_iota(jnp.int32, (32, 1), 0)
-        start, end = limits(rows, table, utterances)
+        start, end = limits(rows, bounds)
         window = ext_ref[pl.ds(pl.multiple_of(i, 32), 48), :]
         total = jnp.zeros((32, window.shape[1]), jnp.float32)
         for tap in range(7):
@@ -1612,12 +1761,11 @@
         text_low_ref[at, :] = (unit * gain_ref[...] + bias_ref[...]).astype(jnp.bfloat16)
 
     by_rows(32, conv)
+    staged.ship("ext", "unit", "inverse", "mask")
     yield
-    for _ in weights:
+    for _ in expands:
         pass
-    for _ in shares:
-        pass
-    onehot = onehot_of(first, ROWS, table, utterances)
+    onehot = onehot_of(first, ROWS, bounds)
 
     def expand(h, carry):
         expanded = jnp.dot(text_low_ref[...], expand_all[h], preferred_element_type=jnp.float32)
@@ -1629,16 +1777,24 @@
 
     lax.fori_loop(0, 4, expand, 0)
     next(sums)
+    staged.ship("expand", "expanded")
+    for _ in shares:
+        pass
+    for _ in shrinks:
+        pass
+    arriving[1].wait()
     for h in range(4):
         mods_ref[:, 1536 * h : 1536 * (h + 1)] = share_all[h, :16]
         scale_ref[h] = share_all[h, 16:, :512]
     mods = three(mods_ref[:, 5120:6144])
 
     def d_ffn(at, i):
-        gate = pick(onehot_of(first + i, 64, table, utterances), mods)
+        gate = pick(onehot_of(first + i, 64, bounds), mods)
         d_ffn_ref[at, :] = (cot_ref[at, :] * gate).astype(jnp.bfloat16)
 
     by_rows(64, d_ffn)
+    staged.ship("shrink", "mods", "scale", "d_ffn")
+    yield
     for _ in sums:
         pass
     next(text_out)
@@ -1656,7 +1812,9 @@
         return carry
 
     lax.fori_loop(0, 4, shrink, 0)
-    join_low_ref[...] = (text_ref[...] + mask_ref[...] * branch_ref[...]).astype(jnp.bfloat16)
+    join_low_ref[...] = (text_ref[...] + mask_ref[:, :1] * branch_ref[...]).astype(jnp.bfloat16)
+    for copy in arriving[2:]:
+        copy.wait()
 
     def join(n, carry):
         lanes = pl.ds(pl.multiple_of(n * 256, 256), 256)
@@ -1669,75 +1827,92 @@
     shift, scale = three(mods_ref[:, :1024]), three(mods_ref[:, 1024:2048])
 
     def attn(at, i):
-        spots = onehot_of(first + i, 32, table, utterances)
+        spots = onehot_of(first + i, 32, bounds)
         unit, _ = normed(hidden_ref[at, :])
         attn_low_ref[at, :] = (unit * (1.0 + pick(spots, scale)) + pick(spots, shift)).astype(
             jnp.bfloat16
         )
 
     by_rows(32, attn)
+    next(rows_out)
+    staged.ship("grn", "total", "join_low", "hidden")
     for _ in rows_out:
         pass
     for _ in text_out:
         pass
+    staged.wait()
 
 
 def gather_scratch(count, cuts):
     return [DMA((count,)), DMA((count, cuts)), DMA((count, cuts)), DMA((count,)), DMA((count,)), DMA((count, cuts)), DMA((count, cuts))]
 
 
-def text_forward(table, text, mel, cot, mask, taps, gain, bias, expand, shrink, join, share, utterances):
-    def f32(*shape):
-        return jax.ShapeDtypeStruct(shape, jnp.float32)
-
-    def low(*shape):
-        return jax.ShapeDtypeStruct(shape, jnp.bfloat16)
-
+def f32(*shape):
+    return jax.ShapeDtypeStruct(shape, jnp.float32)
+
+
+def low(*shape):
+    return jax.ShapeDtypeStruct(shape, jnp.bfloat16)
+
+
+def room(shape):
+    return pltpu.VMEM(shape.shape, shape.dtype)
+
+
+def text_forward(lengths, text, mel, cot, mask, taps, gain, bias, expand, shrink, join, embed, modulation, gamma, beta):
     width, wide = text.shape[1], mel.shape[1]
-    outs = [
-        (f32(ROWS + 16, width), VMEM),
-        (f32(ROWS, width), VMEM),
-        (f32(ROWS, 128), VMEM),
-        (low(ROWS, width), VMEM),
-        (low(4, width, 256), VMEM),
-        (low(4, 256, width), VMEM),
-        (f32(16, 6 * wide), VMEM),
-        (f32(4, 8, 512), VMEM),
-        (f32(4, ROWS, 256), VMEM),
-        (low(4, ROWS, 256), VMEM),
-        (f32(4, 16, 256), VMEM),
-        (low(ROWS, width), VMEM),
-        (f32(ROWS, wide), VMEM),
-        (low(ROWS, wide), VMEM),
-        (low(4, ROWS, wide), HBM),
-        (low(ROWS, wide), VMEM),
-        (low(4, ROWS, width), HBM),
+    staged = [
+        f32(ROWS + 16, width),
+        f32(ROWS, width),
+        f32(ROWS, 128),
+        low(4, width, 256),
+        low(4, 256, width),
+        f32(16, 6 * wide),
+        f32(4, 8, 512),
+        f32(4, ROWS, 256),
+        low(4, ROWS, 256),
+        f32(4, 16, 256),
+        low(ROWS, width),
+        f32(ROWS, wide),
+        low(ROWS, wide),
+        f32(ROWS, 128),
     ]
+    share = (24, modulation.shape[1])
     return Task(
-        partial(text_body, utterances),
-        [table, text, mel, cot, mask, taps, gain, bias, expand, shrink, join, share],
-        [o for o, _ in outs],
-        [
+        text_body,
+        [lengths, text, mel, cot, mask, taps, gain, bias, expand, shrink, join, embed, modulation, gamma, beta],
+        staged + [low(4, ROWS, wide), low(4, ROWS, width)],
+        [room(s) for s in staged]
+        + [
+            DMA((len(staged),)),
+            pltpu.VMEM((ROWS, width), jnp.bfloat16),
+            pltpu.VMEM((ROWS, wide), jnp.bfloat16),
             pltpu.VMEM((16, 256), jnp.float32),
             pltpu.VMEM((4, ROWS, 256), jnp.float32),
             pltpu.VMEM((4, 16, 256), jnp.float32),
-            pltpu.VMEM((4,) + share.shape, jnp.float32),
+            pltpu.VMEM(share, jnp.float32),
+            pltpu.VMEM((4,) + share, jnp.float32),
             pltpu.VMEM((ROWS, width), jnp.float32),
+            pltpu.VMEM(mel.shape, jnp.float32),
+            pltpu.VMEM(cot.shape, jnp.float32),
+            pltpu.VMEM(join.shape, jnp.bfloat16),
+            pltpu.VMEM(modulation.shape, jnp.bfloat16),
+            DMA((4,)),
             DMA((4,)),
         ]
-        + gather_scratch(2, 1)
         + gather_scratch(1, 1)
-        + gather_scratch(1, 2)
+        + gather_scratch(1, 1)
+        + gather_scratch(1, 1)
+        + gather_scratch(1, 4)
         + gather_scratch(1, 1)
         + all_sum_scratch(16, 256),
-        [SMEM] + [VMEM] * 11,
-        [s for _, s in outs],
+        [SMEM, VMEM, HBM, HBM] + [VMEM] * 4 + [HBM, HBM, HBM, VMEM, HBM, VMEM, VMEM],
+        HBM,
     )
 
 
 def middle_kernel(
-    utterances,
-    table,
+    lengths,
     tiles_ref,
     out_ref,
     up_hbm,
@@ -1763,6 +1938,7 @@
     d_in_ref,
     sems,
 ):
+    bounds = bounds_of(lengths)
     copies = []
     for h in range(4):
         copies.append(
@@ -1791,7 +1967,7 @@
     mods = [three(mods_ref[:, 1024 * k : 1024 * (k + 1)]) for k in range(6)]
 
     def enter(at, i):
-        spots = onehot_of(first + i, 32, table, utterances)
+        spots = onehot_of(first + i, 32, bounds)
         middle = hidden_ref[at, :] + pick(spots, mods[2]) * attn_ref[at, :]
         middle_ref[at, :] = middle
         unit, _ = normed(middle)
@@ -1824,7 +2000,7 @@
     d_mods_ref[...] = jnp.zeros_like(d_mods_ref)
 
     def leave(at, i):
-        spots = onehot_of(first + i, 32, table, utterances)
+        spots = onehot_of(first + i, 32, bounds)
         middle, cot, d_in, rows = middle_ref[at, :], cot_ref[at, :], d_in_ref[at, :], rows_ref[at, :]
         layer_ref[at, :] = middle + pick(spots, mods[5]) * rows
         unit, inverse = normed(middle)
@@ -1846,17 +2022,11 @@
             d_tiles_ref[4 * h + 2 * k + 1] = odd.astype(jnp.bfloat16)
 
 
-def middle_part(table, tiles, out, up, down, hidden, mods, cot, d_ffn, utterances):
+def middle_part(lengths, tiles, out, up, down, hidden, mods, cot, d_ffn):
     wide = hidden.shape[1]
 
-    def f32(*shape):
-        return jax.ShapeDtypeStruct(shape, jnp.float32)
-
-    def low(*shape):
-        return jax.ShapeDtypeStruct(shape, jnp.bfloat16)
-
     return pl.pallas_call(
-        partial(middle_kernel, utterances),
+        middle_kernel,
         out_shape=[
             low(4, ROWS, 256),
             f32(ROWS, wide),
@@ -1881,12 +2051,12 @@
         ],
         compiler_params=LOCAL,
         name="middle_part",
-    )(table, tiles, out, up, down, hidden, mods, cot, d_ffn)
-
-
-def back_body(utterances, ins, outs, scratch):
+    )(lengths, tiles, out, up, down, hidden, mods, cot, d_ffn)
+
+
+def back_body(ins, outs, scratch):
     (
-        table,
+        lengths,
         tiles_ref,
         qkv_ref,
         hidden_ref,
@@ -1923,6 +2093,7 @@
         scratch[:9]
     )
     rim_sems, rest = scratch[9], scratch[10:]
+    bounds = bounds_of(lengths)
     swap = exchange_body((d_qkv_ref,), (d_qkv_all,), rest[:3])
     branch_out = gather_body(1, (d_branch_ref,), (d_branch_all,), rest[3:10])
     expanded_out = exchange_body((d_expanded_ref,), (d_expanded_all,), rest[10:13])
@@ -1962,7 +2133,7 @@
     d_mods_ref[...] = jnp.zeros_like(d_mods_ref)
 
     def hidden_back(at, i):
-        spots = onehot_of(first + i, 32, table, utterances)
+        spots = onehot_of(first + i, 32, bounds)
         unit, inverse = normed(hidden_ref[at, :])
         d_in = d_in_ref[at, :]
         mel = d_middle_ref[at, :] + normed_back(d_in * (1.0 + pick(spots, scale)), unit, inverse)
@@ -1976,9 +2147,9 @@
         d_joined_ref[...], join_ref[...], ROWS_TO_ROWS, preferred_element_type=jnp.float32
     )
     d_text_ref[...] = d_text
-    d_branch_ref[...] = (mask_ref[...] * d_text).astype(jnp.bfloat16)
+    d_branch_ref[...] = (mask_ref[:, :1] * d_text).astype(jnp.bfloat16)
     next(branch_out)
-    onehot = onehot_of(first, ROWS, table, utterances)
+    onehot = onehot_of(first, ROWS, bounds)
     norm, mean = ratio_of(squares_ref[...])
     ratio_ref[...] = norm / mean
 
@@ -2044,7 +2215,7 @@
 
     def taps_back(at, i):
         rows = first + i + lax.broadcasted_iota(jnp.int32, (32, 1), 0)
-        start, end = limits(rows, table, utterances)
+        start, end = limits(rows, bounds)
         window = ext_ref[pl.ds(pl.multiple_of(i, 32), 48), :]
         grad = d_conv_ref[at, :]
         for tap in range(7):
@@ -2057,7 +2228,7 @@
 
     def text_back(at, i):
         rows = first + i + lax.broadcasted_iota(jnp.int32, (32, 1), 0)
-        start, end = limits(rows, table, utterances)
+        start, end = limits(rows, bounds)
         window = d_ext_ref[pl.ds(pl.multiple_of(i, 32), 48), :]
         total = d_text_ref[at, :]
         for tap in range(7):
@@ -2073,13 +2244,7 @@
             pass
 
 
-def text_backward(operands, utterances):
-    def f32(*shape):
-        return jax.ShapeDtypeStruct(shape, jnp.float32)
-
-    def low(*shape):
-        return jax.ShapeDtypeStruct(shape, jnp.bfloat16)
-
+def text_backward(operands):
     wide, width = 1024, 512
     outs = [
         (low(4, ROWS, 768), VMEM),
@@ -2096,7 +2261,7 @@
         (low(4, ROWS, 256), HBM),
     ]
     return Task(
-        partial(back_body, utterances),
+        back_body,
         operands,
         [o for o, _ in outs],
         [
@@ -2120,7 +2285,47 @@
     )
 
 
-WIDE = 48 << 20
+def finish_kernel(qkv_ref, small_ref, mod_ref, embed_ref, sums_ref, *refs):
+    plain = refs[: (len(refs) - 6) // 2]
+    outs = refs[len(plain) :]
+    for source, target in zip(plain, outs):
+        target[...] = source[...]
+    o_qkv, o_conv, o_gain, o_bias, o_mod, o_pair = outs[len(plain) :]
+    for k in range(3):
+        o_qkv[k] = qkv_ref[:, 256 * k : 256 * (k + 1)]
+    o_conv[...] = small_ref[:7, :16]
+    o_gain[...] = small_ref[7:8, :16]
+    o_bias[...] = small_ref[8:9, :16]
+    embed = embed_ref[...]
+    cond = (embed * (1.0 / (1.0 + jnp.exp(-embed)))).astype(jnp.bfloat16)
+    total = None
+    for term in three(mod_ref[...]):
+        part = lax.dot_general(
+            term, cond, (((0,), (0,)), ((), ())), preferred_element_type=jnp.float32
+        )
+        total = part if total is None else total + part
+    o_mod[...] = total[: o_mod.shape[0]]
+    o_pair[...] = sums_ref[8:10, :]
+
+
+def finish(qkv, small, mod, embed, sums, plain, columns):
+    rows = qkv.shape[0]
+    return pl.pallas_call(
+        finish_kernel,
+        out_shape=[like(a) for a in plain]
+        + [
+            f32(3, rows, 256),
+            f32(7, 16),
+            f32(1, 16),
+            f32(1, 16),
+            f32(columns, embed.shape[1]),
+            f32(2, 256),
+        ],
+        in_specs=[VMEM] * (5 + len(plain)),
+        out_specs=[VMEM] * (len(plain) + 6),
+        compiler_params=LOCAL,
+        name="finish",
+    )(qkv, small, mod, embed, sums, *plain)
 
 
 def blocks_of(array):
@@ -2129,13 +2334,6 @@
 
 def rows_of(gathered):
     return gathered.reshape((gathered.shape[0] * gathered.shape[1],) + gathered.shape[2:])
-
-
-def angles_of(places, lanes):
-    half_width = HEAD_DIM // 2
-    inverse = 10000.0 ** (-jnp.arange(half_width, dtype=jnp.float32) * 2.0 / HEAD_DIM)
-    inverse = jnp.concatenate([inverse] * (lanes // half_width) + [jnp.zeros((128 - lanes,))])
-    return places.astype(jnp.float32) * inverse
 
 
 def on_eight_by_four(
@@ -2159,49 +2357,21 @@
     down_weight,
     cotangent,
 ):
-    rows_here = text_in.shape[0]
-    frames_here = rows_here * 4
-    seq_index = lax.axis_index("seq")
-    head_index = lax.axis_index("head")
-    core = lax.rem(head_index, 2)
     utterances = lengths.shape[0]
-    taps_count = conv_weight.shape[0]
-    wide = mel_in.shape[1]
-
-    all_ids = jnp.arange(8 * frames_here, dtype=jnp.int32)
-    places = position_of(all_ids, lengths, segment_of(all_ids, lengths))
-    table = attention_table(lengths, core)
-    own_angles = angles_of(
-        lax.dynamic_slice_in_dim(places, seq_index * frames_here, frames_here)[:, None], 128
-    )
-    own_cos, own_sin = jnp.cos(own_angles), jnp.sin(own_angles)
-    tiles = lax.dynamic_index_in_dim(
-        places.reshape(8, 2, 2, 2, HALF), core, 2, keepdims=False
-    )
-    query_angles = angles_of(
-        jnp.where(jnp.arange(128) < 64, tiles[:, :, 0, :, None], tiles[:, :, 1, :, None]), 128
-    ).reshape(8, QUARTER, 128)
-    key_angles = angles_of(tiles.reshape(8, 2 * QUARTER)[:, :, None], 64)
-
-    cond_low = jax.nn.silu(time_embed).astype(jnp.bfloat16)
-    mod_part = narrow_dot(cond_low, modulation)
-    share = jnp.concatenate(
-        [
-            mod_part,
-            jnp.zeros((16 - utterances, mod_part.shape[1]), jnp.float32),
-            jnp.pad(
-                jnp.concatenate([grn_gamma, grn_beta])[None, :],
-                ((0, 7), (0, mod_part.shape[1] - 2 * grn_gamma.shape[0])),
-            ),
-        ]
-    )
-    mask_rows = text_mask.astype(jnp.float32)[:, None]
+    half_width = HEAD_DIM // 2
+    inverse = 10000.0 ** (-jnp.arange(half_width, dtype=jnp.float32) * 2.0 / HEAD_DIM)
+    rates = jnp.pad(
+        jnp.stack(
+            [jnp.tile(inverse, 4), jnp.concatenate([jnp.tile(inverse, 2), jnp.zeros(64)])]
+        ),
+        ((0, 6), (0, 0)),
+    )
+
     (
         (
             extended,
             text_unit,
             text_inverse,
-            _,
             expand_all,
             shrink_all,
             mods,
@@ -2211,56 +2381,57 @@
             squares,
             join_low,
             hidden,
-            _,
+            d_ffn_low,
+            mask_rows,
             attn_all,
-            d_ffn_low,
             text_all,
         ),
+        (own_cos, own_sin),
     ) = communicate(
         [
             text_forward(
-                table,
+                lengths,
                 text_in,
                 mel_in,
                 cotangent,
-                mask_rows,
+                text_mask[None, :],
                 conv_weight,
                 norm_gain[None, :],
                 norm_bias[None, :],
                 expand_weight,
                 shrink_weight,
                 join_weight,
-                share,
-                utterances,
-            )
+                time_embed,
+                modulation,
+                grn_gamma[None, :],
+                grn_beta[None, :],
+            ),
+            own_turns(lengths, rates),
         ],
         0,
-        WIDE,
     )
 
     qkv_near = qkv_weight.transpose(1, 0, 2)
-    attn_all, out_near, up_near, down_near, qkv_late = lax.optimization_barrier(
-        (attn_all, out_weight, up_weight, down_weight, qkv_near)
-    )
-    out_full, up_full, down_full, qkv_full = (
-        lax.all_gather(w, "head", axis=0) for w in (out_near, up_near, down_near, qkv_late)
-    )
-    attn_all = rows_of(attn_all)
+    attn_all, out_near, up_near, down_near = lax.optimization_barrier(
+        (attn_all, out_weight, up_weight, down_weight)
+    )
+    out_full, up_full, down_full = (
+        lax.all_gather(w, "head", axis=0) for w in (out_near, up_near, down_near)
+    )
     (packed,), (query_cos, query_sin, key_cos, key_sin), (d_ffn_all,) = communicate(
         [
-            spread_out(project(attn_all, qkv_near, own_cos, own_sin)),
-            turns([query_angles, key_angles]),
+            spread_out(rows_of(attn_all), qkv_near, own_cos, own_sin),
+            turns(lengths, rates),
             gathered([d_ffn_low]),
         ],
         1,
-        WIDE,
-    )
-    context_here, logsum = attend(table, packed, utterances)
+    )
+    context_here, logsum = attend(lengths, packed)
     (context_tiles,), (grn_all,) = communicate([to_rows(context_here), exchanged([grn_low])], 2)
 
     (
         context_blocks,
-        transformer_layer_output,
+        layer_output,
         ffn_low,
         gelu_low,
         d_up_low,
@@ -2269,24 +2440,22 @@
         d_context_tiles,
         d_mods_middle,
     ) = middle_part(
-        table, context_tiles, out_full, up_full, down_full, hidden, mods, cotangent, d_ffn_low, utterances
+        lengths, context_tiles, out_full, up_full, down_full, hidden, mods, cotangent, d_ffn_low
     )
 
     (d_context,), (ffn_all,), (context_all,) = communicate(
         [to_heads(d_context_tiles), gathered([ffn_low]), exchanged([context_blocks])], 3
     )
-    d_query, d_pair = attend_back(
-        table, packed, d_context, logsum, query_cos, query_sin, utterances
-    )
-    halves = (8, 2, QUARTER, 128)
+    d_context, qkv_late = lax.optimization_barrier((d_context, qkv_near))
+    qkv_full = lax.all_gather(qkv_late, "head", axis=0)
+    d_query, d_pair = attend_back(lengths, packed, d_context, logsum, query_cos, query_sin)
     (d_tiles,), (d_attn_all,), (gelu_all, d_up_all) = communicate(
         [
-            sent_home(d_query, d_pair, key_cos.reshape(halves), key_sin.reshape(halves)),
+            sent_home(d_query, d_pair, key_cos, key_sin),
             gathered([d_attn_low]),
             exchanged([gelu_low, d_up_low]),
         ],
         4,
-        WIDE,
     )
     ffn_all, d_ffn_all, context_all, d_attn_all, gelu_all, d_up_all, grn_all, text_all = (
         rows_of(g)
@@ -2316,7 +2485,7 @@
         [
             text_backward(
                 [
-                    table,
+                    lengths,
                     d_tiles,
                     qkv_full,
                     hidden,
@@ -2334,8 +2503,7 @@
                     norm_gain[None, :],
                     conv_weight,
                     extended,
-                ],
-                utterances,
+                ]
             ),
             seq_scattered(
                 [
@@ -2346,56 +2514,55 @@
             ),
         ],
         5,
-        56 << 20,
-    )
-
-    small = jnp.pad(small.reshape(16, 8, 64).transpose(1, 0, 2), ((0, 0), (0, 0), (0, 64)))
+    )
+
+    small = small.reshape(16, 8, 4, 16).transpose(1, 2, 0, 3).reshape(8, 64, 16)
+    small = jnp.pad(small, ((0, 0), (0, 0), (0, 112)))
     d_mods = jnp.concatenate([d_mods_attn, d_mods_middle], axis=1)[:utterances]
+    columns = d_mods.shape[1] // 32
+    d_mods = d_mods.reshape(utterances, 8, 4, columns).transpose(1, 2, 0, 3)
+    d_mods = jnp.pad(
+        d_mods.reshape(8, 4 * utterances, columns), ((0, 0), (0, 0), (0, -columns % 128))
+    )
     ((qkv, shrink, expand, join, small, mod),) = communicate(
         [
-            seq_scattered(
+            all_scattered(
                 [
-                    blocks_of(part(attn_all, rows_of(d_qkv_all))),
+                    blocks_of(part(rows_of(attn_all), rows_of(d_qkv_all))),
                     blocks_of(part(rows_of(d_branch_all), grn_all)),
                     blocks_of(part(text_all, rows_of(d_expanded_all))),
                     blocks_of(part(d_joined_low, join_low)),
                     small,
-                    d_mods.reshape(utterances, 8, -1).transpose(1, 0, 2),
-                ]
+                    d_mods,
+                ],
+                3,
             )
         ],
         6,
-        WIDE,
-    )
-    ((join, small, mod),) = communicate(
-        [
-            head_blocks(
-                [
-                    join.reshape(4, -1, join.shape[1]),
-                    jnp.pad(
-                        small[:, :64].reshape(16, 4, 16).transpose(1, 0, 2),
-                        ((0, 0), (0, 0), (0, 112)),
-                    ),
-                    mod.reshape(utterances, 4, -1).transpose(1, 0, 2),
-                ]
-            )
-        ],
-        7,
+    )
+    grad_text, grad_mel, expand, shrink, join, out, up, down, qkv, conv, gain, bias, mod, pair = finish(
+        qkv,
+        small,
+        mod,
+        time_embed,
+        own_sums,
+        [grad_text, grad_mel, expand, shrink, join, out, up, down],
+        columns,
     )
     return (
-        transformer_layer_output,
+        layer_output,
         grad_text,
         grad_mel,
-        small[:taps_count, :16],
-        small[taps_count, :16],
-        small[taps_count + 1, :16],
+        conv,
+        gain[0],
+        bias[0],
         expand,
-        own_sums[8],
-        own_sums[9],
+        pair[0],
+        pair[1],
         shrink.T,
         join.T,
-        exact_inner(mod, cond_low.astype(jnp.float32)).T,
-        qkv.reshape(qkv.shape[0], 3, -1),
+        mod.T,
+        qkv.transpose(1, 0, 2),
         out,
         up,
         down,

time: 573 us -> 500 us (0.87); the launches traced: 564 us -> 497 us
  Pallas kernels: 487 us -> 459 us
  local copies, waits for them, and re-layouts: 30.2 us -> 3.77 us
  other arithmetic: 13.6 us -> 0.63 us
    pallas_call x8 -> x7, Pallas kernels: 377 us -> 349 us  [communicate(): pl.pallas_call(kernel, out_shape=[o for t in tasks for o in t.outs], in_s...]
    unnamed x109 -> x30, local copies, waits for them, and re-layouts: 23.1 us -> 0.06 us
  transfers between devices with their start and end apart: 4 -> 4, of which waited for: 0 -> 1; matrix products, arithmetic and copies ran while one was open for 2% -> 2% of each run, Pallas kernels for 51% -> 45%
where the time goes in v4:
time: 500 us; the launch traced here: 497 us
  Pallas kernels  459 us (92%)
  matrix products  16.1 us (3%)
  between operations  14 us (3%)
    pallas_call x7, Pallas kernels, communicate(): pl.pallas_call(kernel, out_shape=[o for t in tasks for o in t.outs], in_s...  349 us
    pallas_call x1, Pallas kernels, attend_back(): pl.pallas_call(attend_back_kernel, out_shape=[jax.ShapeDtypeStruct((8, QU...  49.9 us
    pallas_call x1, Pallas kernels, attend(): pl.pallas_call(attend_kernel, out_shape=[jax.ShapeDtypeStruct((8, QUARTER...  36.3 us
    pallas_call x1, Pallas kernels, middle_part(): pl.pallas_call(middle_kernel, out_shape=[low(4, ROWS, 256), f32(ROWS, wid...  20 us
    dot_general x7, matrix products, inner_rows(): lax.dot_general(left, right, (((0,), (0,)), ((), ())), preferred_element_...  16.1 us
  transfers between devices with their start and end apart: 4, of which 1 were waited for; matrix products, arithmetic and copies ran while one was open for 2% of the time, Pallas kernels for 45%

profile of v4, /device:TPU:0, one launch (start us, length us, event | category | flops | bytes accessed | tf_op | source)
XLA Modules:
  0.0 497.3 jit_solution(1693814119851230084)
XLA Ops:
  7.2 0.0 all-gather.9.cloned.1.call-start
  7.2 0.1 tile.8
  7.3 0.1 stack_tile.3
  7.4 0.6 select_maximum_fusion.refs_16_.refs_5_
  8.0 56.6 %communicate_0.1 = (f32[272,512]{1,0:T(8,128)}, f32[256,512]{1,0:T(8,128)}, f32[256,128]{1,0:T(8,128)}, bf16[4,512,256]{2,1,0:T(8,128)(2,1)}, bf16[4,256,512]{2,...) custom-call(s32[8]{0:T(128)} %refs_0_.3, ...), custom_call_target="tpu_custom_call" | custom-call | tf_op jit(solution)/shard_map/communicate_0/pallas_call | solution.py:556
  64.7 0.0 all-gather.9.cloned.1.call-update
  64.7 0.0 all-gather.11.cloned.1.call-start
  64.7 0.7 all-gather.11.cloned.1.call-update
  65.4 0.0 all-gather.13.cloned.1.call-start
  65.5 0.7 all-gather.13.cloned.1.call-update
  66.2 0.0 all-gather.15.cloned.1.call-start
  66.2 46.3 %communicate_1.1 = (bf16[8,1536,128]{2,1,0:T(8,128)(2,1)}, f32[8,256,128]{2,1,0:T(8,128)}, f32[8,256,128]{2,1,0:T(8,128)}, f32[8,2,256,128]{3,2,1,0:T(8,128)}, f...) custom-call(bf16[1024,1024]{1,0:T(8,128)(2,1)} %bitcast.72, bf16[3,1024,256]{2,1,0:T(8,128)(2,1)} %bitcast.67, ...), custom_call_target="tpu_custom_call" | custom-call | tf_op jit(solution)/shard_map/communicate_1/pallas_call | solution.py:556
  112.6 36.3 %attend.1 = (bf16[8,256,128]{2,1,0:T(8,128)(2,1)}, f32[8,2,8,256]{3,2,1,0:T(8,128)}) custom-call(s32[8]{0:T(128)} %refs_0_.3, bf16[8,1536,128]{2,1,0:T(8,128)(2,1)} %get-tuple-element.105.x_ref), custom_call_target="tpu_custom_call" | custom-call | tf_op jit(solution)/shard_map/attend/pallas_call | solution.py:1430
  148.9 28.1 %communicate_2.1 = (bf16[16,128,128]{2,1,0:T(8,128)(2,1)}, bf16[4,256,256]{2,1,0:T(8,128)(2,1)}) custom-call(bf16[8,256,128]{2,1,0:T(8,128)(2,1)} %get-tuple-element.106.refs_0_, bf16[4,256,256]{2,1,0:T(8,128)(2,1)} %get-tuple-element.107.refs_1_), custom_call_target="tpu_custom_call" | custom-call | tf_op jit(solution)/shard_map/communicate_2/pallas_call | solution.py:556
  176.9 0.0 all-gather.9.cloned.1.call-done
  177.0 0.0 all-gather.11.cloned.1.call-done
  177.0 1.6 all-gather.13.cloned.1.call-done
  178.6 20.0 %middle_part.1 = (bf16[4,256,256]{2,1,0:T(8,128)(2,1)}, f32[256,1024]{1,0:T(8,128)}, bf16[256,1024]{1,0:T(8,128)(2,1)}, bf16[4,256,512]{2,1,0:T(8,128)(2,1)}, bf...) custom-call(s32[8]{0:T(128)} %refs_0_.3, ...), custom_call_target="tpu_custom_call" | custom-call | tf_op jit(solution)/shard_map/middle_part/pallas_call | solution.py:2028
  198.7 29.9 %communicate_3.1 = (bf16[8,256,128]{2,1,0:T(8,128)(2,1)}, bf16[4,256,1024]{2,1,0:T(8,128)(2,1)}, bf16[4,256,256]{2,1,0:T(8,128)(2,1)}) custom-call(bf16[16,128,128]{2,1,0:T(8,128)(2,1)} %get-tuple-element.115.refs_0_, bf16[256,1024]{1,0:T(8,128)(2,1)} %get-tuple-element.116.refs_1_, bf16[4,256,256]{2,1,0:T(8,128)(2,1)} %get-tuple-element.117.refs_2_), custom_call_target="tpu_custom_call" | custom-call | tf_op jit(solution)/shard_map/communicate_3/pallas_call | solution.py:556
  228.6 0.0 all-gather.15.cloned.1.call-update
  228.6 49.9 %attend_back.1 = (bf16[8,256,128]{2,1,0:T(8,128)(2,1)}, f32[9216,128]{1,0:T(8,128)}) custom-call(s32[8]{0:T(128)} %refs_0_.3, bf16[8,1536,128]{2,1,0:T(8,128)(2,1)} %get-tuple-element.105.x_ref, bf16[8,256,128]{2,1,0:T(8,128)(2,1)} %get-tuple-element.119.g_ref, f32[8,2,8,256]{3,2,1,0:T(8,128)} %get-tuple-element.120.l_ref, ...), custom_call_target="tpu_custom_call" | custom-call | tf_op jit(solution)/shard_map/attend_back/pallas_call | solution.py:1500
  278.5 0.0 copy-start.4
  278.5 63.9 %communicate_4.1 = (bf16[16,384,128]{2,1,0:T(8,128)(2,1)}, bf16[4,256,1024]{2,1,0:T(8,128)(2,1)}, bf16[4,256,512]{2,1,0:T(8,128)(2,1)}, bf16[4,256,512]{2,1,0:T(8,128)(2,1)}) custom-call(bf16[8,256,128]{2,1,0:T(8,128)(2,1)} %get-tuple-element.123.refs_0_, f32[9216,128]{1,0:T(8,128)} %get-tuple-element.124.refs_1_, ...), custom_call_target="tpu_custom_call" | custom-call | tf_op jit(solution)/shard_map/communicate_4/pallas_call | solution.py:556
  342.5 0.0 copy-start.1
  342.5 0.0 copy-start.2
  342.5 0.0 copy-done.4
  342.5 3.3 fusion.refs_20_
  345.7 0.0 copy-done.1
  345.7 0.0 copy-done.2
  345.8 0.0 copy-start.9
  345.8 0.0 copy-start.12
  345.8 2.3 bitcast_convert_fusion.1.refs_19_
  348.0 0.0 copy-done.9
  348.0 0.0 copy-done.12
  348.0 2.3 bitcast_convert_fusion.2
  350.3 64.5 %communicate_5.1 = (bf16[4,256,768]{2,1,0:T(8,128)(2,1)}, f32[256,1024]{1,0:T(8,128)}, bf16[256,1024]{1,0:T(8,128)(2,1)}, bf16[256,512]{1,0:T(8,128)(2,1)}, bf16...) custom-call(s32[8]{0:T(128)} %refs_0_.3, ...), custom_call_target="tpu_custom_call" | custom-call | tf_op jit(solution)/shard_map/communicate_5/pallas_call | solution.py:556
  414.8 0.0 copy-done
  414.9 0.0 copy-start.6
  414.9 0.0 copy-start.7
  414.9 0.0 copy-start.8
  414.9 4.5 bitcast_convert_fusion
  419.4 0.0 copy-done.6
  419.4 0.0 copy-done.7
  419.4 0.2 reshape.88
  419.7 0.2 copy.58
  419.8 0.0 copy-done.8
  419.8 0.0 copy-start.13
  419.8 0.2 reshape.86
  420.1 0.0 copy-start.11
  420.1 0.2 copy.49
  420.2 0.7 pad.15.refs_5_
  421.0 0.7 pad.14.refs_4_
  421.7 0.0 copy-done.10
  421.7 0.0 copy-done.14
  421.7 1.2 fusion.2
  422.9 0.0 copy-done.13
  422.9 0.0 copy-done.11
  422.9 1.2 fusion.1
  424.1 0.0 copy-done.3
  424.1 0.0 copy-done.5
  424.1 1.4 convolution_convert_fusion
  425.5 59.6 %communicate_6.1 = (f32[128,768]{1,0:T(8,128)}, f32[64,256]{1,0:T(8,128)}, f32[64,256]{1,0:T(8,128)}, f32[32,512]{1,0:T(8,128)}, f32[16,128]{1,0:T(8,128)}, /*index=5*/f32[8,256]{1,0:T(8,128)}) custom-call(bf16[8,128,768]{2,1,0:T(8,128)(2,1)} %bitcast.74, bf16[8,64,256]{2,1,0:T(8,128)(2,1)} %bitcast.79, bf16[8,64,256]{2,1,0:T(8,128)(2,1)} %bitcast.78, ...), custom_call_target="tpu_custom_call" | custom-call | tf_op jit(solution)/shard_map/communicate_6/pallas_call | solution.py:556
  485.2 4.2 finish.1
  489.4 1.3 fusion.3
  (11 shorter events, 0.0 us)
Async XLA Ops:
  7.2 169.8 %all-gather.9.cloned.1.call-start = ((), (), s32[]{:S(2)}) async-start(), calls=%async_computation | async-start | bytes 2621440 | tf_op jit(solution)/shard_map/all_gather | solution.py:2419
  64.7 112.3 %all-gather.11.cloned.1.call-start = ((), (), s32[]{:S(2)}) async-start(), calls=%async_computation.1 | async-start | bytes 5242880 | tf_op jit(solution)/shard_map/all_gather | solution.py:2419
  65.4 113.2 %all-gather.13.cloned.1.call-start = ((), (), s32[]{:S(2)}) async-start(), calls=%async_computation.2 | async-start | bytes 5242880 | tf_op jit(solution)/shard_map/all_gather | solution.py:2419
  66.2 284.1 %all-gather.15.cloned.1.call-start = ((), (), s32[]{:S(2)}) async-start(), calls=%async_computation.3 | async-start | bytes 7864320 | tf_op jit(solution)/shard_map/all_gather | solution.py:2450
  278.5 64.0 %copy-start.4 = (bf16[4,256,256]{2,1,0:T(8,128)(2,1)S(1)}, bf16[4,256,256]{2,1,0:T(8,128)(2,1)}, u32[]{:S(2)}) copy-start(bf16[4,256,256]{2,1,0:T(8,128)(2,1)} %get-tuple-element.146) | copy-start | bytes 1572868
  342.5 3.3 copy-start.1
  342.5 3.3 copy-start.2
  345.8 2.3 copy-start.9
  345.8 2.3 copy-start.12
  350.3 64.5 %copy-start = (bf16[4,256,1024]{2,1,0:T(8,128)(2,1)S(1)}, bf16[4,256,1024]{2,1,0:T(8,128)(2,1)}, u32[]{:S(2)}) copy-start(bf16[4,256,1024]{2,1,0:T(8,128)(2,1)} %get-tuple-element.101) | copy-start | bytes 6291460
  414.9 4.6 copy-start.6
  414.9 4.5 copy-start.7
  414.9 4.9 copy-start.8
  419.4 2.3 copy-start.10
  419.4 2.3 copy-start.14
  419.8 3.1 copy-start.13
  420.1 2.8 copy-start.11
  421.7 2.4 copy-start.3
  421.7 2.4 copy-start.5
Sparse Core Ops, SparseCore 0:
  64.8 30.9 all-gather.8
  97.4 33.8 all-gather.10
  132.9 45.7 all-gather.12
  228.7 42.7 all-gather.14

commit v5 on v4

--- a/solution.py
+++ b/solution.py
@@ -911,25 +911,18 @@
         hop.wait_send()
 
 
-def sent_home(dq, dkv, cosine, sine):
-    return Task(
-        home_body,
-        [dq, dkv, cosine, sine],
-        [jax.ShapeDtypeStruct((16, HALF + QUARTER, 128), jnp.bfloat16)],
-        [
-            pltpu.VMEM((8, 2, QUARTER, 128), jnp.float32),
-            pltpu.VMEM((8, 2, QUARTER, 128), jnp.bfloat16),
-            DMA((2,)),
-            DMA((8, 2)),
-            DMA((8, 2)),
-            DMA((16,)),
-            DMA((16,)),
-            DMA((16,)),
-            DMA((16,)),
-        ],
-        VMEM,
-        HBM,
-    )
+def home_scratch():
+    return [
+        pltpu.VMEM((8, 2, QUARTER, 128), jnp.float32),
+        pltpu.VMEM((8, 2, QUARTER, 128), jnp.bfloat16),
+        DMA((2,)),
+        DMA((8, 2)),
+        DMA((8, 2)),
+        DMA((16,)),
+        DMA((16,)),
+        DMA((16,)),
+        DMA((16,)),
+    ]
 
 
 def owned(ref, owner):
@@ -939,7 +932,7 @@
     return ref.at[:, pl.ds(pl.multiple_of(owner * width, width), width)]
 
 
-def seq_scatter_body(ins, outs, scratch):
+def seq_scatter_body(ins, outs, scratch, makers=None):
     count = len(ins)
     own, inbox, post, final = (scratch[k * count : (k + 1) * count] for k in range(4))
     l_sem, x_send, x_recv, z_send, z_recv = scratch[4 * count :]
@@ -951,6 +944,8 @@
     yield greet([(peer, head) for peer in [beside] + [2 * lax.rem(z + o, 4) + x for o in (1, 2, 3)]])
     hops = []
     for i in range(count):
+        if makers is not None and makers[i] is not None:
+            makers[i]()
         for o in (1, 2, 3, 0):
             zt = lax.rem(z + o, 4)
             hop = send(
@@ -996,15 +991,20 @@
         far.wait_send()
 
 
+def seq_scratch(shapes, kinds):
+    count = len(shapes)
+    return [
+        pltpu.VMEM((k,) + shape, kind) for k in (4, 4, 3, 3) for shape, kind in zip(shapes, kinds)
+    ] + [DMA((count, 4)), DMA((count, 4)), DMA((count, 4)), DMA((count, 3)), DMA((count, 3))]
+
+
 def seq_scattered(arrays):
-    count = len(arrays)
     shapes = [a.shape[1:] if a.ndim == 3 else (a.shape[0], a.shape[1] // 8) for a in arrays]
     return Task(
         seq_scatter_body,
         arrays,
         [jax.ShapeDtypeStruct(s, jnp.float32) for s in shapes],
-        [pltpu.VMEM((k,) + s, a.dtype) for k in (4, 4, 3, 3) for s, a in zip(shapes, arrays)]
-        + [DMA((count, 4)), DMA((count, 4)), DMA((count, 4)), DMA((count, 3)), DMA((count, 3))],
+        seq_scratch(shapes, [a.dtype for a in arrays]),
         HBM,
         VMEM,
     )
@@ -1126,69 +1126,144 @@
         below.wait_send()
 
 
-def all_scatter_body(tail, ins, outs, scratch):
-    count = len(ins)
-    split = count - tail
-    fixed = 4 * count + 5
-    sums = scratch[fixed : fixed + tail]
-    inbox = scratch[fixed + tail : fixed + 2 * tail]
-    h_send, h_recv = scratch[fixed + 2 * tail :]
+def inner_product(left, right, part):
+    blocked = len(part.shape) == 3
+    step = part.shape[1] if blocked else 128
+    for k in range(left.shape[2] // step):
+        total = None
+        for h in range(4):
+            one = lax.dot_general(
+                left[h, :, step * k : step * (k + 1)],
+                right[h],
+                (((0,), (0,)), ((), ())),
+                preferred_element_type=jnp.float32,
+            )
+            total = one if total is None else total + one
+        if blocked:
+            part[k] = total.astype(part.dtype)
+        else:
+            part[step * k : step * (k + 1), :] = total.astype(part.dtype)
+
+
+def last_body(utterances, ins, outs, scratch):
+    pairs, (small_ref, first_mods, last_mods) = ins[:-3], ins[-3:]
+    count = len(pairs) // 2
+    parts, scratch = scratch[: count + 2], scratch[count + 2 :]
+    sums, inbox = scratch[:3], scratch[3:5]
+    r_send, r_recv, h_send, h_recv = scratch[5:9]
     seq = lax.axis_index("seq")
     head = lax.axis_index("head")
     others = [lax.rem(head + o, 4) for o in (2, 1, 3)]
-    inner = seq_scatter_body(ins, list(outs[:split]) + list(sums), scratch[:fixed])
-    yield next(inner) + greet([(seq, other) for other in others])
+    goal = (2 * head + seq // 4, lax.rem(seq, 4))
+    source = (4 * lax.rem(seq, 2) + head, seq // 2)
+    stays = jnp.logical_and(goal[0] == seq, goal[1] == head)
+    columns = (first_mods.shape[1] + last_mods.shape[1]) // 32
+
+    @pl.when(jnp.logical_not(stays))
+    def _():
+        hail(*source)
+
+    def product(i):
+        return partial(inner_product, pairs[2 * i], pairs[2 * i + 1], parts[2 + i])
+
+    def make_small():
+        for k in range(32):
+            parts[0][k // 4, 16 * (k % 4) : 16 * (k % 4 + 1), :16] = small_ref[:, 16 * k : 16 * (k + 1)]
+
+    def make_mods():
+        wide = first_mods.shape[1]
+        for k in range(32):
+            low_end, high_end = columns * k, columns * (k + 1)
+            at = slice(utterances * (k % 4), utterances * (k % 4 + 1))
+            if high_end <= wide:
+                parts[1][k // 4, at, :columns] = first_mods[:utterances, low_end:high_end]
+            elif low_end >= wide:
+                parts[1][k // 4, at, :columns] = last_mods[:utterances, low_end - wide : high_end - wide]
+            else:
+                cut = wide - low_end
+                parts[1][k // 4, at, :cut] = first_mods[:utterances, low_end:]
+                parts[1][k // 4, at, cut:columns] = last_mods[:utterances, : high_end - wide]
+
+    order = list(range(2, count + 2)) + [0, 1]
+    makers = [product(i) for i in range(count)] + [make_small, make_mods]
+    results = list(outs[: count - 1]) + list(sums)
+    inner = seq_scatter_body([parts[k] for k in order], results, scratch[9:], makers)
+    yield next(inner) + greet([(seq, other) for other in others]) + jnp.where(stays, 0, 1)
+    parts[0][...] = jnp.zeros_like(parts[0])
+    parts[1][...] = jnp.zeros_like(parts[1])
     for _ in inner:
         yield
     hops = []
 
     def rows(i, h):
-        count_of = sums[i].shape[0] // 4
+        count_of = sums[1 + i].shape[0] // 4
         return pl.ds(pl.multiple_of(h * count_of, 8), count_of)
 
-    for i in range(tail):
+    @pl.when(jnp.logical_not(stays))
+    def _():
+        send(sums[0], outs[count - 1], r_send, r_recv, *goal).start()
+
+    @pl.when(stays)
+    def _():
+        outs[count - 1][...] = sums[0][...]
+
+    for i in range(2):
+        block = sums[1 + i]
         for o, other in enumerate(others):
             hop = send(
-                sums[i].at[rows(i, other)],
-                inbox[i].at[head],
-                h_send.at[i, o],
-                h_recv.at[i, head],
-                seq,
-                other,
+                block.at[rows(i, other)], inbox[i].at[head], h_send.at[i, o], h_recv.at[i, head], seq, other
             )
             hop.start()
             hops.append(hop)
-        inbox[i][head] = sums[i][rows(i, head), :]
-    for i in range(tail):
+        inbox[i][head] = block[rows(i, head), :]
+    for i in range(2):
         for o, other in enumerate(others):
             send(
-                sums[i].at[rows(i, other)],
+                sums[1 + i].at[rows(i, other)],
                 inbox[i].at[other],
                 h_send.at[i, o],
                 h_recv.at[i, other],
                 seq,
                 other,
             ).wait_recv()
-        outs[split + i][...] = inbox[i][0] + inbox[i][1] + inbox[i][2] + inbox[i][3]
+        outs[count + i][...] = inbox[i][0] + inbox[i][1] + inbox[i][2] + inbox[i][3]
     for hop in hops:
         hop.wait_send()
 
-
-def all_scattered(arrays, tail):
-    inner = seq_scattered(arrays)
-    last = inner.outs[len(arrays) - tail :]
-    short = [(o.shape[0] // 4,) + o.shape[1:] for o in last]
+    @pl.when(jnp.logical_not(stays))
+    def _():
+        hop = send(sums[0], outs[count - 1], r_send, r_recv, *goal)
+        hop.wait_recv()
+        hop.wait_send()
+
+
+def last_gradients(pairs, small, first_mods, last_mods, utterances):
+    columns = (first_mods.shape[1] + last_mods.shape[1]) // 32
+    shapes = []
+    for k, (left, right) in enumerate(pairs):
+        m, n = left.shape[2], right.shape[2]
+        shapes.append((m, n) if k in LAST_BY_COLUMNS else (8, m // 8, n))
+    blocks = [(8, 64, 128), (8, 4 * utterances, columns + -columns % 128)]
+    kept = [s[1:] if len(s) == 3 else (s[0], s[1] // 8) for s in shapes]
+    tails = [s[1:] for s in blocks]
+    short = [(s[0] // 4,) + s[1:] for s in tails]
+    kinds = [jnp.bfloat16] * len(shapes) + [jnp.float32] * 2
     return Task(
-        partial(all_scatter_body, tail),
-        arrays,
-        inner.outs[: len(arrays) - tail] + [jax.ShapeDtypeStruct(s, jnp.float32) for s in short],
-        inner.scratch
-        + [pltpu.VMEM(o.shape, jnp.float32) for o in last]
+        partial(last_body, utterances),
+        [a for pair in pairs for a in pair] + [small, first_mods, last_mods],
+        [jax.ShapeDtypeStruct(s, jnp.float32) for s in kept + short],
+        [pltpu.VMEM(s, jnp.float32) for s in blocks]
+        + [pltpu.VMEM(s, jnp.bfloat16) for s in shapes]
+        + [pltpu.VMEM(s, jnp.float32) for s in kept[-1:] + tails]
         + [pltpu.VMEM((4,) + s, jnp.float32) for s in short]
-        + [DMA((tail, 3)), DMA((tail, 4))],
-        HBM,
+        + [DMA, DMA, DMA((2, 3)), DMA((2, 4))]
+        + seq_scratch(kept + tails, kinds),
         VMEM,
-    )
+        VMEM,
+    )
+
+
+LAST_BY_COLUMNS = (0,)
 
 
 def places_of(rows, bounds):
@@ -1911,33 +1986,54 @@
     )
 
 
-def middle_kernel(
-    lengths,
-    tiles_ref,
-    out_ref,
-    up_hbm,
-    down_hbm,
-    hidden_ref,
-    mods_ref,
-    cot_ref,
-    d_ffn_ref,
-    context_ref,
-    layer_ref,
-    ffn_low_ref,
-    gelu_ref,
-    d_up_ref,
-    d_attn_ref,
-    d_middle_ref,
-    d_tiles_ref,
-    d_mods_ref,
-    up_ref,
-    down_ref,
-    attn_ref,
-    middle_ref,
-    rows_ref,
-    d_in_ref,
-    sems,
-):
+def middle_body(ins, outs, scratch):
+    (
+        lengths,
+        here_ref,
+        out_ref,
+        up_hbm,
+        down_hbm,
+        hidden_ref,
+        mods_ref,
+        cot_ref,
+        d_ffn_ref,
+    ) = ins
+    (
+        layer_ref,
+        d_attn_ref,
+        d_middle_ref,
+        d_mods_ref,
+        d_context_ref,
+        ffn_all,
+        context_all,
+        gelu_all,
+        d_up_all,
+    ) = outs
+    (
+        tiles_ref,
+        context_ref,
+        ffn_low_ref,
+        gelu_ref,
+        d_up_ref,
+        d_tiles_ref,
+        up_ref,
+        down_ref,
+        attn_ref,
+        middle_ref,
+        rows_ref,
+        d_in_ref,
+        sems,
+        own_sems,
+        feed_send,
+        feed_recv,
+    ) = scratch[:16]
+    rest = scratch[16:]
+    arrive = rows_heads_body(False, (here_ref,), (tiles_ref,), rest[:3])
+    depart = rows_heads_body(True, (d_tiles_ref,), (d_context_ref,), rest[3:6])
+    contexts = exchange_body((context_ref,), (context_all,), rest[6:9])
+    ffns = gather_body(2, (ffn_low_ref,), (ffn_all,), rest[9:16])
+    yield sum(next(one) for one in (arrive, depart, contexts, ffns))
+    seq, head, _, _, _ = head_places()
     bounds = bounds_of(lengths)
     copies = []
     for h in range(4):
@@ -1949,7 +2045,14 @@
         )
         for copy in copies[-1]:
             copy.start()
+    next(arrive)
     first = own_first()
+    rows_ref[...] = jnp.zeros_like(rows_ref)
+    d_in_ref[...] = jnp.zeros_like(d_in_ref)
+    attn_ref[...] = jnp.zeros_like(attn_ref)
+    d_mods_ref[...] = jnp.zeros_like(d_mods_ref)
+    for _ in arrive:
+        pass
     for pair in range(8):
         upper, lower = pair_up(
             tiles_ref[2 * pair].astype(jnp.float32), tiles_ref[2 * pair + 1].astype(jnp.float32)
@@ -1957,7 +2060,7 @@
         lanes = slice(128 * (pair % 2), 128 * (pair % 2) + 128)
         context_ref[pair // 2, pl.ds(0, HALF), lanes] = upper.astype(jnp.bfloat16)
         context_ref[pair // 2, pl.ds(HALF, HALF), lanes] = lower.astype(jnp.bfloat16)
-    attn_ref[...] = jnp.zeros_like(attn_ref)
+    next(contexts)
 
     def project_out(h, carry):
         attn_ref[...] += jnp.dot(context_ref[h], out_ref[h], preferred_element_type=jnp.float32)
@@ -1976,13 +2079,25 @@
         )
 
     by_rows(32, enter)
-    rows_ref[...] = jnp.zeros_like(rows_ref)
-    d_in_ref[...] = jnp.zeros_like(d_in_ref)
+    next(ffns)
     for h in range(4):
         for copy in copies[h]:
             copy.wait()
 
-    def feed(h, carry):
+    def passed(h):
+        return [
+            send(one.at[h], every.at[head], feed_send.at[k, h], feed_recv.at[k, head], seq, h)
+            for k, (one, every) in enumerate(((gelu_ref, gelu_all), (d_up_ref, d_up_all)))
+        ]
+
+    def kept():
+        return [
+            pltpu.make_async_copy(one.at[head], every.at[head], own_sems.at[k])
+            for k, (one, every) in enumerate(((gelu_ref, gelu_all), (d_up_ref, d_up_all)))
+        ]
+
+    def feed(i, carry):
+        h = lax.rem(head + 2 + i, 4)
         upward = jnp.dot(ffn_low_ref[...], up_ref[h], preferred_element_type=jnp.float32)
         value, slope = gelu_tanh(upward)
         gelu_ref[h] = value.astype(jnp.bfloat16)
@@ -1990,6 +2105,12 @@
             d_ffn_ref[...], down_ref[h], ROWS_TO_ROWS, preferred_element_type=jnp.float32
         )
         d_up_ref[h] = (grad * slope).astype(jnp.bfloat16)
+
+        @pl.when(h != head)
+        def _():
+            for hop in passed(h):
+                hop.start()
+
         rows_ref[...] += jnp.dot(gelu_ref[h], down_ref[h], preferred_element_type=jnp.float32)
         d_in_ref[...] += lax.dot_general(
             d_up_ref[h], up_ref[h], ROWS_TO_ROWS, preferred_element_type=jnp.float32
@@ -1997,7 +2118,9 @@
         return carry
 
     lax.fori_loop(0, 4, feed, 0)
-    d_mods_ref[...] = jnp.zeros_like(d_mods_ref)
+    for copy in kept():
+        copy.start()
+    next(ffns)
 
     def leave(at, i):
         spots = onehot_of(first + i, 32, bounds)
@@ -2020,27 +2143,46 @@
             even, odd = pair_up(piece[:HALF, lanes], piece[HALF:, lanes])
             d_tiles_ref[4 * h + 2 * k] = even.astype(jnp.bfloat16)
             d_tiles_ref[4 * h + 2 * k + 1] = odd.astype(jnp.bfloat16)
-
-
-def middle_part(lengths, tiles, out, up, down, hidden, mods, cot, d_ffn):
-    wide = hidden.shape[1]
-
-    return pl.pallas_call(
-        middle_kernel,
-        out_shape=[
-            low(4, ROWS, 256),
-            f32(ROWS, wide),
-            low(ROWS, wide),
-            low(4, ROWS, up.shape[2]),
-            low(4, ROWS, up.shape[2]),
-            low(ROWS, wide),
-            f32(ROWS, wide),
-            low(16, HALF, 128),
-            f32(16, 4 * wide),
-        ],
-        in_specs=[SMEM, VMEM, VMEM, HBM, HBM] + [VMEM] * 4,
-        out_specs=[VMEM] * 9,
-        scratch_shapes=[
+    next(depart)
+    for one in (ffns, contexts, depart):
+        for _ in one:
+            pass
+    for o in range(1, 4):
+        other = lax.rem(head + o, 4)
+        for k, (one, every) in enumerate(((gelu_ref, gelu_all), (d_up_ref, d_up_all))):
+            send(
+                one.at[other], every.at[other], feed_send.at[k, other], feed_recv.at[k, other], seq, other
+            ).wait_recv()
+        for hop in passed(other):
+            hop.wait_send()
+    for copy in kept():
+        copy.wait()
+
+
+def middle_part(lengths, here, out, up, down, hidden, mods, cot, d_ffn):
+    wide, short = hidden.shape[1], up.shape[2]
+    outs = [
+        (f32(ROWS, wide), VMEM),
+        (low(ROWS, wide), VMEM),
+        (f32(ROWS, wide), VMEM),
+        (f32(16, 4 * wide), VMEM),
+        (low(8, QUARTER, 128), HBM),
+        (low(4, ROWS, wide), HBM),
+        (low(4, ROWS, 256), HBM),
+        (low(4, ROWS, short), HBM),
+        (low(4, ROWS, short), HBM),
+    ]
+    return Task(
+        middle_body,
+        [lengths, here, out, up, down, hidden, mods, cot, d_ffn],
+        [o for o, _ in outs],
+        [
+            pltpu.VMEM((16, HALF, 128), jnp.bfloat16),
+            pltpu.VMEM((4, ROWS, 256), jnp.bfloat16),
+            pltpu.VMEM((ROWS, wide), jnp.bfloat16),
+            pltpu.VMEM((4, ROWS, short), jnp.bfloat16),
+            pltpu.VMEM((4, ROWS, short), jnp.bfloat16),
+            pltpu.VMEM((16, HALF, 128), jnp.bfloat16),
             pltpu.VMEM(up.shape, jnp.bfloat16),
             pltpu.VMEM(down.shape, jnp.bfloat16),
             pltpu.VMEM((ROWS, wide), jnp.float32),
@@ -2048,17 +2190,28 @@
             pltpu.VMEM((ROWS, wide), jnp.float32),
             pltpu.VMEM((ROWS, wide), jnp.float32),
             DMA((8,)),
-        ],
-        compiler_params=LOCAL,
-        name="middle_part",
-    )(lengths, tiles, out, up, down, hidden, mods, cot, d_ffn)
+            DMA((2,)),
+            DMA((2, 4)),
+            DMA((2, 4)),
+        ]
+        + [DMA, DMA((16,)), DMA((16,))]
+        + [DMA, DMA((16,)), DMA((16,))]
+        + [DMA((1,)), DMA((1, 3)), DMA((1, 4))]
+        + gather_scratch(1, 2),
+        [SMEM, HBM, VMEM, HBM, HBM] + [VMEM] * 4,
+        [s for _, s in outs],
+    )
 
 
 def back_body(ins, outs, scratch):
     (
         lengths,
-        tiles_ref,
-        qkv_ref,
+        dq_ref,
+        dkv_ref,
+        k_cos,
+        k_sin,
+        d_attn_ref,
+        qkv_hbm,
         hidden_ref,
         d_middle_ref,
         mods_ref,
@@ -2074,21 +2227,42 @@
         gain_ref,
         taps_ref,
         ext_ref,
+        attn_hbm,
+        grn_ref,
+        d_ffn_ref,
+        up_part,
+        gelu_all,
     ) = ins
     (
-        d_qkv_ref,
         mel_ref,
-        d_joined_ref,
-        d_branch_ref,
-        d_expanded_ref,
         text_ref,
         d_mods_ref,
         small_ref,
         own_ref,
-        d_qkv_all,
+        qkv_grad,
+        d_attn_all,
+        d_joined_all,
         d_branch_all,
         d_expanded_all,
+        grn_all,
+        up_grad,
+        down_grad,
     ) = outs
+    (
+        tiles_ref,
+        qkv_ref,
+        attn_all,
+        in_sems,
+        d_joined_ref,
+        d_branch_ref,
+        d_expanded_ref,
+        d_qkv_ref,
+        d_qkv_all,
+        qkv_part,
+        d_ffn_all,
+        down_part,
+    ) = scratch[:12]
+    scratch = scratch[12:]
     d_in_ref, d_text_ref, d_grn_ref, sums_ref, total_ref, d_norm_ref, ratio_ref, d_conv_ref, d_ext_ref = (
         scratch[:9]
     )
@@ -2098,9 +2272,41 @@
     branch_out = gather_body(1, (d_branch_ref,), (d_branch_all,), rest[3:10])
     expanded_out = exchange_body((d_expanded_ref,), (d_expanded_all,), rest[10:13])
     sums = all_sum_body((sums_ref,), (total_ref, own_ref), rest[13:22])
+    joined_out = exchange_body((d_joined_ref,), (d_joined_all,), rest[22:25])
     rim = rim_body(d_conv_ref, d_ext_ref, rim_sems)
-    running = (swap, branch_out, expanded_out, sums, rim)
+    scatter = seq_scatter_body((qkv_part,), (qkv_grad,), rest[25:34])
+    home = home_body((dq_ref, dkv_ref, k_cos, k_sin), (tiles_ref,), rest[34:43])
+    attns = gather_body(2, (d_attn_ref,), (d_attn_all,), rest[43:50])
+    d_ffns = gather_body(2, (d_ffn_ref,), (d_ffn_all,), rest[50:57])
+    grns = exchange_body((grn_ref,), (grn_all,), rest[57:60])
+    early = seq_scatter_body(
+        (up_part, down_part),
+        (up_grad, down_grad),
+        rest[60:],
+        [None, partial(inner_product, gelu_all, d_ffn_all, down_part)],
+    )
+    running = (
+        swap, branch_out, expanded_out, sums, rim, joined_out, scatter, home, attns, d_ffns, grns, early
+    )
+    arriving = [
+        pltpu.make_async_copy(qkv_hbm, qkv_ref, in_sems.at[0]),
+        pltpu.make_async_copy(attn_hbm, attn_all, in_sems.at[1]),
+    ]
+    for copy in arriving:
+        copy.start()
     yield sum(next(one) for one in running)
+    next(home)
+    next(attns)
+    next(grns)
+    next(d_ffns)
+    for _ in home:
+        pass
+    for _ in attns:
+        pass
+    for _ in d_ffns:
+        pass
+    for copy in arriving:
+        copy.wait()
     first = own_first()
     for pair in range(8):
         even, odd = tiles_ref.at[2 * pair], tiles_ref.at[2 * pair + 1]
@@ -2118,6 +2324,7 @@
         d_qkv_ref[pair // 2, :, 256 + at : 384 + at] = keys.astype(jnp.bfloat16)
         d_qkv_ref[pair // 2, :, 512 + at : 640 + at] = values.astype(jnp.bfloat16)
     next(swap)
+    next(early)
     d_in_ref[...] = jnp.zeros_like(d_in_ref)
 
     def enter(h, carry):
@@ -2138,17 +2345,22 @@
         d_in = d_in_ref[at, :]
         mel = d_middle_ref[at, :] + normed_back(d_in * (1.0 + pick(spots, scale)), unit, inverse)
         mel_ref[at, :] = mel
-        d_joined_ref[at, :] = mel.astype(jnp.bfloat16)
+        for h in range(4):
+            d_joined_ref[h, at, :] = mel[:, 256 * h : 256 * (h + 1)].astype(jnp.bfloat16)
         for k, grad in enumerate((d_in, d_in * unit)):
             d_mods_ref[:, 1024 * k : 1024 * (k + 1)] += sum_by(spots, grad)
 
     by_rows(32, hidden_back)
-    d_text = lax.dot_general(
-        d_joined_ref[...], join_ref[...], ROWS_TO_ROWS, preferred_element_type=jnp.float32
-    )
+    d_text = 0.0
+    for h in range(4):
+        d_text += lax.dot_general(
+            d_joined_ref[h],
+            join_ref[:, 256 * h : 256 * (h + 1)],
+            ROWS_TO_ROWS,
+            preferred_element_type=jnp.float32,
+        )
     d_text_ref[...] = d_text
     d_branch_ref[...] = (mask_ref[:, :1] * d_text).astype(jnp.bfloat16)
-    next(branch_out)
     onehot = onehot_of(first, ROWS, bounds)
     norm, mean = ratio_of(squares_ref[...])
     ratio_ref[...] = norm / mean
@@ -2173,10 +2385,32 @@
         return carry
 
     lax.fori_loop(0, 4, grn_back, 0)
+    next(early)
+    next(early)
     next(sums)
+    for _ in swap:
+        pass
+
+    def qkv_grads(owner, carry):
+        lanes = pl.ds(pl.multiple_of(owner * 128, 128), 128)
+        total = 0.0
+        for h in range(4):
+            total += lax.dot_general(
+                attn_all[h, :, lanes],
+                d_qkv_all[h],
+                (((0,), (0,)), ((), ())),
+                preferred_element_type=jnp.float32,
+            )
+        qkv_part[owner] = total.astype(jnp.bfloat16)
+        return carry
+
+    lax.fori_loop(0, 8, qkv_grads, 0)
+    next(scatter)
     yield
     for _ in sums:
         pass
+    next(joined_out)
+    next(branch_out)
     d_ratio = total_ref[...]
     d_mean = -jnp.sum(jnp.sum(d_ratio * norm, axis=2, keepdims=True), axis=0, keepdims=True) / (
         mean * mean
@@ -2211,6 +2445,7 @@
 
     by_rows(32, norm_back)
     next(rim)
+    next(scatter)
     yield
 
     def taps_back(at, i):
@@ -2239,7 +2474,7 @@
         text_ref[at, :] = total
 
     by_rows(32, text_back)
-    for one in (swap, branch_out, expanded_out):
+    for one in (early, scatter, grns, branch_out, joined_out, expanded_out):
         for _ in one:
             pass
 
@@ -2247,24 +2482,37 @@
 def text_backward(operands):
     wide, width = 1024, 512
     outs = [
-        (low(4, ROWS, 768), VMEM),
         (f32(ROWS, wide), VMEM),
-        (low(ROWS, wide), VMEM),
-        (low(ROWS, width), VMEM),
-        (low(4, ROWS, 256), VMEM),
         (f32(ROWS, width), VMEM),
         (f32(16, 2 * wide), VMEM),
         (f32(16, width), VMEM),
         (f32(16, 256), VMEM),
-        (low(4, ROWS, 768), HBM),
+        (f32(128, 768), VMEM),
+        (low(4, ROWS, wide), HBM),
+        (low(4, ROWS, 256), HBM),
         (low(4, ROWS, width), HBM),
         (low(4, ROWS, 256), HBM),
+        (low(4, ROWS, 256), HBM),
+        (f32(128, 512), VMEM),
+        (f32(512, 128), VMEM),
     ]
     return Task(
         back_body,
         operands,
         [o for o, _ in outs],
         [
+            room(low(16, HALF + QUARTER, 128)),
+            room(low(4, 3, wide, 256)),
+            room(low(4, ROWS, wide)),
+            DMA((2,)),
+            room(low(4, ROWS, 256)),
+            room(low(ROWS, width)),
+            room(low(4, ROWS, 256)),
+            room(low(4, ROWS, 768)),
+            room(low(4, ROWS, 768)),
+            room(low(8, 128, 768)),
+            room(low(4, ROWS, wide)),
+            room(low(512, wide)),
             pltpu.VMEM((ROWS, wide), jnp.float32),
             pltpu.VMEM((ROWS, width), jnp.float32),
             pltpu.VMEM((4, ROWS, 256), jnp.float32),
@@ -2279,13 +2527,21 @@
         + [DMA((1,)), DMA((1, 3)), DMA((1, 4))]
         + gather_scratch(1, 1)
         + [DMA((1,)), DMA((1, 3)), DMA((1, 4))]
-        + all_sum_scratch(16, 256),
-        [SMEM] + [VMEM] * (len(operands) - 1),
+        + all_sum_scratch(16, 256)
+        + [DMA((1,)), DMA((1, 3)), DMA((1, 4))]
+        + seq_scratch([(128, 768)], [jnp.bfloat16])
+        + home_scratch()
+        + gather_scratch(1, 2)
+        + gather_scratch(1, 2)
+        + [DMA((1,)), DMA((1, 3)), DMA((1, 4))]
+        + seq_scratch([(128, 512), (512, 128)], [jnp.bfloat16] * 2),
+        [SMEM] + [VMEM] * 4 + [HBM, HBM] + [VMEM] * 15 + [HBM] * 4 + [VMEM],
         [s for _, s in outs],
     )
 
 
-def finish_kernel(qkv_ref, small_ref, mod_ref, embed_ref, sums_ref, *refs):
+def finish_kernel(held, qkv_ref, small_ref, mod_ref, embed_ref, sums_ref, *refs):
+    refs = refs[held:]
     plain = refs[: (len(refs) - 6) // 2]
     outs = refs[len(plain) :]
     for source, target in zip(plain, outs):
@@ -2308,10 +2564,10 @@
     o_pair[...] = sums_ref[8:10, :]
 
 
-def finish(qkv, small, mod, embed, sums, plain, columns):
+def finish(qkv, small, mod, embed, sums, held, plain, columns):
     rows = qkv.shape[0]
     return pl.pallas_call(
-        finish_kernel,
+        partial(finish_kernel, len(held)),
         out_shape=[like(a) for a in plain]
         + [
             f32(3, rows, 256),
@@ -2321,11 +2577,11 @@
             f32(columns, embed.shape[1]),
             f32(2, 256),
         ],
-        in_specs=[VMEM] * (5 + len(plain)),
+        in_specs=[VMEM] * 5 + [HBM] * len(held) + [VMEM] * len(plain),
         out_specs=[VMEM] * (len(plain) + 6),
         compiler_params=LOCAL,
         name="finish",
-    )(qkv, small, mod, embed, sums, *plain)
+    )(qkv, small, mod, embed, sums, *held, *plain)
 
 
 def blocks_of(array):
@@ -2412,81 +2668,77 @@
     )
 
     qkv_near = qkv_weight.transpose(1, 0, 2)
-    attn_all, out_near, up_near, down_near = lax.optimization_barrier(
-        (attn_all, out_weight, up_weight, down_weight)
-    )
-    out_full, up_full, down_full = (
-        lax.all_gather(w, "head", axis=0) for w in (out_near, up_near, down_near)
-    )
-    (packed,), (query_cos, query_sin, key_cos, key_sin), (d_ffn_all,) = communicate(
+    attn_all, up_near, down_near = lax.optimization_barrier((attn_all, up_weight, down_weight))
+    up_full, down_full = (lax.all_gather(w, "head", axis=0) for w in (up_near, down_near))
+    (packed,), (query_cos, query_sin, key_cos, key_sin), (join_all, out_full) = communicate(
         [
             spread_out(rows_of(attn_all), qkv_near, own_cos, own_sin),
             turns(lengths, rates),
-            gathered([d_ffn_low]),
+            gathered([join_low, out_weight]),
         ],
         1,
     )
     context_here, logsum = attend(lengths, packed)
-    (context_tiles,), (grn_all,) = communicate([to_rows(context_here), exchanged([grn_low])], 2)
 
     (
-        context_blocks,
-        layer_output,
-        ffn_low,
-        gelu_low,
-        d_up_low,
-        d_attn_low,
-        d_middle,
-        d_context_tiles,
-        d_mods_middle,
-    ) = middle_part(
-        lengths, context_tiles, out_full, up_full, down_full, hidden, mods, cotangent, d_ffn_low
-    )
-
-    (d_context,), (ffn_all,), (context_all,) = communicate(
-        [to_heads(d_context_tiles), gathered([ffn_low]), exchanged([context_blocks])], 3
-    )
+        (
+            layer_output,
+            d_attn_low,
+            d_middle,
+            d_mods_middle,
+            d_context,
+            ffn_all,
+            context_all,
+            gelu_all,
+            d_up_all,
+        ),
+    ) = communicate(
+        [
+            middle_part(
+                lengths,
+                context_here,
+                out_full,
+                up_full,
+                down_full,
+                hidden,
+                mods,
+                cotangent,
+                d_ffn_low,
+            )
+        ],
+        2,
+    )
+
     d_context, qkv_late = lax.optimization_barrier((d_context, qkv_near))
     qkv_full = lax.all_gather(qkv_late, "head", axis=0)
     d_query, d_pair = attend_back(lengths, packed, d_context, logsum, query_cos, query_sin)
-    (d_tiles,), (d_attn_all,), (gelu_all, d_up_all) = communicate(
-        [
-            sent_home(d_query, d_pair, key_cos, key_sin),
-            gathered([d_attn_low]),
-            exchanged([gelu_low, d_up_low]),
-        ],
-        4,
-    )
-    ffn_all, d_ffn_all, context_all, d_attn_all, gelu_all, d_up_all, grn_all, text_all = (
-        rows_of(g)
-        for g in (ffn_all, d_ffn_all, context_all, d_attn_all, gelu_all, d_up_all, grn_all, text_all)
-    )
-
-    def part(left, right):
-        return inner_rows(left, right).astype(jnp.bfloat16)
-
+    up_part = blocks_of(inner_rows(rows_of(ffn_all), rows_of(d_up_all)).astype(jnp.bfloat16))
     (
         (
-            _,
             grad_mel,
-            d_joined_low,
-            _,
-            _,
             grad_text,
             d_mods_attn,
             small,
             own_sums,
-            d_qkv_all,
+            qkv,
+            d_attn_all,
+            d_joined_all,
             d_branch_all,
             d_expanded_all,
+            grn_all,
+            up,
+            down,
         ),
-        (up, down, out),
     ) = communicate(
         [
             text_backward(
                 [
                     lengths,
-                    d_tiles,
+                    d_query,
+                    d_pair,
+                    key_cos,
+                    key_sin,
+                    d_attn_low,
                     qkv_full,
                     hidden,
                     d_middle,
@@ -2503,42 +2755,34 @@
                     norm_gain[None, :],
                     conv_weight,
                     extended,
+                    attn_all,
+                    grn_low,
+                    d_ffn_low,
+                    up_part,
+                    gelu_all,
                 ]
-            ),
-            seq_scattered(
-                [
-                    blocks_of(part(ffn_all, d_up_all)),
-                    part(gelu_all, d_ffn_all),
-                    part(context_all, d_attn_all),
-                ]
-            ),
-        ],
-        5,
-    )
-
-    small = small.reshape(16, 8, 4, 16).transpose(1, 2, 0, 3).reshape(8, 64, 16)
-    small = jnp.pad(small, ((0, 0), (0, 0), (0, 112)))
-    d_mods = jnp.concatenate([d_mods_attn, d_mods_middle], axis=1)[:utterances]
-    columns = d_mods.shape[1] // 32
-    d_mods = d_mods.reshape(utterances, 8, 4, columns).transpose(1, 2, 0, 3)
-    d_mods = jnp.pad(
-        d_mods.reshape(8, 4 * utterances, columns), ((0, 0), (0, 0), (0, -columns % 128))
-    )
-    ((qkv, shrink, expand, join, small, mod),) = communicate(
-        [
-            all_scattered(
-                [
-                    blocks_of(part(rows_of(attn_all), rows_of(d_qkv_all))),
-                    blocks_of(part(rows_of(d_branch_all), grn_all)),
-                    blocks_of(part(text_all, rows_of(d_expanded_all))),
-                    blocks_of(part(d_joined_low, join_low)),
-                    small,
-                    d_mods,
-                ],
-                3,
             )
         ],
-        6,
+        3,
+    )
+
+    columns = mods.shape[1] // 32
+    ((out, shrink, expand, join, small, mod),) = communicate(
+        [
+            last_gradients(
+                [
+                    (context_all, d_attn_all),
+                    (d_branch_all, grn_all),
+                    (text_all, d_expanded_all),
+                    (d_joined_all, join_all),
+                ],
+                small,
+                d_mods_attn,
+                d_mods_middle,
+                utterances,
+            )
+        ],
+        4,
     )
     grad_text, grad_mel, expand, shrink, join, out, up, down, qkv, conv, gain, bias, mod, pair = finish(
         qkv,
@@ -2546,6 +2790,7 @@
         mod,
         time_embed,
         own_sums,
+        [],
         [grad_text, grad_mel, expand, shrink, join, out, up, down],
         columns,
     )

time: 500 us -> 460 us (0.920)
  Pallas kernels: 459 us -> 432 us
  matrix products: 16.1 us -> 2.25 us
    pallas_call x2 -> x1, Pallas kernels: 24.2 us -> 4.27 us  [finish(): pl.pallas_call(partial(finish_kernel, len(held)), out_shape=[like(a) for...]
    dot_general x7 -> x1, matrix products: 16.1 us -> 2.25 us  [inner_rows(): lax.dot_general(left, right, (((0,), (0,)), ((), ())), preferred_element_...]
    pallas_call x7 -> x5, Pallas kernels: 349 us -> 338 us  [communicate(): pl.pallas_call(kernel, out_shape=[o for t in tasks for o in t.outs], in_s...]
  transfers between devices with their start and end apart: 4 -> 3, of which waited for: 1 -> 0; matrix products, arithmetic and copies ran while one was open for 2% -> 0% of each run, Pallas kernels for 45% -> 30%
where the time goes in v5:
time: 460 us; the launch traced here: 453 us
  Pallas kernels  432 us (94%)
  between operations  14.3 us (3%)
    pallas_call x5, Pallas kernels, communicate(): pl.pallas_call(kernel, out_shape=[o for t in tasks for o in t.outs], in_s...  338 us
    pallas_call x1, Pallas kernels, attend_back(): pl.pallas_call(attend_back_kernel, out_shape=[jax.ShapeDtypeStruct((8, QU...  52.1 us
    pallas_call x1, Pallas kernels, attend(): pl.pallas_call(attend_kernel, out_shape=[jax.ShapeDtypeStruct((8, QUARTER...  37.9 us
  transfers between devices with their start and end apart: 3, of which 0 were waited for; matrix products, arithmetic and copies ran while one was open for 0% of the time, Pallas kernels for 30%

profile of v5, /device:TPU:0, one launch (start us, length us, event | category | flops | bytes accessed | tf_op | source)
XLA Modules:
  0.0 453.1 jit_solution(3266247488171261381)
XLA Ops:
  7.2 0.0 all-gather.7.cloned.1.call-start
  7.2 0.1 tile.8
  7.3 0.1 stack_tile.3
  7.4 0.6 select_maximum_fusion.refs_16_.refs_5_
  8.0 56.6 %communicate_0.1 = (f32[272,512]{1,0:T(8,128)}, f32[256,512]{1,0:T(8,128)}, f32[256,128]{1,0:T(8,128)}, bf16[4,512,256]{2,1,0:T(8,128)(2,1)}, bf16[4,256,512]{2,...) custom-call(s32[8]{0:T(128)} %refs_0_.5, ...), custom_call_target="tpu_custom_call" | custom-call | tf_op jit(solution)/shard_map/communicate_0/pallas_call | solution.py:556
  64.7 0.0 all-gather.7.cloned.1.call-update
  64.7 0.0 all-gather.9.cloned.1.call-start
  64.8 0.7 all-gather.9.cloned.1.call-update
  65.5 0.0 all-gather.11.cloned.1.call-start
  65.5 46.3 %communicate_1.1 = (bf16[8,1536,128]{2,1,0:T(8,128)(2,1)}, f32[8,256,128]{2,1,0:T(8,128)}, f32[8,256,128]{2,1,0:T(8,128)}, f32[8,2,256,128]{3,2,1,0:T(8,128)}, f...) custom-call(bf16[1024,1024]{1,0:T(8,128)(2,1)} %bitcast.25, ...), custom_call_target="tpu_custom_call" | custom-call | tf_op jit(solution)/shard_map/communicate_1/pallas_call | solution.py:556
  111.9 37.9 %attend.1 = (bf16[8,256,128]{2,1,0:T(8,128)(2,1)}, f32[8,2,8,256]{3,2,1,0:T(8,128)}) custom-call(s32[8]{0:T(128)} %refs_0_.5, bf16[8,1536,128]{2,1,0:T(8,128)(2,1)} %get-tuple-element.97.x_ref), custom_call_target="tpu_custom_call" | custom-call | tf_op jit(solution)/shard_map/attend/pallas_call | solution.py:1505
  149.8 0.0 all-gather.7.cloned.1.call-done
  149.8 0.0 all-gather.9.cloned.1.call-done
  149.8 69.8 %communicate_2.1 = (f32[256,1024]{1,0:T(8,128)}, bf16[256,1024]{1,0:T(8,128)(2,1)}, f32[256,1024]{1,0:T(8,128)}, f32[16,4096]{1,0:T(8,128)}, bf16[8,256,128]{2,1...) custom-call(s32[8]{0:T(128)} %refs_0_.5, ...), custom_call_target="tpu_custom_call" | custom-call | tf_op jit(solution)/shard_map/communicate_2/pallas_call | solution.py:556
  219.6 0.0 all-gather.11.cloned.1.call-update
  219.6 0.0 copy-start.1
  219.6 0.0 copy-start.2
  219.6 52.1 %attend_back.1 = (bf16[8,256,128]{2,1,0:T(8,128)(2,1)}, f32[9216,128]{1,0:T(8,128)}) custom-call(s32[8]{0:T(128)} %refs_0_.5, bf16[8,1536,128]{2,1,0:T(8,128)(2,1)} %get-tuple-element.97.x_ref, bf16[8,256,128]{2,1,0:T(8,128)(2,1)} %get-tuple-element.107.g_ref, f32[8,2,8,256]{3,2,1,0:T(8,128)} %get-tuple-element.108.l_ref, ...), custom_call_target="tpu_custom_call" | custom-call | tf_op jit(solution)/shard_map/attend_back/pallas_call | solution.py:1575
  271.7 0.0 copy-done.1
  271.7 0.0 copy-done.2
  271.7 2.3 bitcast_convert_fusion
  274.0 0.0 all-gather.11.cloned.1.call-done
  274.0 126.5 %communicate_3.1 = (f32[256,1024]{1,0:T(8,128)}, f32[256,512]{1,0:T(8,128)}, f32[16,2048]{1,0:T(8,128)}, f32[16,512]{1,0:T(8,128)}, f32[16,256]{1,0:T(8,128)}, /...) custom-call(s32[8]{0:T(128)} %refs_0_.5, ...), custom_call_target="tpu_custom_call" | custom-call | tf_op jit(solution)/shard_map/communicate_3/pallas_call | solution.py:556
  400.5 39.0 %communicate_4.1 = (f32[256,128]{1,0:T(8,128)}, f32[64,256]{1,0:T(8,128)}, f32[64,256]{1,0:T(8,128)}, f32[32,512]{1,0:T(8,128)}, f32[16,128]{1,0:T(8,128)}, /*index=5*/f32[8,256]{1,0:T(8,128)}) custom-call(bf16[4,256,256]{2,1,0:T(8,128)(2,1)} %get-tuple-element.132.refs_0_, bf16[4,256,1024]{2,1,0:T(8,128)(2,1)} %get-tuple-element.133.refs_1_, ...), custom_call_target="tpu_custom_call" | custom-call | tf_op jit(solution)/shard_map/communicate_4/pallas_call | solution.py:556
  439.5 0.0 copy-start
  439.5 4.3 finish.1
  443.8 1.3 fusion
  445.1 0.0 copy-done
  445.1 1.0 copy.39
  (4 shorter events, 0.0 us)
Async XLA Ops:
  7.2 142.6 %all-gather.7.cloned.1.call-start = ((), (), s32[]{:S(2)}) async-start(), calls=%async_computation | async-start | bytes 5242880 | tf_op jit(solution)/shard_map/all_gather | solution.py:2672
  64.7 85.1 %all-gather.9.cloned.1.call-start = ((), (), s32[]{:S(2)}) async-start(), calls=%async_computation.1 | async-start | bytes 5242880 | tf_op jit(solution)/shard_map/all_gather | solution.py:2672
  65.5 208.5 %all-gather.11.cloned.1.call-start = ((), (), s32[]{:S(2)}) async-start(), calls=%async_computation.2 | async-start | bytes 7864320 | tf_op jit(solution)/shard_map/all_gather | solution.py:2713
  219.6 52.1 %copy-start.1 = (bf16[4,256,1024]{2,1,0:T(8,128)(2,1)S(1)}, bf16[4,256,1024]{2,1,0:T(8,128)(2,1)}, u32[]{:S(2)}) copy-start(bf16[4,256,1024]{2,1,0:T(8,128)(2,1)} %get-tuple-element.128) | copy-start | bytes 6291460
  219.6 52.1 %copy-start.2 = (bf16[4,256,512]{2,1,0:T(8,128)(2,1)S(1)}, bf16[4,256,512]{2,1,0:T(8,128)(2,1)}, u32[]{:S(2)}) copy-start(bf16[4,256,512]{2,1,0:T(8,128)(2,1)} %get-tuple-element.129) | copy-start | bytes 3145732
  439.5 5.6 %copy-start = (f32[256,1024]{1,0:T(8,128)S(1)}, f32[256,1024]{1,0:T(8,128)}, u32[]{:S(2)}) copy-start(f32[256,1024]{1,0:T(8,128)} %get-tuple-element.186) | copy-start | bytes 3145732
Sparse Core Ops, SparseCore 0:
  64.8 47.1 all-gather.6
  113.6 33.8 all-gather.8
  219.7 46.3 all-gather.10

commit v6 on v5

--- a/solution.py
+++ b/solution.py
@@ -581,7 +581,7 @@
     return cuts if rows % (16 * cuts) == 0 else 1
 
 
-def gather_body(most, ins, outs, scratch):
+def gather_body(most, ins, outs, scratch, patience=1):
     local, y_send, y_recv, c_send, c_recv, f_send, f_recv = scratch
     seq, head, mate, across, _ = head_places()
     yield greet([(seq, mate), (seq, across)])
@@ -603,7 +603,8 @@
         own = pltpu.make_async_copy(ins[i], outs[i].at[head], local.at[i])
         own.start()
         waits += [beside, own]
-    yield
+    for _ in range(patience):
+        yield
     for i, k, part, hop in hops:
         hop.wait_recv()
         onward = send(
@@ -623,10 +624,10 @@
         hop.wait_send()
 
 
-def gathered(arrays, cuts=2):
+def gathered(arrays, cuts=2, patience=1):
     count = len(arrays)
     return Task(
-        partial(gather_body, cuts),
+        partial(gather_body, cuts, patience=patience),
         arrays,
         [like(a, 4, *a.shape) for a in arrays],
         [
@@ -641,7 +642,7 @@
     )
 
 
-def exchange_body(ins, outs, scratch):
+def exchange_body(ins, outs, scratch, patience=2):
     local, h_send, h_recv = scratch
     seq, head, mate, across, diagonal = head_places()
     others = (across, diagonal, mate)
@@ -660,8 +661,8 @@
     ]
     for own in owns:
         own.start()
-    yield
-    yield
+    for _ in range(patience):
+        yield
     for o, other in enumerate(others):
         for i in range(len(ins)):
             send(
@@ -673,10 +674,10 @@
         hop.wait_send()
 
 
-def exchanged(arrays):
+def exchanged(arrays, patience=2):
     count = len(arrays)
     return Task(
-        exchange_body,
+        partial(exchange_body, patience=patience),
         arrays,
         [like(a) for a in arrays],
         [DMA((count,)), DMA((count, 3)), DMA((count, 4))],
@@ -837,12 +838,13 @@
 
 
 def home_body(ins, outs, scratch):
-    (dq_ref, dkv_ref, c_ref, s_ref), (o_ref,) = ins, outs
-    inbox, post, local, p_send, p_recv, k_send, q_send, k_recv, q_recv = scratch
+    (lengths, rates_ref, dq_ref, dkv_hbm), (o_ref,) = ins, outs
+    inbox, kept, post, cosines, sines, local, own_sems, p_send, p_recv, k_send, q_send, k_recv, q_recv = scratch
     seq, head, mate, _, _ = head_places()
     core = lax.rem(head, 2)
     plane = head // 2
     mine = 8 * plane + seq
+    bounds = bounds_of(lengths)
     q_part, k_part = pl.ds(0, HALF), pl.ds(HALF, QUARTER)
     yield greet(
         [(lax.rem(seq + o, 8), core + 2 * p) for o in range(1, 8) for p in range(2)]
@@ -854,10 +856,10 @@
     def rows(s, p, c):
         return pl.ds(pl.multiple_of(s * 1024 + (c + 2 * p) * QUARTER, QUARTER), QUARTER)
 
-    halves = []
+    halves, owns = [], []
     for s, p in places:
         hop = send(
-            dkv_ref.at[rows(s, p, 1 - core)],
+            dkv_hbm.at[rows(s, p, 1 - core)],
             inbox.at[s, p],
             p_send.at[s, p],
             p_recv.at[s, p],
@@ -866,6 +868,10 @@
         )
         hop.start()
         halves.append(hop)
+        owns.append(
+            pltpu.make_async_copy(dkv_hbm.at[rows(s, p, core)], kept.at[s, p], own_sems.at[s, p])
+        )
+        owns[-1].start()
     finals = []
     for s, p in places[:-1]:
         g = 8 * p + s
@@ -882,11 +888,25 @@
     )
     own.start()
     yield
+    def table(i, at):
+        k = at + i
+        o = jnp.where(k < 14, 4 + jnp.where(lax.rem(k // 2, 2) == 1, -1, 1) * ((k // 2 + 1) // 2), 0)
+        s = lax.rem(seq + o, 8)
+        p = lax.rem(plane + 1 - lax.rem(k, 2), 2)
+        first = s * 1024 + (core + 2 * p) * QUARTER
+        angles = places_of(column(first, QUARTER), bounds) * rates_ref[1:2, :]
+        cosines[i], sines[i] = jnp.cos(angles), jnp.sin(angles)
+        return at
+
     for k, (s, p) in enumerate(places):
         g = 8 * p + s
+        if k % 2 == 0:
+            lax.fori_loop(0, 2, table, k)
+        cosine, sine = cosines[k % 2], sines[k % 2]
+        owns[k].wait()
         halves[k].wait_recv()
-        total = dkv_ref[rows(s, p, core), :] + inbox[s, p]
-        total = total * c_ref[s, p] + turn(total * s_ref[s, p], -1)
+        total = kept[s, p] + inbox[s, p]
+        total = total * cosine + turn(total * sine, -1)
         post[s, p] = total.astype(jnp.bfloat16)
         if k < 15:
             out = send(
@@ -897,12 +917,12 @@
                 (out, send(post.at[s, p], o_ref.at[g, k_part], k_send.at[g], k_recv.at[g], s, core + 2 * p))
             )
         else:
-            kept = pltpu.make_async_copy(post.at[s, p], o_ref.at[mine, k_part], local.at[1])
-            kept.start()
+            last = pltpu.make_async_copy(post.at[s, p], o_ref.at[mine, k_part], local.at[1])
+            last.start()
         if k % 2:
             yield
     own.wait()
-    kept.wait()
+    last.wait()
     for _, back in finals:
         back.wait_recv()
     for out, _ in finals:
@@ -914,8 +934,12 @@
 def home_scratch():
     return [
         pltpu.VMEM((8, 2, QUARTER, 128), jnp.float32),
+        pltpu.VMEM((8, 2, QUARTER, 128), jnp.float32),
         pltpu.VMEM((8, 2, QUARTER, 128), jnp.bfloat16),
+        pltpu.VMEM((2, QUARTER, 128), jnp.float32),
+        pltpu.VMEM((2, QUARTER, 128), jnp.float32),
         DMA((2,)),
+        DMA((8, 2)),
         DMA((8, 2)),
         DMA((8, 2)),
         DMA((16,)),
@@ -1044,6 +1068,7 @@
         hop.start()
         hops.append(hop)
     o_ref[head] = total
+    yield
     for o, other in enumerate(others):
         send(q_ref, o_ref.at[other], h_send.at[o], h_recv.at[other], seq, other).wait_recv()
     for hop in hops:
@@ -1145,125 +1170,90 @@
             part[step * k : step * (k + 1), :] = total.astype(part.dtype)
 
 
-def last_body(utterances, ins, outs, scratch):
-    pairs, (small_ref, first_mods, last_mods) = ins[:-3], ins[-3:]
-    count = len(pairs) // 2
-    parts, scratch = scratch[: count + 2], scratch[count + 2 :]
-    sums, inbox = scratch[:3], scratch[3:5]
-    r_send, r_recv, h_send, h_recv = scratch[5:9]
+def keeper_body(ins, outs, scratch):
+    (x_ref,), (o_ref,), (r_send, r_recv) = ins, outs, scratch
+    seq = lax.axis_index("seq")
+    head = lax.axis_index("head")
+    goal = (2 * head + seq // 4, lax.rem(seq, 4))
+    source = (4 * lax.rem(seq, 2) + head, seq // 2)
+    stays = jnp.logical_and(goal[0] == seq, goal[1] == head)
+    moves = jnp.logical_not(stays)
+
+    @pl.when(moves)
+    def _():
+        hail(*source)
+
+    yield jnp.where(stays, 0, 1)
+
+    @pl.when(moves)
+    def _():
+        send(x_ref, o_ref, r_send, r_recv, *goal).start()
+
+    @pl.when(stays)
+    def _():
+        o_ref[...] = x_ref[...]
+
+    yield
+
+    @pl.when(moves)
+    def _():
+        hop = send(x_ref, o_ref, r_send, r_recv, *goal)
+        hop.wait_recv()
+        hop.wait_send()
+
+
+def head_sum_body(ins, outs, scratch):
+    inbox, (h_send, h_recv) = scratch[: len(ins)], scratch[len(ins) :]
     seq = lax.axis_index("seq")
     head = lax.axis_index("head")
     others = [lax.rem(head + o, 4) for o in (2, 1, 3)]
-    goal = (2 * head + seq // 4, lax.rem(seq, 4))
-    source = (4 * lax.rem(seq, 2) + head, seq // 2)
-    stays = jnp.logical_and(goal[0] == seq, goal[1] == head)
-    columns = (first_mods.shape[1] + last_mods.shape[1]) // 32
-
-    @pl.when(jnp.logical_not(stays))
-    def _():
-        hail(*source)
-
-    def product(i):
-        return partial(inner_product, pairs[2 * i], pairs[2 * i + 1], parts[2 + i])
-
-    def make_small():
-        for k in range(32):
-            parts[0][k // 4, 16 * (k % 4) : 16 * (k % 4 + 1), :16] = small_ref[:, 16 * k : 16 * (k + 1)]
-
-    def make_mods():
-        wide = first_mods.shape[1]
-        for k in range(32):
-            low_end, high_end = columns * k, columns * (k + 1)
-            at = slice(utterances * (k % 4), utterances * (k % 4 + 1))
-            if high_end <= wide:
-                parts[1][k // 4, at, :columns] = first_mods[:utterances, low_end:high_end]
-            elif low_end >= wide:
-                parts[1][k // 4, at, :columns] = last_mods[:utterances, low_end - wide : high_end - wide]
-            else:
-                cut = wide - low_end
-                parts[1][k // 4, at, :cut] = first_mods[:utterances, low_end:]
-                parts[1][k // 4, at, cut:columns] = last_mods[:utterances, : high_end - wide]
-
-    order = list(range(2, count + 2)) + [0, 1]
-    makers = [product(i) for i in range(count)] + [make_small, make_mods]
-    results = list(outs[: count - 1]) + list(sums)
-    inner = seq_scatter_body([parts[k] for k in order], results, scratch[9:], makers)
-    yield next(inner) + greet([(seq, other) for other in others]) + jnp.where(stays, 0, 1)
-    parts[0][...] = jnp.zeros_like(parts[0])
-    parts[1][...] = jnp.zeros_like(parts[1])
-    for _ in inner:
-        yield
+    yield greet([(seq, other) for other in others])
     hops = []
 
-    def rows(i, h):
-        count_of = sums[1 + i].shape[0] // 4
+    def rows(block, h):
+        count_of = block.shape[0] // 4
         return pl.ds(pl.multiple_of(h * count_of, 8), count_of)
 
-    @pl.when(jnp.logical_not(stays))
-    def _():
-        send(sums[0], outs[count - 1], r_send, r_recv, *goal).start()
-
-    @pl.when(stays)
-    def _():
-        outs[count - 1][...] = sums[0][...]
-
-    for i in range(2):
-        block = sums[1 + i]
+    for i, block in enumerate(ins):
         for o, other in enumerate(others):
             hop = send(
-                block.at[rows(i, other)], inbox[i].at[head], h_send.at[i, o], h_recv.at[i, head], seq, other
+                block.at[rows(block, other)], inbox[i].at[head], h_send.at[i, o], h_recv.at[i, head], seq, other
             )
             hop.start()
             hops.append(hop)
-        inbox[i][head] = block[rows(i, head), :]
-    for i in range(2):
+        inbox[i][head] = block[rows(block, head), :]
+    yield
+    for i, block in enumerate(ins):
         for o, other in enumerate(others):
             send(
-                sums[1 + i].at[rows(i, other)],
-                inbox[i].at[other],
-                h_send.at[i, o],
-                h_recv.at[i, other],
-                seq,
-                other,
+                block.at[rows(block, other)], inbox[i].at[other], h_send.at[i, o], h_recv.at[i, other], seq, other
             ).wait_recv()
-        outs[count + i][...] = inbox[i][0] + inbox[i][1] + inbox[i][2] + inbox[i][3]
+        outs[i][...] = inbox[i][0] + inbox[i][1] + inbox[i][2] + inbox[i][3]
     for hop in hops:
         hop.wait_send()
 
-    @pl.when(jnp.logical_not(stays))
-    def _():
-        hop = send(sums[0], outs[count - 1], r_send, r_recv, *goal)
-        hop.wait_recv()
-        hop.wait_send()
-
-
-def last_gradients(pairs, small, first_mods, last_mods, utterances):
-    columns = (first_mods.shape[1] + last_mods.shape[1]) // 32
-    shapes = []
-    for k, (left, right) in enumerate(pairs):
-        m, n = left.shape[2], right.shape[2]
-        shapes.append((m, n) if k in LAST_BY_COLUMNS else (8, m // 8, n))
-    blocks = [(8, 64, 128), (8, 4 * utterances, columns + -columns % 128)]
-    kept = [s[1:] if len(s) == 3 else (s[0], s[1] // 8) for s in shapes]
-    tails = [s[1:] for s in blocks]
-    short = [(s[0] // 4,) + s[1:] for s in tails]
-    kinds = [jnp.bfloat16] * len(shapes) + [jnp.float32] * 2
-    return Task(
-        partial(last_body, utterances),
-        [a for pair in pairs for a in pair] + [small, first_mods, last_mods],
-        [jax.ShapeDtypeStruct(s, jnp.float32) for s in kept + short],
-        [pltpu.VMEM(s, jnp.float32) for s in blocks]
-        + [pltpu.VMEM(s, jnp.bfloat16) for s in shapes]
-        + [pltpu.VMEM(s, jnp.float32) for s in kept[-1:] + tails]
-        + [pltpu.VMEM((4,) + s, jnp.float32) for s in short]
-        + [DMA, DMA, DMA((2, 3)), DMA((2, 4))]
-        + seq_scratch(kept + tails, kinds),
-        VMEM,
-        VMEM,
-    )
-
-
-LAST_BY_COLUMNS = (0,)
+
+def cut_small(small_ref, blocks):
+    blocks[...] = jnp.zeros_like(blocks)
+    for k in range(32):
+        blocks[k // 4, 16 * (k % 4) : 16 * (k % 4 + 1), :16] = small_ref[:, 16 * k : 16 * (k + 1)]
+
+
+def cut_mods(utterances, first_mods, last_mods, blocks):
+    wide = first_mods.shape[1]
+    columns = (wide + last_mods.shape[1]) // 32
+    blocks[...] = jnp.zeros_like(blocks)
+    for k in range(32):
+        start, end = columns * k, columns * (k + 1)
+        at = slice(utterances * (k % 4), utterances * (k % 4 + 1))
+        if end <= wide:
+            blocks[k // 4, at, :columns] = first_mods[:utterances, start:end]
+        elif start >= wide:
+            blocks[k // 4, at, :columns] = last_mods[:utterances, start - wide : end - wide]
+        else:
+            cut = wide - start
+            blocks[k // 4, at, :cut] = first_mods[:utterances, start:]
+            blocks[k // 4, at, cut:columns] = last_mods[:utterances, : end - wide]
 
 
 def places_of(rows, bounds):
@@ -1298,7 +1288,7 @@
 
 
 def turns_body(ins, outs, scratch):
-    (lengths, rates_ref), (q_cos, q_sin, k_cos, k_sin) = ins, outs
+    (lengths, rates_ref), (q_cos, q_sin) = ins, outs
     yield 0
     yield
     bounds = bounds_of(lengths)
@@ -1313,9 +1303,6 @@
         at = pl.ds(pl.multiple_of(sub * HALF, HALF), HALF)
         q_cos[source, at, :] = jnp.cos(angles)
         q_sin[source, at, :] = jnp.sin(angles)
-        angles = places_of(column(first, QUARTER), bounds) * rates_ref[1:2, :]
-        k_cos[source, sub] = jnp.cos(angles)
-        k_sin[source, sub] = jnp.sin(angles)
         return carry
 
     for part in range(4):
@@ -1325,8 +1312,7 @@
 
 def turns(lengths, rates):
     query = jax.ShapeDtypeStruct((8, QUARTER, 128), jnp.float32)
-    key = jax.ShapeDtypeStruct((8, 2, QUARTER, 128), jnp.float32)
-    return Task(turns_body, [lengths, rates], [query, query, key, key], [], [SMEM, VMEM], VMEM)
+    return Task(turns_body, [lengths, rates], [query, query], [], [SMEM, VMEM], VMEM)
 
 
 QUARTER = 256
@@ -1418,20 +1404,25 @@
     for bound in bounds:
         low = jnp.where(bound <= top, bound, low)
     first = low // 128 * 128
-    count = (high - first + SPAN - 1) // SPAN
+    halves = (high - first + SPAN // 2 - 1) // (SPAN // 2)
+    count, rest = halves // 2, lax.rem(halves, 2)
     in_low = (low - first + SPAN - 1) // SPAN
     in_high = (high - first) // SPAN
     plain = jnp.logical_and(base_end == high, in_low < in_high)
-    ends = (count, jnp.where(plain, in_low, count), jnp.where(plain, in_high, count))
+    ends = (count, jnp.where(plain, in_low, count), jnp.where(plain, in_high, count), rest)
     rows = top + lax.broadcasted_iota(jnp.int32, (1, QUARTER), 1)
     return source, sub, pl.multiple_of(first, 128), ends, limits(rows, bounds)
 
 
-def in_three(ends, body, carry):
-    count, in_low, in_high = ends
-    carry = lax.fori_loop(0, in_low, partial(body, True), carry)
-    carry = lax.fori_loop(in_low, in_high, partial(body, False), carry)
-    return lax.fori_loop(in_high, count, partial(body, True), carry)
+def in_spans(ends, body, carry, edges=False):
+    count, in_low, in_high, rest = ends
+    if edges:
+        carry = lax.fori_loop(0, in_low, partial(body, SPAN, True), carry)
+        carry = lax.fori_loop(in_low, in_high, partial(body, SPAN, False), carry)
+        carry = lax.fori_loop(in_high, count, partial(body, SPAN, True), carry)
+    else:
+        carry = lax.fori_loop(0, count, partial(body, SPAN, False), carry)
+    return lax.fori_loop(count, count + rest, partial(body, SPAN // 2, edges), carry)
 
 
 def masked(raw, place, limit):
@@ -1454,36 +1445,36 @@
         at = pl.ds(pl.multiple_of(sub * HALF, HALF), HALF)
         query = opened(q_ref[source, at, :].astype(jnp.float32)).astype(jnp.bfloat16)
 
-        def scores(edge, i, top):
+        def scores(size, edge, i, top):
             place = pl.multiple_of(first + i * SPAN, 128)
             raw = lax.dot_general(
-                pairs[pl.ds(place, SPAN), :], query, ROWS_TO_ROWS, preferred_element_type=jnp.float32
+                pairs[pl.ds(place, size), :], query, ROWS_TO_ROWS, preferred_element_type=jnp.float32
             )
             if edge:
                 raw = masked(raw, place, limit)
-            held[i] = raw
+            held[i, pl.ds(0, size), :] = raw
             return fold(jnp.maximum, top, raw)
 
-        top = in_three(ends, scores, jnp.full((8, QUARTER), -1e30, jnp.float32))
+        top = in_spans(ends, scores, jnp.full((8, QUARTER), -1e30, jnp.float32), True)
         top = jnp.max(top, axis=0, keepdims=True)
 
-        def weights(i, total):
-            raised = jnp.exp(held[i] - top)
-            held[i] = raised
+        def weights(size, edge, i, total):
+            raised = jnp.exp(held[i, pl.ds(0, size), :] - top)
+            held[i, pl.ds(0, size), :] = raised
             return fold(jnp.add, total, raised)
 
-        total = lax.fori_loop(0, ends[0], weights, jnp.zeros((8, QUARTER), jnp.float32))
+        total = in_spans(ends, weights, jnp.zeros((8, QUARTER), jnp.float32))
         total = jnp.sum(total, axis=0, keepdims=True)
         share = 1.0 / total
 
-        def mix(i, acc):
-            probs = (held[i] * share).astype(jnp.bfloat16)
+        def mix(size, edge, i, acc):
+            probs = (held[i, pl.ds(0, size), :] * share).astype(jnp.bfloat16)
             place = pl.multiple_of(first + i * SPAN, 128)
             return acc + jnp.dot(
-                turned[:, pl.ds(place, SPAN)], probs, preferred_element_type=jnp.float32
+                turned[:, pl.ds(place, size)], probs, preferred_element_type=jnp.float32
             )
 
-        acc = lax.fori_loop(0, ends[0], mix, jnp.zeros((128, QUARTER), jnp.float32))
+        acc = in_spans(ends, mix, jnp.zeros((128, QUARTER), jnp.float32))
         o_ref[source, at, :] = closed(swap_halves(acc.T)).astype(jnp.bfloat16)
         l_ref[source, sub] = jnp.broadcast_to(top + jnp.log(total), (8, QUARTER))
         return carry
@@ -1532,36 +1523,36 @@
         both = jnp.concatenate([query, grad], axis=0).astype(jnp.bfloat16)
         logsum = l_ref[source, sub][:1, :]
 
-        def slopes(edge, i, inner):
+        def slopes(size, edge, i, inner):
             place = pl.multiple_of(first + i * SPAN, 128)
             pair = lax.dot_general(
-                pairs[pl.ds(place, SPAN), :], both, ROWS_TO_ROWS, preferred_element_type=jnp.float32
+                pairs[pl.ds(place, size), :], both, ROWS_TO_ROWS, preferred_element_type=jnp.float32
             )
             raw, d_probs = pair[:, :QUARTER], pair[:, QUARTER:]
             if edge:
                 raw = masked(raw, place, limit)
             probs = jnp.exp(raw - logsum)
-            held_p[i] = probs
-            held_d[i] = d_probs
+            held_p[i, pl.ds(0, size), :] = probs
+            held_d[i, pl.ds(0, size), :] = d_probs
             return fold(jnp.add, inner, probs * d_probs)
 
-        inner = in_three(ends, slopes, jnp.zeros((8, QUARTER), jnp.float32))
+        inner = in_spans(ends, slopes, jnp.zeros((8, QUARTER), jnp.float32), True)
         inner = jnp.sum(inner, axis=0, keepdims=True)
 
-        def mix(i, acc):
+        def mix(size, edge, i, acc):
             place = pl.multiple_of(first + i * SPAN, 128)
-            probs = held_p[i]
-            d_scores = (probs * (held_d[i] - inner)).astype(jnp.bfloat16)
-            dkv_ref[pl.ds(place, SPAN), :] += jnp.dot(
+            probs = held_p[i, pl.ds(0, size), :]
+            d_scores = (probs * (held_d[i, pl.ds(0, size), :] - inner)).astype(jnp.bfloat16)
+            dkv_ref[pl.ds(place, size), :] += jnp.dot(
                 jnp.concatenate([d_scores, probs.astype(jnp.bfloat16)], axis=1),
                 both,
                 preferred_element_type=jnp.float32,
             )
             return acc + jnp.dot(
-                turned[:, pl.ds(place, SPAN)], d_scores, preferred_element_type=jnp.float32
+                turned[:, pl.ds(place, size)], d_scores, preferred_element_type=jnp.float32
             )
 
-        acc = lax.fori_loop(0, ends[0], mix, jnp.zeros((128, QUARTER), jnp.float32))
+        acc = in_spans(ends, mix, jnp.zeros((128, QUARTER), jnp.float32))
         d_query = closed(acc.T) * 0.125
         d_query = d_query * c_ref[source, at, :] + turn(d_query * s_ref[source, at, :], -1)
         dq_ref[source, at, :] = d_query.astype(jnp.bfloat16)
@@ -2203,18 +2194,17 @@
     )
 
 
-def back_body(ins, outs, scratch):
+def back_body(utterances, ins, outs, scratch):
     (
         lengths,
+        rates_ref,
         dq_ref,
-        dkv_ref,
-        k_cos,
-        k_sin,
+        dkv_hbm,
         d_attn_ref,
         qkv_hbm,
         hidden_ref,
         d_middle_ref,
-        mods_ref,
+        mods_hbm,
         join_ref,
         shrink_all,
         expand_all,
@@ -2229,68 +2219,133 @@
         ext_ref,
         attn_hbm,
         grn_ref,
-        d_ffn_ref,
+        d_ffn_hbm,
         up_part,
         gelu_all,
+        context_hbm,
+        text_hbm,
+        joins_hbm,
+        last_mods,
     ) = ins
     (
         mel_ref,
         text_ref,
-        d_mods_ref,
-        small_ref,
         own_ref,
         qkv_grad,
-        d_attn_all,
-        d_joined_all,
-        d_branch_all,
-        d_expanded_all,
-        grn_all,
         up_grad,
         down_grad,
+        out_grad,
+        shrink_grad,
+        expand_grad,
+        join_grad,
+        small_sum,
+        mods_sum,
     ) = outs
     (
         tiles_ref,
         qkv_ref,
         attn_all,
+        context_all,
+        text_all,
+        join_all,
         in_sems,
         d_joined_ref,
         d_branch_ref,
         d_expanded_ref,
         d_qkv_ref,
         d_qkv_all,
+        d_attn_all,
+        d_joined_all,
+        d_branch_all,
+        d_expanded_all,
+        grn_all,
+        d_ffn_all,
         qkv_part,
-        d_ffn_all,
         down_part,
-    ) = scratch[:12]
-    scratch = scratch[12:]
+        out_part,
+        shrink_part,
+        expand_part,
+        join_part,
+        small_part,
+        mods_part,
+        join_total,
+        small_total,
+        mods_total,
+        d_mods_ref,
+        small_ref,
+        mods_ref,
+    ) = scratch[:32]
+    scratch = scratch[32:]
     d_in_ref, d_text_ref, d_grn_ref, sums_ref, total_ref, d_norm_ref, ratio_ref, d_conv_ref, d_ext_ref = (
         scratch[:9]
     )
     rim_sems, rest = scratch[9], scratch[10:]
     bounds = bounds_of(lengths)
-    swap = exchange_body((d_qkv_ref,), (d_qkv_all,), rest[:3])
-    branch_out = gather_body(1, (d_branch_ref,), (d_branch_all,), rest[3:10])
-    expanded_out = exchange_body((d_expanded_ref,), (d_expanded_all,), rest[10:13])
-    sums = all_sum_body((sums_ref,), (total_ref, own_ref), rest[13:22])
-    joined_out = exchange_body((d_joined_ref,), (d_joined_all,), rest[22:25])
+    taken = [0]
+
+    def take(count):
+        taken[0] += count
+        return rest[taken[0] - count : taken[0]]
+
+    swap = exchange_body((d_qkv_ref,), (d_qkv_all,), take(3))
+    branch_out = gather_body(1, (d_branch_ref,), (d_branch_all,), take(7))
+    expanded_out = exchange_body((d_expanded_ref,), (d_expanded_all,), take(3))
+    sums = all_sum_body((sums_ref,), (total_ref, own_ref), take(9))
+    joined_out = exchange_body((d_joined_ref,), (d_joined_all,), take(3))
     rim = rim_body(d_conv_ref, d_ext_ref, rim_sems)
-    scatter = seq_scatter_body((qkv_part,), (qkv_grad,), rest[25:34])
-    home = home_body((dq_ref, dkv_ref, k_cos, k_sin), (tiles_ref,), rest[34:43])
-    attns = gather_body(2, (d_attn_ref,), (d_attn_all,), rest[43:50])
-    d_ffns = gather_body(2, (d_ffn_ref,), (d_ffn_all,), rest[50:57])
-    grns = exchange_body((grn_ref,), (grn_all,), rest[57:60])
+    scatter = seq_scatter_body(
+        (qkv_part, out_part),
+        (qkv_grad, out_grad),
+        take(13),
+        [None, partial(inner_product, context_all, d_attn_all, out_part)],
+    )
+    home = home_body((lengths, rates_ref, dq_ref, dkv_hbm), (tiles_ref,), take(13))
+    attns = gather_body(2, (d_attn_ref,), (d_attn_all,), take(7))
+    grns = exchange_body((grn_ref,), (grn_all,), take(3))
     early = seq_scatter_body(
         (up_part, down_part),
         (up_grad, down_grad),
-        rest[60:],
+        take(13),
         [None, partial(inner_product, gelu_all, d_ffn_all, down_part)],
     )
+    late = seq_scatter_body(
+        (shrink_part, join_part),
+        (shrink_grad, join_total),
+        take(13),
+        [
+            partial(inner_product, d_branch_all, grn_all, shrink_part),
+            partial(inner_product, d_joined_all, join_all, join_part),
+        ],
+    )
+    last = seq_scatter_body(
+        (expand_part, small_part, mods_part),
+        (expand_grad, small_total, mods_total),
+        take(17),
+        [
+            partial(inner_product, text_all, d_expanded_all, expand_part),
+            partial(cut_small, small_ref, small_part),
+            partial(cut_mods, utterances, d_mods_ref, last_mods, mods_part),
+        ],
+    )
+    keeper = keeper_body((join_total,), (join_grad,), take(2))
+    heads = head_sum_body((small_total, mods_total), (small_sum, mods_sum), take(4))
     running = (
-        swap, branch_out, expanded_out, sums, rim, joined_out, scatter, home, attns, d_ffns, grns, early
+        swap, branch_out, expanded_out, sums, rim, joined_out, scatter, home, attns, grns,
+        early, late, last, keeper, heads,
     )
     arriving = [
-        pltpu.make_async_copy(qkv_hbm, qkv_ref, in_sems.at[0]),
-        pltpu.make_async_copy(attn_hbm, attn_all, in_sems.at[1]),
+        pltpu.make_async_copy(source, target, in_sems.at[k])
+        for k, (source, target) in enumerate(
+            (
+                (qkv_hbm, qkv_ref),
+                (attn_hbm, attn_all),
+                (context_hbm, context_all),
+                (text_hbm, text_all),
+                (joins_hbm, join_all),
+                (d_ffn_hbm, d_ffn_all),
+                (mods_hbm.at[:, pl.ds(1024, 1024)], mods_ref),
+            )
+        )
     ]
     for copy in arriving:
         copy.start()
@@ -2298,12 +2353,10 @@
     next(home)
     next(attns)
     next(grns)
-    next(d_ffns)
-    for _ in home:
-        pass
+    for step, _ in enumerate(home):
+        if step in (5, 6):
+            next(attns)
     for _ in attns:
-        pass
-    for _ in d_ffns:
         pass
     for copy in arriving:
         copy.wait()
@@ -2336,7 +2389,7 @@
 
     lax.fori_loop(0, 4, enter, 0)
     yield
-    scale = three(mods_ref[:, 1024:2048])
+    scale = three(mods_ref[...])
     d_mods_ref[...] = jnp.zeros_like(d_mods_ref)
 
     def hidden_back(at, i):
@@ -2385,9 +2438,9 @@
         return carry
 
     lax.fori_loop(0, 4, grn_back, 0)
+    next(sums)
     next(early)
     next(early)
-    next(sums)
     for _ in swap:
         pass
 
@@ -2406,11 +2459,11 @@
 
     lax.fori_loop(0, 8, qkv_grads, 0)
     next(scatter)
-    yield
+    next(sums)
+    next(joined_out)
+    next(branch_out)
     for _ in sums:
         pass
-    next(joined_out)
-    next(branch_out)
     d_ratio = total_ref[...]
     d_mean = -jnp.sum(jnp.sum(d_ratio * norm, axis=2, keepdims=True), axis=0, keepdims=True) / (
         mean * mean
@@ -2446,7 +2499,6 @@
     by_rows(32, norm_back)
     next(rim)
     next(scatter)
-    yield
 
     def taps_back(at, i):
         rows = first + i + lax.broadcasted_iota(jnp.int32, (32, 1), 0)
@@ -2474,69 +2526,111 @@
         text_ref[at, :] = total
 
     by_rows(32, text_back)
-    for one in (early, scatter, grns, branch_out, joined_out, expanded_out):
+    next(scatter)
+    for one in (grns, joined_out, branch_out):
         for _ in one:
             pass
-
-
-def text_backward(operands):
+    next(late)
+    for _ in expanded_out:
+        pass
+    next(last)
+    for one in (early, scatter, late):
+        for _ in one:
+            pass
+    next(keeper)
+    for _ in last:
+        pass
+    next(heads)
+    for one in (keeper, heads):
+        for _ in one:
+            pass
+
+
+def text_backward(operands, utterances):
     wide, width = 1024, 512
+    columns = 6 * wide // 32
+    block = 4 * utterances, columns + -columns % 128
     outs = [
-        (f32(ROWS, wide), VMEM),
-        (f32(ROWS, width), VMEM),
-        (f32(16, 2 * wide), VMEM),
-        (f32(16, width), VMEM),
-        (f32(16, 256), VMEM),
-        (f32(128, 768), VMEM),
-        (low(4, ROWS, wide), HBM),
-        (low(4, ROWS, 256), HBM),
-        (low(4, ROWS, width), HBM),
-        (low(4, ROWS, 256), HBM),
-        (low(4, ROWS, 256), HBM),
-        (f32(128, 512), VMEM),
-        (f32(512, 128), VMEM),
+        f32(ROWS, wide),
+        f32(ROWS, width),
+        f32(16, 256),
+        f32(128, 768),
+        f32(128, 512),
+        f32(512, 128),
+        f32(256, 128),
+        f32(64, 256),
+        f32(64, 256),
+        f32(32, 512),
+        f32(16, 128),
+        f32(utterances, block[1]),
     ]
+    swap = [DMA((1,)), DMA((1, 3)), DMA((1, 4))]
+    half = [jnp.bfloat16] * 3
+    full = [jnp.bfloat16, jnp.float32, jnp.float32]
     return Task(
-        back_body,
+        partial(back_body, utterances),
         operands,
-        [o for o, _ in outs],
+        outs,
         [
             room(low(16, HALF + QUARTER, 128)),
             room(low(4, 3, wide, 256)),
             room(low(4, ROWS, wide)),
-            DMA((2,)),
+            room(low(4, ROWS, 256)),
+            room(low(4, ROWS, width)),
+            room(low(4, ROWS, width)),
+            DMA((7,)),
             room(low(4, ROWS, 256)),
             room(low(ROWS, width)),
             room(low(4, ROWS, 256)),
             room(low(4, ROWS, 768)),
             room(low(4, ROWS, 768)),
+            room(low(4, ROWS, wide)),
+            room(low(4, ROWS, 256)),
+            room(low(4, ROWS, width)),
+            room(low(4, ROWS, 256)),
+            room(low(4, ROWS, 256)),
+            room(low(4, ROWS, wide)),
             room(low(8, 128, 768)),
-            room(low(4, ROWS, wide)),
             room(low(512, wide)),
-            pltpu.VMEM((ROWS, wide), jnp.float32),
-            pltpu.VMEM((ROWS, width), jnp.float32),
-            pltpu.VMEM((4, ROWS, 256), jnp.float32),
-            pltpu.VMEM((4, 16, 256), jnp.float32),
-            pltpu.VMEM((4, 16, 256), jnp.float32),
-            pltpu.VMEM((4, 16, 256), jnp.float32),
-            pltpu.VMEM((4, 16, 256), jnp.float32),
-            pltpu.VMEM((ROWS, width), jnp.float32),
-            pltpu.VMEM((ROWS + 16, width), jnp.float32),
+            room(low(256, wide)),
+            room(low(8, 64, 256)),
+            room(low(8, 64, 256)),
+            room(low(8, 32, 512)),
+            room(f32(8, 64, 128)),
+            room(f32(8, *block)),
+            room(f32(32, 512)),
+            room(f32(64, 128)),
+            room(f32(*block)),
+            room(f32(16, 2 * wide)),
+            room(f32(16, width)),
+            room(f32(16, wide)),
+            room(f32(ROWS, wide)),
+            room(f32(ROWS, width)),
+            room(f32(4, ROWS, 256)),
+            room(f32(4, 16, 256)),
+            room(f32(4, 16, 256)),
+            room(f32(4, 16, 256)),
+            room(f32(4, 16, 256)),
+            room(f32(ROWS, width)),
+            room(f32(ROWS + 16, width)),
             DMA((4,)),
         ]
-        + [DMA((1,)), DMA((1, 3)), DMA((1, 4))]
+        + swap
         + gather_scratch(1, 1)
-        + [DMA((1,)), DMA((1, 3)), DMA((1, 4))]
+        + swap
         + all_sum_scratch(16, 256)
-        + [DMA((1,)), DMA((1, 3)), DMA((1, 4))]
-        + seq_scratch([(128, 768)], [jnp.bfloat16])
+        + swap
+        + seq_scratch([(128, 768), (256, 128)], half[:2])
         + home_scratch()
         + gather_scratch(1, 2)
-        + gather_scratch(1, 2)
-        + [DMA((1,)), DMA((1, 3)), DMA((1, 4))]
-        + seq_scratch([(128, 512), (512, 128)], [jnp.bfloat16] * 2),
-        [SMEM] + [VMEM] * 4 + [HBM, HBM] + [VMEM] * 15 + [HBM] * 4 + [VMEM],
-        [s for _, s in outs],
+        + swap
+        + seq_scratch([(128, 512), (512, 128)], half[:2])
+        + seq_scratch([(64, 256), (32, 512)], half[:2])
+        + seq_scratch([(64, 256), (64, 128), block], full)
+        + [DMA, DMA]
+        + [room(f32(4, 16, 128)), room(f32(4, utterances, block[1])), DMA((2, 3)), DMA((2, 4))],
+        [SMEM, VMEM, VMEM, HBM, VMEM, HBM] + [VMEM] * 2 + [HBM] + [VMEM] * 12 + [HBM] * 4 + [VMEM] + [HBM] * 3 + [VMEM],
+        VMEM,
     )
 
 
@@ -2670,14 +2764,16 @@
     qkv_near = qkv_weight.transpose(1, 0, 2)
     attn_all, up_near, down_near = lax.optimization_barrier((attn_all, up_weight, down_weight))
     up_full, down_full = (lax.all_gather(w, "head", axis=0) for w in (up_near, down_near))
-    (packed,), (query_cos, query_sin, key_cos, key_sin), (join_all, out_full) = communicate(
+    (packed,), (query_cos, query_sin), (join_all, out_full) = communicate(
         [
             spread_out(rows_of(attn_all), qkv_near, own_cos, own_sin),
             turns(lengths, rates),
-            gathered([join_low, out_weight]),
+            gathered([join_low, out_weight], patience=12),
         ],
         1,
     )
+    packed, d_ffn_late = lax.optimization_barrier((packed, d_ffn_low))
+    d_ffn_all = lax.all_gather(d_ffn_late, "head", axis=0)
     context_here, logsum = attend(lengths, packed)
 
     (
@@ -2717,27 +2813,25 @@
         (
             grad_mel,
             grad_text,
-            d_mods_attn,
-            small,
             own_sums,
             qkv,
-            d_attn_all,
-            d_joined_all,
-            d_branch_all,
-            d_expanded_all,
-            grn_all,
             up,
             down,
+            out,
+            shrink,
+            expand,
+            join,
+            small,
+            mod,
         ),
     ) = communicate(
         [
             text_backward(
                 [
                     lengths,
+                    rates,
                     d_query,
                     d_pair,
-                    key_cos,
-                    key_sin,
                     d_attn_low,
                     qkv_full,
                     hidden,
@@ -2757,32 +2851,18 @@
                     extended,
                     attn_all,
                     grn_low,
-                    d_ffn_low,
+                    d_ffn_all,
                     up_part,
                     gelu_all,
-                ]
+                    context_all,
+                    text_all,
+                    join_all,
+                    d_mods_middle,
+                ],
+                utterances,
             )
         ],
         3,
-    )
-
-    columns = mods.shape[1] // 32
-    ((out, shrink, expand, join, small, mod),) = communicate(
-        [
-            last_gradients(
-                [
-                    (context_all, d_attn_all),
-                    (d_branch_all, grn_all),
-                    (text_all, d_expanded_all),
-                    (d_joined_all, join_all),
-                ],
-                small,
-                d_mods_attn,
-                d_mods_middle,
-                utterances,
-            )
-        ],
-        4,
     )
     grad_text, grad_mel, expand, shrink, join, out, up, down, qkv, conv, gain, bias, mod, pair = finish(
         qkv,
@@ -2790,9 +2870,9 @@
         mod,
         time_embed,
         own_sums,
-        [],
+        [d_ffn_late],
         [grad_text, grad_mel, expand, shrink, join, out, up, down],
-        columns,
+        mods.shape[1] // 32,
     )
     return (
         layer_output,

time: 460 us -> 435 us (0.946)
  Pallas kernels: 432 us -> 408 us
    pallas_call x5 -> x4, Pallas kernels: 338 us -> 313 us  [communicate(): pl.pallas_call(kernel, out_shape=[o for t in tasks for o in t.outs], in_s...]
  transfers between devices with their start and end apart: 3 -> 4, of which waited for: 0 -> 0; matrix products, arithmetic and copies ran while one was open for 0% -> 1% of each run, Pallas kernels for 30% -> 49%
where the time goes in v6:
time: 435 us; the launch traced here: 429 us
  Pallas kernels  408 us (94%)
  between operations  14.3 us (3%)
    pallas_call x4, Pallas kernels, communicate(): pl.pallas_call(kernel, out_shape=[o for t in tasks for o in t.outs], in_s...  313 us
    pallas_call x1, Pallas kernels, attend_back(): pl.pallas_call(attend_back_kernel, out_shape=[jax.ShapeDtypeStruct((8, QU...  52.5 us
    pallas_call x1, Pallas kernels, attend(): pl.pallas_call(attend_kernel, out_shape=[jax.ShapeDtypeStruct((8, QUARTER...  38.5 us
  transfers between devices with their start and end apart: 4, of which 0 were waited for; matrix products, arithmetic and copies ran while one was open for 1% of the time, Pallas kernels for 49%

profile of v6, /device:TPU:0, one launch (start us, length us, event | category | flops | bytes accessed | tf_op | source)
XLA Modules:
  0.0 429.3 jit_solution(6285792317790449269)
XLA Ops:
  7.2 0.0 all-gather.9.cloned.1.call-start
  7.2 0.1 stack_tile.3
  7.3 0.1 tile.8
  7.4 0.6 select_maximum_fusion.refs_16_.refs_5_.refs_1_
  8.0 56.6 %communicate_0.1 = (f32[272,512]{1,0:T(8,128)}, f32[256,512]{1,0:T(8,128)}, f32[256,128]{1,0:T(8,128)}, bf16[4,512,256]{2,1,0:T(8,128)(2,1)}, bf16[4,256,512]{2,...) custom-call(s32[8]{0:T(128)} %refs_0_.5, ...), custom_call_target="tpu_custom_call" | custom-call | tf_op jit(solution)/shard_map/communicate_0/pallas_call | solution.py:556
  64.7 0.0 all-gather.9.cloned.1.call-update
  64.7 0.0 all-gather.11.cloned.1.call-start
  64.7 0.7 all-gather.11.cloned.1.call-update
  65.4 0.0 all-gather.15.cloned.1.call-start
  65.5 47.4 %communicate_1.1 = (bf16[8,1536,128]{2,1,0:T(8,128)(2,1)}, f32[8,256,128]{2,1,0:T(8,128)}, f32[8,256,128]{2,1,0:T(8,128)}, bf16[4,256,512]{2,1,0:T(8,128)(2,1)}, bf16[4,256,1024]{2,1,0:T(8,128)(2,1)}) custom-call(bf16[1024,1024]{1,0:T(8,128)(2,1)} %bitcast.26, bf16[3,1024,256]{2,1,0:T(8,128)(2,1)} %bitcast.28, f32[1024,128]{1,0:T(8,128)} %get-tuple-element.87.refs_2_, ...), custom_call_target="tpu_custom_call" | custom-call | tf_op jit(solution)/shard_map/communicate_1/pallas_call | solution.py:556
  112.9 0.0 all-gather.15.cloned.1.call-update
  112.9 0.2 all-gather.13.cloned.1.call-start
  113.1 38.5 %attend.1 = (bf16[8,256,128]{2,1,0:T(8,128)(2,1)}, f32[8,2,8,256]{3,2,1,0:T(8,128)}) custom-call(s32[8]{0:T(128)} %refs_0_.5, bf16[8,1536,128]{2,1,0:T(8,128)(2,1)} %get-tuple-element.92.x_ref), custom_call_target="tpu_custom_call" | custom-call | tf_op jit(solution)/shard_map/attend/pallas_call | solution.py:1496
  151.7 0.0 all-gather.9.cloned.1.call-done
  151.7 0.0 all-gather.11.cloned.1.call-done
  151.7 71.6 %communicate_2.1 = (f32[256,1024]{1,0:T(8,128)}, bf16[256,1024]{1,0:T(8,128)(2,1)}, f32[256,1024]{1,0:T(8,128)}, f32[16,4096]{1,0:T(8,128)}, bf16[8,256,128]{2,1...) custom-call(s32[8]{0:T(128)} %refs_0_.5, ...), custom_call_target="tpu_custom_call" | custom-call | tf_op jit(solution)/shard_map/communicate_2/pallas_call | solution.py:556
  223.3 0.0 all-gather.13.cloned.1.call-update
  223.3 0.0 copy-start.1
  223.3 0.0 copy-start.2
  223.3 52.5 %attend_back.1 = (bf16[8,256,128]{2,1,0:T(8,128)(2,1)}, f32[9216,128]{1,0:T(8,128)}) custom-call(s32[8]{0:T(128)} %refs_0_.5, bf16[8,1536,128]{2,1,0:T(8,128)(2,1)} %get-tuple-element.92.x_ref, bf16[8,256,128]{2,1,0:T(8,128)(2,1)} %get-tuple-element.101.g_ref, f32[8,2,8,256]{3,2,1,0:T(8,128)} %get-tuple-element.102.l_ref, ...), custom_call_target="tpu_custom_call" | custom-call | tf_op jit(solution)/shard_map/attend_back/pallas_call | solution.py:1566
  275.9 0.0 copy-done.1
  275.9 0.0 copy-done.2
  275.9 2.2 bitcast_convert_fusion
  278.2 0.0 all-gather.15.cloned.1.call-done
  278.2 0.0 all-gather.13.cloned.1.call-done
  278.2 137.6 %communicate_3.1 = (f32[256,1024]{1,0:T(8,128)}, f32[256,512]{1,0:T(8,128)}, f32[16,256]{1,0:T(8,128)}, f32[128,768]{1,0:T(8,128)}, f32[128,512]{1,0:T(8,128)}, ...) custom-call(s32[8]{0:T(128)} %refs_0_.5, ...), custom_call_target="tpu_custom_call" | custom-call | tf_op jit(solution)/shard_map/communicate_3/pallas_call | solution.py:556
  415.7 0.0 copy-start
  415.7 4.3 finish.1
  420.0 1.3 fusion
  421.4 0.0 copy-done
  421.4 1.0 copy.39
  (4 shorter events, 0.0 us)
Async XLA Ops:
  7.2 144.5 %all-gather.9.cloned.1.call-start = ((), (), s32[]{:S(2)}) async-start(), calls=%async_computation | async-start | bytes 5242880 | tf_op jit(solution)/shard_map/all_gather | solution.py:2766
  64.7 87.0 %all-gather.11.cloned.1.call-start = ((), (), s32[]{:S(2)}) async-start(), calls=%async_computation.1 | async-start | bytes 5242880 | tf_op jit(solution)/shard_map/all_gather | solution.py:2766
  65.4 212.7 %all-gather.15.cloned.1.call-start = ((), (), s32[]{:S(2)}) async-start(), calls=%async_computation.3 | async-start | bytes 2621440 | tf_op jit(solution)/shard_map/all_gather | solution.py:2776
  112.9 165.2 %all-gather.13.cloned.1.call-start = ((), (), s32[]{:S(2)}) async-start(), calls=%async_computation.2 | async-start | bytes 7864320 | tf_op jit(solution)/shard_map/all_gather | solution.py:2809
  223.3 52.6 %copy-start.1 = (bf16[4,256,1024]{2,1,0:T(8,128)(2,1)S(1)}, bf16[4,256,1024]{2,1,0:T(8,128)(2,1)}, u32[]{:S(2)}) copy-start(bf16[4,256,1024]{2,1,0:T(8,128)(2,1)} %get-tuple-element.121) | copy-start | bytes 6291460
  223.3 52.6 %copy-start.2 = (bf16[4,256,512]{2,1,0:T(8,128)(2,1)S(1)}, bf16[4,256,512]{2,1,0:T(8,128)(2,1)}, u32[]{:S(2)}) copy-start(bf16[4,256,512]{2,1,0:T(8,128)(2,1)} %get-tuple-element.122) | copy-start | bytes 3145732
  415.7 5.6 %copy-start = (f32[256,1024]{1,0:T(8,128)S(1)}, f32[256,1024]{1,0:T(8,128)}, u32[]{:S(2)}) copy-start(f32[256,1024]{1,0:T(8,128)} %get-tuple-element.172) | copy-start | bytes 3145732
Sparse Core Ops, SparseCore 0:
  64.8 47.1 all-gather.8
  113.6 33.8 all-gather.10
  149.1 33.8 all-gather.14
  223.4 44.9 all-gather.12

commit v7 on v6

--- a/solution.py
+++ b/solution.py
@@ -1996,13 +1996,12 @@
         d_mods_ref,
         d_context_ref,
         ffn_all,
-        context_all,
+        context_ref,
         gelu_all,
         d_up_all,
     ) = outs
     (
         tiles_ref,
-        context_ref,
         ffn_low_ref,
         gelu_ref,
         d_up_ref,
@@ -2017,13 +2016,12 @@
         own_sems,
         feed_send,
         feed_recv,
-    ) = scratch[:16]
-    rest = scratch[16:]
+    ) = scratch[:15]
+    rest = scratch[15:]
     arrive = rows_heads_body(False, (here_ref,), (tiles_ref,), rest[:3])
     depart = rows_heads_body(True, (d_tiles_ref,), (d_context_ref,), rest[3:6])
-    contexts = exchange_body((context_ref,), (context_all,), rest[6:9])
-    ffns = gather_body(2, (ffn_low_ref,), (ffn_all,), rest[9:16])
-    yield sum(next(one) for one in (arrive, depart, contexts, ffns))
+    ffns = gather_body(2, (ffn_low_ref,), (ffn_all,), rest[6:13])
+    yield sum(next(one) for one in (arrive, depart, ffns))
     seq, head, _, _, _ = head_places()
     bounds = bounds_of(lengths)
     copies = []
@@ -2051,7 +2049,6 @@
         lanes = slice(128 * (pair % 2), 128 * (pair % 2) + 128)
         context_ref[pair // 2, pl.ds(0, HALF), lanes] = upper.astype(jnp.bfloat16)
         context_ref[pair // 2, pl.ds(HALF, HALF), lanes] = lower.astype(jnp.bfloat16)
-    next(contexts)
 
     def project_out(h, carry):
         attn_ref[...] += jnp.dot(context_ref[h], out_ref[h], preferred_element_type=jnp.float32)
@@ -2135,7 +2132,7 @@
             d_tiles_ref[4 * h + 2 * k] = even.astype(jnp.bfloat16)
             d_tiles_ref[4 * h + 2 * k + 1] = odd.astype(jnp.bfloat16)
     next(depart)
-    for one in (ffns, contexts, depart):
+    for one in (ffns, depart):
         for _ in one:
             pass
     for o in range(1, 4):
@@ -2159,7 +2156,7 @@
         (f32(16, 4 * wide), VMEM),
         (low(8, QUARTER, 128), HBM),
         (low(4, ROWS, wide), HBM),
-        (low(4, ROWS, 256), HBM),
+        (low(4, ROWS, 256), VMEM),
         (low(4, ROWS, short), HBM),
         (low(4, ROWS, short), HBM),
     ]
@@ -2169,7 +2166,6 @@
         [o for o, _ in outs],
         [
             pltpu.VMEM((16, HALF, 128), jnp.bfloat16),
-            pltpu.VMEM((4, ROWS, 256), jnp.bfloat16),
             pltpu.VMEM((ROWS, wide), jnp.bfloat16),
             pltpu.VMEM((4, ROWS, short), jnp.bfloat16),
             pltpu.VMEM((4, ROWS, short), jnp.bfloat16),
@@ -2187,7 +2183,6 @@
         ]
         + [DMA, DMA((16,)), DMA((16,))]
         + [DMA, DMA((16,)), DMA((16,))]
-        + [DMA((1,)), DMA((1, 3)), DMA((1, 4))]
         + gather_scratch(1, 2),
         [SMEM, HBM, VMEM, HBM, HBM] + [VMEM] * 4,
         [s for _, s in outs],
@@ -2301,7 +2296,7 @@
     )
     home = home_body((lengths, rates_ref, dq_ref, dkv_hbm), (tiles_ref,), take(13))
     attns = gather_body(2, (d_attn_ref,), (d_attn_all,), take(7))
-    grns = exchange_body((grn_ref,), (grn_all,), take(3))
+    grns = exchange_body((grn_ref, context_hbm), (grn_all, context_all), take(3))
     early = seq_scatter_body(
         (up_part, down_part),
         (up_grad, down_grad),
@@ -2339,7 +2334,6 @@
             (
                 (qkv_hbm, qkv_ref),
                 (attn_hbm, attn_all),
-                (context_hbm, context_all),
                 (text_hbm, text_all),
                 (joins_hbm, join_all),
                 (d_ffn_hbm, d_ffn_all),
@@ -2458,6 +2452,8 @@
         return carry
 
     lax.fori_loop(0, 8, qkv_grads, 0)
+    for _ in grns:
+        pass
     next(scatter)
     next(sums)
     next(joined_out)
@@ -2578,7 +2574,7 @@
             room(low(4, ROWS, 256)),
             room(low(4, ROWS, width)),
             room(low(4, ROWS, width)),
-            DMA((7,)),
+            DMA((6,)),
             room(low(4, ROWS, 256)),
             room(low(ROWS, width)),
             room(low(4, ROWS, 256)),
@@ -2623,7 +2619,7 @@
         + seq_scratch([(128, 768), (256, 128)], half[:2])
         + home_scratch()
         + gather_scratch(1, 2)
-        + swap
+        + [DMA((2,)), DMA((2, 3)), DMA((2, 4))]
         + seq_scratch([(128, 512), (512, 128)], half[:2])
         + seq_scratch([(64, 256), (32, 512)], half[:2])
         + seq_scratch([(64, 256), (64, 128), block], full)
@@ -2784,7 +2780,7 @@
             d_mods_middle,
             d_context,
             ffn_all,
-            context_all,
+            context_blocks,
             gelu_all,
             d_up_all,
         ),
@@ -2854,7 +2850,7 @@
                     d_ffn_all,
                     up_part,
                     gelu_all,
-                    context_all,
+                    context_blocks,
                     text_all,
                     join_all,
                     d_mods_middle,

time: 435 us -> 434 us (level); the launches traced: 429 us -> 434 us
  Pallas kernels: 408 us -> 413 us
    pallas_call x4, Pallas kernels: 313 us -> 318 us  [communicate(): pl.pallas_call(kernel, out_shape=[o for t in tasks for o in t.outs], in_s...]
  transfers between devices with their start and end apart: 4 -> 4, of which waited for: 0 -> 0; matrix products, arithmetic and copies ran while one was open for 1% -> 1% of each run, Pallas kernels for 49% -> 47%
where the time goes in v7:
time: 434 us
  Pallas kernels  413 us (95%)
  between operations  14.3 us (3%)
    pallas_call x4, Pallas kernels, communicate(): pl.pallas_call(kernel, out_shape=[o for t in tasks for o in t.outs], in_s...  318 us
    pallas_call x1, Pallas kernels, attend_back(): pl.pallas_call(attend_back_kernel, out_shape=[jax.ShapeDtypeStruct((8, QU...  52.1 us
    pallas_call x1, Pallas kernels, attend(): pl.pallas_call(attend_kernel, out_shape=[jax.ShapeDtypeStruct((8, QUARTER...  38.3 us
  transfers between devices with their start and end apart: 4, of which 0 were waited for; matrix products, arithmetic and copies ran while one was open for 1% of the time, Pallas kernels for 47%

profile of v7, /device:TPU:0, one launch (start us, length us, event | category | flops | bytes accessed | tf_op | source)
XLA Modules:
  0.0 433.5 jit_solution(1253356657215199754)
XLA Ops:
  7.2 0.0 all-gather.9.cloned.1.call-start
  7.2 0.1 stack_tile.3
  7.3 0.1 tile.8
  7.4 0.6 select_maximum_fusion.refs_16_.refs_5_.refs_1_
  8.0 56.6 %communicate_0.1 = (f32[272,512]{1,0:T(8,128)}, f32[256,512]{1,0:T(8,128)}, f32[256,128]{1,0:T(8,128)}, bf16[4,512,256]{2,1,0:T(8,128)(2,1)}, bf16[4,256,512]{2,...) custom-call(s32[8]{0:T(128)} %refs_0_.5, ...), custom_call_target="tpu_custom_call" | custom-call | tf_op jit(solution)/shard_map/communicate_0/pallas_call | solution.py:556
  64.7 0.0 all-gather.9.cloned.1.call-update
  64.7 0.0 all-gather.11.cloned.1.call-start
  64.7 0.7 all-gather.11.cloned.1.call-update
  65.4 0.0 all-gather.15.cloned.1.call-start
  65.5 47.4 %communicate_1.1 = (bf16[8,1536,128]{2,1,0:T(8,128)(2,1)}, f32[8,256,128]{2,1,0:T(8,128)}, f32[8,256,128]{2,1,0:T(8,128)}, bf16[4,256,512]{2,1,0:T(8,128)(2,1)}, bf16[4,256,1024]{2,1,0:T(8,128)(2,1)}) custom-call(bf16[1024,1024]{1,0:T(8,128)(2,1)} %bitcast.26, bf16[3,1024,256]{2,1,0:T(8,128)(2,1)} %bitcast.28, f32[1024,128]{1,0:T(8,128)} %get-tuple-element.87.refs_2_, ...), custom_call_target="tpu_custom_call" | custom-call | tf_op jit(solution)/shard_map/communicate_1/pallas_call | solution.py:556
  112.9 0.0 all-gather.15.cloned.1.call-update
  112.9 0.2 all-gather.13.cloned.1.call-start
  113.1 38.3 %attend.1 = (bf16[8,256,128]{2,1,0:T(8,128)(2,1)}, f32[8,2,8,256]{3,2,1,0:T(8,128)}) custom-call(s32[8]{0:T(128)} %refs_0_.5, bf16[8,1536,128]{2,1,0:T(8,128)(2,1)} %get-tuple-element.92.x_ref), custom_call_target="tpu_custom_call" | custom-call | tf_op jit(solution)/shard_map/attend/pallas_call | solution.py:1496
  151.4 0.0 all-gather.9.cloned.1.call-done
  151.5 0.0 all-gather.11.cloned.1.call-done
  151.5 67.2 %communicate_2.1 = (f32[256,1024]{1,0:T(8,128)}, bf16[256,1024]{1,0:T(8,128)(2,1)}, f32[256,1024]{1,0:T(8,128)}, f32[16,4096]{1,0:T(8,128)}, bf16[8,256,128]{2,1...) custom-call(s32[8]{0:T(128)} %refs_0_.5, ...), custom_call_target="tpu_custom_call" | custom-call | tf_op jit(solution)/shard_map/communicate_2/pallas_call | solution.py:556
  218.7 0.0 all-gather.13.cloned.1.call-update
  218.7 0.0 copy-start.1
  218.7 0.0 copy-start.2
  218.7 52.1 %attend_back.1 = (bf16[8,256,128]{2,1,0:T(8,128)(2,1)}, f32[9216,128]{1,0:T(8,128)}) custom-call(s32[8]{0:T(128)} %refs_0_.5, bf16[8,1536,128]{2,1,0:T(8,128)(2,1)} %get-tuple-element.92.x_ref, bf16[8,256,128]{2,1,0:T(8,128)(2,1)} %get-tuple-element.101.g_ref, f32[8,2,8,256]{3,2,1,0:T(8,128)} %get-tuple-element.102.l_ref, ...), custom_call_target="tpu_custom_call" | custom-call | tf_op jit(solution)/shard_map/attend_back/pallas_call | solution.py:1566
  270.9 0.0 copy-done.1
  270.9 0.0 copy-done.2
  270.9 2.3 bitcast_convert_fusion
  273.1 0.0 all-gather.15.cloned.1.call-done
  273.1 0.0 all-gather.13.cloned.1.call-done
  273.1 146.8 %communicate_3.1 = (f32[256,1024]{1,0:T(8,128)}, f32[256,512]{1,0:T(8,128)}, f32[16,256]{1,0:T(8,128)}, f32[128,768]{1,0:T(8,128)}, f32[128,512]{1,0:T(8,128)}, ...) custom-call(s32[8]{0:T(128)} %refs_0_.5, ...), custom_call_target="tpu_custom_call" | custom-call | tf_op jit(solution)/shard_map/communicate_3/pallas_call | solution.py:556
  420.0 0.0 copy-start
  420.0 4.3 finish.1
  424.3 1.3 fusion
  425.6 0.0 copy-done
  425.6 1.0 copy.39
  (4 shorter events, 0.0 us)
Async XLA Ops:
  7.2 144.3 %all-gather.9.cloned.1.call-start = ((), (), s32[]{:S(2)}) async-start(), calls=%async_computation | async-start | bytes 5242880 | tf_op jit(solution)/shard_map/all_gather | solution.py:2762
  64.7 86.8 %all-gather.11.cloned.1.call-start = ((), (), s32[]{:S(2)}) async-start(), calls=%async_computation.1 | async-start | bytes 5242880 | tf_op jit(solution)/shard_map/all_gather | solution.py:2762
  65.4 207.7 %all-gather.15.cloned.1.call-start = ((), (), s32[]{:S(2)}) async-start(), calls=%async_computation.3 | async-start | bytes 2621440 | tf_op jit(solution)/shard_map/all_gather | solution.py:2772
  112.9 160.2 %all-gather.13.cloned.1.call-start = ((), (), s32[]{:S(2)}) async-start(), calls=%async_computation.2 | async-start | bytes 7864320 | tf_op jit(solution)/shard_map/all_gather | solution.py:2805
  218.7 52.1 %copy-start.1 = (bf16[4,256,1024]{2,1,0:T(8,128)(2,1)S(1)}, bf16[4,256,1024]{2,1,0:T(8,128)(2,1)}, u32[]{:S(2)}) copy-start(bf16[4,256,1024]{2,1,0:T(8,128)(2,1)} %get-tuple-element.121) | copy-start | bytes 6291460
  218.7 52.1 %copy-start.2 = (bf16[4,256,512]{2,1,0:T(8,128)(2,1)S(1)}, bf16[4,256,512]{2,1,0:T(8,128)(2,1)}, u32[]{:S(2)}) copy-start(bf16[4,256,512]{2,1,0:T(8,128)(2,1)} %get-tuple-element.122) | copy-start | bytes 3145732
  420.0 5.6 %copy-start = (f32[256,1024]{1,0:T(8,128)S(1)}, f32[256,1024]{1,0:T(8,128)}, u32[]{:S(2)}) copy-start(f32[256,1024]{1,0:T(8,128)} %get-tuple-element.172) | copy-start | bytes 3145732
Sparse Core Ops, SparseCore 0:
  64.8 47.1 all-gather.8
  113.6 33.8 all-gather.10
  149.1 28.1 all-gather.14
  218.8 45.6 all-gather.12
